TPU v7x, 32 devices: a whole 2x2x4 slice. The times are simulated.
32 devices in a mesh: shard: 8 (over z, y), ctx: 2 (over core), tp: 2 (over x).
Axes of the slice: x: 2, y: 2, z: 4, core: 2. Of those that a mesh axis runs over, the one named last changes fastest.
Arguments:
- tokens: bfloat16 [8192, 2048], P(('shard', 'ctx')), may hold values from -6 to 6
- segments: int32 [8, 1024], P('shard'), may hold values from 0 to 15, never falling along the last dimension, each value on 1 to 512 neighbouring positions
- gain_attn: bfloat16 [2048], P(('shard', 'ctx')), may hold values from 0.5 to 1.5
- w_query: bfloat16 [2048, 2048], P(('shard', 'ctx'), 'tp'), may hold values from -0.125 to 0.125
- w_key: bfloat16 [2048, 2048], P(('shard', 'ctx'), 'tp'), may hold values from -0.125 to 0.125
- w_value: bfloat16 [2048, 2048], P(('shard', 'ctx'), 'tp'), may hold values from -0.125 to 0.125
- w_out: bfloat16 [2048, 2048], P(('shard', 'ctx'), 'tp'), may hold values from -3 to 3
- gain_mlp: bfloat16 [2048], P(('shard', 'ctx')), may hold values from 0.5 to 1.5
- w_gate: bfloat16 [2048, 8192], P(('shard', 'ctx'), 'tp'), may hold values from -0.125 to 0.125
- w_up: bfloat16 [2048, 8192], P(('shard', 'ctx'), 'tp'), may hold values from -0.125 to 0.125
- w_down: bfloat16 [2048, 8192], P(('shard', 'ctx'), 'tp'), may hold values from -0.0625 to 0.0625
- cotangent: bfloat16 [8192, 2048], P(('shard', 'ctx')), may hold values from -6 to 6
Outputs:
- output: bfloat16 [8192, 2048], P(('shard', 'ctx'))
- grad_tokens: bfloat16 [8192, 2048], P(('shard', 'ctx'))
- grad_gain_attn: float32 [2048], P(('shard', 'ctx'))
- grad_w_query: float32 [2048, 2048], P(('shard', 'ctx'), 'tp')
- grad_w_key: float32 [2048, 2048], P(('shard', 'ctx'), 'tp')
- grad_w_value: float32 [2048, 2048], P(('shard', 'ctx'), 'tp')
- grad_w_out: float32 [2048, 2048], P(('shard', 'ctx'), 'tp')
- grad_gain_mlp: float32 [2048], P(('shard', 'ctx'))
- grad_w_gate: float32 [2048, 8192], P(('shard', 'ctx'), 'tp')
- grad_w_up: float32 [2048, 8192], P(('shard', 'ctx'), 'tp')
- grad_w_down: float32 [2048, 8192], P(('shard', 'ctx'), 'tp')
Inputs may be any that keep to these rules, and one draw needn't show every extreme that they name: `segments`: within each sequence the segment numbers never fall; each number marks one document of consecutive tokens, and some document holds exactly 512 tokens.
All inputs are finite; a program needn't handle non-finite values.
Results may differ from a plain program's by a relative error of at most 0.015.
Values may be sent and summed in bfloat16 or wider, within the bound.
No kernel may reach another device: no remote copies, remote signals or barrier semaphores. Data moves between devices by JAX's collectives and lax.ppermute only.
A program may use at most 320 MiB of HBM per device.

v0:
```python
import math

import jax
import jax.numpy as jnp
from jax import lax
from jax.sharding import PartitionSpec as P

HD = 128
LENGTH = 1024


norm_eps = 1e-05
rope_base = 10000.0


def matmul(left, right):
    return jnp.dot(left, right, preferred_element_type=jnp.float32)


def contract_rows(left, right):
    return lax.dot_general(
        left, right, (((0,), (0,)), ((), ())), preferred_element_type=jnp.float32
    )


def contract_cols(left, right):
    return lax.dot_general(
        left, right, (((1,), (1,)), ((), ())), preferred_element_type=jnp.float32
    )


def norm_parts(values):
    inverse = lax.rsqrt(jnp.mean(values * values, axis=-1, keepdims=True) + norm_eps)
    return (values * inverse, inverse)


def norm_back(grad_scaled, normed, inverse):
    return inverse * (grad_scaled - normed * jnp.mean(grad_scaled * normed, axis=-1, keepdims=True))


def doc_positions(seg_row):
    places = jnp.arange(seg_row.shape[0], dtype=jnp.int32)
    starts_here = jnp.concatenate([jnp.ones((1,), dtype=jnp.bool_), seg_row[1:] != seg_row[:-1]])
    starts = lax.cummax(jnp.where(starts_here, places, jnp.zeros_like(places)), axis=0)
    return places - starts


def rope_tables(positions):
    half_dim = HD // 2
    freqs = rope_base ** (-(jnp.arange(half_dim, dtype=jnp.float32) * (2.0 / HD)))
    angles = positions.astype(jnp.float32)[:, None] * freqs[None, :]
    return (jnp.cos(angles)[:, None, :], jnp.sin(angles)[:, None, :])


def rotate(values, cosine, sine_table):
    half_dim = values.shape[-1] // 2
    first_half = values[..., :half_dim]
    second_half = values[..., half_dim:]
    return jnp.concatenate(
        [
            first_half * cosine - second_half * sine_table,
            second_half * cosine + first_half * sine_table,
        ],
        axis=-1,
    )


def unrotate(values, cosine, sine_table):
    half_dim = values.shape[-1] // 2
    first_half = values[..., :half_dim]
    second_half = values[..., half_dim:]
    return jnp.concatenate(
        [
            first_half * cosine + second_half * sine_table,
            second_half * cosine - first_half * sine_table,
        ],
        axis=-1,
    )


def visible(places, seg_row, start_row, end_row):
    rows_q = places[start_row:end_row]
    rows_k = places[:end_row]
    same_doc = seg_row[start_row:end_row][:, None] == seg_row[:end_row][None, :]
    return (rows_q[:, None] >= rows_k[None, :]) & same_doc


def block_scores(queries, key_rows, start_row, end_row):
    raw_scores = jnp.einsum(
        "qhd,khd->hqk",
        queries[start_row:end_row],
        key_rows[:end_row],
        preferred_element_type=jnp.float32,
    )
    return raw_scores * (1.0 / math.sqrt(HD)) - math.log(LENGTH)


def attend_forward(query_heads, key_heads, value_heads, seg_row):
    length = seg_row.shape[0]
    head_count = query_heads.shape[1] // HD
    queries = query_heads.reshape(length, head_count, HD)
    key_rows = key_heads.reshape(length, head_count, HD)
    value_rows = value_heads.reshape(length, head_count, HD)
    block_rows = min(512, length)
    places = jnp.arange(length, dtype=jnp.int32)
    pieces = []
    for block_number in range(length // block_rows):
        start_row = block_number * block_rows
        end_row = start_row + block_rows
        allowed = visible(places, seg_row, start_row, end_row)
        scores = block_scores(queries, key_rows, start_row, end_row)
        weights = jnp.where(allowed[None], jax.nn.sigmoid(scores), 0.0).astype(jnp.bfloat16)
        pieces.append(
            jnp.einsum(
                "hqk,khd->qhd", weights, value_rows[:end_row], preferred_element_type=jnp.float32
            )
        )
    return jnp.concatenate(pieces, axis=0).reshape(length, head_count * HD).astype(jnp.bfloat16)


def attend_backward(query_heads, key_heads, value_heads, grad_heads, seg_row, cosine, sine_table):
    length = seg_row.shape[0]
    head_count = query_heads.shape[1] // HD
    queries = query_heads.reshape(length, head_count, HD)
    key_rows = key_heads.reshape(length, head_count, HD)
    value_rows = value_heads.reshape(length, head_count, HD)
    grad_rows = grad_heads.reshape(length, head_count, HD)
    scale = 1.0 / math.sqrt(HD)
    block_rows = min(512, length)
    places = jnp.arange(length, dtype=jnp.int32)
    query_grads = []
    key_grad = jnp.zeros((length, head_count, HD), jnp.float32)
    value_grad = jnp.zeros((length, head_count, HD), jnp.float32)
    for block_number in range(length // block_rows):
        start_row = block_number * block_rows
        end_row = start_row + block_rows
        allowed = visible(places, seg_row, start_row, end_row)
        scores = block_scores(queries, key_rows, start_row, end_row)
        sig_scores = jax.nn.sigmoid(scores)
        weights = jnp.where(allowed[None], sig_scores, 0.0).astype(jnp.bfloat16)
        grad_block = grad_rows[start_row:end_row]
        value_grad = value_grad.at[:end_row].add(
            jnp.einsum("hqk,qhd->khd", weights, grad_block, preferred_element_type=jnp.float32)
        )
        grad_probs = jnp.einsum(
            "qhd,khd->hqk", grad_block, value_rows[:end_row], preferred_element_type=jnp.float32
        )
        grad_scores = jnp.where(
            allowed[None], grad_probs * sig_scores * (1.0 - sig_scores), 0.0
        ).astype(jnp.bfloat16)
        query_grads.append(
            jnp.einsum(
                "hqk,khd->qhd", grad_scores, key_rows[:end_row], preferred_element_type=jnp.float32
            )
            * scale
        )
        key_grad = key_grad.at[:end_row].add(
            jnp.einsum(
                "hqk,qhd->khd",
                grad_scores,
                queries[start_row:end_row],
                preferred_element_type=jnp.float32,
            )
            * scale
        )
    query_grad = unrotate(jnp.concatenate(query_grads, axis=0), cosine, sine_table)
    key_grad = unrotate(key_grad, cosine, sine_table)
    stacked = jnp.stack(
        [
            query_grad.reshape(length, head_count * HD),
            key_grad.reshape(length, head_count * HD),
            value_grad.reshape(length, head_count * HD),
        ]
    )
    return stacked.astype(jnp.bfloat16)


def per_device(
    tokens,
    segments,
    gain_attn,
    w_query,
    w_key,
    w_value,
    w_out,
    gain_mlp,
    w_gate,
    w_up,
    w_down,
    cotangent,
):
    gain_a, weight_q, weight_k, weight_v, weight_o = (
        lax.all_gather(gain_attn, ("shard", "ctx"), axis=0, tiled=True),
        lax.all_gather(w_query, ("shard", "ctx"), axis=0, tiled=True),
        lax.all_gather(w_key, ("shard", "ctx"), axis=0, tiled=True),
        lax.all_gather(w_value, ("shard", "ctx"), axis=0, tiled=True),
        lax.all_gather(w_out, ("shard", "ctx"), axis=0, tiled=True),
    )
    gain_m, weight_g, weight_u, weight_d = (
        lax.all_gather(gain_mlp, ("shard", "ctx"), axis=0, tiled=True),
        lax.all_gather(w_gate, ("shard", "ctx"), axis=0, tiled=True),
        lax.all_gather(w_up, ("shard", "ctx"), axis=0, tiled=True),
        lax.all_gather(w_down, ("shard", "ctx"), axis=0, tiled=True),
    )
    token_rows = tokens.shape[0]
    seg_row = segments[0]
    cosine, sine_table = rope_tables(doc_positions(seg_row))
    own_start = lax.axis_index("ctx") * token_rows
    cos_own = lax.dynamic_slice_in_dim(cosine, own_start, token_rows, 0)
    sin_own = lax.dynamic_slice_in_dim(sine_table, own_start, token_rows, 0)
    local_heads = weight_q.shape[1] // HD
    x_wide = tokens.astype(jnp.float32)
    normed_one, inverse_one = norm_parts(x_wide)
    h_one = (normed_one * gain_a.astype(jnp.float32)).astype(jnp.bfloat16)
    query_tok = rotate(
        matmul(h_one, weight_q).reshape(token_rows, local_heads, HD), cos_own, sin_own
    )
    key_tok = rotate(matmul(h_one, weight_k).reshape(token_rows, local_heads, HD), cos_own, sin_own)
    value_tok = matmul(h_one, weight_v)
    stacked = jnp.stack(
        [
            query_tok.reshape(token_rows, local_heads * HD),
            key_tok.reshape(token_rows, local_heads * HD),
            value_tok,
        ]
    ).astype(jnp.bfloat16)
    qkv_heads = lax.all_to_all(stacked, "ctx", split_axis=2, concat_axis=1, tiled=True)
    out_heads = attend_forward(qkv_heads[0], qkv_heads[1], qkv_heads[2], seg_row)
    out_tok = lax.all_to_all(out_heads, "ctx", split_axis=0, concat_axis=1, tiled=True)
    attn_total = lax.psum(contract_cols(out_tok, weight_o), "tp")
    after_attn = x_wide + attn_total
    normed_two, inverse_two = norm_parts(after_attn)
    h_two = (normed_two * gain_m.astype(jnp.float32)).astype(jnp.bfloat16)
    gate_pre = matmul(h_two, weight_g)
    up_pre = matmul(h_two, weight_u)
    gate_sig = jax.nn.sigmoid(gate_pre)
    gate_act = gate_pre * gate_sig
    hidden = (gate_act * up_pre).astype(jnp.bfloat16)
    mlp_total = lax.psum(contract_cols(hidden, weight_d).astype(jnp.bfloat16), "tp").astype(
        jnp.float32
    )
    output = (after_attn + mlp_total).astype(jnp.bfloat16)
    gain_m, weight_g, weight_u, weight_d = (
        lax.all_gather(gain_mlp, ("shard", "ctx"), axis=0, tiled=True),
        lax.all_gather(w_gate, ("shard", "ctx"), axis=0, tiled=True),
        lax.all_gather(w_up, ("shard", "ctx"), axis=0, tiled=True),
        lax.all_gather(w_down, ("shard", "ctx"), axis=0, tiled=True),
    )
    grad_y = cotangent.astype(jnp.float32)
    grad_hidden = matmul(cotangent, weight_d)
    grad_w_down = contract_rows(cotangent, hidden)
    grad_gate = (grad_hidden * up_pre * gate_sig * (1.0 + gate_pre * (1.0 - gate_sig))).astype(
        jnp.bfloat16
    )
    grad_up = (grad_hidden * gate_act).astype(jnp.bfloat16)
    grad_w_gate = contract_rows(h_two, grad_gate)
    grad_w_up = contract_rows(h_two, grad_up)
    grad_h_two = lax.psum(
        contract_cols(grad_gate, weight_g) + contract_cols(grad_up, weight_u), "tp"
    )
    grad_gain_m = jnp.sum(grad_h_two * normed_two, axis=0)
    grad_after = grad_y + norm_back(
        grad_h_two * gain_m.astype(jnp.float32), normed_two, inverse_two
    )
    mlp_grads = (
        lax.psum_scatter(grad_gain_m, ("shard", "ctx"), scatter_dimension=0, tiled=True),
        lax.psum_scatter(grad_w_gate, ("shard", "ctx"), scatter_dimension=0, tiled=True),
        lax.psum_scatter(grad_w_up, ("shard", "ctx"), scatter_dimension=0, tiled=True),
        lax.psum_scatter(grad_w_down, ("shard", "ctx"), scatter_dimension=0, tiled=True),
    )
    gain_a, weight_q, weight_k, weight_v, weight_o = (
        lax.all_gather(gain_attn, ("shard", "ctx"), axis=0, tiled=True),
        lax.all_gather(w_query, ("shard", "ctx"), axis=0, tiled=True),
        lax.all_gather(w_key, ("shard", "ctx"), axis=0, tiled=True),
        lax.all_gather(w_value, ("shard", "ctx"), axis=0, tiled=True),
        lax.all_gather(w_out, ("shard", "ctx"), axis=0, tiled=True),
    )
    grad_attn = grad_after.astype(jnp.bfloat16)
    grad_out_tok = matmul(grad_attn, weight_o).astype(jnp.bfloat16)
    grad_w_out = contract_rows(grad_attn, out_tok)
    grad_out_heads = lax.all_to_all(grad_out_tok, "ctx", split_axis=1, concat_axis=0, tiled=True)
    grad_qkv_heads = attend_backward(
        qkv_heads[0], qkv_heads[1], qkv_heads[2], grad_out_heads, seg_row, cosine, sine_table
    )
    grad_qkv = lax.all_to_all(grad_qkv_heads, "ctx", split_axis=1, concat_axis=2, tiled=True)
    grad_w_query = contract_rows(h_one, grad_qkv[0])
    grad_w_key = contract_rows(h_one, grad_qkv[1])
    grad_w_value = contract_rows(h_one, grad_qkv[2])
    grad_h_part = (
        contract_cols(grad_qkv[0], weight_q)
        + contract_cols(grad_qkv[1], weight_k)
        + contract_cols(grad_qkv[2], weight_v)
    )
    grad_h_one = lax.psum(grad_h_part.astype(jnp.bfloat16), "tp").astype(jnp.float32)
    grad_gain_a = jnp.sum(grad_h_one * normed_one, axis=0)
    grad_input = grad_after + norm_back(
        grad_h_one * gain_a.astype(jnp.float32), normed_one, inverse_one
    )
    attn_grads = (
        lax.psum_scatter(grad_gain_a, ("shard", "ctx"), scatter_dimension=0, tiled=True),
        lax.psum_scatter(grad_w_query, ("shard", "ctx"), scatter_dimension=0, tiled=True),
        lax.psum_scatter(grad_w_key, ("shard", "ctx"), scatter_dimension=0, tiled=True),
        lax.psum_scatter(grad_w_value, ("shard", "ctx"), scatter_dimension=0, tiled=True),
        lax.psum_scatter(grad_w_out, ("shard", "ctx"), scatter_dimension=0, tiled=True),
    )
    return (
        output,
        grad_input.astype(jnp.bfloat16),
        attn_grads[0],
        attn_grads[1],
        attn_grads[2],
        attn_grads[3],
        attn_grads[4],
        mlp_grads[0],
        mlp_grads[1],
        mlp_grads[2],
        mlp_grads[3],
    )


def solution(mesh):
    placed = (
        P(("shard", "ctx"), None),
        P("shard", None),
        P(("shard", "ctx")),
        P(("shard", "ctx"), "tp"),
        P(("shard", "ctx"), "tp"),
        P(("shard", "ctx"), "tp"),
        P(("shard", "ctx"), "tp"),
        P(("shard", "ctx")),
        P(("shard", "ctx"), "tp"),
        P(("shard", "ctx"), "tp"),
        P(("shard", "ctx"), "tp"),
        P(("shard", "ctx"), None),
    )
    return jax.shard_map(
        per_device,
        mesh=mesh,
        in_specs=placed,
        out_specs=(
            P(("shard", "ctx"), None),
            P(("shard", "ctx"), None),
            P(("shard", "ctx")),
            P(("shard", "ctx"), "tp"),
            P(("shard", "ctx"), "tp"),
            P(("shard", "ctx"), "tp"),
            P(("shard", "ctx"), "tp"),
            P(("shard", "ctx")),
            P(("shard", "ctx"), "tp"),
            P(("shard", "ctx"), "tp"),
            P(("shard", "ctx"), "tp"),
        ),
        check_vma=False,
    )
```

profile of v0, /device:TPU:0, one launch (start us, length us, event | category | flops | bytes accessed | tf_op | source)
XLA Modules:
  0.0 2502.1 jit_solution(3662851226561099260)
XLA Ops:
  11.6 23.4 all-gather
  40.6 22.7 all-gather.10.cloned.1.call-done
  69.7 44.8 %all-gather.12.cloned.1.call-done = bf16[2048,1024]{1,0:T(8,128)(2,1)} async-done(((bf16[128,1024]{1,0:T(8,128)(2,1)}), bf16[2048,1024]{1,0:T(8,128)(2,1)}) %all-gather.12.cloned.1.call-update) | async-done | bytes 4194320 | tf_op jit(solution)/shard_map/all_gather | solution.py:195
  131.9 33.7 %all-gather.14.cloned.1.call-done = bf16[2048,1024]{1,0:T(8,128)(2,1)} async-done(((bf16[128,1024]{1,0:T(8,128)(2,1)}), bf16[2048,1024]{1,0:T(8,128)(2,1)}) %all-gather.14.cloned.1.call-update) | async-done | bytes 4194320 | tf_op jit(solution)/shard_map/all_gather | solution.py:196
  172.2 7.7 copy.78
  179.9 8.9 all_to_all.62
  231.3 19.0 all-gather.1
  250.3 85.4 %all-reduce.10.cloned.1.call-done = f32[512,2048]{1,0:T(8,128)} async-done(((f32[512,2048]{1,0:T(8,128)}), f32[512,2048]{1,0:T(8,128)}) %all-reduce.10.cloned.1.call-update) | async-done | bytes 4194320 | tf_op jit(solution)/shard_map/psum | solution.py:230
  341.0 123.2 %all-gather.18.cloned.1.call-done = bf16[2048,4096]{1,0:T(8,128)(2,1)} async-done(((bf16[128,4096]{1,0:T(8,128)(2,1)}), bf16[2048,4096]{1,0:T(8,128)(2,1)}) %all-gather.18.cloned.1.call-update) | async-done | bytes 16777232 | tf_op jit(solution)/shard_map/all_gather | solution.py:201
  464.2 14.4 fusion.47
  478.7 112.4 %all-gather.20.cloned.1.call-done = bf16[2048,4096]{1,0:T(8,128)(2,1)} async-done(((bf16[128,4096]{1,0:T(8,128)(2,1)}), bf16[2048,4096]{1,0:T(8,128)(2,1)}) %all-gather.20.cloned.1.call-update) | async-done | bytes 16777232 | tf_op jit(solution)/shard_map/all_gather | solution.py:202
  591.0 14.4 fusion.48
  605.4 112.4 %all-gather.22.cloned.1.call-done = bf16[2048,4096]{1,0:T(8,128)(2,1)} async-done(((bf16[128,4096]{1,0:T(8,128)(2,1)}), bf16[2048,4096]{1,0:T(8,128)(2,1)}) %all-gather.22.cloned.1.call-update) | async-done | bytes 16777232 | tf_op jit(solution)/shard_map/all_gather | solution.py:203
  717.8 22.3 multiply_convert_fusion
  740.1 13.3 fusion.49
  753.4 13.9 convolution_add_fusion
  767.4 15.7 convolution_convert_fusion
  783.1 90.5 %all-reduce.12.cloned.1.call-done = f32[512,2048]{1,0:T(8,128)} async-done(((f32[512,2048]{1,0:T(8,128)}), f32[512,2048]{1,0:T(8,128)}) %all-reduce.12.cloned.1.call-update) | async-done | bytes 4194320 | tf_op jit(solution)/shard_map/psum | solution.py:258
  922.3 8.5 pad_maximum_fusion
  955.1 18.1 convolution_bitcast_fusion
  996.9 7.8 fusion.24
  1004.8 18.9 fusion.52
  1023.9 18.3 fusion.53
  1044.1 17.5 all-reduce.14.cloned.1.call-done
  1064.5 61.0 %all-reduce.4 = (f32[2048]{0:T(1024)S(1)}, f32[2048]{0:T(1024)S(1)}) all-reduce(f32[2048]{0:T(1024)S(1)} %get-tuple-element.121, f32[2048]{0:T(1024)S(1)} %copy-done.47), channel_id=2, replica_groups=mesh['shard'=8,'ctx'=2,'tp'=2] {'shard','ctx'}, use_global_device_ids=true, to_apply=%region_11.12.clone | all-reduce | flops 4096 | bytes 32768
  1134.4 261.9 %reduce-scatter.20.cloned.1.call-done = f32[128,4096]{0,1:T(8,128)} async-done(((f32[2048,4096]{0,1:T(8,128)}), f32[128,4096]{0,1:T(8,128)}) %reduce-scatter.20.cloned.1.call-update) | async-done | bytes 2097168 | tf_op jit(solution)/shard_map/reduce_scatter | solution.py:269
  1399.1 104.2 %reduce-scatter.8.cloned.1.call-done = f32[128,1024]{1,0:T(8,128)} async-done(((f32[2048,1024]{1,0:T(8,128)}), f32[128,1024]{1,0:T(8,128)}) %reduce-scatter.8.cloned.1.call-update) | async-done | bytes 524304 | tf_op jit(solution)/shard_map/reduce_scatter | solution.py:301
  1503.3 107.8 %reduce-scatter.10.cloned.1.call-done = f32[128,1024]{1,0:T(8,128)} async-done(((f32[2048,1024]{1,0:T(8,128)}), f32[128,1024]{1,0:T(8,128)}) %reduce-scatter.10.cloned.1.call-update) | async-done | bytes 524304 | tf_op jit(solution)/shard_map/reduce_scatter | solution.py:302
  1611.1 107.6 %reduce-scatter.12.cloned.1.call-done = f32[128,1024]{1,0:T(8,128)} async-done(((f32[2048,1024]{1,0:T(8,128)}), f32[128,1024]{1,0:T(8,128)}) %reduce-scatter.12.cloned.1.call-update) | async-done | bytes 524304 | tf_op jit(solution)/shard_map/reduce_scatter | solution.py:303
  1718.7 107.6 %reduce-scatter.14.cloned.1.call-done = f32[128,1024]{1,0:T(8,128)} async-done(((f32[2048,1024]{1,0:T(8,128)}), f32[128,1024]{1,0:T(8,128)}) %reduce-scatter.14.cloned.1.call-update) | async-done | bytes 524304 | tf_op jit(solution)/shard_map/reduce_scatter | solution.py:304
  1826.3 334.8 %reduce-scatter.16.cloned.1.call-done = f32[128,4096]{1,0:T(8,128)} async-done(((f32[2048,4096]{1,0:T(8,128)}), f32[128,4096]{1,0:T(8,128)}) %reduce-scatter.16.cloned.1.call-update) | async-done | bytes 2097168 | tf_op jit(solution)/shard_map/reduce_scatter | solution.py:267
  2161.1 334.3 %reduce-scatter.18.cloned.1.call-done = f32[128,4096]{1,0:T(8,128)} async-done(((f32[2048,4096]{1,0:T(8,128)}), f32[128,4096]{1,0:T(8,128)}) %reduce-scatter.18.cloned.1.call-update) | async-done | bytes 2097168 | tf_op jit(solution)/shard_map/reduce_scatter | solution.py:268
  (246 shorter events, 200.2 us)
Async XLA Ops:
  7.2 31.8 %copy-start.46 = (s32[1,1024]{1,0:T(1,128)S(1)}, s32[1,1024]{1,0:T(1,128)}, u32[]{:S(2)}) copy-start(s32[1,1024]{1,0:T(1,128)} %param.25) | copy-start | bytes 12292
  7.2 31.3 %copy-start.8 = (bf16[512,2048]{1,0:T(8,128)(2,1)S(1)}, bf16[512,2048]{1,0:T(8,128)(2,1)}, u32[]{:S(2)}) copy-start(bf16[512,2048]{1,0:T(8,128)(2,1)} %param.24) | copy-start | bytes 6291460
  7.2 56.2 %all-gather.10.cloned.1.call-start = ((), (), s32[]{:S(2)}) async-start(), calls=%async_computation.11 | async-start | bytes 4456448 | tf_op jit(solution)/shard_map/all_gather | solution.py:194
  7.9 106.5 %all-gather.12.cloned.1.call-start = ((), (), s32[]{:S(2)}) async-start(), calls=%async_computation.12 | async-start | bytes 4456448 | tf_op jit(solution)/shard_map/all_gather | solution.py:195
  8.7 156.9 %all-gather.14.cloned.1.call-start = ((), (), s32[]{:S(2)}) async-start(), calls=%async_computation.13 | async-start | bytes 4456448 | tf_op jit(solution)/shard_map/all_gather | solution.py:196
  9.4 212.6 %all-gather.16.cloned.1.call-start = ((), (), s32[]{:S(2)}) async-start(), calls=%async_computation.14 | async-start | bytes 4456448 | tf_op jit(solution)/shard_map/all_gather | solution.py:197
  10.0 325.8 %all-reduce.10.cloned.1.call-start = ((), (), s32[]{:S(2)}) async-start(), calls=%async_computation.15 | async-start | bytes 8388608 | tf_op jit(solution)/shard_map/psum | solution.py:230
  35.0 130.6 %copy-start.44 = (f32[16,1,128]{2,1,0:T(1,128)}, f32[16,1,128]{2,1,0:T(1,128)S(1)}, u32[]{:S(2)}) copy-start(f32[16,1,128]{2,1,0:T(1,128)S(1)} %convert_element_type.104) | copy-start | bytes 24580
  39.0 126.6 %copy-start.48 = (f32[512]{0:T(512)}, f32[512]{0:T(512)S(1)}, u32[]{:S(2)}) copy-start(f32[512]{0:T(512)S(1)} %add_rsqrt_fusion.1) | copy-start | bytes 6148
  39.3 167.1 %copy-start.26 = (pred[512,512]{1,0:T(8,128)(4,1)}, pred[512,512]{1,0:T(8,128)(4,1)S(1)}, u32[]{:S(2)}) copy-start(pred[512,512]{1,0:T(8,128)(4,1)S(1)} %compare_and_fusion) | copy-start | bytes 786436
  131.9 38.4 %copy-start.23 = (bf16[1,512,1024]{2,1,0:T(8,128)(2,1)S(1)}, bf16[1,512,1024]{2,1,0:T(8,128)(2,1)}, u32[]{:S(2)}) copy-start(bf16[1,512,1024]{2,1,0:T(8,128)(2,1)} %stack_reshape.21) | copy-start | bytes 3145732
  196.2 14.9 copy-start.13
  222.1 6.9 copy-start.20
  229.0 235.2 %all-gather.18.cloned.1.call-start = ((), (), s32[]{:S(2)}) async-start(), calls=%async_computation.16 | async-start | bytes 17825792 | tf_op jit(solution)/shard_map/all_gather | solution.py:201
  229.6 361.4 %all-gather.20.cloned.1.call-start = ((), (), s32[]{:S(2)}) async-start(), calls=%async_computation.17 | async-start | bytes 17825792 | tf_op jit(solution)/shard_map/all_gather | solution.py:202
  230.3 487.5 %all-gather.22.cloned.1.call-start = ((), (), s32[]{:S(2)}) async-start(), calls=%async_computation.18 | async-start | bytes 17825792 | tf_op jit(solution)/shard_map/all_gather | solution.py:203
  231.1 642.5 %all-reduce.12.cloned.1.call-start = ((), (), s32[]{:S(2)}) async-start(), calls=%async_computation.19 | async-start | bytes 8388608 | tf_op jit(solution)/shard_map/psum | solution.py:258
  341.0 250.1 %copy-start.30 = (bf16[512,2048]{1,0:T(8,128)(2,1)}, bf16[512,2048]{1,0:T(8,128)(2,1)S(1)}, u32[]{:S(2)}) copy-start(bf16[512,2048]{1,0:T(8,128)(2,1)S(1)} %multiply_convert_fusion.3) | copy-start | bytes 6291460
  740.1 13.3 copy-start.55
  767.3 294.3 %all-reduce.14.cloned.1.call-start = ((), (), s32[]{:S(2)}) async-start(), calls=%async_computation.27 | async-start | bytes 8388608 | tf_op jit(solution)/shard_map/psum | solution.py:239
  767.4 111.4 %copy-start.35 = (bf16[512,2048]{1,0:T(8,128)(2,1)S(1)}, bf16[512,2048]{1,0:T(8,128)(2,1)}, u32[]{:S(2)}) copy-start(bf16[512,2048]{1,0:T(8,128)(2,1)} %param.35) | copy-start | bytes 6291460
  873.6 5.9 copy-start.12
  885.0 5.9 copy-start.27
  885.6 5.4 copy-start.7
  953.5 442.7 %reduce-scatter.20.cloned.1.call-start = ((), (), s32[]{:S(2)}) async-start(), calls=%async_computation.26 | async-start | bytes 35651584 | tf_op jit(solution)/shard_map/reduce_scatter | solution.py:269
  973.2 530.1 %reduce-scatter.8.cloned.1.call-start = ((), (), s32[]{:S(2)}) async-start(), calls=%async_computation.20 | async-start | bytes 8912896 | tf_op jit(solution)/shard_map/reduce_scatter | solution.py:301
  982.1 629.0 %reduce-scatter.10.cloned.1.call-start = ((), (), s32[]{:S(2)}) async-start(), calls=%async_computation.21 | async-start | bytes 8912896 | tf_op jit(solution)/shard_map/reduce_scatter | solution.py:302
  989.3 729.4 %reduce-scatter.12.cloned.1.call-start = ((), (), s32[]{:S(2)}) async-start(), calls=%async_computation.22 | async-start | bytes 8912896 | tf_op jit(solution)/shard_map/reduce_scatter | solution.py:303
  995.6 830.6 %reduce-scatter.14.cloned.1.call-start = ((), (), s32[]{:S(2)}) async-start(), calls=%async_computation.23 | async-start | bytes 8912896 | tf_op jit(solution)/shard_map/reduce_scatter | solution.py:304
  1004.7 1156.4 %reduce-scatter.16.cloned.1.call-start = ((), (), s32[]{:S(2)}) async-start(), calls=%async_computation.24 | async-start | bytes 35651584 | tf_op jit(solution)/shard_map/reduce_scatter | solution.py:267
  1023.7 1471.7 %reduce-scatter.18.cloned.1.call-start = ((), (), s32[]{:S(2)}) async-start(), calls=%async_computation.25 | async-start | bytes 35651584 | tf_op jit(solution)/shard_map/reduce_scatter | solution.py:268
  1042.2 22.3 copy-start.47
  (43 other events, 109.5 us)
Sparse Core Ops, SparseCore 0:
  10.2 53.1 all-gather.9
  65.5 48.9 all-gather.11
  116.6 48.9 all-gather.13
  167.6 48.9 all-gather.15
  229.1 106.5 all-reduce.9
  337.8 126.4 all-gather.17
  466.4 124.5 all-gather.19
  593.2 124.5 all-gather.21
  767.4 106.0 all-reduce.11
  953.6 107.9 all-reduce.13
  1065.9 330.3 reduce-scatter.19
  1400.8 102.5 reduce-scatter.7
  1508.0 103.0 reduce-scatter.9
  1615.6 103.0 reduce-scatter.11
  1723.1 103.0 reduce-scatter.13
  1830.9 330.0 reduce-scatter.15
  2165.8 329.5 reduce-scatter.17
where the time goes:
time: 2510 us; the launch traced here: 2500 us
  waiting for transfers between devices  2010 us (80%)
  matrix products  233 us (9%)
  blocking collectives  129 us (5%)
  local copies, waits for them, and re-layouts  72.8 us (3%)
  other arithmetic  44.7 us (2%)
    reduce_scatter x1, waiting for transfers between devices, per_device(): lax.psum_scatter(grad_w_gate, ('shard', 'ctx'), scatter_dimension=0, tile...  335 us
    reduce_scatter x1, waiting for transfers between devices, per_device(): lax.psum_scatter(grad_w_up, ('shard', 'ctx'), scatter_dimension=0, tiled=...  334 us
    reduce_scatter x1, waiting for transfers between devices, per_device(): lax.psum_scatter(grad_w_down, ('shard', 'ctx'), scatter_dimension=0, tile...  262 us
    all_gather x1, waiting for transfers between devices, per_device(): lax.all_gather(w_gate, ('shard', 'ctx'), axis=0, tiled=True)  123 us
    all_gather x1, waiting for transfers between devices, per_device(): lax.all_gather(w_down, ('shard', 'ctx'), axis=0, tiled=True)  112 us
    all_gather x1, waiting for transfers between devices, per_device(): lax.all_gather(w_up, ('shard', 'ctx'), axis=0, tiled=True)  112 us
    reduce_scatter x1, waiting for transfers between devices, per_device(): lax.psum_scatter(grad_w_key, ('shard', 'ctx'), scatter_dimension=0, tiled...  108 us
    reduce_scatter x1, waiting for transfers between devices, per_device(): lax.psum_scatter(grad_w_out, ('shard', 'ctx'), scatter_dimension=0, tiled...  108 us
  transfers between devices with their start and end apart: 17, of which 16 were waited for; matrix products, arithmetic and copies ran while one was open for 8% of the time, Pallas kernels for 0%

commit v1 on v0

v1 whole, which is shorter than its diff:
```python
import math

import jax
import jax.numpy as jnp
from jax import lax
from jax.sharding import PartitionSpec as P

HD = 128
LENGTH = 1024


norm_eps = 1e-05
rope_base = 10000.0

bf16 = jnp.bfloat16
f32 = jnp.float32


def matmul(left, right):
    return jnp.dot(left, right, preferred_element_type=jnp.float32)


def contract_rows(left, right):
    return lax.dot_general(
        left, right, (((0,), (0,)), ((), ())), preferred_element_type=jnp.float32
    )


def contract_cols(left, right):
    return lax.dot_general(
        left, right, (((1,), (1,)), ((), ())), preferred_element_type=jnp.float32
    )


def norm_parts(values):
    inverse = lax.rsqrt(jnp.mean(values * values, axis=-1, keepdims=True) + norm_eps)
    return (values * inverse, inverse)


def norm_back(grad_scaled, normed, inverse):
    return inverse * (grad_scaled - normed * jnp.mean(grad_scaled * normed, axis=-1, keepdims=True))


def doc_positions(seg_row):
    places = jnp.arange(seg_row.shape[0], dtype=jnp.int32)
    starts_here = jnp.concatenate([jnp.ones((1,), dtype=jnp.bool_), seg_row[1:] != seg_row[:-1]])
    starts = lax.cummax(jnp.where(starts_here, places, jnp.zeros_like(places)), axis=0)
    return places - starts


def rope_tables(positions):
    half_dim = HD // 2
    freqs = rope_base ** (-(jnp.arange(half_dim, dtype=jnp.float32) * (2.0 / HD)))
    angles = positions.astype(jnp.float32)[:, None] * freqs[None, :]
    return (jnp.cos(angles)[:, None, :], jnp.sin(angles)[:, None, :])


def rotate(values, cosine, sine_table):
    half_dim = values.shape[-1] // 2
    first_half = values[..., :half_dim]
    second_half = values[..., half_dim:]
    return jnp.concatenate(
        [
            first_half * cosine - second_half * sine_table,
            second_half * cosine + first_half * sine_table,
        ],
        axis=-1,
    )


def unrotate(values, cosine, sine_table):
    half_dim = values.shape[-1] // 2
    first_half = values[..., :half_dim]
    second_half = values[..., half_dim:]
    return jnp.concatenate(
        [
            first_half * cosine + second_half * sine_table,
            second_half * cosine - first_half * sine_table,
        ],
        axis=-1,
    )


def visible(places, seg_row, start_row, end_row):
    rows_q = places[start_row:end_row]
    rows_k = places[:end_row]
    same_doc = seg_row[start_row:end_row][:, None] == seg_row[:end_row][None, :]
    return (rows_q[:, None] >= rows_k[None, :]) & same_doc


def block_scores(queries, key_rows, start_row, end_row):
    raw_scores = jnp.einsum(
        "qhd,khd->hqk",
        queries[start_row:end_row],
        key_rows[:end_row],
        preferred_element_type=jnp.float32,
    )
    return raw_scores * (1.0 / math.sqrt(HD)) - math.log(LENGTH)


def attend_forward(query_heads, key_heads, value_heads, seg_row):
    length = seg_row.shape[0]
    head_count = query_heads.shape[1] // HD
    queries = query_heads.reshape(length, head_count, HD)
    key_rows = key_heads.reshape(length, head_count, HD)
    value_rows = value_heads.reshape(length, head_count, HD)
    block_rows = min(512, length)
    places = jnp.arange(length, dtype=jnp.int32)
    pieces = []
    for block_number in range(length // block_rows):
        start_row = block_number * block_rows
        end_row = start_row + block_rows
        allowed = visible(places, seg_row, start_row, end_row)
        scores = block_scores(queries, key_rows, start_row, end_row)
        weights = jnp.where(allowed[None], jax.nn.sigmoid(scores), 0.0).astype(jnp.bfloat16)
        pieces.append(
            jnp.einsum(
                "hqk,khd->qhd", weights, value_rows[:end_row], preferred_element_type=jnp.float32
            )
        )
    return jnp.concatenate(pieces, axis=0).reshape(length, head_count * HD).astype(jnp.bfloat16)


def attend_backward(query_heads, key_heads, value_heads, grad_heads, seg_row, cosine, sine_table):
    length = seg_row.shape[0]
    head_count = query_heads.shape[1] // HD
    queries = query_heads.reshape(length, head_count, HD)
    key_rows = key_heads.reshape(length, head_count, HD)
    value_rows = value_heads.reshape(length, head_count, HD)
    grad_rows = grad_heads.reshape(length, head_count, HD)
    scale = 1.0 / math.sqrt(HD)
    block_rows = min(512, length)
    places = jnp.arange(length, dtype=jnp.int32)
    query_grads = []
    key_grad = jnp.zeros((length, head_count, HD), jnp.float32)
    value_grad = jnp.zeros((length, head_count, HD), jnp.float32)
    for block_number in range(length // block_rows):
        start_row = block_number * block_rows
        end_row = start_row + block_rows
        allowed = visible(places, seg_row, start_row, end_row)
        scores = block_scores(queries, key_rows, start_row, end_row)
        sig_scores = jax.nn.sigmoid(scores)
        weights = jnp.where(allowed[None], sig_scores, 0.0).astype(jnp.bfloat16)
        grad_block = grad_rows[start_row:end_row]
        value_grad = value_grad.at[:end_row].add(
            jnp.einsum("hqk,qhd->khd", weights, grad_block, preferred_element_type=jnp.float32)
        )
        grad_probs = jnp.einsum(
            "qhd,khd->hqk", grad_block, value_rows[:end_row], preferred_element_type=jnp.float32
        )
        grad_scores = jnp.where(
            allowed[None], grad_probs * sig_scores * (1.0 - sig_scores), 0.0
        ).astype(jnp.bfloat16)
        query_grads.append(
            jnp.einsum(
                "hqk,khd->qhd", grad_scores, key_rows[:end_row], preferred_element_type=jnp.float32
            )
            * scale
        )
        key_grad = key_grad.at[:end_row].add(
            jnp.einsum(
                "hqk,qhd->khd",
                grad_scores,
                queries[start_row:end_row],
                preferred_element_type=jnp.float32,
            )
            * scale
        )
    query_grad = unrotate(jnp.concatenate(query_grads, axis=0), cosine, sine_table)
    key_grad = unrotate(key_grad, cosine, sine_table)
    return jnp.concatenate(
        [
            query_grad.reshape(length, head_count * HD),
            key_grad.reshape(length, head_count * HD),
            value_grad.reshape(length, head_count * HD),
        ],
        axis=1,
    ).astype(jnp.bfloat16)


def cat(parts, axis=0):
    return jnp.concatenate(parts, axis=axis)


def rows_of(values, start, size):
    return lax.dynamic_slice_in_dim(values, start, size, 0)


def cols_of(values, start, size):
    return lax.dynamic_slice_in_dim(values, start, size, 1)


def ordered(index, own, other, axis=0):
    return jnp.where(index == 0, cat([own, other], axis), cat([other, own], axis))


def build(shards):
    far = [k << 2 for k in range(1, shards // 4)]
    line = [k << 1 for k in range(1, shards // 2)]

    def across(values, mask):
        return lax.ppermute(values, "shard", [(i, i ^ mask) for i in range(shards)])

    def swap_core(values):
        return lax.ppermute(values, "ctx", [(0, 1), (1, 0)])

    def swap_tp(values):
        return lax.ppermute(values, "tp", [(0, 1), (1, 0)])

    order = [(m << 1) | y for y in (0, 1) for m in range(shards // 2)]

    def gather_line(block):
        near = [block] + [across(block, mask) for mask in line]
        return cat(near + [across(part, 1) for part in near])

    def gather_far(block):
        near = [block] + [across(block, mask) for mask in far]
        return cat(near + [across(part, 1) for part in near])

    def per_device(
        tokens,
        segments,
        gain_attn,
        w_query,
        w_key,
        w_value,
        w_out,
        gain_mlp,
        w_gate,
        w_up,
        w_down,
        cotangent,
    ):
        shard = lax.axis_index("shard")
        core = lax.axis_index("ctx")
        half = lax.axis_index("tp")
        zl = (shard >> 1) & 1
        rows, width = tokens.shape
        part = rows // 2
        block = width // shards
        unit = block // 2
        n_attn = w_query.shape[1] // 2
        n_ff = w_gate.shape[1] // 4

        def relative(values):
            return cat([cols_of(values, (shard ^ mask) * block, block) for mask in order], 1)

        def natural(values):
            place = {mask: i for i, mask in enumerate(order)}
            spread = cat([values[:, place[m] * block : (place[m] + 1) * block] for m in range(shards)], 1)
            return cat([cols_of(spread, (shard ^ m) * block, block) for m in range(shards)], 1)

        def flip_zl(values):
            split = values.reshape(values.shape[0], shards // 2, 2, block)
            return jnp.where(zl == 0, split, split[:, :, ::-1]).reshape(values.shape)

        gains = jnp.stack([gain_attn, gain_mlp])
        gains = ordered(core, gains, swap_core(gains), 1)
        for bit in range(1, shards.bit_length() - 1):
            gains = cat([gains, across(gains, 1 << bit)], 1)
        gains = cat([gains, across(gains, 1)], 1).astype(f32)
        gain_a, gain_m = gains[0:1], gains[1:2]

        def core_rows(weights):
            each = [w.shape[1] // 2 for w in weights]
            keep = cat([cols_of(w, core * n, n) for w, n in zip(weights, each)], 1)
            send = cat([cols_of(w, (1 - core) * n, n) for w, n in zip(weights, each)], 1)
            return ordered(core, keep, swap_core(send))

        block_a = core_rows([w_query, w_key, w_value, w_out])
        weight_qkv = gather_line(block_a[:, : 3 * n_attn])
        weight_o = gather_line(block_a[:, 3 * n_attn :])

        block_f = core_rows([w_gate, w_up, w_down])

        def ff_weight(i):
            own = block_f[:, i * 2 * n_ff : (i + 1) * 2 * n_ff]
            keep = cols_of(own, zl * n_ff, n_ff)
            send = cols_of(own, (1 - zl) * n_ff, n_ff)
            return gather_far(ordered(zl, keep, across(send, 2)))

        weight_g, weight_u, weight_d = ff_weight(0), ff_weight(1), ff_weight(2)

        seg_row = segments[0]
        cosine, sine_table = rope_tables(doc_positions(seg_row))
        length = seg_row.shape[0]
        heads = n_attn // HD
        x_rel = relative(tokens).astype(f32)
        normed_one, inverse_one = norm_parts(x_rel)
        h_own = (normed_one * gain_a).astype(bf16)
        h_one = ordered(core, h_own, swap_core(h_own))
        qkv = matmul(h_one, weight_qkv)
        query = rotate(qkv[:, :n_attn].reshape(length, heads, HD), cosine, sine_table)
        query = query.reshape(length, n_attn).astype(bf16)
        key = rotate(qkv[:, n_attn : 2 * n_attn].reshape(length, heads, HD), cosine, sine_table)
        key = key.reshape(length, n_attn).astype(bf16)
        value = qkv[:, 2 * n_attn :].astype(bf16)
        mixed = attend_forward(query, key, value, seg_row)

        def to_slice(operand, project):
            away = project(rows_of(operand, (1 - core) * rows, rows)).astype(bf16)
            here = rows_of(operand, core * rows, rows)
            away = swap_core(away)
            other = project(rows_of(here, (1 - half) * part, part)) + rows_of(
                away, (1 - half) * part, part
            ).astype(f32)
            other = swap_tp(other.astype(bf16))
            own = project(rows_of(here, half * part, part)) + rows_of(
                away, half * part, part
            ).astype(f32)
            return own + other.astype(f32)

        x_part = rows_of(x_rel, half * part, part)
        after_attn = x_part + to_slice(mixed, lambda v: contract_cols(v, weight_o))
        normed_two, inverse_two = norm_parts(after_attn)
        h_part = flip_zl((normed_two * gain_m).astype(bf16))

        def spread_tokens(own):
            by_tp, by_zl = swap_tp(own), across(own, 2)
            mid = own.shape[0] // 2
            both = cat([across(by_tp[:mid], 2), swap_tp(by_zl[mid:])])
            near = [own, by_tp, by_zl, both]
            return cat(near + [swap_core(v) for v in near])

        h_two = spread_tokens(h_part)
        dy_rel = relative(cotangent)
        dy_ff = flip_zl(cat([rows_of(dy_rel, half * part, part), rows_of(dy_rel, (1 - half) * part, part)]))
        dy_zl = across(dy_ff[:part], 2)
        near = [dy_ff, dy_zl, swap_tp(dy_zl)]
        grad_out = cat(near + [swap_core(v) for v in near])

        gate_pre = matmul(h_two, weight_g)
        up_pre = matmul(h_two, weight_u)
        gate_sig = jax.nn.sigmoid(gate_pre)
        gate_act = gate_pre * gate_sig
        hidden = (gate_act * up_pre).astype(bf16)

        def from_tokens(project):
            count = 4 * part
            away = swap_core(project(slice(count, 2 * count)).astype(bf16))
            total = project(slice(0, count)) + away.astype(f32)
            mid = width // 2
            low, high = total[:, :mid], total[:, mid:]

            def pick(values, i):
                return values[i * part : (i + 1) * part]

            low_tp = swap_tp(cat([pick(low, 1), pick(low, 3)]).astype(bf16)).astype(f32)
            high_zl = across(cat([pick(high, 2), pick(high, 3)]).astype(bf16), 2).astype(f32)
            low_zl = across((pick(low, 2) + pick(low_tp, 1)).astype(bf16), 2).astype(f32)
            high_tp = swap_tp((pick(high, 1) + pick(high_zl, 1)).astype(bf16)).astype(f32)
            low_sum = pick(low, 0) + pick(low_tp, 0) + low_zl
            high_sum = pick(high, 0) + pick(high_zl, 0) + high_tp
            return flip_zl(cat([low_sum, high_sum], 1))

        mlp = from_tokens(lambda where: contract_cols(hidden[where], weight_d))
        out_part = (after_attn + mlp).astype(bf16)
        output = natural(ordered(half, out_part, swap_tp(out_part)))

        grad_hidden = matmul(grad_out, weight_d)
        grad_gate = (grad_hidden * up_pre * gate_sig * (1.0 + gate_pre * (1.0 - gate_sig))).astype(bf16)
        grad_up = (grad_hidden * gate_act).astype(bf16)
        grad_h_two = from_tokens(
            lambda where: contract_cols(grad_gate[where], weight_g)
            + contract_cols(grad_up[where], weight_u)
        )

        def rows_far(left, right):
            mid = width // 2
            away = across(contract_rows(left[:, mid:], right).astype(bf16), 1)
            total = contract_rows(left[:, :mid], right) + away.astype(f32)
            step = 2 * block
            own = total[:step]
            for i, mask in enumerate(far):
                sent = total[(i + 1) * step : (i + 2) * step].astype(bf16)
                own = own + across(sent, mask).astype(f32)
            own = own.astype(bf16)
            other = across(rows_of(own, (1 - zl) * block, block), 2)
            own = ordered(zl, rows_of(own, zl * block, block), other, 1)
            other = swap_core(rows_of(own, (1 - core) * unit, unit))
            return ordered(core, rows_of(own, core * unit, unit), other, 1).astype(f32)

        grad_w_down = rows_far(grad_out, hidden)
        grad_w_gate = rows_far(h_two, grad_gate)
        grad_w_up = rows_far(h_two, grad_up)

        grad_gain_m = jnp.sum(grad_h_two * normed_two, axis=0, keepdims=True)
        dy_part = rows_of(dy_rel, half * part, part).astype(f32)
        grad_after = dy_part + norm_back(grad_h_two * gain_m, normed_two, inverse_two)

        grad_part = grad_after.astype(bf16)
        grad_half = ordered(half, grad_part, swap_tp(grad_part))
        grad_attn = ordered(core, grad_half, swap_core(grad_half))
        grad_mixed = matmul(grad_attn, weight_o).astype(bf16)

        def rows_line(left, right):
            mid = width // 2
            away = across(contract_rows(left[:, mid:], right).astype(bf16), 1)
            total = contract_rows(left[:, :mid], right) + away.astype(f32)
            own = total[:block]
            for i, mask in enumerate(line):
                sent = total[(i + 1) * block : (i + 2) * block].astype(bf16)
                own = own + across(sent, mask).astype(f32)
            other = swap_core(rows_of(own, (1 - core) * unit, unit).astype(bf16))
            return ordered(core, rows_of(own, core * unit, unit), other.astype(f32), 1)

        grad_w_out = rows_line(grad_attn, mixed)
        grad_qkv = attend_backward(query, key, value, grad_mixed, seg_row, cosine, sine_table)
        grad_w_query = rows_line(h_one, grad_qkv[:, :n_attn])
        grad_w_key = rows_line(h_one, grad_qkv[:, n_attn : 2 * n_attn])
        grad_w_value = rows_line(h_one, grad_qkv[:, 2 * n_attn :])
        grad_h_one = to_slice(grad_qkv, lambda v: contract_cols(v, weight_qkv))
        normed_part = rows_of(normed_one, half * part, part)
        inverse_part = rows_of(inverse_one, half * part, part)
        grad_gain_a = jnp.sum(grad_h_one * normed_part, axis=0, keepdims=True)
        grad_x = (grad_after + norm_back(grad_h_one * gain_a, normed_part, inverse_part)).astype(bf16)
        grad_tokens = natural(ordered(half, grad_x, swap_tp(grad_x)))

        grad_gains = cat([grad_gain_a, grad_gain_m])
        grad_gains = grad_gains + swap_tp(grad_gains)
        for mask in [1] + [1 << bit for bit in range(shards.bit_length() - 2, 0, -1)]:
            mid = grad_gains.shape[1] // 2
            grad_gains = grad_gains[:, :mid] + across(grad_gains[:, mid:], mask)
        grad_gains = cols_of(grad_gains, core * unit, unit) + swap_core(
            cols_of(grad_gains, (1 - core) * unit, unit)
        )

        return (
            output,
            grad_tokens,
            grad_gains[0],
            grad_w_query,
            grad_w_key,
            grad_w_value,
            grad_w_out,
            grad_gains[1],
            grad_w_gate,
            grad_w_up,
            grad_w_down,
        )

    return per_device


def solution(mesh):
    wide = P(("shard", "ctx"), None)
    flat = P(("shard", "ctx"))
    both = P(("shard", "ctx"), "tp")
    placed = (wide, P("shard", None), flat, both, both, both, both, flat, both, both, both, wide)
    return jax.shard_map(
        build(mesh.shape["shard"]),
        mesh=mesh,
        in_specs=placed,
        out_specs=(wide, wide, flat, both, both, both, both, flat, both, both, both),
        check_vma=False,
    )
```

time: 2510 us -> 1230 us (0.49)
  waiting for transfers between devices: 2010 us -> 554 us
  starting transfers between devices: 1.43 us -> 149 us
  blocking collectives: 129 us -> 0 us
  local copies, waits for them, and re-layouts: 72.8 us -> 172 us
  other arithmetic: 44.7 us -> 124 us
    reduce_scatter x7 -> x0, waiting for transfers between devices: 1360 us -> none  [the longest x1 335 us: per_device(): lax.psum_scatter(grad_w_gate, ('shard', 'ctx'), scatter_dimension=0, tile...]
    ppermute x0 -> x101, waiting for transfers between devices: none -> 554 us  [the longest x64 479 us: across(): return lax.ppermute(values, 'shard', [(i, i ^ mask) for i in range(shards)])]
    all_gather x7 -> x0, waiting for transfers between devices: 449 us -> none  [the longest x1 123 us: per_device(): lax.all_gather(w_gate, ('shard', 'ctx'), axis=0, tiled=True)]
    psum x3 -> x0, waiting for transfers between devices: 193 us -> none  [the longest x1 90.5 us: per_device(): lax.psum(contract_cols(grad_gate, weight_g) + contract_cols(grad_up, weig...]
    ppermute x0 -> x101, starting transfers between devices: none -> 149 us  [the longest x64 130 us: across(): return lax.ppermute(values, 'shard', [(i, i ^ mask) for i in range(shards)])]
    unnamed x1 -> x0, blocking collectives: 61 us -> none
    select_n x0 -> x21, other arithmetic: none -> 53.1 us  [the longest x17 45 us: ordered(): jnp.where(index == 0, cat([own, other], axis), cat([other, own], axis))]
    rev x0 -> x4, local copies, waits for them, and re-layouts: none -> 43.7 us  [flip_zl(): return jnp.where(zl == 0, split, split[:, :, ::-1]).reshape(values.shape)]
  transfers between devices with their start and end apart: 17 -> 101, of which waited for: 16 -> 42; matrix products, arithmetic and copies ran while one was open for 8% -> 34% of each run, Pallas kernels for 0% -> 0%
where the time goes in v1:
time: 1230 us; the launch traced here: 1220 us
  waiting for transfers between devices  554 us (45%)
  matrix products  218 us (18%)
  local copies, waits for them, and re-layouts  172 us (14%)
  starting transfers between devices  149 us (12%)
  other arithmetic  124 us (10%)
    ppermute x64, waiting for transfers between devices, across(): return lax.ppermute(values, 'shard', [(i, i ^ mask) for i in range(shards)])  479 us
    ppermute x64, starting transfers between devices, across(): return lax.ppermute(values, 'shard', [(i, i ^ mask) for i in range(shards)])  130 us
    ppermute x13, waiting for transfers between devices, swap_tp(): return lax.ppermute(values, 'tp', [(0, 1), (1, 0)])  74.9 us
    dot_general x12, matrix products, contract_cols(): lax.dot_general(left, right, (((1,), (1,)), ((), ())), preferred_element_...  70.8 us
    dot_general x14, matrix products, contract_rows(): lax.dot_general(left, right, (((0,), (0,)), ((), ())), preferred_element_...  68 us
    dot_general x5, matrix products, matmul(): return jnp.dot(left, right, preferred_element_type=jnp.float32)  61.8 us
    unnamed x297, local copies, waits for them, and re-layouts  55.1 us
    select_n x17, other arithmetic, ordered(): jnp.where(index == 0, cat([own, other], axis), cat([other, own], axis))  45 us
  transfers between devices with their start and end apart: 101, of which 42 were waited for; matrix products, arithmetic and copies ran while one was open for 34% of the time, Pallas kernels for 0%

profile of v1, /device:TPU:0, one launch (start us, length us, event | category | flops | bytes accessed | tf_op | source)
XLA Modules:
  0.0 1221.0 jit_solution(2454379071721546627)
XLA Ops:
  36.8 19.3 %rev.14 = bf16[512,4,2,256]{3,2,1,0:T(2,128)(2,1)} reverse(bf16[512,4,2,256]{3,2,1,0:T(2,128)(2,1)} %reshape.460), dimensions={2} | reverse | bytes 4194304 | tf_op jit(solution)/shard_map/rev | solution.py:255
  124.3 14.5 %collective-permute-done.18 = bf16[256,512]{1,0:T(8,128)(2,1)S(1)} collective-permute-done((bf16[256,512]{1,0:T(8,128)(2,1)S(1)}, bf16[256,512]{1,0:T(8,128)(2,1)S(1)}, u32[]{:S(2)}, u32[]{:S(2)}) %collective-permute-start.18) | collective-permute-done | bytes 262176 | tf_op jit(solution)/shard_map/ppermute | solution.py:202
  148.2 27.5 %collective-permute-done.7 = bf16[256,1536]{1,0:T(8,128)(2,1)S(1)} collective-permute-done((bf16[256,1536]{1,0:T(8,128)(2,1)S(1)}, bf16[256,1536]{1,0:T(8,128)(2,1)S(1)}, u32[]{:S(2)}, u32[]{:S(2)}) %collective-permute-start.7) | collective-permute-done | bytes 786464 | tf_op jit(solution)/shard_map/ppermute | solution.py:202
  178.2 13.7 %collective-permute-done.49 = bf16[256,2048]{1,0:T(8,128)(2,1)} collective-permute-done((bf16[256,2048]{1,0:T(8,128)(2,1)S(1)}, bf16[256,2048]{1,0:T(8,128)(2,1)}, u32[]{:S(2)}, u32[]{:S(2)}) %collective-permute-start.49) | collective-permute-done | bytes 1048608 | tf_op jit(solution)/shard_map/ppermute | solution.py:202
  241.0 17.6 %maximum_select_fusion.2 = bf16[256,6144]{1,0:T(8,128)(2,1)S(1)} fusion(bf16[128,6144]{1,0:T(8,128)(2,1)} %collective-permute-done.30, bf16[128,2048]{1,0:T(8,128)(2,1)S(1)} %copy-done.58, bf16[128,2048]{1,0:T(8,128)(2,1)S(1)} %copy-done.57, bf16[128,2048]{1,0:T(8,128)(2,1)S(1)} %copy-done.56, pred[]{:T(512)S(6)} %eq.31), kind=kLoop, calls=%fused_computation.38 | loop fusion | flops 26738688 | bytes 6291457 | tf_op jit(solution)/shard_map/jit(_where)/select_n | solution.py:194
  263.9 10.2 collective-permute-done.39
  291.5 12.1 collective-permute-done.31
  315.0 44.7 %collective-permute-done.40 = bf16[512,1024]{1,0:T(8,128)(2,1)} collective-permute-done((bf16[512,1024]{1,0:T(8,128)(2,1)}, bf16[512,1024]{1,0:T(8,128)(2,1)}, u32[]{:S(2)}, u32[]{:S(2)}) %collective-permute-start.40) | collective-permute-done | bytes 1048608 | tf_op jit(solution)/shard_map/ppermute | solution.py:202
  374.3 10.5 collective-permute-done.42
  384.8 15.6 %fusion.140 = f32[2048,1024]{1,0:T(8,128)} fusion(bf16[2048,2048]{1,0:T(8,128)(2,1)} %constant_dynamic-update-slice_fusion.25, bf16[512,1024]{1,0:T(8,128)(2,1)} %collective-permute-done.42, bf16[512,1024]{1,0:T(8,128)(2,1)} %collective-permute-done.41, bf16[512,1024]{1,0:T(8,128)(2,1)} %collective-permute-done.40, bf16[512,1024]{1,0:T(8,128)(2,1)} %maximum_select_fusion.9), kind=kOutput, calls=%fused_computation.379 | convolution fusion | flops 8606711808 | bytes 20971520 | tf_op jit(solution)/shard_map/dot_general | solution.py:20
  406.5 11.8 collective-permute-done.25
  422.7 43.1 %collective-permute-done.32 = bf16[512,1024]{1,0:T(8,128)(2,1)S(1)} collective-permute-done((bf16[512,1024]{1,0:T(8,128)(2,1)S(1)}, bf16[512,1024]{1,0:T(8,128)(2,1)S(1)}, u32[]{:S(2)}, u32[]{:S(2)}) %collective-permute-start.32) | collective-permute-done | bytes 1048608 | tf_op jit(solution)/shard_map/ppermute | solution.py:202
  468.2 13.0 %fusion.141 = f32[2048,1024]{1,0:T(8,128)} fusion(bf16[2048,2048]{1,0:T(8,128)(2,1)S(1)} %constant_dynamic-update-slice_fusion.16, bf16[512,1024]{1,0:T(8,128)(2,1)S(1)} %collective-permute-done.38, bf16[512,1024]{1,0:T(8,128)(2,1)S(1)} %collective-permute-done.37, bf16[512,1024]{1,0:T(8,128)(2,1)} %collective-permute-done.36, ...), kind=kOutput, calls=%fused_computation.380 | convolution fusion | flops 8606711808 | bytes 20971520 | tf_op jit(solution)/shard_map/dot_general | solution.py:20
  481.3 10.6 collective-permute-done.33
  492.8 20.7 %collective-permute-done.34 = bf16[512,1024]{1,0:T(8,128)(2,1)} collective-permute-done((bf16[512,1024]{1,0:T(8,128)(2,1)S(1)}, bf16[512,1024]{1,0:T(8,128)(2,1)}, u32[]{:S(2)}, u32[]{:S(2)}) %collective-permute-start.34) | collective-permute-done | bytes 1048608 | tf_op jit(solution)/shard_map/ppermute | solution.py:202
  513.4 22.4 %multiply_convert_fusion.1 = (bf16[2048,1024]{1,0:T(8,128)(2,1)}, bf16[2048,1024]{1,0:T(8,128)(2,1)}, bf16[2048,1024]{1,0:T(8,128)(2,1)}) fusion(f32[2048,1024]{1,0:T(8,128)} %fusion.140, f32[2048,1024]{1,0:T(8,128)} %fusion.141, bf16[2048,2048]{1,0:T(8,128)(2,1)} %copy-done.74, bf16[512,1024]{1,0:T(8,128)(2,1)} %collective-permute-done.34, ...), kind=kOutput, calls=%fused_computation.4 | convolution fusion | flops 8638169088 | bytes 41943040 | tf_op jit(solution)/shard_map/dot_general | solution.py:20
  579.4 10.5 add_convert_fusion
  615.6 35.5 %collective-permute-done.93 = bf16[1024,1024]{0,1:T(8,128)(2,1)} collective-permute-done((bf16[1024,1024]{0,1:T(8,128)(2,1)}, bf16[1024,1024]{0,1:T(8,128)(2,1)}, u32[]{:S(2)}, u32[]{:S(2)}) %collective-permute-start.93) | collective-permute-done | bytes 2097184 | tf_op jit(solution)/shard_map/ppermute | solution.py:202
  661.9 32.4 %collective-permute-done.89 = bf16[1024,1024]{0,1:T(8,128)(2,1)} collective-permute-done((bf16[1024,1024]{0,1:T(8,128)(2,1)}, bf16[1024,1024]{0,1:T(8,128)(2,1)}, u32[]{:S(2)}, u32[]{:S(2)}) %collective-permute-start.89) | collective-permute-done | bytes 2097184 | tf_op jit(solution)/shard_map/ppermute | solution.py:202
  723.6 28.1 %collective-permute-done.90 = bf16[512,1024]{0,1:T(8,128)(2,1)} collective-permute-done((bf16[512,1024]{0,1:T(8,128)(2,1)}, bf16[512,1024]{0,1:T(8,128)(2,1)}, u32[]{:S(2)}, u32[]{:S(2)}) %collective-permute-start.90) | collective-permute-done | bytes 1048608 | tf_op jit(solution)/shard_map/ppermute | solution.py:202
  758.9 28.7 %collective-permute-done.91 = bf16[256,1024]{0,1:T(8,128)(2,1)} collective-permute-done((bf16[256,1024]{0,1:T(8,128)(2,1)}, bf16[256,1024]{0,1:T(8,128)(2,1)}, u32[]{:S(2)}, u32[]{:S(2)}) %collective-permute-start.91) | collective-permute-done | bytes 524320 | tf_op jit(solution)/shard_map/ppermute | solution.py:202
  796.1 11.3 fusion.160
  848.0 10.3 collective-permute-done.59
  886.0 11.0 rev.13
  959.1 16.6 %collective-permute-done.84 = bf16[1024,512]{0,1:T(8,128)(2,1)} collective-permute-done((bf16[1024,512]{0,1:T(8,128)(2,1)S(1)}, bf16[1024,512]{0,1:T(8,128)(2,1)}, u32[]{:S(2)}, u32[]{:S(2)}) %collective-permute-start.84) | collective-permute-done | bytes 1048608 | tf_op jit(solution)/shard_map/ppermute | solution.py:202
  980.4 61.7 %collective-permute-done.69 = bf16[1024,512]{0,1:T(8,128)(2,1)} collective-permute-done((bf16[1024,512]{0,1:T(8,128)(2,1)}, bf16[1024,512]{0,1:T(8,128)(2,1)}, u32[]{:S(2)}, u32[]{:S(2)}) %collective-permute-start.69) | collective-permute-done | bytes 1048608 | tf_op jit(solution)/shard_map/ppermute | solution.py:202
  1066.3 14.6 %collective-permute-done.86 = bf16[256,512]{0,1:T(8,128)(2,1)S(1)} collective-permute-done((bf16[256,512]{0,1:T(8,128)(2,1)S(1)}, bf16[256,512]{0,1:T(8,128)(2,1)S(1)}, u32[]{:S(2)}, u32[]{:S(2)}) %collective-permute-start.86) | collective-permute-done | bytes 262176 | tf_op jit(solution)/shard_map/ppermute | solution.py:202
  1083.7 12.9 %collective-permute-start.76 = (bf16[256,512]{0,1:T(8,128)(2,1)S(1)}, bf16[256,512]{0,1:T(8,128)(2,1)S(1)}, u32[]{:S(2)}, u32[]{:S(2)}) collective-permute-start(bf16[256,512]{0,1:T(8,128)(2,1)S(1)} %get-tuple-element.159), channel_id=1, source_target_pairs={{0,16},{4,20},{8,24},{12,28},{16,0},{20,4},{24,8},{28,12},{1,17},{... | collective-permute-start | bytes 786440 | tf_op jit(solution)/shard_map/ppermute | solution.py:202
  1104.5 14.6 %collective-permute-start.81 = (bf16[256,512]{0,1:T(8,128)(2,1)S(1)}, bf16[256,512]{0,1:T(8,128)(2,1)S(1)}, u32[]{:S(2)}, u32[]{:S(2)}) collective-permute-start(bf16[256,512]{0,1:T(8,128)(2,1)S(1)} %get-tuple-element.156), channel_id=1, source_target_pairs={{0,16},{4,20},{8,24},{12,28},{16,0},{20,4},{24,8},{28,12},{1,17},{... | collective-permute-start | bytes 786440 | tf_op jit(solution)/shard_map/ppermute | solution.py:202
  1136.5 20.5 %collective-permute-done.62 = bf16[256,2048]{1,0:T(8,128)(2,1)S(1)} collective-permute-done((bf16[256,2048]{1,0:T(8,128)(2,1)S(1)}, bf16[256,2048]{1,0:T(8,128)(2,1)S(1)}, u32[]{:S(2)}, u32[]{:S(2)}) %collective-permute-start.62) | collective-permute-done | bytes 1048608 | tf_op jit(solution)/shard_map/ppermute | solution.py:208
  1182.9 15.1 %collective-permute-done.48 = bf16[256,2048]{1,0:T(8,128)(2,1)} collective-permute-done((bf16[256,2048]{1,0:T(8,128)(2,1)}, bf16[256,2048]{1,0:T(8,128)(2,1)}, u32[]{:S(2)}, u32[]{:S(2)}) %collective-permute-start.48) | collective-permute-done | bytes 1048608 | tf_op jit(solution)/shard_map/ppermute | solution.py:208
  1201.8 15.0 %collective-permute-done.63 = bf16[256,2048]{1,0:T(8,128)(2,1)S(1)} collective-permute-done((bf16[256,2048]{1,0:T(8,128)(2,1)S(1)}, bf16[256,2048]{1,0:T(8,128)(2,1)S(1)}, u32[]{:S(2)}, u32[]{:S(2)}) %collective-permute-start.63) | collective-permute-done | bytes 1048608 | tf_op jit(solution)/shard_map/ppermute | solution.py:208
  (693 shorter events, 571.6 us)
Async XLA Ops:
  1.4 68.9 %collective-permute-start = (bf16[2,128]{1,0:T(2,128)(2,1)S(1)}, bf16[2,128]{1,0:T(2,128)(2,1)S(1)}, u32[]{:S(2)}, u32[]{:S(2)}) collective-permute-start(bf16[2,128]{1,0:T(2,128)(2,1)S(1)} %pad_maximum_fusion.20), channel_id=1, source_target_pairs={{0,2},{2,0},{1,3},{3,1},{4,6},{6,4},{5,7},{7,5},{8,10},{10,8},{9,1... | collective-permute-start | bytes 1544 | tf_op jit(solution)/shard_map/ppermute | solution.py:205
  8.8 82.8 %collective-permute-start.5 = (bf16[128,2048]{1,0:T(8,128)(2,1)}, bf16[128,2048]{1,0:T(8,128)(2,1)}, u32[]{:S(2)}, u32[]{:S(2)}) collective-permute-start(bf16[128,2048]{1,0:T(8,128)(2,1)} %pad_maximum_fusion.16), channel_id=1, source_target_pairs={{0,2},{2,0},{1,3},{3,1},{4,6},{6,4},{5,7},{7,5},{8,10},{10,8},{9,1... | collective-permute-start | bytes 1572872 | tf_op jit(solution)/shard_map/ppermute | solution.py:205
  117.8 57.9 %collective-permute-start.7 = (bf16[256,1536]{1,0:T(8,128)(2,1)S(1)}, bf16[256,1536]{1,0:T(8,128)(2,1)S(1)}, u32[]{:S(2)}, u32[]{:S(2)}) collective-permute-start(bf16[256,1536]{1,0:T(8,128)(2,1)S(1)} %get-tuple-element.179), channel_id=1, source_target_pairs={{0,16},{4,20},{8,24},{12,28},{16,0},{20,4},{24,8},{28,12},{1,17},{... | collective-permute-start | bytes 2359304 | tf_op jit(solution)/shard_map/ppermute | solution.py:202
  138.7 62.5 %collective-permute-start.4 = (bf16[512,2048]{1,0:T(8,128)(2,1)S(1)}, bf16[512,2048]{1,0:T(8,128)(2,1)S(1)}, u32[]{:S(2)}, u32[]{:S(2)}) collective-permute-start(bf16[512,2048]{1,0:T(8,128)(2,1)S(1)} %get-tuple-element.130), channel_id=1, source_target_pairs={{0,2},{2,0},{1,3},{3,1},{4,6},{6,4},{5,7},{7,5},{8,10},{10,8},{9,1... | collective-permute-start | bytes 6291464 | tf_op jit(solution)/shard_map/ppermute | solution.py:205
  140.1 51.8 %collective-permute-start.49 = (bf16[256,2048]{1,0:T(8,128)(2,1)S(1)}, bf16[256,2048]{1,0:T(8,128)(2,1)}, u32[]{:S(2)}, u32[]{:S(2)}) collective-permute-start(bf16[256,2048]{1,0:T(8,128)(2,1)S(1)} %copy-done.68), channel_id=1, source_target_pairs={{0,8},{4,12},{8,0},{12,4},{16,24},{20,28},{24,16},{28,20},{1,9},{5... | collective-permute-start | bytes 3145736 | tf_op jit(solution)/shard_map/ppermute | solution.py:202
  178.0 130.9 %collective-permute-start.51 = (bf16[512,2048]{1,0:T(8,128)(2,1)}, bf16[512,2048]{1,0:T(8,128)(2,1)}, u32[]{:S(2)}, u32[]{:S(2)}) collective-permute-start(bf16[512,2048]{1,0:T(8,128)(2,1)} %reshape.461), channel_id=1, source_target_pairs={{0,2},{2,0},{1,3},{3,1},{4,6},{6,4},{5,7},{7,5},{8,10},{10,8},{9,1... | collective-permute-start | bytes 6291464 | tf_op jit(solution)/shard_map/ppermute | solution.py:205
  191.8 49.1 %collective-permute-start.30 = (bf16[128,6144]{1,0:T(8,128)(2,1)}, bf16[128,6144]{1,0:T(8,128)(2,1)}, u32[]{:S(2)}, u32[]{:S(2)}) collective-permute-start(bf16[128,6144]{1,0:T(8,128)(2,1)} %pad_maximum_fusion.8), channel_id=1, source_target_pairs={{0,2},{2,0},{1,3},{3,1},{4,6},{6,4},{5,7},{7,5},{8,10},{10,8},{9,1... | collective-permute-start | bytes 4718600 | tf_op jit(solution)/shard_map/ppermute | solution.py:205
  192.8 94.1 %collective-permute-start.50 = (bf16[256,2048]{1,0:T(8,128)(2,1)}, bf16[256,2048]{1,0:T(8,128)(2,1)}, u32[]{:S(2)}, u32[]{:S(2)}) collective-permute-start(bf16[256,2048]{1,0:T(8,128)(2,1)} %collective-permute-done.49), channel_id=1, source_target_pairs={{0,1},{1,0},{2,3},{3,2},{4,5},{5,4},{6,7},{7,6},{8,9},{9,8},{10,11... | collective-permute-start | bytes 3145736 | tf_op jit(solution)/shard_map/ppermute | solution.py:208
  240.9 49.5 %collective-permute-start.20 = (bf16[512,2048]{1,0:T(8,128)(2,1)S(1)}, bf16[512,2048]{1,0:T(8,128)(2,1)S(1)}, u32[]{:S(2)}, u32[]{:S(2)}) collective-permute-start(bf16[512,2048]{1,0:T(8,128)(2,1)S(1)} %convolution_convert_fusion.2), channel_id=1, source_target_pairs={{0,2},{2,0},{1,3},{3,1},{4,6},{6,4},{5,7},{7,5},{8,10},{10,8},{9,1... | collective-permute-start | bytes 6291464 | tf_op jit(solution)/shard_map/ppermute | solution.py:205
  286.9 72.8 %collective-permute-start.40 = (bf16[512,1024]{1,0:T(8,128)(2,1)}, bf16[512,1024]{1,0:T(8,128)(2,1)}, u32[]{:S(2)}, u32[]{:S(2)}) collective-permute-start(bf16[512,1024]{1,0:T(8,128)(2,1)} %maximum_select_fusion.9), channel_id=1, source_target_pairs={{0,16},{4,20},{8,24},{12,28},{16,0},{20,4},{24,8},{28,12},{1,17},{... | collective-permute-start | bytes 3145736 | tf_op jit(solution)/shard_map/ppermute | solution.py:202
  290.4 71.1 %collective-permute-start.53 = (bf16[256,2048]{1,0:T(8,128)(2,1)}, bf16[256,2048]{1,0:T(8,128)(2,1)S(1)}, u32[]{:S(2)}, u32[]{:S(2)}) collective-permute-start(bf16[256,2048]{1,0:T(8,128)(2,1)} %collective-permute-done.50), channel_id=1, source_target_pairs={{0,2},{2,0},{1,3},{3,1},{4,6},{6,4},{5,7},{7,5},{8,10},{10,8},{9,1... | collective-permute-start | bytes 3145736 | tf_op jit(solution)/shard_map/ppermute | solution.py:205
  303.6 58.8 %collective-permute-start.21 = (bf16[256,2048]{1,0:T(8,128)(2,1)S(1)}, bf16[256,2048]{1,0:T(8,128)(2,1)S(1)}, u32[]{:S(2)}, u32[]{:S(2)}) collective-permute-start(bf16[256,2048]{1,0:T(8,128)(2,1)S(1)} %fusion.16), channel_id=1, source_target_pairs={{0,1},{1,0},{2,3},{3,2},{4,5},{5,4},{6,7},{7,6},{8,9},{9,8},{10,11... | collective-permute-start | bytes 3145736 | tf_op jit(solution)/shard_map/ppermute | solution.py:208
  308.9 65.4 %collective-permute-start.41 = (bf16[512,1024]{1,0:T(8,128)(2,1)}, bf16[512,1024]{1,0:T(8,128)(2,1)}, u32[]{:S(2)}, u32[]{:S(2)}) collective-permute-start(bf16[512,1024]{1,0:T(8,128)(2,1)} %maximum_select_fusion.9), channel_id=1, source_target_pairs={{0,4},{4,0},{8,12},{12,8},{16,20},{20,16},{24,28},{28,24},{1,5},{5... | collective-permute-start | bytes 3145736 | tf_op jit(solution)/shard_map/ppermute | solution.py:202
  314.0 105.8 %collective-permute-start.36 = (bf16[512,1024]{1,0:T(8,128)(2,1)}, bf16[512,1024]{1,0:T(8,128)(2,1)}, u32[]{:S(2)}, u32[]{:S(2)}) collective-permute-start(bf16[512,1024]{1,0:T(8,128)(2,1)} %maximum_select_fusion.8), channel_id=1, source_target_pairs={{0,16},{4,20},{8,24},{12,28},{16,0},{20,4},{24,8},{28,12},{1,17},{... | collective-permute-start | bytes 3145736 | tf_op jit(solution)/shard_map/ppermute | solution.py:202
  418.3 47.5 %collective-permute-start.32 = (bf16[512,1024]{1,0:T(8,128)(2,1)S(1)}, bf16[512,1024]{1,0:T(8,128)(2,1)S(1)}, u32[]{:S(2)}, u32[]{:S(2)}) collective-permute-start(bf16[512,1024]{1,0:T(8,128)(2,1)S(1)} %copy-done.67), channel_id=1, source_target_pairs={{0,16},{4,20},{8,24},{12,28},{16,0},{20,4},{24,8},{28,12},{1,17},{... | collective-permute-start | bytes 3145736 | tf_op jit(solution)/shard_map/ppermute | solution.py:202
  419.6 47.9 %collective-permute-start.28 = (bf16[256,2048]{1,0:T(8,128)(2,1)S(1)}, bf16[256,2048]{1,0:T(8,128)(2,1)S(1)}, u32[]{:S(2)}, u32[]{:S(2)}) collective-permute-start(bf16[256,2048]{1,0:T(8,128)(2,1)S(1)} %collective-permute-done.23), channel_id=1, source_target_pairs={{0,2},{2,0},{1,3},{3,1},{4,6},{6,4},{5,7},{7,5},{8,10},{10,8},{9,1... | collective-permute-start | bytes 3145736 | tf_op jit(solution)/shard_map/ppermute | solution.py:205
  419.7 48.2 %collective-permute-start.29 = (bf16[256,2048]{1,0:T(8,128)(2,1)S(1)}, bf16[256,2048]{1,0:T(8,128)(2,1)S(1)}, u32[]{:S(2)}, u32[]{:S(2)}) collective-permute-start(bf16[256,2048]{1,0:T(8,128)(2,1)S(1)} %pad_maximum_fusion.10), channel_id=1, source_target_pairs={{0,2},{2,0},{1,3},{3,1},{4,6},{6,4},{5,7},{7,5},{8,10},{10,8},{9,1... | collective-permute-start | bytes 3145736 | tf_op jit(solution)/shard_map/ppermute | solution.py:205
  420.4 47.7 %collective-permute-start.37 = (bf16[512,1024]{1,0:T(8,128)(2,1)}, bf16[512,1024]{1,0:T(8,128)(2,1)S(1)}, u32[]{:S(2)}, u32[]{:S(2)}) collective-permute-start(bf16[512,1024]{1,0:T(8,128)(2,1)} %maximum_select_fusion.8), channel_id=1, source_target_pairs={{0,4},{4,0},{8,12},{12,8},{16,20},{20,16},{24,28},{28,24},{1,5},{5... | collective-permute-start | bytes 3145736 | tf_op jit(solution)/shard_map/ppermute | solution.py:202
  557.3 48.9 %collective-permute-start.97 = (bf16[1024,1024]{0,1:T(8,128)(2,1)}, bf16[1024,1024]{0,1:T(8,128)(2,1)}, u32[]{:S(2)}, u32[]{:S(2)}) collective-permute-start(bf16[1024,1024]{0,1:T(8,128)(2,1)} %fusion.48), channel_id=1, source_target_pairs={{0,4},{4,0},{8,12},{12,8},{16,20},{20,16},{24,28},{28,24},{1,5},{5... | collective-permute-start | bytes 6291464 | tf_op jit(solution)/shard_map/ppermute | solution.py:202
  559.1 92.0 %collective-permute-start.93 = (bf16[1024,1024]{0,1:T(8,128)(2,1)}, bf16[1024,1024]{0,1:T(8,128)(2,1)}, u32[]{:S(2)}, u32[]{:S(2)}) collective-permute-start(bf16[1024,1024]{0,1:T(8,128)(2,1)} %fusion.45), channel_id=1, source_target_pairs={{0,4},{4,0},{8,12},{12,8},{16,20},{20,16},{24,28},{28,24},{1,5},{5... | collective-permute-start | bytes 6291464 | tf_op jit(solution)/shard_map/ppermute | solution.py:202
  559.4 134.9 %collective-permute-start.89 = (bf16[1024,1024]{0,1:T(8,128)(2,1)}, bf16[1024,1024]{0,1:T(8,128)(2,1)}, u32[]{:S(2)}, u32[]{:S(2)}) collective-permute-start(bf16[1024,1024]{0,1:T(8,128)(2,1)} %fusion.42), channel_id=1, source_target_pairs={{0,4},{4,0},{8,12},{12,8},{16,20},{20,16},{24,28},{28,24},{1,5},{5... | collective-permute-start | bytes 6291464 | tf_op jit(solution)/shard_map/ppermute | solution.py:202
  569.8 226.2 %collective-permute-start.43 = (bf16[1024,2048]{1,0:T(8,128)(2,1)}, bf16[1024,2048]{1,0:T(8,128)(2,1)}, u32[]{:S(2)}, u32[]{:S(2)}) collective-permute-start(bf16[1024,2048]{1,0:T(8,128)(2,1)} %convolution_convert_fusion), channel_id=1, source_target_pairs={{0,2},{2,0},{1,3},{3,1},{4,6},{6,4},{5,7},{7,5},{8,10},{10,8},{9,1... | collective-permute-start | bytes 12582920 | tf_op jit(solution)/shard_map/ppermute | solution.py:205
  590.0 123.4 %collective-permute-start.54 = (bf16[1024,2048]{1,0:T(8,128)(2,1)}, bf16[1024,2048]{1,0:T(8,128)(2,1)}, u32[]{:S(2)}, u32[]{:S(2)}) collective-permute-start(bf16[1024,2048]{1,0:T(8,128)(2,1)} %add_convert_fusion), channel_id=1, source_target_pairs={{0,2},{2,0},{1,3},{3,1},{4,6},{6,4},{5,7},{7,5},{8,10},{10,8},{9,1... | collective-permute-start | bytes 12582920 | tf_op jit(solution)/shard_map/ppermute | solution.py:205
  614.1 91.8 %collective-permute-start.98 = (bf16[512,1024]{0,1:T(8,128)(2,1)S(1)}, bf16[512,1024]{0,1:T(8,128)(2,1)S(1)}, u32[]{:S(2)}, u32[]{:S(2)}) collective-permute-start(bf16[512,1024]{0,1:T(8,128)(2,1)S(1)} %slice.929), channel_id=1, source_target_pairs={{0,16},{4,20},{8,24},{12,28},{16,0},{20,4},{24,8},{28,12},{1,17},{... | collective-permute-start | bytes 3145736 | tf_op jit(solution)/shard_map/ppermute | solution.py:202
  660.4 50.2 %collective-permute-start.94 = (bf16[512,1024]{0,1:T(8,128)(2,1)S(1)}, bf16[512,1024]{0,1:T(8,128)(2,1)}, u32[]{:S(2)}, u32[]{:S(2)}) collective-permute-start(bf16[512,1024]{0,1:T(8,128)(2,1)S(1)} %slice.930), channel_id=1, source_target_pairs={{0,16},{4,20},{8,24},{12,28},{16,0},{20,4},{24,8},{28,12},{1,17},{... | collective-permute-start | bytes 3145736 | tf_op jit(solution)/shard_map/ppermute | solution.py:202
  722.1 68.6 %collective-permute-start.55 = (bf16[512,1024]{1,0:T(8,128)(2,1)}, bf16[512,1024]{1,0:T(8,128)(2,1)S(1)}, u32[]{:S(2)}, u32[]{:S(2)}) collective-permute-start(bf16[512,1024]{1,0:T(8,128)(2,1)} %pad_maximum_fusion.12), channel_id=1, source_target_pairs={{0,1},{1,0},{2,3},{3,2},{4,5},{5,4},{6,7},{7,6},{8,9},{9,8},{10,11... | collective-permute-start | bytes 3145736 | tf_op jit(solution)/shard_map/ppermute | solution.py:208
  758.9 83.0 %collective-permute-start.100 = (bf16[128,2048]{0,1:T(8,128)(2,1)}, bf16[128,2048]{0,1:T(8,128)(2,1)}, u32[]{:S(2)}, u32[]{:S(2)}) collective-permute-start(bf16[128,2048]{0,1:T(8,128)(2,1)} %get-tuple-element.140), channel_id=1, source_target_pairs={{0,2},{2,0},{1,3},{3,1},{4,6},{6,4},{5,7},{7,5},{8,10},{10,8},{9,1... | collective-permute-start | bytes 1572872 | tf_op jit(solution)/shard_map/ppermute | solution.py:205
  951.3 101.7 %collective-permute-start.79 = (bf16[1024,512]{0,1:T(8,128)(2,1)S(1)}, bf16[1024,512]{0,1:T(8,128)(2,1)S(1)}, u32[]{:S(2)}, u32[]{:S(2)}) collective-permute-start(bf16[1024,512]{0,1:T(8,128)(2,1)S(1)} %fusion.72), channel_id=1, source_target_pairs={{0,4},{4,0},{8,12},{12,8},{16,20},{20,16},{24,28},{28,24},{1,5},{5... | collective-permute-start | bytes 3145736 | tf_op jit(solution)/shard_map/ppermute | solution.py:202
  951.6 98.7 %collective-permute-start.74 = (bf16[1024,512]{0,1:T(8,128)(2,1)}, bf16[1024,512]{0,1:T(8,128)(2,1)}, u32[]{:S(2)}, u32[]{:S(2)}) collective-permute-start(bf16[1024,512]{0,1:T(8,128)(2,1)} %fusion.75), channel_id=1, source_target_pairs={{0,4},{4,0},{8,12},{12,8},{16,20},{20,16},{24,28},{28,24},{1,5},{5... | collective-permute-start | bytes 3145736 | tf_op jit(solution)/shard_map/ppermute | solution.py:202
  953.3 88.8 %collective-permute-start.69 = (bf16[1024,512]{0,1:T(8,128)(2,1)}, bf16[1024,512]{0,1:T(8,128)(2,1)}, u32[]{:S(2)}, u32[]{:S(2)}) collective-permute-start(bf16[1024,512]{0,1:T(8,128)(2,1)} %fusion.78), channel_id=1, source_target_pairs={{0,4},{4,0},{8,12},{12,8},{16,20},{20,16},{24,28},{28,24},{1,5},{5... | collective-permute-start | bytes 3145736 | tf_op jit(solution)/shard_map/ppermute | solution.py:202
  959.0 167.0 %collective-permute-start.61 = (bf16[512,2048]{1,0:T(8,128)(2,1)}, bf16[512,2048]{1,0:T(8,128)(2,1)}, u32[]{:S(2)}, u32[]{:S(2)}) collective-permute-start(bf16[512,2048]{1,0:T(8,128)(2,1)} %convolution_convert_fusion.1), channel_id=1, source_target_pairs={{0,2},{2,0},{1,3},{3,1},{4,6},{6,4},{5,7},{7,5},{8,10},{10,8},{9,1... | collective-permute-start | bytes 6291464 | tf_op jit(solution)/shard_map/ppermute | solution.py:205
  978.3 76.7 %collective-permute-start.85 = (bf16[256,512]{0,1:T(8,128)(2,1)S(1)}, bf16[256,512]{0,1:T(8,128)(2,1)S(1)}, u32[]{:S(2)}, u32[]{:S(2)}) collective-permute-start(bf16[256,512]{0,1:T(8,128)(2,1)S(1)} %get-tuple-element.151), channel_id=1, source_target_pairs={{0,8},{4,12},{8,0},{12,4},{16,24},{20,28},{24,16},{28,20},{1,9},{5... | collective-permute-start | bytes 786440 | tf_op jit(solution)/shard_map/ppermute | solution.py:202
  (181 other events, 3530.1 us)

commit v2 on v1

v2 whole, which is shorter than its diff:
```python
import math

import jax
import jax.numpy as jnp
from jax import lax
from jax.experimental import pallas as pl
from jax.experimental.pallas import tpu as pltpu
from jax.sharding import PartitionSpec as P

HD = 128
LENGTH = 1024


norm_eps = 1e-05
rope_base = 10000.0

bf16 = jnp.bfloat16
f32 = jnp.float32


def matmul(left, right):
    return jnp.dot(left, right, preferred_element_type=jnp.float32)


def contract_rows(left, right):
    return lax.dot_general(
        left, right, (((0,), (0,)), ((), ())), preferred_element_type=jnp.float32
    )


def contract_cols(left, right):
    return lax.dot_general(
        left, right, (((1,), (1,)), ((), ())), preferred_element_type=jnp.float32
    )


def norm_parts(values):
    inverse = lax.rsqrt(jnp.mean(values * values, axis=-1, keepdims=True) + norm_eps)
    return (values * inverse, inverse)


def norm_back(grad_scaled, normed, inverse):
    return inverse * (grad_scaled - normed * jnp.mean(grad_scaled * normed, axis=-1, keepdims=True))


def doc_positions(seg_row):
    places = jnp.arange(seg_row.shape[0], dtype=jnp.int32)
    starts_here = jnp.concatenate([jnp.ones((1,), dtype=jnp.bool_), seg_row[1:] != seg_row[:-1]])
    starts = lax.cummax(jnp.where(starts_here, places, jnp.zeros_like(places)), axis=0)
    return places - starts


def rope_tables(positions):
    half_dim = HD // 2
    freqs = rope_base ** (-(jnp.arange(half_dim, dtype=jnp.float32) * (2.0 / HD)))
    angles = positions.astype(jnp.float32)[:, None] * freqs[None, :]
    cosine, sine = jnp.cos(angles), jnp.sin(angles)
    return cat([cosine, cosine], 1), cat([-sine, sine], 1)


def cat(parts, axis=0):
    return jnp.concatenate(parts, axis=axis)


def rows_of(values, start, size):
    return lax.dynamic_slice_in_dim(values, start, size, 0)


def ordered(index, own, other, axis=0):
    return jnp.where(index == 0, cat([own, other], axis), cat([other, own], axis))


def after(values, *events):
    return lax.optimization_barrier((values, events))[0]


def small_call(body, scalars, arrays, outs):
    scalars = jnp.stack([jnp.asarray(v, jnp.int32) for v in scalars])
    return pl.pallas_call(
        body,
        grid_spec=pltpu.PrefetchScalarGridSpec(
            num_scalar_prefetch=1,
            grid=(1,),
            in_specs=[pl.BlockSpec(a.shape, lambda i, s: (0, 0)) for a in arrays],
            out_specs=[pl.BlockSpec(o.shape, lambda i, s: (0, 0)) for o in outs],
        ),
        out_shape=outs,
    )(scalars, *arrays)


def array_of(rows, cols, dtype=bf16):
    return jax.ShapeDtypeStruct((rows, cols), dtype)


def permute_cols(values, index, block):
    rows, width = values.shape
    step = min(rows, 128)
    count = width // block
    if block % 128:
        return cat([lax.dynamic_slice_in_dim(values, index[j] * block, block, 1) for j in range(count)], 1)

    def body(index_ref, in_ref, out_ref):
        for j in range(count):
            start = pl.multiple_of(index_ref[j] * block, block)
            out_ref[:, j * block : (j + 1) * block] = in_ref[:, pl.ds(start, block)]

    spec = pl.BlockSpec((step, width), lambda i, s: (i, 0))
    return pl.pallas_call(
        body,
        grid_spec=pltpu.PrefetchScalarGridSpec(
            num_scalar_prefetch=1, grid=(rows // step,), in_specs=[spec], out_specs=spec
        ),
        out_shape=jax.ShapeDtypeStruct(values.shape, values.dtype),
    )(index, values)


def join_tokens(own, other, half, index, block):
    rows, width = own.shape
    count = width // block
    if block % 128:
        return permute_cols(ordered(half, own, other), index, block)

    def body(index_ref, own_ref, other_ref, out_ref):
        here = pl.program_id(0) == index_ref[count]

        def move(ref):
            for j in range(count):
                start = pl.multiple_of(index_ref[j] * block, block)
                out_ref[:, j * block : (j + 1) * block] = ref[:, pl.ds(start, block)]

        pl.when(here)(lambda: move(own_ref))
        pl.when(jnp.logical_not(here))(lambda: move(other_ref))

    whole = pl.BlockSpec((rows, width), lambda i, s: (0, 0))
    return pl.pallas_call(
        body,
        grid_spec=pltpu.PrefetchScalarGridSpec(
            num_scalar_prefetch=1,
            grid=(2,),
            in_specs=[whole, whole],
            out_specs=pl.BlockSpec((rows, width), lambda i, s: (i, 0)),
        ),
        out_shape=jax.ShapeDtypeStruct((2 * rows, width), own.dtype),
    )(cat([index, half[None]]), own, other)


def score_parts(query, keys, rows_seg, cols_seg, diagonal):
    scores = contract_cols(query, keys) * (1.0 / math.sqrt(HD)) - math.log(LENGTH)
    allowed = rows_seg == cols_seg
    if diagonal:
        size = query.shape[0]
        places = lax.broadcasted_iota(jnp.int32, (size, size), 0)
        allowed = allowed & (places >= lax.broadcasted_iota(jnp.int32, (size, size), 1))
    return jax.nn.sigmoid(scores), allowed


def swap_halves(values):
    return pltpu.roll(values, HD // 2, 1)


def attend_forward(qkv, seg_row, cosine, sine, tile=256):
    length = seg_row.shape[0]
    heads = qkv.shape[1] // (3 * HD)
    tiles = length // tile

    def body(seg_ref, qkv_ref, cos_ref, sin_ref, seg_col, seg_line, out_ref, kept_ref, acc):
        cos_t, sin_t = cos_ref[...], sin_ref[...]
        for part in (0, 1):
            where = slice(part * HD, (part + 1) * HD)
            value = qkv_ref[:, where]
            kept_ref[:, where] = (value * cos_t + swap_halves(value) * sin_t).astype(bf16)
        kept_ref[:, 2 * HD :] = qkv_ref[:, 2 * HD :].astype(bf16)
        for i in range(tiles):
            rows = slice(i * tile, (i + 1) * tile)

            def step(j, diagonal, rows=rows):
                cols = slice(j * tile, (j + 1) * tile)
                sig, allowed = score_parts(
                    kept_ref[rows, :HD], kept_ref[cols, HD : 2 * HD],
                    seg_col[rows, :], seg_line[:, cols], diagonal,
                )
                weights = jnp.where(allowed, sig, 0.0).astype(bf16)
                return matmul(weights, kept_ref[cols, 2 * HD :])

            acc[...] = step(i, True)
            for j in range(i):

                @pl.when(seg_ref[(j + 1) * tile - 1] == seg_ref[i * tile])
                def _(j=j):
                    acc[...] += step(j, False)

            out_ref[rows, :] = acc[...].astype(bf16)

    full = pl.BlockSpec((length, HD), lambda h, s: (0, 0))
    return pl.pallas_call(
        body,
        grid_spec=pltpu.PrefetchScalarGridSpec(
            num_scalar_prefetch=1,
            grid=(heads,),
            in_specs=[
                pl.BlockSpec((length, 3 * HD), lambda h, s: (0, h)),
                full,
                full,
                pl.BlockSpec((length, 1), lambda h, s: (0, 0)),
                pl.BlockSpec((1, length), lambda h, s: (0, 0)),
            ],
            out_specs=[
                pl.BlockSpec((length, HD), lambda h, s: (0, h)),
                pl.BlockSpec((length, 3 * HD), lambda h, s: (0, h)),
            ],
            scratch_shapes=[pltpu.VMEM((tile, HD), f32)],
        ),
        out_shape=[array_of(length, heads * HD), array_of(length, 3 * heads * HD)],
    )(seg_row, qkv, cosine, sine, seg_row[:, None], seg_row[None, :])


def attend_backward(kept, grad_heads, seg_row, cosine, sine, first, heads, tile=256):
    length = seg_row.shape[0]
    tiles = length // tile
    scale = 1.0 / math.sqrt(HD)

    def body(seg_ref, kept_ref, do_ref, cos_ref, sin_ref, seg_col, seg_line, out_ref, dq, dk, dv):
        dk[...] = jnp.zeros_like(dk)
        dv[...] = jnp.zeros_like(dv)
        for i in range(tiles):
            rows = slice(i * tile, (i + 1) * tile)

            def step(j, diagonal, rows=rows):
                cols = slice(j * tile, (j + 1) * tile)
                query, grad = kept_ref[rows, :HD], do_ref[rows, :]
                keys = kept_ref[cols, HD : 2 * HD]
                sig, allowed = score_parts(query, keys, seg_col[rows, :], seg_line[:, cols], diagonal)
                weights = jnp.where(allowed, sig, 0.0).astype(bf16)
                dv[cols, :] += contract_rows(weights, grad)
                grad_probs = contract_cols(grad, kept_ref[cols, 2 * HD :])
                grad_scores = jnp.where(allowed, grad_probs * sig * (1.0 - sig), 0.0).astype(bf16)
                dk[cols, :] += contract_rows(grad_scores, query)
                return matmul(grad_scores, keys)

            dq[rows, :] = step(i, True)
            for j in range(i):

                @pl.when(seg_ref[(j + 1) * tile - 1] == seg_ref[i * tile])
                def _(j=j, rows=rows):
                    dq[rows, :] += step(j, False)

        cos_t, sin_t = cos_ref[...], sin_ref[...]
        for part, ref in ((0, dq), (1, dk)):
            grad = ref[...] * scale
            out_ref[:, part * HD : (part + 1) * HD] = (grad * cos_t - swap_halves(grad) * sin_t).astype(bf16)
        out_ref[:, 2 * HD :] = dv[...].astype(bf16)

    full = pl.BlockSpec((length, HD), lambda h, s: (0, 0))
    return pl.pallas_call(
        body,
        grid_spec=pltpu.PrefetchScalarGridSpec(
            num_scalar_prefetch=1,
            grid=(heads,),
            in_specs=[
                pl.BlockSpec((length, 3 * HD), lambda h, s: (0, first + h)),
                pl.BlockSpec((length, HD), lambda h, s: (0, first + h)),
                full,
                full,
                pl.BlockSpec((length, 1), lambda h, s: (0, 0)),
                pl.BlockSpec((1, length), lambda h, s: (0, 0)),
            ],
            out_specs=pl.BlockSpec((length, 3 * HD), lambda h, s: (0, h)),
            scratch_shapes=[pltpu.VMEM((length, HD), f32)] * 3,
        ),
        out_shape=array_of(length, 3 * heads * HD),
    )(seg_row, kept, grad_heads, cosine, sine, seg_row[:, None], seg_row[None, :])


def build(shards):
    far = [k << 2 for k in range(1, shards // 4)]
    line = [k << 1 for k in range(1, shards // 2)]

    def across(values, mask):
        return lax.ppermute(values, "shard", [(i, i ^ mask) for i in range(shards)])

    def swap_core(values):
        return lax.ppermute(values, "ctx", [(0, 1), (1, 0)])

    def swap_tp(values):
        return lax.ppermute(values, "tp", [(0, 1), (1, 0)])

    def per_device(
        tokens,
        segments,
        gain_attn,
        w_query,
        w_key,
        w_value,
        w_out,
        gain_mlp,
        w_gate,
        w_up,
        w_down,
        cotangent,
    ):
        shard = lax.axis_index("shard").astype(jnp.int32)
        core = lax.axis_index("ctx").astype(jnp.int32)
        half = lax.axis_index("tp").astype(jnp.int32)
        y, zl = shard & 1, (shard >> 1) & 1
        rows, width = tokens.shape
        part = rows // 2
        block = width // shards
        unit = block // 2
        n_attn = w_query.shape[1] // 2
        n_ff = w_gate.shape[1] // 4
        heads = n_attn // HD
        half_s = shards // 2
        pad = 16

        place = jnp.arange(shards, dtype=jnp.int32)
        rel = (((shard >> 2) ^ ((place % half_s) >> 1)) << 2) | ((place & 1) << 1) | (y ^ (place // half_s))
        nat = ((y ^ (place & 1)) * half_s) | (((shard >> 2) ^ (place >> 2)) << 1) | ((place >> 1) & 1)

        attn_w = [w_query, w_key, w_value, w_out]
        ff_w = [w_gate, w_up, w_down]

        def send_attn(s_ref, q, k, v, o, out):
            start = pl.multiple_of((1 - s_ref[0]) * n_attn, n_attn)
            for h in range(heads):
                for i, ref in enumerate((q, k, v)):
                    out[:, (3 * h + i) * HD : (3 * h + i + 1) * HD] = ref[:, pl.ds(start + h * HD, HD)]
            out[:, 3 * n_attn :] = o[:, pl.ds(start, n_attn)]

        (sent_a,) = small_call(send_attn, [core], attn_w, [array_of(unit, 4 * n_attn)])
        other_a = swap_core(sent_a)
        gains = jnp.stack([gain_attn, gain_mlp])
        other_gains = swap_core(gains)

        def keep_attn(s_ref, q, k, v, o, other, own_g, other_g, out_qkv, out_o):
            me = s_ref[0]
            start = pl.multiple_of(me * n_attn, n_attn)
            mine, theirs = pl.ds(me * unit, unit), pl.ds((1 - me) * unit, unit)
            for h in range(heads):
                for i, ref in enumerate((q, k, v)):
                    where = slice((3 * h + i) * HD, (3 * h + i + 1) * HD)
                    out_qkv[mine, where] = ref[:, pl.ds(start + h * HD, HD)]
            out_o[mine, :] = o[:, pl.ds(start, n_attn)]
            out_qkv[theirs, :] = other[:, : 3 * n_attn]
            out_o[theirs, :] = other[:, 3 * n_attn :]
            first, second = own_g[...], other_g[...]
            low = jnp.where(me == 0, first, second)
            high = jnp.where(me == 0, second, first)
            line_g = cat([low, high, jnp.zeros((2, 3 * n_attn - block), bf16)], 1)
            out_qkv[block:, :] = cat([line_g, jnp.zeros((pad - 2, 3 * n_attn), bf16)])

        block_qkv, block_o = small_call(
            keep_attn, [core], attn_w + [other_a, gains, other_gains],
            [array_of(block + pad, 3 * n_attn), array_of(block, n_attn)],
        )

        def gather_line(own, gate):
            near = [own] + [across(own, mask) for mask in line]
            return near + [across(v, 1) for v in near]

        def place_line(parts, take):
            full = jnp.zeros((width, parts[0].shape[1]), bf16)
            for i, v in enumerate(parts):
                where = (i & ~1) | ((i & 1) ^ zl)
                full = lax.dynamic_update_slice_in_dim(full, take(v), where * block, 0)
            return full

        parts_qkv = gather_line(block_qkv, None)
        weight_qkv = place_line(parts_qkv, lambda v: v[:block])
        gain_rows = [v[block : block + 2, :block] for v in parts_qkv]
        gain_pairs = [ordered(zl, gain_rows[i], gain_rows[i + 1], 1) for i in range(0, shards, 2)]
        gains_rel = cat(gain_pairs, 1).astype(f32)
        gain_a, gain_m = gains_rel[0:1], gains_rel[1:2]

        block_o = after(block_o, parts_qkv[1])
        parts_o = gather_line(block_o, None)
        weight_o = place_line(parts_o, lambda v: v)

        def send_ff(s_ref, g, u, d, out):
            start = pl.multiple_of((1 - s_ref[0]) * 2 * n_ff, n_ff)
            for i, ref in enumerate((g, u, d)):
                out[:, i * 2 * n_ff : (i + 1) * 2 * n_ff] = ref[:, pl.ds(start, 2 * n_ff)]

        (sent_f,) = small_call(send_ff, [core], [after(w_gate, other_a)] + ff_w[1:], [array_of(unit, 6 * n_ff)])
        other_f = swap_core(sent_f)

        def keep_ff(s_ref, w, other, keep, send):
            me, low = s_ref[0], s_ref[1]
            mine, theirs = pl.ds(me * unit, unit), pl.ds((1 - me) * unit, unit)
            for out, which in ((keep, low), (send, 1 - low)):
                start = pl.multiple_of(which * n_ff, n_ff)
                out[mine, :] = w[:, pl.ds(pl.multiple_of(me * 2 * n_ff, n_ff) + start, n_ff)]
                out[theirs, :] = other[:, pl.ds(start, n_ff)]

        def pair_rows(s_ref, own, other, out):
            low = s_ref[0]
            out[pl.ds(low * block, block), :] = own[...]
            out[pl.ds((1 - low) * block, block), :] = other[...]

        def ff_weight(i, gate):
            keep, send = small_call(
                keep_ff, [core, zl], [ff_w[i], other_f[:, i * 2 * n_ff : (i + 1) * 2 * n_ff]],
                [array_of(block, n_ff)] * 2,
            )
            send = after(send, gate)
            (own,) = small_call(pair_rows, [zl], [keep, across(send, 2)], [array_of(2 * block, n_ff)])
            near = [own] + [across(own, mask) for mask in far]
            return near[1], cat(near + [across(v, 1) for v in near])

        event_g, weight_g = ff_weight(0, parts_o[1])
        event_u, weight_u = ff_weight(1, event_g)
        event_d, weight_d = ff_weight(2, event_u)

        seg_row = segments[0]
        cosine, sine = rope_tables(doc_positions(seg_row))
        x_own = permute_cols(tokens, rel, block)
        x_both = ordered(core, x_own, swap_core(x_own))
        normed_all, inverse_all = norm_parts(x_both.astype(f32))
        h_one = (normed_all * gain_a).astype(bf16)
        qkv = matmul(h_one, weight_qkv)
        mixed, kept = attend_forward(qkv, seg_row, cosine, sine)

        def to_slice(operand, project):
            away = project(rows_of(operand, (1 - core) * rows, rows)).astype(bf16)
            here = rows_of(operand, core * rows, rows)
            away = swap_core(away)
            other = project(rows_of(here, (1 - half) * part, part)) + rows_of(
                away, (1 - half) * part, part
            ).astype(f32)
            other = swap_tp(other.astype(bf16))
            own = project(rows_of(here, half * part, part)) + rows_of(
                away, half * part, part
            ).astype(f32)
            return own + other.astype(f32)

        x_part = rows_of(x_own, half * part, part).astype(f32)
        after_attn = x_part + to_slice(mixed, lambda v: contract_cols(v, weight_o))
        normed_two, inverse_two = norm_parts(after_attn)
        h_part = (normed_two * gain_m).astype(bf16)

        by_tp, by_zl = swap_tp(h_part), across(h_part, 2)
        mid = part // 2
        near = cat([h_part, by_tp, by_zl])
        far_near = swap_core(near)
        both = cat([across(by_tp[:mid], 2), swap_tp(by_zl[mid:])])
        h_two = cat([near, both, far_near, swap_core(both)])

        dy_rel = permute_cols(after(cotangent, event_g), rel, block)
        dy_ff = cat([rows_of(dy_rel, half * part, part), rows_of(dy_rel, (1 - half) * part, part)])
        dy_zl = across(dy_ff[:part], 2)
        near = cat([dy_ff, dy_zl, swap_tp(dy_zl)])
        grad_out = cat([near, swap_core(near)])

        gate_pre = matmul(h_two, weight_g)
        up_pre = matmul(h_two, weight_u)
        gate_sig = jax.nn.sigmoid(gate_pre)
        gate_act = gate_pre * gate_sig
        hidden = (gate_act * up_pre).astype(bf16)

        def from_tokens(project):
            count = 4 * part
            away = swap_core(project(slice(count, 2 * count)).astype(bf16))
            total = project(slice(0, count)) + away.astype(f32)
            mid = width // 2
            low, high = total[:, :mid], total[:, mid:]

            def pick(values, i):
                return values[i * part : (i + 1) * part]

            low_tp = swap_tp(cat([pick(low, 1), pick(low, 3)]).astype(bf16)).astype(f32)
            high_zl = across(cat([pick(high, 2), pick(high, 3)]).astype(bf16), 2).astype(f32)
            low_zl = across((pick(low, 2) + pick(low_tp, 1)).astype(bf16), 2).astype(f32)
            high_tp = swap_tp((pick(high, 1) + pick(high_zl, 1)).astype(bf16)).astype(f32)
            low_sum = pick(low, 0) + pick(low_tp, 0) + low_zl
            high_sum = pick(high, 0) + pick(high_zl, 0) + high_tp
            return away, cat([low_sum, high_sum], 1)

        grad_hidden = matmul(grad_out, weight_d)
        grad_gate = (grad_hidden * up_pre * gate_sig * (1.0 + gate_pre * (1.0 - gate_sig))).astype(bf16)
        grad_up = (grad_hidden * gate_act).astype(bf16)
        event_h, grad_h_two = from_tokens(
            lambda where: contract_cols(grad_gate[where], weight_g)
            + contract_cols(grad_up[where], weight_u)
        )
        late_gate, late_up, late_hidden = after((grad_gate, grad_up, hidden), event_h)

        def away_rows(left, right, mask=1):
            return across(contract_rows(left[:, width // 2 :], right).astype(bf16), mask)

        away_d = away_rows(grad_out, late_hidden)
        away_g = away_rows(h_two, late_gate)
        away_u = away_rows(h_two, late_up)
        late_hidden = after(late_hidden, grad_h_two)
        event_m, mlp = from_tokens(lambda where: contract_cols(late_hidden[where], weight_d))
        out_part = (after_attn + mlp).astype(bf16)
        output = join_tokens(out_part, swap_tp(out_part), half, nat, block)

        grad_gain_m = jnp.sum(grad_h_two * normed_two, axis=0, keepdims=True)
        dy_part = rows_of(dy_rel, half * part, part).astype(f32)
        grad_after = dy_part + norm_back(grad_h_two * gain_m, normed_two, inverse_two)

        grad_part = grad_after.astype(bf16)
        grad_half = ordered(half, grad_part, swap_tp(grad_part))
        grad_attn = ordered(core, grad_half, swap_core(grad_half))
        grad_mixed = matmul(grad_attn, weight_o).astype(bf16)

        def rows_far(left, right, away, event):
            away = after(away, event)
            total = contract_rows(left[:, : width // 2], right) + away.astype(f32)
            step = 2 * block
            own = total[:step]
            for i, mask in enumerate(far):
                sent = total[(i + 1) * step : (i + 2) * step].astype(bf16)
                own = own + across(sent, mask).astype(f32)
            own = own.astype(bf16)
            other = across(rows_of(own, (1 - zl) * block, block), 2)

            def send_rows(s_ref, mine, theirs, out):
                low, away_rows = s_ref[1], (1 - s_ref[0]) * unit
                out[:, pl.ds(pl.multiple_of(low * n_ff, n_ff), n_ff)] = mine[pl.ds(low * block + away_rows, unit), :]
                out[:, pl.ds(pl.multiple_of((1 - low) * n_ff, n_ff), n_ff)] = theirs[pl.ds(away_rows, unit), :]

            (sent,) = small_call(send_rows, [core, zl], [own, other], [array_of(unit, 2 * n_ff)])
            third = swap_core(sent)

            def join_rows(s_ref, mine, theirs, third_ref, out):
                me, low = s_ref[0], s_ref[1]
                start = pl.multiple_of(me * 2 * n_ff, n_ff)
                out[:, pl.ds(start + pl.multiple_of(low * n_ff, n_ff), n_ff)] = mine[
                    pl.ds(low * block + me * unit, unit), :
                ].astype(f32)
                out[:, pl.ds(start + pl.multiple_of((1 - low) * n_ff, n_ff), n_ff)] = theirs[
                    pl.ds(me * unit, unit), :
                ].astype(f32)
                out[:, pl.ds(pl.multiple_of((1 - me) * 2 * n_ff, n_ff), 2 * n_ff)] = third_ref[...].astype(f32)

            (full,) = small_call(join_rows, [core, zl], [own, other, third], [array_of(unit, 4 * n_ff, f32)])
            return full

        def rows_line(left, right, away, event):
            if event is not None:
                away = after(away, event)
            total = contract_rows(left[:, : width // 2], right) + away.astype(f32)
            own = rows_of(total, zl * block, block)
            for i, mask in enumerate(line):
                k = i + 1
                where = (k & ~1) | ((k & 1) ^ zl)
                sent = rows_of(total, where * block, block).astype(bf16)
                own = own + across(sent, mask).astype(f32)
            return own

        def send_unit(s_ref, own, out):
            out[...] = own[pl.ds((1 - s_ref[0]) * unit, unit), :].astype(bf16)

        away_o = away_rows(grad_attn, mixed)
        first_heads = heads // 2
        n_first = 3 * first_heads * HD
        grad_low = attend_backward(kept, grad_mixed, seg_row, cosine, sine, 0, first_heads)
        away_low = away_rows(h_one, grad_low)
        grad_high = attend_backward(kept, grad_mixed, seg_row, cosine, sine, first_heads, heads - first_heads)
        away_high = away_rows(h_one, grad_high)
        grad_qkv = cat([grad_low, grad_high], 1)

        event_q = grad_mixed
        grad_w_down = rows_far(grad_out, late_hidden, away_d, event_q)
        grad_w_gate = rows_far(h_two, late_gate, away_g, event_q)
        grad_w_up = rows_far(h_two, late_up, away_u, event_q)

        grad_h_one = to_slice(grad_qkv, lambda v: contract_cols(v, weight_qkv))

        own_o = rows_line(grad_attn, mixed, away_o, None)
        own_low = rows_line(h_one, grad_low, away_low, None)
        own_high = rows_line(h_one, grad_high, away_high, None)
        own_a = cat([own_low, own_high, own_o], 1)
        (sent_g,) = small_call(send_unit, [core], [own_a], [array_of(unit, 4 * n_attn)])
        other_a = swap_core(sent_g)

        def join_attn(s_ref, own, other, q, k, v, o):
            me = s_ref[0]
            mine = pl.ds(pl.multiple_of(me * unit, unit), unit)
            here, there = me * n_attn, (1 - me) * n_attn
            for start, load in (
                (here, lambda c: own[mine, c]),
                (there, lambda c: other[:, c].astype(f32)),
            ):
                start = pl.multiple_of(start, n_attn)
                for h in range(heads):
                    for i, ref in enumerate((q, k, v)):
                        ref[:, pl.ds(start + h * HD, HD)] = load(slice((3 * h + i) * HD, (3 * h + i + 1) * HD))
                o[:, pl.ds(start, n_attn)] = load(slice(3 * n_attn, 4 * n_attn))

        grad_w_query, grad_w_key, grad_w_value, grad_w_out = small_call(
            join_attn, [core], [own_a, other_a], [array_of(unit, 2 * n_attn, f32)] * 4
        )

        normed_part = rows_of(normed_all, core * rows + half * part, part)
        inverse_part = rows_of(inverse_all, core * rows + half * part, part)
        grad_gain_a = jnp.sum(grad_h_one * normed_part, axis=0, keepdims=True)
        grad_x = (grad_after + norm_back(grad_h_one * gain_a, normed_part, inverse_part)).astype(bf16)
        grad_tokens = join_tokens(grad_x, swap_tp(grad_x), half, nat, block)

        grad_gains = cat([grad_gain_a, grad_gain_m])
        grad_gains = grad_gains + swap_tp(grad_gains)
        for mask in [1] + [1 << bit for bit in range(shards.bit_length() - 2, 1, -1)]:
            mid = grad_gains.shape[1] // 2
            grad_gains = grad_gains[:, :mid] + across(grad_gains[:, mid:], mask)
        first, second = grad_gains[:, :block], grad_gains[:, block:]
        grad_gains = jnp.where(zl == 0, first, second) + across(jnp.where(zl == 0, second, first), 2)
        first, second = grad_gains[:, :unit], grad_gains[:, unit:]
        grad_gains = jnp.where(core == 0, first, second) + swap_core(jnp.where(core == 0, second, first))

        return (
            output,
            grad_tokens,
            grad_gains[0],
            grad_w_query,
            grad_w_key,
            grad_w_value,
            grad_w_out,
            grad_gains[1],
            grad_w_gate,
            grad_w_up,
            grad_w_down,
        )

    return per_device


def solution(mesh):
    wide = P(("shard", "ctx"), None)
    flat = P(("shard", "ctx"))
    both = P(("shard", "ctx"), "tp")
    placed = (wide, P("shard", None), flat, both, both, both, both, flat, both, both, both, wide)
    return jax.shard_map(
        build(mesh.shape["shard"]),
        mesh=mesh,
        in_specs=placed,
        out_specs=(wide, wide, flat, both, both, both, both, flat, both, both, both),
        check_vma=False,
    )
```

time: 1230 us -> 1120 us (0.911)
  local copies, waits for them, and re-layouts: 172 us -> 55.3 us
  Pallas kernels: 0 us -> 111 us
  other arithmetic: 124 us -> 55.2 us
  starting transfers between devices: 149 us -> 83.8 us
  waiting for transfers between devices: 554 us -> 597 us
    pallas_call x0 -> x24, Pallas kernels: none -> 111 us  [the longest x17 48.8 us: small_call(): pl.pallas_call(body, grid_spec=pltpu.PrefetchScalarGridSpec(num_scalar_pr...]
    ppermute x64 -> x57, starting transfers between devices: 130 us -> 71 us  [across(): return lax.ppermute(values, 'shard', [(i, i ^ mask) for i in range(shards)])]
    ppermute x64 -> x57, waiting for transfers between devices: 479 us -> 536 us  [across(): return lax.ppermute(values, 'shard', [(i, i ^ mask) for i in range(shards)])]
    rev x4 -> x0, local copies, waits for them, and re-layouts: 43.7 us -> none  [flip_zl(): return jnp.where(zl == 0, split, split[:, :, ::-1]).reshape(values.shape)]
    select_n x17 -> x6, other arithmetic: 45 us -> 3.8 us  [ordered(): jnp.where(index == 0, cat([own, other], axis), cat([other, own], axis))]
    reshape x10 -> x0, local copies, waits for them, and re-layouts: 31 us -> none  [the longest x4 13.6 us: flip_zl(): return jnp.where(zl == 0, split, split[:, :, ::-1]).reshape(values.shape)]
    unnamed x297 -> x153, local copies, waits for them, and re-layouts: 55.1 us -> 26.4 us
    ppermute x13, waiting for transfers between devices: 74.9 us -> 53 us  [swap_tp(): return lax.ppermute(values, 'tp', [(0, 1), (1, 0)])]
  transfers between devices with their start and end apart: 101 -> 87, of which waited for: 42 -> 42; matrix products, arithmetic and copies ran while one was open for 34% -> 21% of each run, Pallas kernels for 0% -> 8%
where the time goes in v2:
time: 1120 us; the launch traced here: 1110 us
  waiting for transfers between devices  597 us (53%)
  matrix products  210 us (19%)
  Pallas kernels  111 us (10%)
  starting transfers between devices  83.8 us (7%)
  local copies, waits for them, and re-layouts  55.3 us (5%)
  other arithmetic  55.2 us (5%)
    ppermute x57, waiting for transfers between devices, across(): return lax.ppermute(values, 'shard', [(i, i ^ mask) for i in range(shards)])  536 us
    dot_general x12, matrix products, contract_cols(): lax.dot_general(left, right, (((1,), (1,)), ((), ())), preferred_element_...  88.3 us
    ppermute x57, starting transfers between devices, across(): return lax.ppermute(values, 'shard', [(i, i ^ mask) for i in range(shards)])  71 us
    dot_general x5, matrix products, matmul(): return jnp.dot(left, right, preferred_element_type=jnp.float32)  62.8 us
    dot_general x12, matrix products, contract_rows(): lax.dot_general(left, right, (((0,), (0,)), ((), ())), preferred_element_...  58.7 us
    ppermute x13, waiting for transfers between devices, swap_tp(): return lax.ppermute(values, 'tp', [(0, 1), (1, 0)])  53 us
    pallas_call x17, Pallas kernels, small_call(): pl.pallas_call(body, grid_spec=pltpu.PrefetchScalarGridSpec(num_scalar_pr...  48.8 us
    pallas_call x2, Pallas kernels, attend_backward(): pl.pallas_call(body, grid_spec=pltpu.PrefetchScalarGridSpec(num_scalar_pr...  30.9 us
  transfers between devices with their start and end apart: 87, of which 42 were waited for; matrix products, arithmetic and copies ran while one was open for 21% of the time, Pallas kernels for 8%

profile of v2, /device:TPU:0, one launch (start us, length us, event | category | flops | bytes accessed | tf_op | source)
XLA Modules:
  0.0 1114.5 jit_solution(9847463739061923698)
XLA Ops:
  25.7 11.6 %collective-permute-done.3 = bf16[272,1536]{1,0:T(8,128)(2,1)S(1)} collective-permute-done((bf16[272,1536]{1,0:T(8,128)(2,1)}, bf16[272,1536]{1,0:T(8,128)(2,1)S(1)}, u32[]{:S(2)}, u32[]{:S(2)}) %collective-permute-start.3) | collective-permute-done | bytes 835616 | tf_op jit(solution)/shard_map/ppermute | solution.py:279
  39.6 56.7 %collective-permute-done.4 = bf16[272,1536]{1,0:T(8,128)(2,1)S(1)} collective-permute-done((bf16[272,1536]{1,0:T(8,128)(2,1)S(1)}, bf16[272,1536]{1,0:T(8,128)(2,1)S(1)}, u32[]{:S(2)}, u32[]{:S(2)}) %collective-permute-start.4) | collective-permute-done | bytes 835616 | tf_op jit(solution)/shard_map/ppermute | solution.py:279
  104.4 11.7 %collective-permute-done.11 = bf16[256,512]{1,0:T(8,128)(2,1)S(1)} collective-permute-done((bf16[256,512]{1,0:T(8,128)(2,1)S(1)}, bf16[256,512]{1,0:T(8,128)(2,1)S(1)}, u32[]{:S(2)}, u32[]{:S(2)}) %collective-permute-start.11) | collective-permute-done | bytes 262176 | tf_op jit(solution)/shard_map/ppermute | solution.py:279
  147.1 14.0 %collective-permute-done.8 = bf16[272,1536]{1,0:T(8,128)(2,1)S(1)} collective-permute-done((bf16[272,1536]{1,0:T(8,128)(2,1)S(1)}, bf16[272,1536]{1,0:T(8,128)(2,1)S(1)}, u32[]{:S(2)}, u32[]{:S(2)}) %collective-permute-start.8) | collective-permute-done | bytes 835616 | tf_op jit(solution)/shard_map/ppermute | solution.py:279
  161.1 16.0 %collective-permute-done.7 = bf16[272,1536]{1,0:T(8,128)(2,1)S(1)} collective-permute-done((bf16[272,1536]{1,0:T(8,128)(2,1)S(1)}, bf16[272,1536]{1,0:T(8,128)(2,1)S(1)}, u32[]{:S(2)}, u32[]{:S(2)}) %collective-permute-start.7) | collective-permute-done | bytes 835616 | tf_op jit(solution)/shard_map/ppermute | solution.py:279
  193.3 14.7 %shard_map.206 = (bf16[1024,512]{1,0:T(8,128)(2,1)}, bf16[1024,1536]{1,0:T(8,128)(2,1)}) custom-call(s32[1024]{0:T(1024)} %bitcast.50, f32[1024,1536]{1,0:T(8,128)} %fusion.118.qkv_ref, f32[1024,128]{1,0:T(8,128)} %get-tuple-element.117.cos_ref, f32[1024,128]{1,0:T(8,128)} %get-tuple-element.118.sin_ref, s32[1024,1]{1,0:T(8,128)} %copy.26.seg_col, ...), custom_call_target="tpu_custom_call" | custom-call | tf_op jit(solution)/shard_map/pallas_call | solution.py:195
  227.4 14.0 %collective-permute-done.20.other = bf16[256,1024]{1,0:T(8,128)(2,1)} collective-permute-done((bf16[256,1024]{1,0:T(8,128)(2,1)}, bf16[256,1024]{1,0:T(8,128)(2,1)}, u32[]{:S(2)}, u32[]{:S(2)}) %collective-permute-start.20) | collective-permute-done | bytes 524320 | tf_op jit(solution)/shard_map/ppermute | solution.py:279
  255.8 35.7 %collective-permute-done.21 = bf16[512,1024]{1,0:T(8,128)(2,1)} collective-permute-done((bf16[512,1024]{1,0:T(8,128)(2,1)}, bf16[512,1024]{1,0:T(8,128)(2,1)}, u32[]{:S(2)}, u32[]{:S(2)}) %collective-permute-start.21) | collective-permute-done | bytes 1048608 | tf_op jit(solution)/shard_map/ppermute | solution.py:279
  303.7 31.2 %collective-permute-done.25.other = bf16[256,1024]{1,0:T(8,128)(2,1)} collective-permute-done((bf16[256,1024]{1,0:T(8,128)(2,1)}, bf16[256,1024]{1,0:T(8,128)(2,1)}, u32[]{:S(2)}, u32[]{:S(2)}) %collective-permute-start.25) | collective-permute-done | bytes 524320 | tf_op jit(solution)/shard_map/ppermute | solution.py:279
  342.7 42.3 %collective-permute-done.26 = bf16[512,1024]{1,0:T(8,128)(2,1)} collective-permute-done((bf16[512,1024]{1,0:T(8,128)(2,1)}, bf16[512,1024]{1,0:T(8,128)(2,1)}, u32[]{:S(2)}, u32[]{:S(2)}) %collective-permute-start.26) | collective-permute-done | bytes 1048608 | tf_op jit(solution)/shard_map/ppermute | solution.py:279
  432.2 36.2 %collective-permute-done.28 = bf16[512,1024]{1,0:T(8,128)(2,1)S(1)} collective-permute-done((bf16[512,1024]{1,0:T(8,128)(2,1)S(1)}, bf16[512,1024]{1,0:T(8,128)(2,1)S(1)}, u32[]{:S(2)}, u32[]{:S(2)}) %collective-permute-start.28) | collective-permute-done | bytes 1048608 | tf_op jit(solution)/shard_map/ppermute | solution.py:279
  469.8 14.4 %fusion.108 = f32[2048,1024]{1,0:T(8,128)} fusion(bf16[2048,2048]{1,0:T(8,128)(2,1)} %constant_dynamic-update-slice_fusion.5, bf16[512,1024]{1,0:T(8,128)(2,1)} %collective-permute-done.40, bf16[512,1024]{1,0:T(8,128)(2,1)} %collective-permute-done.39, bf16[512,1024]{1,0:T(8,128)(2,1)} %collective-permute-done.21, bf16[512,1024]{1,0:T(8,128)(2,1)S(1)} %copy-done.24), kind=kOutput, calls=%fused_computation.229 | convolution fusion | flops 8606711808 | bytes 20971520 | tf_op jit(solution)/shard_map/dot_general | solution.py:22
  484.8 13.8 %collective-permute-done.29 = bf16[512,1024]{1,0:T(8,128)(2,1)S(1)} collective-permute-done((bf16[512,1024]{1,0:T(8,128)(2,1)S(1)}, bf16[512,1024]{1,0:T(8,128)(2,1)S(1)}, u32[]{:S(2)}, u32[]{:S(2)}) %collective-permute-start.29) | collective-permute-done | bytes 1048608 | tf_op jit(solution)/shard_map/ppermute | solution.py:279
  498.6 22.0 %collective-permute-done.30 = bf16[512,1024]{1,0:T(8,128)(2,1)S(1)} collective-permute-done((bf16[512,1024]{1,0:T(8,128)(2,1)S(1)}, bf16[512,1024]{1,0:T(8,128)(2,1)S(1)}, u32[]{:S(2)}, u32[]{:S(2)}) %collective-permute-start.30) | collective-permute-done | bytes 1048608 | tf_op jit(solution)/shard_map/ppermute | solution.py:279
  520.6 11.1 fusion.110
  532.7 22.2 %multiply_convert_fusion = (bf16[2048,1024]{1,0:T(8,128)(2,1)}, bf16[2048,1024]{1,0:T(8,128)(2,1)}, bf16[2048,1024]{1,0:T(8,128)(2,1)}) fusion(f32[2048,1024]{1,0:T(8,128)} %fusion.108, f32[2048,1024]{1,0:T(8,128)} %fusion.110, bf16[2048,2048]{1,0:T(8,128)(2,1)} %constant_dynamic-update-slice_fusion.5, bf16[512,1024]{1,0:T(8,128)(2,1)} %collective-permute-done.38, ...), kind=kOutput, calls=%fused_computation.6 | convolution fusion | flops 8638169088 | bytes 41943040 | tf_op jit(solution)/shard_map/dot_general | solution.py:22
  554.9 10.3 fusion.29
  582.2 11.0 convolution_convert_fusion
  602.8 12.2 %fusion.116 = (bf16[1024,2048]{1,0:T(8,128)(2,1)}, f32[1024,2048]{1,0:T(8,128)}) fusion(bf16[1024,2048]{1,0:T(8,128)(2,1)} %collective-permute-done.41, f32[1024,2048]{1,0:T(8,128)} %fusion.26, bf16[512,1024]{1,0:T(8,128)(2,1)} %collective-permute-done.40, bf16[512,1024]{1,0:T(8,128)(2,1)} %collective-permute-done.39, ...), kind=kOutput, calls=%fused_computation.237 | convolution fusion | flops 4320133120 | bytes 31457280 | tf_op jit(solution)/shard_map/dot_general | solution.py:32
  633.7 11.6 %collective-permute-done.42 = bf16[512,1024]{1,0:T(8,128)(2,1)S(1)} collective-permute-done((bf16[512,1024]{1,0:T(8,128)(2,1)S(1)}, bf16[512,1024]{1,0:T(8,128)(2,1)S(1)}, u32[]{:S(2)}, u32[]{:S(2)}) %collective-permute-start.42) | collective-permute-done | bytes 1048608 | tf_op jit(solution)/shard_map/ppermute | solution.py:285
  651.5 15.4 %collective-permute-done.47 = bf16[512,1024]{1,0:T(8,128)(2,1)S(1)} collective-permute-done((bf16[512,1024]{1,0:T(8,128)(2,1)S(1)}, bf16[512,1024]{1,0:T(8,128)(2,1)S(1)}, u32[]{:S(2)}, u32[]{:S(2)}) %collective-permute-start.47) | collective-permute-done | bytes 1048608 | tf_op jit(solution)/shard_map/ppermute | solution.py:285
  668.8 16.5 %collective-permute-done.43 = bf16[256,1024]{1,0:T(8,128)(2,1)S(1)} collective-permute-done((bf16[256,1024]{1,0:T(8,128)(2,1)S(1)}, bf16[256,1024]{1,0:T(8,128)(2,1)S(1)}, u32[]{:S(2)}, u32[]{:S(2)}) %collective-permute-start.43) | collective-permute-done | bytes 524320 | tf_op jit(solution)/shard_map/ppermute | solution.py:279
  721.9 13.3 %collective-permute-done.52 = bf16[256,2048]{1,0:T(8,128)(2,1)S(1)} collective-permute-done((bf16[256,2048]{1,0:T(8,128)(2,1)S(1)}, bf16[256,2048]{1,0:T(8,128)(2,1)S(1)}, u32[]{:S(2)}, u32[]{:S(2)}) %collective-permute-start.52) | collective-permute-done | bytes 1048608 | tf_op jit(solution)/shard_map/ppermute | solution.py:285
  759.2 15.1 %shard_map.216 = bf16[1024,768]{1,0:T(8,128)(2,1)} custom-call(s32[1024]{0:T(1024)} %bitcast.51, bf16[1024,1536]{1,0:T(8,128)(2,1)} %get-tuple-element.55.kept_ref, bf16[1024,512]{1,0:T(8,128)(2,1)} %convolution_convert_fusion.3.do_ref, f32[1024,128]{1,0:T(8,128)} %get-tuple-element.117.cos_ref, f32[1024,128]{1,0:T(8,128)} %get-tuple-element.118.sin_ref, ...), custom_call_target="tpu_custom_call" | custom-call | tf_op jit(solution)/shard_map/pallas_call | solution.py:254
  774.3 15.7 %shard_map.217 = bf16[1024,768]{1,0:T(8,128)(2,1)} custom-call(s32[1024]{0:T(1024)} %bitcast.52, bf16[1024,1536]{1,0:T(8,128)(2,1)} %get-tuple-element.55.kept_ref, bf16[1024,512]{1,0:T(8,128)(2,1)} %convolution_convert_fusion.3.do_ref, f32[1024,128]{1,0:T(8,128)} %get-tuple-element.117.cos_ref, f32[1024,128]{1,0:T(8,128)} %get-tuple-element.118.sin_ref, ...), custom_call_target="tpu_custom_call" | custom-call | tf_op jit(solution)/shard_map/pallas_call | solution.py:254
  828.0 31.2 %collective-permute-done.83 = bf16[1024,1024]{1,0:T(8,128)(2,1)} collective-permute-done((bf16[1024,1024]{1,0:T(8,128)(2,1)}, bf16[1024,1024]{1,0:T(8,128)(2,1)}, u32[]{:S(2)}, u32[]{:S(2)}) %collective-permute-start.83) | collective-permute-done | bytes 2097184 | tf_op jit(solution)/shard_map/ppermute | solution.py:279
  870.9 10.8 collective-permute-done.70
  887.0 18.7 %collective-permute-done.76 = bf16[512,1024]{1,0:T(8,128)(2,1)S(1)} collective-permute-done((bf16[512,1024]{1,0:T(8,128)(2,1)S(1)}, bf16[512,1024]{1,0:T(8,128)(2,1)S(1)}, u32[]{:S(2)}, u32[]{:S(2)}) %collective-permute-start.76) | collective-permute-done | bytes 1048608 | tf_op jit(solution)/shard_map/ppermute | solution.py:279
  909.6 24.2 %collective-permute-done.80 = bf16[512,1024]{1,0:T(8,128)(2,1)S(1)} collective-permute-done((bf16[512,1024]{1,0:T(8,128)(2,1)S(1)}, bf16[512,1024]{1,0:T(8,128)(2,1)S(1)}, u32[]{:S(2)}, u32[]{:S(2)}) %collective-permute-start.80) | collective-permute-done | bytes 1048608 | tf_op jit(solution)/shard_map/ppermute | solution.py:279
  934.1 27.7 %collective-permute-done.84 = bf16[512,1024]{1,0:T(8,128)(2,1)S(1)} collective-permute-done((bf16[512,1024]{1,0:T(8,128)(2,1)S(1)}, bf16[512,1024]{1,0:T(8,128)(2,1)S(1)}, u32[]{:S(2)}, u32[]{:S(2)}) %collective-permute-start.84) | collective-permute-done | bytes 1048608 | tf_op jit(solution)/shard_map/ppermute | solution.py:279
  985.1 13.5 %collective-permute-done.62 = bf16[1024,768]{1,0:T(8,128)(2,1)S(1)} collective-permute-done((bf16[1024,768]{1,0:T(8,128)(2,1)S(1)}, bf16[1024,768]{1,0:T(8,128)(2,1)S(1)}, u32[]{:S(2)}, u32[]{:S(2)}) %collective-permute-start.62) | collective-permute-done | bytes 1572896 | tf_op jit(solution)/shard_map/ppermute | solution.py:279
  1026.8 27.1 %collective-permute-done.68 = bf16[256,768]{1,0:T(8,128)(2,1)} collective-permute-done((bf16[256,768]{1,0:T(8,128)(2,1)}, bf16[256,768]{1,0:T(8,128)(2,1)}, u32[]{:S(2)}, u32[]{:S(2)}) %collective-permute-start.68) | collective-permute-done | bytes 393248 | tf_op jit(solution)/shard_map/ppermute | solution.py:279
  (464 shorter events, 470.5 us)
Async XLA Ops:
  9.1 134.8 %collective-permute-start = (bf16[512,2048]{1,0:T(8,128)(2,1)}, bf16[512,2048]{1,0:T(8,128)(2,1)}, u32[]{:S(2)}, u32[]{:S(2)}) collective-permute-start(bf16[512,2048]{1,0:T(8,128)(2,1)} %shard_map.203), channel_id=1, source_target_pairs={{0,2},{2,0},{1,3},{3,1},{4,6},{6,4},{5,7},{7,5},{8,10},{10,8},{9,1... | collective-permute-start | bytes 6291464 | tf_op jit(solution)/shard_map/ppermute | solution.py:282
  21.0 75.3 %collective-permute-start.5 = (bf16[272,1536]{1,0:T(8,128)(2,1)S(1)}, bf16[272,1536]{1,0:T(8,128)(2,1)S(1)}, u32[]{:S(2)}, u32[]{:S(2)}) collective-permute-start(bf16[272,1536]{1,0:T(8,128)(2,1)S(1)} %copy-done.28), channel_id=1, source_target_pairs={{0,24},{4,28},{8,16},{12,20},{16,8},{20,12},{24,0},{28,4},{1,25},{... | collective-permute-start | bytes 2506760 | tf_op jit(solution)/shard_map/ppermute | solution.py:279
  23.5 72.8 %collective-permute-start.4 = (bf16[272,1536]{1,0:T(8,128)(2,1)S(1)}, bf16[272,1536]{1,0:T(8,128)(2,1)S(1)}, u32[]{:S(2)}, u32[]{:S(2)}) collective-permute-start(bf16[272,1536]{1,0:T(8,128)(2,1)S(1)} %copy-done.28), channel_id=1, source_target_pairs={{0,16},{4,20},{8,24},{12,28},{16,0},{20,4},{24,8},{28,12},{1,17},{... | collective-permute-start | bytes 2506760 | tf_op jit(solution)/shard_map/ppermute | solution.py:279
  23.7 75.5 %collective-permute-start.6 = (bf16[272,1536]{1,0:T(8,128)(2,1)S(1)}, bf16[272,1536]{1,0:T(8,128)(2,1)S(1)}, u32[]{:S(2)}, u32[]{:S(2)}) collective-permute-start(bf16[272,1536]{1,0:T(8,128)(2,1)S(1)} %copy-done.28), channel_id=1, source_target_pairs={{0,4},{4,0},{8,12},{12,8},{16,20},{20,16},{24,28},{28,24},{1,5},{5... | collective-permute-start | bytes 2506760 | tf_op jit(solution)/shard_map/ppermute | solution.py:279
  37.4 65.7 %collective-permute-start.10 = (bf16[256,512]{1,0:T(8,128)(2,1)S(1)}, bf16[256,512]{1,0:T(8,128)(2,1)S(1)}, u32[]{:S(2)}, u32[]{:S(2)}) collective-permute-start(bf16[256,512]{1,0:T(8,128)(2,1)S(1)} %copy-done.36), channel_id=1, source_target_pairs={{0,8},{4,12},{8,0},{12,4},{16,24},{20,28},{24,16},{28,20},{1,9},{5... | collective-permute-start | bytes 786440 | tf_op jit(solution)/shard_map/ppermute | solution.py:279
  243.6 47.9 %collective-permute-start.21 = (bf16[512,1024]{1,0:T(8,128)(2,1)}, bf16[512,1024]{1,0:T(8,128)(2,1)}, u32[]{:S(2)}, u32[]{:S(2)}) collective-permute-start(bf16[512,1024]{1,0:T(8,128)(2,1)} %shard_map.209), channel_id=1, source_target_pairs={{0,16},{4,20},{8,24},{12,28},{16,0},{20,4},{24,8},{28,12},{1,17},{... | collective-permute-start | bytes 3145736 | tf_op jit(solution)/shard_map/ppermute | solution.py:279
  251.6 48.9 %collective-permute-start.31 = (bf16[256,2048]{1,0:T(8,128)(2,1)}, bf16[256,2048]{1,0:T(8,128)(2,1)}, u32[]{:S(2)}, u32[]{:S(2)}) collective-permute-start(bf16[256,2048]{1,0:T(8,128)(2,1)} %get-tuple-element.76), channel_id=1, source_target_pairs={{0,1},{1,0},{2,3},{3,2},{4,5},{5,4},{6,7},{7,6},{8,9},{9,8},{10,11... | collective-permute-start | bytes 3145736 | tf_op jit(solution)/shard_map/ppermute | solution.py:285
  303.7 115.8 %collective-permute-start.35 = (bf16[768,2048]{1,0:T(8,128)(2,1)}, bf16[768,2048]{1,0:T(8,128)(2,1)}, u32[]{:S(2)}, u32[]{:S(2)}) collective-permute-start(bf16[768,2048]{1,0:T(8,128)(2,1)} %pad_maximum_fusion.4), channel_id=1, source_target_pairs={{0,2},{2,0},{1,3},{3,1},{4,6},{6,4},{5,7},{7,5},{8,10},{10,8},{9,1... | collective-permute-start | bytes 9437192 | tf_op jit(solution)/shard_map/ppermute | solution.py:282
  337.1 47.9 %collective-permute-start.26 = (bf16[512,1024]{1,0:T(8,128)(2,1)}, bf16[512,1024]{1,0:T(8,128)(2,1)}, u32[]{:S(2)}, u32[]{:S(2)}) collective-permute-start(bf16[512,1024]{1,0:T(8,128)(2,1)} %shard_map.213), channel_id=1, source_target_pairs={{0,16},{4,20},{8,24},{12,28},{16,0},{20,4},{24,8},{28,12},{1,17},{... | collective-permute-start | bytes 3145736 | tf_op jit(solution)/shard_map/ppermute | solution.py:279
  337.1 66.8 %collective-permute-start.23 = (bf16[256,2048]{1,0:T(8,128)(2,1)}, bf16[256,2048]{1,0:T(8,128)(2,1)}, u32[]{:S(2)}, u32[]{:S(2)}) collective-permute-start(bf16[256,2048]{1,0:T(8,128)(2,1)} %collective-permute-done.22), channel_id=1, source_target_pairs={{0,1},{1,0},{2,3},{3,2},{4,5},{5,4},{6,7},{7,6},{8,9},{9,8},{10,11... | collective-permute-start | bytes 3145736 | tf_op jit(solution)/shard_map/ppermute | solution.py:285
  340.7 89.5 %collective-permute-start.39 = (bf16[512,1024]{1,0:T(8,128)(2,1)}, bf16[512,1024]{1,0:T(8,128)(2,1)}, u32[]{:S(2)}, u32[]{:S(2)}) collective-permute-start(bf16[512,1024]{1,0:T(8,128)(2,1)} %shard_map.209), channel_id=1, source_target_pairs={{0,4},{4,0},{8,12},{12,8},{16,20},{20,16},{24,28},{28,24},{1,5},{5... | collective-permute-start | bytes 3145736 | tf_op jit(solution)/shard_map/ppermute | solution.py:279
  342.2 88.5 %collective-permute-start.40 = (bf16[512,1024]{1,0:T(8,128)(2,1)}, bf16[512,1024]{1,0:T(8,128)(2,1)}, u32[]{:S(2)}, u32[]{:S(2)}) collective-permute-start(bf16[512,1024]{1,0:T(8,128)(2,1)} %collective-permute-done.21), channel_id=1, source_target_pairs={{0,4},{4,0},{8,12},{12,8},{16,20},{20,16},{24,28},{28,24},{1,5},{5... | collective-permute-start | bytes 3145736 | tf_op jit(solution)/shard_map/ppermute | solution.py:279
  415.5 68.7 %collective-permute-start.24 = (bf16[1024,2048]{1,0:T(8,128)(2,1)S(1)}, bf16[1024,2048]{1,0:T(8,128)(2,1)S(1)}, u32[]{:S(2)}, u32[]{:S(2)}) collective-permute-start(bf16[1024,2048]{1,0:T(8,128)(2,1)S(1)} %pad_maximum_fusion), channel_id=1, source_target_pairs={{0,2},{2,0},{1,3},{3,1},{4,6},{6,4},{5,7},{7,5},{8,10},{10,8},{9,1... | collective-permute-start | bytes 12582920 | tf_op jit(solution)/shard_map/ppermute | solution.py:282
  419.4 48.9 %collective-permute-start.28 = (bf16[512,1024]{1,0:T(8,128)(2,1)S(1)}, bf16[512,1024]{1,0:T(8,128)(2,1)S(1)}, u32[]{:S(2)}, u32[]{:S(2)}) collective-permute-start(bf16[512,1024]{1,0:T(8,128)(2,1)S(1)} %copy-done.26), channel_id=1, source_target_pairs={{0,16},{4,20},{8,24},{12,28},{16,0},{20,4},{24,8},{28,12},{1,17},{... | collective-permute-start | bytes 3145736 | tf_op jit(solution)/shard_map/ppermute | solution.py:279
  427.6 104.1 %collective-permute-start.37 = (bf16[512,1024]{1,0:T(8,128)(2,1)S(1)}, bf16[512,1024]{1,0:T(8,128)(2,1)S(1)}, u32[]{:S(2)}, u32[]{:S(2)}) collective-permute-start(bf16[512,1024]{1,0:T(8,128)(2,1)S(1)} %copy-done.25), channel_id=1, source_target_pairs={{0,4},{4,0},{8,12},{12,8},{16,20},{20,16},{24,28},{28,24},{1,5},{5... | collective-permute-start | bytes 3145736 | tf_op jit(solution)/shard_map/ppermute | solution.py:279
  430.1 102.5 %collective-permute-start.38 = (bf16[512,1024]{1,0:T(8,128)(2,1)}, bf16[512,1024]{1,0:T(8,128)(2,1)}, u32[]{:S(2)}, u32[]{:S(2)}) collective-permute-start(bf16[512,1024]{1,0:T(8,128)(2,1)} %collective-permute-done.26), channel_id=1, source_target_pairs={{0,4},{4,0},{8,12},{12,8},{16,20},{20,16},{24,28},{28,24},{1,5},{5... | collective-permute-start | bytes 3145736 | tf_op jit(solution)/shard_map/ppermute | solution.py:279
  430.8 67.8 %collective-permute-start.29 = (bf16[512,1024]{1,0:T(8,128)(2,1)S(1)}, bf16[512,1024]{1,0:T(8,128)(2,1)S(1)}, u32[]{:S(2)}, u32[]{:S(2)}) collective-permute-start(bf16[512,1024]{1,0:T(8,128)(2,1)S(1)} %copy-done.26), channel_id=1, source_target_pairs={{0,4},{4,0},{8,12},{12,8},{16,20},{20,16},{24,28},{28,24},{1,5},{5... | collective-permute-start | bytes 3145736 | tf_op jit(solution)/shard_map/ppermute | solution.py:279
  468.4 52.2 %collective-permute-start.30 = (bf16[512,1024]{1,0:T(8,128)(2,1)S(1)}, bf16[512,1024]{1,0:T(8,128)(2,1)S(1)}, u32[]{:S(2)}, u32[]{:S(2)}) collective-permute-start(bf16[512,1024]{1,0:T(8,128)(2,1)S(1)} %collective-permute-done.28), channel_id=1, source_target_pairs={{0,4},{4,0},{8,12},{12,8},{16,20},{20,16},{24,28},{28,24},{1,5},{5... | collective-permute-start | bytes 3145736 | tf_op jit(solution)/shard_map/ppermute | solution.py:279
  720.5 83.0 %collective-permute-start.75 = (bf16[1024,1024]{1,0:T(8,128)(2,1)}, bf16[1024,1024]{1,0:T(8,128)(2,1)}, u32[]{:S(2)}, u32[]{:S(2)}) collective-permute-start(bf16[1024,1024]{1,0:T(8,128)(2,1)} %fusion.41), channel_id=1, source_target_pairs={{0,4},{4,0},{8,12},{12,8},{16,20},{20,16},{24,28},{28,24},{1,5},{5... | collective-permute-start | bytes 6291464 | tf_op jit(solution)/shard_map/ppermute | solution.py:279
  742.1 72.2 %collective-permute-start.79 = (bf16[1024,1024]{1,0:T(8,128)(2,1)}, bf16[1024,1024]{1,0:T(8,128)(2,1)}, u32[]{:S(2)}, u32[]{:S(2)}) collective-permute-start(bf16[1024,1024]{1,0:T(8,128)(2,1)} %fusion.44), channel_id=1, source_target_pairs={{0,4},{4,0},{8,12},{12,8},{16,20},{20,16},{24,28},{28,24},{1,5},{5... | collective-permute-start | bytes 6291464 | tf_op jit(solution)/shard_map/ppermute | solution.py:279
  749.3 110.0 %collective-permute-start.83 = (bf16[1024,1024]{1,0:T(8,128)(2,1)}, bf16[1024,1024]{1,0:T(8,128)(2,1)}, u32[]{:S(2)}, u32[]{:S(2)}) collective-permute-start(bf16[1024,1024]{1,0:T(8,128)(2,1)} %fusion.47), channel_id=1, source_target_pairs={{0,4},{4,0},{8,12},{12,8},{16,20},{20,16},{24,28},{28,24},{1,5},{5... | collective-permute-start | bytes 6291464 | tf_op jit(solution)/shard_map/ppermute | solution.py:279
  796.7 184.1 %collective-permute-start.54 = (bf16[512,2048]{1,0:T(8,128)(2,1)S(1)}, bf16[512,2048]{1,0:T(8,128)(2,1)S(1)}, u32[]{:S(2)}, u32[]{:S(2)}) collective-permute-start(bf16[512,2048]{1,0:T(8,128)(2,1)S(1)} %convolution_convert_fusion.1), channel_id=1, source_target_pairs={{0,2},{2,0},{1,3},{3,1},{4,6},{6,4},{5,7},{7,5},{8,10},{10,8},{9,1... | collective-permute-start | bytes 6291464 | tf_op jit(solution)/shard_map/ppermute | solution.py:282
  799.1 82.6 %collective-permute-start.70 = (bf16[1024,512]{1,0:T(8,128)(2,1)}, bf16[1024,512]{1,0:T(8,128)(2,1)}, u32[]{:S(2)}, u32[]{:S(2)}) collective-permute-start(bf16[1024,512]{1,0:T(8,128)(2,1)} %fusion.72), channel_id=1, source_target_pairs={{0,4},{4,0},{8,12},{12,8},{16,20},{20,16},{24,28},{28,24},{1,5},{5... | collective-permute-start | bytes 3145736 | tf_op jit(solution)/shard_map/ppermute | solution.py:279
  803.5 173.0 %collective-permute-start.66 = (bf16[1024,768]{1,0:T(8,128)(2,1)}, bf16[1024,768]{1,0:T(8,128)(2,1)S(1)}, u32[]{:S(2)}, u32[]{:S(2)}) collective-permute-start(bf16[1024,768]{1,0:T(8,128)(2,1)} %fusion.65), channel_id=1, source_target_pairs={{0,4},{4,0},{8,12},{12,8},{16,20},{20,16},{24,28},{28,24},{1,5},{5... | collective-permute-start | bytes 4718600 | tf_op jit(solution)/shard_map/ppermute | solution.py:279
  814.3 91.3 %collective-permute-start.76 = (bf16[512,1024]{1,0:T(8,128)(2,1)S(1)}, bf16[512,1024]{1,0:T(8,128)(2,1)S(1)}, u32[]{:S(2)}, u32[]{:S(2)}) collective-permute-start(bf16[512,1024]{1,0:T(8,128)(2,1)S(1)} %slice.547), channel_id=1, source_target_pairs={{0,16},{4,20},{8,24},{12,28},{16,0},{20,4},{24,8},{28,12},{1,17},{... | collective-permute-start | bytes 3145736 | tf_op jit(solution)/shard_map/ppermute | solution.py:279
  859.2 74.5 %collective-permute-start.80 = (bf16[512,1024]{1,0:T(8,128)(2,1)S(1)}, bf16[512,1024]{1,0:T(8,128)(2,1)S(1)}, u32[]{:S(2)}, u32[]{:S(2)}) collective-permute-start(bf16[512,1024]{1,0:T(8,128)(2,1)S(1)} %slice.546), channel_id=1, source_target_pairs={{0,16},{4,20},{8,24},{12,28},{16,0},{20,4},{24,8},{28,12},{1,17},{... | collective-permute-start | bytes 3145736 | tf_op jit(solution)/shard_map/ppermute | solution.py:279
  881.7 80.1 %collective-permute-start.84 = (bf16[512,1024]{1,0:T(8,128)(2,1)S(1)}, bf16[512,1024]{1,0:T(8,128)(2,1)S(1)}, u32[]{:S(2)}, u32[]{:S(2)}) collective-permute-start(bf16[512,1024]{1,0:T(8,128)(2,1)S(1)} %slice.545), channel_id=1, source_target_pairs={{0,16},{4,20},{8,24},{12,28},{16,0},{20,4},{24,8},{28,12},{1,17},{... | collective-permute-start | bytes 3145736 | tf_op jit(solution)/shard_map/ppermute | solution.py:279
  905.6 57.4 %collective-permute-start.73 = (bf16[256,512]{1,0:T(8,128)(2,1)S(1)}, bf16[256,512]{1,0:T(8,128)(2,1)S(1)}, u32[]{:S(2)}, u32[]{:S(2)}) collective-permute-start(bf16[256,512]{1,0:T(8,128)(2,1)S(1)} %get-tuple-element.97), channel_id=1, source_target_pairs={{0,24},{4,28},{8,16},{12,20},{16,8},{20,12},{24,0},{28,4},{1,25},{... | collective-permute-start | bytes 786440 | tf_op jit(solution)/shard_map/ppermute | solution.py:279
  983.6 74.2 %collective-permute-start.55 = (bf16[256,2048]{1,0:T(8,128)(2,1)}, bf16[256,2048]{1,0:T(8,128)(2,1)}, u32[]{:S(2)}, u32[]{:S(2)}) collective-permute-start(bf16[256,2048]{1,0:T(8,128)(2,1)} %fusion.18), channel_id=1, source_target_pairs={{0,1},{1,0},{2,3},{3,2},{4,5},{5,4},{6,7},{7,6},{8,9},{9,8},{10,11... | collective-permute-start | bytes 3145736 | tf_op jit(solution)/shard_map/ppermute | solution.py:285
  1000.4 53.5 %collective-permute-start.68 = (bf16[256,768]{1,0:T(8,128)(2,1)}, bf16[256,768]{1,0:T(8,128)(2,1)}, u32[]{:S(2)}, u32[]{:S(2)}) collective-permute-start(bf16[256,768]{1,0:T(8,128)(2,1)} %get-tuple-element.95), channel_id=1, source_target_pairs={{0,16},{4,20},{8,24},{12,28},{16,0},{20,4},{24,8},{28,12},{1,17},{... | collective-permute-start | bytes 1179656 | tf_op jit(solution)/shard_map/ppermute | solution.py:279
  1005.7 48.2 %collective-permute-start.67 = (bf16[256,768]{1,0:T(8,128)(2,1)S(1)}, bf16[256,768]{1,0:T(8,128)(2,1)}, u32[]{:S(2)}, u32[]{:S(2)}) collective-permute-start(bf16[256,768]{1,0:T(8,128)(2,1)S(1)} %get-tuple-element.93), channel_id=1, source_target_pairs={{0,8},{4,12},{8,0},{12,4},{16,24},{20,28},{24,16},{28,20},{1,9},{5... | collective-permute-start | bytes 1179656 | tf_op jit(solution)/shard_map/ppermute | solution.py:279
  1018.1 71.0 %collective-permute-start.51 = (bf16[256,2048]{1,0:T(8,128)(2,1)}, bf16[256,2048]{1,0:T(8,128)(2,1)}, u32[]{:S(2)}, u32[]{:S(2)}) collective-permute-start(bf16[256,2048]{1,0:T(8,128)(2,1)} %get-tuple-element.99.own_ref), channel_id=1, source_target_pairs={{0,1},{1,0},{2,3},{3,2},{4,5},{5,4},{6,7},{7,6},{8,9},{9,8},{10,11... | collective-permute-start | bytes 3145736 | tf_op jit(solution)/shard_map/ppermute | solution.py:285
  (127 other events, 2518.4 us)

commit v3 on v2

--- a/solution.py
+++ b/solution.py
@@ -272,8 +272,10 @@
 
 
 def build(shards):
-    far = [k << 2 for k in range(1, shards // 4)]
     line = [k << 1 for k in range(1, shards // 2)]
+
+    groups = [[i for i in range(shards) if (i >> 1) & 1 == bit] for bit in (0, 1)]
+    every = [[(i & ~3) | ((i & 1) << 1) | ((i >> 1) & 1) for i in range(shards)]]
 
     def across(values, mask):
         return lax.ppermute(values, "shard", [(i, i ^ mask) for i in range(shards)])
@@ -312,9 +314,11 @@
         half_s = shards // 2
         pad = 16
 
-        place = jnp.arange(shards, dtype=jnp.int32)
-        rel = (((shard >> 2) ^ ((place % half_s) >> 1)) << 2) | ((place & 1) << 1) | (y ^ (place // half_s))
-        nat = ((y ^ (place & 1)) * half_s) | (((shard >> 2) ^ (place >> 2)) << 1) | ((place >> 1) & 1)
+        def place_of(number):
+            return (number & ~3) | ((number & 1) << 1) | ((number >> 1) & 1)
+
+        rel = place_of(jnp.arange(shards, dtype=jnp.int32))
+        nat = rel
 
         attn_w = [w_query, w_key, w_value, w_out]
         ff_w = [w_gate, w_up, w_down]
@@ -353,62 +357,58 @@
             [array_of(block + pad, 3 * n_attn), array_of(block, n_attn)],
         )
 
-        def gather_line(own, gate):
-            near = [own] + [across(own, mask) for mask in line]
-            return near + [across(v, 1) for v in near]
+        def shard_at(i):
+            return shard ^ (((i % half_s) << 1) | (i // half_s))
 
         def place_line(parts, take):
             full = jnp.zeros((width, parts[0].shape[1]), bf16)
             for i, v in enumerate(parts):
-                where = (i & ~1) | ((i & 1) ^ zl)
-                full = lax.dynamic_update_slice_in_dim(full, take(v), where * block, 0)
+                full = lax.dynamic_update_slice_in_dim(full, take(v), place_of(shard_at(i)) * block, 0)
             return full
 
-        parts_qkv = gather_line(block_qkv, None)
+        near_qkv = [block_qkv] + [across(block_qkv, mask) for mask in line]
+        parts_qkv = near_qkv + [across(v, 1) for v in near_qkv]
         weight_qkv = place_line(parts_qkv, lambda v: v[:block])
-        gain_rows = [v[block : block + 2, :block] for v in parts_qkv]
-        gain_pairs = [ordered(zl, gain_rows[i], gain_rows[i + 1], 1) for i in range(0, shards, 2)]
-        gains_rel = cat(gain_pairs, 1).astype(f32)
+        gain_rows = jnp.stack([v[block : block + 2, :block] for v in parts_qkv])
+        away_bits = place_of(jnp.arange(shards, dtype=jnp.int32)) ^ shard
+        gain_rows = gain_rows[(away_bits >> 1) + half_s * (away_bits & 1)]
+        gains_rel = jnp.transpose(gain_rows, (1, 0, 2)).reshape(2, width).astype(f32)
         gain_a, gain_m = gains_rel[0:1], gains_rel[1:2]
 
-        block_o = after(block_o, parts_qkv[1])
-        parts_o = gather_line(block_o, None)
-        weight_o = place_line(parts_o, lambda v: v)
+        block_o = after(block_o, *near_qkv[1:])
+        near_o = cat([block_o] + [across(block_o, mask) for mask in line])
+        parts_o = cat([near_o, across(after(near_o, *parts_qkv[half_s:]), 1)])
+        weight_o = place_line([parts_o[i * block : (i + 1) * block] for i in range(shards)], lambda v: v)
 
         def send_ff(s_ref, g, u, d, out):
             start = pl.multiple_of((1 - s_ref[0]) * 2 * n_ff, n_ff)
             for i, ref in enumerate((g, u, d)):
                 out[:, i * 2 * n_ff : (i + 1) * 2 * n_ff] = ref[:, pl.ds(start, 2 * n_ff)]
 
-        (sent_f,) = small_call(send_ff, [core], [after(w_gate, other_a)] + ff_w[1:], [array_of(unit, 6 * n_ff)])
+        (sent_f,) = small_call(send_ff, [core], ff_w, [array_of(unit, 6 * n_ff)])
         other_f = swap_core(sent_f)
 
-        def keep_ff(s_ref, w, other, keep, send):
+        def keep_ff(s_ref, g, u, d, other, keep, send):
             me, low = s_ref[0], s_ref[1]
-            mine, theirs = pl.ds(me * unit, unit), pl.ds((1 - me) * unit, unit)
+            mine, theirs = pl.ds(pl.multiple_of(me * unit, unit), unit), pl.ds(pl.multiple_of((1 - me) * unit, unit), unit)
             for out, which in ((keep, low), (send, 1 - low)):
                 start = pl.multiple_of(which * n_ff, n_ff)
-                out[mine, :] = w[:, pl.ds(pl.multiple_of(me * 2 * n_ff, n_ff) + start, n_ff)]
-                out[theirs, :] = other[:, pl.ds(start, n_ff)]
+                for i, ref in enumerate((g, u, d)):
+                    cols = slice(i * n_ff, (i + 1) * n_ff)
+                    out[mine, cols] = ref[:, pl.ds(pl.multiple_of(me * 2 * n_ff, n_ff) + start, n_ff)]
+                    out[theirs, cols] = other[:, pl.ds(i * 2 * n_ff + start, n_ff)]
+
+        keep_f, send_f = small_call(keep_ff, [core, zl], ff_w + [other_f], [array_of(block, 3 * n_ff)] * 2)
+        recv_f = across(send_f, 2)
 
         def pair_rows(s_ref, own, other, out):
             low = s_ref[0]
-            out[pl.ds(low * block, block), :] = own[...]
-            out[pl.ds((1 - low) * block, block), :] = other[...]
-
-        def ff_weight(i, gate):
-            keep, send = small_call(
-                keep_ff, [core, zl], [ff_w[i], other_f[:, i * 2 * n_ff : (i + 1) * 2 * n_ff]],
-                [array_of(block, n_ff)] * 2,
-            )
-            send = after(send, gate)
-            (own,) = small_call(pair_rows, [zl], [keep, across(send, 2)], [array_of(2 * block, n_ff)])
-            near = [own] + [across(own, mask) for mask in far]
-            return near[1], cat(near + [across(v, 1) for v in near])
-
-        event_g, weight_g = ff_weight(0, parts_o[1])
-        event_u, weight_u = ff_weight(1, event_g)
-        event_d, weight_d = ff_weight(2, event_u)
+            out[pl.ds(pl.multiple_of(low * block, block), block), :] = own[...]
+            out[pl.ds(pl.multiple_of((1 - low) * block, block), block), :] = other[...]
+
+        (pair_f,) = small_call(pair_rows, [zl], [keep_f, recv_f], [array_of(2 * block, 3 * n_ff)])
+        weight_f = lax.all_gather(pair_f, "shard", axis=0, tiled=True, axis_index_groups=groups)
+        weight_g, weight_u, weight_d = [weight_f[:, i * n_ff : (i + 1) * n_ff] for i in range(3)]
 
         seg_row = segments[0]
         cosine, sine = rope_tables(doc_positions(seg_row))
@@ -444,7 +444,7 @@
         both = cat([across(by_tp[:mid], 2), swap_tp(by_zl[mid:])])
         h_two = cat([near, both, far_near, swap_core(both)])
 
-        dy_rel = permute_cols(after(cotangent, event_g), rel, block)
+        dy_rel = permute_cols(after(cotangent, *parts_qkv[half_s:]), rel, block)
         dy_ff = cat([rows_of(dy_rel, half * part, part), rows_of(dy_rel, (1 - half) * part, part)])
         dy_zl = across(dy_ff[:part], 2)
         near = cat([dy_ff, dy_zl, swap_tp(dy_zl)])
@@ -481,15 +481,7 @@
             lambda where: contract_cols(grad_gate[where], weight_g)
             + contract_cols(grad_up[where], weight_u)
         )
-        late_gate, late_up, late_hidden = after((grad_gate, grad_up, hidden), event_h)
-
-        def away_rows(left, right, mask=1):
-            return across(contract_rows(left[:, width // 2 :], right).astype(bf16), mask)
-
-        away_d = away_rows(grad_out, late_hidden)
-        away_g = away_rows(h_two, late_gate)
-        away_u = away_rows(h_two, late_up)
-        late_hidden = after(late_hidden, grad_h_two)
+        late_hidden = after(hidden, grad_h_two)
         event_m, mlp = from_tokens(lambda where: contract_cols(late_hidden[where], weight_d))
         out_part = (after_attn + mlp).astype(bf16)
         output = join_tokens(out_part, swap_tp(out_part), half, nat, block)
@@ -503,74 +495,61 @@
         grad_attn = ordered(core, grad_half, swap_core(grad_half))
         grad_mixed = matmul(grad_attn, weight_o).astype(bf16)
 
-        def rows_far(left, right, away, event):
-            away = after(away, event)
-            total = contract_rows(left[:, : width // 2], right) + away.astype(f32)
-            step = 2 * block
-            own = total[:step]
-            for i, mask in enumerate(far):
-                sent = total[(i + 1) * step : (i + 2) * step].astype(bf16)
-                own = own + across(sent, mask).astype(f32)
-            own = own.astype(bf16)
+        def scatter(values, members):
+            return lax.psum_scatter(
+                values.astype(bf16), "shard", scatter_dimension=0, tiled=True, axis_index_groups=members
+            )
+
+        def rows_pair(own, count):
             other = across(rows_of(own, (1 - zl) * block, block), 2)
 
             def send_rows(s_ref, mine, theirs, out):
-                low, away_rows = s_ref[1], (1 - s_ref[0]) * unit
-                out[:, pl.ds(pl.multiple_of(low * n_ff, n_ff), n_ff)] = mine[pl.ds(low * block + away_rows, unit), :]
-                out[:, pl.ds(pl.multiple_of((1 - low) * n_ff, n_ff), n_ff)] = theirs[pl.ds(away_rows, unit), :]
-
-            (sent,) = small_call(send_rows, [core, zl], [own, other], [array_of(unit, 2 * n_ff)])
+                low, away_rows = s_ref[1], pl.multiple_of((1 - s_ref[0]) * unit, unit)
+                rows_m = pl.ds(pl.multiple_of(low * block, block) + away_rows, unit)
+                for i in range(count):
+                    cols = slice(i * n_ff, (i + 1) * n_ff)
+                    out[:, pl.ds(i * 2 * n_ff + pl.multiple_of(low * n_ff, n_ff), n_ff)] = mine[rows_m, cols]
+                    out[:, pl.ds(i * 2 * n_ff + pl.multiple_of((1 - low) * n_ff, n_ff), n_ff)] = theirs[
+                        pl.ds(away_rows, unit), cols
+                    ]
+
+            (sent,) = small_call(send_rows, [core, zl], [own, other], [array_of(unit, 2 * count * n_ff)])
             third = swap_core(sent)
 
-            def join_rows(s_ref, mine, theirs, third_ref, out):
+            def join_rows(s_ref, mine, theirs, third_ref, *outs):
                 me, low = s_ref[0], s_ref[1]
                 start = pl.multiple_of(me * 2 * n_ff, n_ff)
-                out[:, pl.ds(start + pl.multiple_of(low * n_ff, n_ff), n_ff)] = mine[
-                    pl.ds(low * block + me * unit, unit), :
-                ].astype(f32)
-                out[:, pl.ds(start + pl.multiple_of((1 - low) * n_ff, n_ff), n_ff)] = theirs[
-                    pl.ds(me * unit, unit), :
-                ].astype(f32)
-                out[:, pl.ds(pl.multiple_of((1 - me) * 2 * n_ff, n_ff), 2 * n_ff)] = third_ref[...].astype(f32)
-
-            (full,) = small_call(join_rows, [core, zl], [own, other, third], [array_of(unit, 4 * n_ff, f32)])
-            return full
-
-        def rows_line(left, right, away, event):
-            if event is not None:
-                away = after(away, event)
-            total = contract_rows(left[:, : width // 2], right) + away.astype(f32)
-            own = rows_of(total, zl * block, block)
-            for i, mask in enumerate(line):
-                k = i + 1
-                where = (k & ~1) | ((k & 1) ^ zl)
-                sent = rows_of(total, where * block, block).astype(bf16)
-                own = own + across(sent, mask).astype(f32)
-            return own
+                away = pl.multiple_of((1 - me) * 2 * n_ff, n_ff)
+                here = pl.multiple_of(me * unit, unit)
+                for i, out in enumerate(outs):
+                    cols = slice(i * n_ff, (i + 1) * n_ff)
+                    out[:, pl.ds(start + pl.multiple_of(low * n_ff, n_ff), n_ff)] = mine[
+                        pl.ds(pl.multiple_of(low * block, block) + here, unit), cols
+                    ].astype(f32)
+                    out[:, pl.ds(start + pl.multiple_of((1 - low) * n_ff, n_ff), n_ff)] = theirs[
+                        pl.ds(here, unit), cols
+                    ].astype(f32)
+                    out[:, pl.ds(away, 2 * n_ff)] = third_ref[:, i * 2 * n_ff : (i + 1) * 2 * n_ff].astype(f32)
+
+            return small_call(join_rows, [core, zl], [own, other, third], [array_of(unit, 4 * n_ff, f32)] * count)
 
         def send_unit(s_ref, own, out):
             out[...] = own[pl.ds((1 - s_ref[0]) * unit, unit), :].astype(bf16)
 
-        away_o = away_rows(grad_attn, mixed)
-        first_heads = heads // 2
-        n_first = 3 * first_heads * HD
-        grad_low = attend_backward(kept, grad_mixed, seg_row, cosine, sine, 0, first_heads)
-        away_low = away_rows(h_one, grad_low)
-        grad_high = attend_backward(kept, grad_mixed, seg_row, cosine, sine, first_heads, heads - first_heads)
-        away_high = away_rows(h_one, grad_high)
-        grad_qkv = cat([grad_low, grad_high], 1)
-
-        event_q = grad_mixed
-        grad_w_down = rows_far(grad_out, late_hidden, away_d, event_q)
-        grad_w_gate = rows_far(h_two, late_gate, away_g, event_q)
-        grad_w_up = rows_far(h_two, late_up, away_u, event_q)
+        own_d = scatter(contract_rows(grad_out, hidden), groups)
+        own_gu = scatter(
+            cat([contract_rows(h_two, grad_gate).astype(bf16), contract_rows(h_two, grad_up).astype(bf16)], 1), groups
+        )
+        own_o = scatter(contract_rows(grad_attn, mixed), every)
+        grad_qkv = attend_backward(kept, grad_mixed, seg_row, cosine, sine, 0, heads)
+        own_qkv = scatter(contract_rows(h_one, grad_qkv), every)
+
+        (grad_w_down,) = rows_pair(own_d, 1)
+        grad_w_gate, grad_w_up = rows_pair(own_gu, 2)
 
         grad_h_one = to_slice(grad_qkv, lambda v: contract_cols(v, weight_qkv))
 
-        own_o = rows_line(grad_attn, mixed, away_o, None)
-        own_low = rows_line(h_one, grad_low, away_low, None)
-        own_high = rows_line(h_one, grad_high, away_high, None)
-        own_a = cat([own_low, own_high, own_o], 1)
+        own_a = cat([own_qkv, own_o], 1)
         (sent_g,) = small_call(send_unit, [core], [own_a], [array_of(unit, 4 * n_attn)])
         other_a = swap_core(sent_g)
 
@@ -579,7 +558,7 @@
             mine = pl.ds(pl.multiple_of(me * unit, unit), unit)
             here, there = me * n_attn, (1 - me) * n_attn
             for start, load in (
-                (here, lambda c: own[mine, c]),
+                (here, lambda c: own[mine, c].astype(f32)),
                 (there, lambda c: other[:, c].astype(f32)),
             ):
                 start = pl.multiple_of(start, n_attn)
@@ -600,11 +579,11 @@
 
         grad_gains = cat([grad_gain_a, grad_gain_m])
         grad_gains = grad_gains + swap_tp(grad_gains)
-        for mask in [1] + [1 << bit for bit in range(shards.bit_length() - 2, 1, -1)]:
+        for mask in [1 << bit for bit in range(shards.bit_length() - 2, 1, -1)] + [1, 2]:
             mid = grad_gains.shape[1] // 2
-            grad_gains = grad_gains[:, :mid] + across(grad_gains[:, mid:], mask)
-        first, second = grad_gains[:, :block], grad_gains[:, block:]
-        grad_gains = jnp.where(zl == 0, first, second) + across(jnp.where(zl == 0, second, first), 2)
+            first, second = grad_gains[:, :mid], grad_gains[:, mid:]
+            low = (shard & mask) == 0
+            grad_gains = jnp.where(low, first, second) + across(jnp.where(low, second, first), mask)
         first, second = grad_gains[:, :unit], grad_gains[:, unit:]
         grad_gains = jnp.where(core == 0, first, second) + swap_core(jnp.where(core == 0, second, first))
 

time: 1120 us -> 1110 us (level)
  starting transfers between devices: 83.8 us -> 55.5 us
  Pallas kernels: 111 us -> 94.9 us
  between operations: 2.22 us -> 14.9 us
    ppermute x57 -> x24, waiting for transfers between devices: 536 us -> 385 us  [across(): return lax.ppermute(values, 'shard', [(i, i ^ mask) for i in range(shards)])]
    reduce_scatter x0 -> x4, waiting for transfers between devices: none -> 86.7 us  [scatter(): lax.psum_scatter(values.astype(bf16), 'shard', scatter_dimension=0, tiled...]
    ppermute x13, waiting for transfers between devices: 53 us -> 122 us  [swap_tp(): return lax.ppermute(values, 'tp', [(0, 1), (1, 0)])]
    ppermute x57 -> x24, starting transfers between devices: 71 us -> 37.3 us  [across(): return lax.ppermute(values, 'shard', [(i, i ^ mask) for i in range(shards)])]
    dynamic_update_slice x16, local copies, waits for them, and re-layouts: 6.23 us -> 23.2 us  [place_line(): lax.dynamic_update_slice_in_dim(full, take(v), place_of(shard_at(i)) * bl...]
    pallas_call x17 -> x11, Pallas kernels: 48.8 us -> 36.4 us  [small_call(): pl.pallas_call(body, grid_spec=pltpu.PrefetchScalarGridSpec(num_scalar_pr...]
    pallas_call x2 -> x1, Pallas kernels: 30.9 us -> 27.4 us  [attend_backward(): pl.pallas_call(body, grid_spec=pltpu.PrefetchScalarGridSpec(num_scalar_pr...]
    unnamed x153 -> x121, local copies, waits for them, and re-layouts: 26.4 us -> 28.1 us
  transfers between devices with their start and end apart: 87 -> 58, of which waited for: 42 -> 28; matrix products, arithmetic and copies ran while one was open for 21% -> 23% of each run, Pallas kernels for 8% -> 8%
where the time goes in v3:
time: 1110 us; the launch traced here: 1100 us
  waiting for transfers between devices  603 us (54%)
  matrix products  213 us (19%)
  Pallas kernels  94.9 us (9%)
  local copies, waits for them, and re-layouts  64.8 us (6%)
  starting transfers between devices  55.5 us (5%)
  other arithmetic  54.5 us (5%)
  between operations  14.9 us (1%)
    ppermute x24, waiting for transfers between devices, across(): return lax.ppermute(values, 'shard', [(i, i ^ mask) for i in range(shards)])  385 us
    ppermute x13, waiting for transfers between devices, swap_tp(): return lax.ppermute(values, 'tp', [(0, 1), (1, 0)])  122 us
    reduce_scatter x4, waiting for transfers between devices, scatter(): lax.psum_scatter(values.astype(bf16), 'shard', scatter_dimension=0, tiled...  86.7 us
    dot_general x12, matrix products, contract_cols(): lax.dot_general(left, right, (((1,), (1,)), ((), ())), preferred_element_...  83.4 us
    dot_general x5, matrix products, matmul(): return jnp.dot(left, right, preferred_element_type=jnp.float32)  71 us
    dot_general x5, matrix products, contract_rows(): lax.dot_general(left, right, (((0,), (0,)), ((), ())), preferred_element_...  58.3 us
    ppermute x24, starting transfers between devices, across(): return lax.ppermute(values, 'shard', [(i, i ^ mask) for i in range(shards)])  37.3 us
    pallas_call x11, Pallas kernels, small_call(): pl.pallas_call(body, grid_spec=pltpu.PrefetchScalarGridSpec(num_scalar_pr...  36.4 us
  transfers between devices with their start and end apart: 58, of which 28 were waited for; matrix products, arithmetic and copies ran while one was open for 23% of the time, Pallas kernels for 8%

profile of v3, /device:TPU:0, one launch (start us, length us, event | category | flops | bytes accessed | tf_op | source)
XLA Modules:
  0.0 1100.1 jit_solution(6419975167901949817)
XLA Ops:
  46.6 56.1 %collective-permute-done.3 = bf16[272,1536]{1,0:T(8,128)(2,1)S(1)} collective-permute-done((bf16[272,1536]{1,0:T(8,128)(2,1)}, bf16[272,1536]{1,0:T(8,128)(2,1)S(1)}, u32[]{:S(2)}, u32[]{:S(2)}) %collective-permute-start.3) | collective-permute-done | bytes 835616 | tf_op jit(solution)/shard_map/ppermute | solution.py:281
  104.4 18.4 %collective-permute-done.5 = bf16[272,1536]{1,0:T(8,128)(2,1)S(1)} collective-permute-done((bf16[272,1536]{1,0:T(8,128)(2,1)}, bf16[272,1536]{1,0:T(8,128)(2,1)S(1)}, u32[]{:S(2)}, u32[]{:S(2)}) %collective-permute-start.5) | collective-permute-done | bytes 835616 | tf_op jit(solution)/shard_map/ppermute | solution.py:281
  154.5 15.7 %collective-permute-done.7 = bf16[272,1536]{1,0:T(8,128)(2,1)S(1)} collective-permute-done((bf16[272,1536]{1,0:T(8,128)(2,1)}, bf16[272,1536]{1,0:T(8,128)(2,1)S(1)}, u32[]{:S(2)}, u32[]{:S(2)}) %collective-permute-start.7) | collective-permute-done | bytes 835616 | tf_op jit(solution)/shard_map/ppermute | solution.py:281
  170.2 35.8 %collective-permute-done.8 = bf16[272,1536]{1,0:T(8,128)(2,1)S(1)} collective-permute-done((bf16[272,1536]{1,0:T(8,128)(2,1)S(1)}, bf16[272,1536]{1,0:T(8,128)(2,1)S(1)}, u32[]{:S(2)}, u32[]{:S(2)}) %collective-permute-start.8) | collective-permute-done | bytes 835616 | tf_op jit(solution)/shard_map/ppermute | solution.py:281
  206.0 24.2 %collective-permute-done.9 = bf16[272,1536]{1,0:T(8,128)(2,1)S(1)} collective-permute-done((bf16[272,1536]{1,0:T(8,128)(2,1)S(1)}, bf16[272,1536]{1,0:T(8,128)(2,1)S(1)}, u32[]{:S(2)}, u32[]{:S(2)}) %collective-permute-start.9) | collective-permute-done | bytes 835616 | tf_op jit(solution)/shard_map/ppermute | solution.py:281
  239.6 14.4 %fusion.29.qkv_ref = f32[1024,1536]{1,0:T(8,128)} fusion(bf16[2048,1536]{1,0:T(8,128)(2,1)} %slice_dynamic-update-slice_fusion, f32[2048]{0:T(1024)S(1)} %bitcast.86, f32[1024]{0:T(1024)S(1)} %add_rsqrt_fusion, bf16[512,2048]{1,0:T(8,128)(2,1)S(1)} %copy-done.2, bf16[512,2048]{1,0:T(8,128)(2,1)} %collective-permute-done, pred[]{:T(512)S(6)} %eq.18), kind=kOutput, calls=%fused_computation.68 | convolution fusion | flops 6469713920 | bytes 16789504 | tf_op jit(solution)/shard_map/dot_general | solution.py:22
  254.1 14.7 %shard_map.206 = (bf16[1024,512]{1,0:T(8,128)(2,1)}, bf16[1024,1536]{1,0:T(8,128)(2,1)}) custom-call(s32[1024]{0:T(1024)} %bitcast.76, f32[1024,1536]{1,0:T(8,128)} %fusion.29.qkv_ref, f32[1024,128]{1,0:T(8,128)} %get-tuple-element.83.cos_ref, f32[1024,128]{1,0:T(8,128)} %get-tuple-element.84.sin_ref, s32[1024,1]{1,0:T(8,128)} %copy.25.seg_col, ...), custom_call_target="tpu_custom_call" | custom-call | tf_op jit(solution)/shard_map/pallas_call | solution.py:195
  290.7 89.7 %collective-permute-done.24 = bf16[256,2048]{1,0:T(8,128)(2,1)} collective-permute-done((bf16[256,2048]{1,0:T(8,128)(2,1)S(1)}, bf16[256,2048]{1,0:T(8,128)(2,1)}, u32[]{:S(2)}, u32[]{:S(2)}) %collective-permute-start.24) | collective-permute-done | bytes 1048608 | tf_op jit(solution)/shard_map/ppermute | solution.py:281
  388.5 18.2 %collective-permute-done.25 = bf16[256,2048]{1,0:T(8,128)(2,1)} collective-permute-done((bf16[256,2048]{1,0:T(8,128)(2,1)}, bf16[256,2048]{1,0:T(8,128)(2,1)}, u32[]{:S(2)}, u32[]{:S(2)}) %collective-permute-start.25) | collective-permute-done | bytes 1048608 | tf_op jit(solution)/shard_map/ppermute | solution.py:287
  412.5 15.8 %collective-permute-done.15 = bf16[256,2048]{1,0:T(8,128)(2,1)} collective-permute-done((bf16[256,2048]{1,0:T(8,128)(2,1)}, bf16[256,2048]{1,0:T(8,128)(2,1)}, u32[]{:S(2)}, u32[]{:S(2)}) %collective-permute-start.15) | collective-permute-done | bytes 1048608 | tf_op jit(solution)/shard_map/ppermute | solution.py:287
  434.5 22.8 %collective-permute-done.16 = bf16[256,2048]{1,0:T(8,128)(2,1)S(1)} collective-permute-done((bf16[256,2048]{1,0:T(8,128)(2,1)S(1)}, bf16[256,2048]{1,0:T(8,128)(2,1)S(1)}, u32[]{:S(2)}, u32[]{:S(2)}) %collective-permute-start.16) | collective-permute-done | bytes 1048608 | tf_op jit(solution)/shard_map/ppermute | solution.py:287
  464.8 9.8 collective-permute-done.18
  482.5 14.6 %fusion.10 = f32[2048,1024]{1,0:T(8,128)} fusion(bf16[2048,2048]{1,0:T(8,128)(2,1)} %constant_dynamic-update-slice_fusion.8, bf16[2048,3072]{1,0:T(8,128)(2,1)} %all-gather.2.cloned.1.call-done), kind=kOutput, calls=%fused_computation.30 | convolution fusion | flops 8589934592 | bytes 20971520 | tf_op jit(solution)/shard_map/dot_general | solution.py:22
  497.1 13.2 %fusion.4 = f32[2048,1024]{1,0:T(8,128)} fusion(bf16[2048,2048]{1,0:T(8,128)(2,1)S(1)} %copy-done.29, bf16[2048,3072]{1,0:T(8,128)(2,1)} %all-gather.2.cloned.1.call-done), kind=kOutput, calls=%fused_computation.24 | convolution fusion | flops 8589934592 | bytes 20971520 | tf_op jit(solution)/shard_map/dot_general | solution.py:22
  510.3 23.1 %multiply_convert_fusion.1 = (bf16[2048,1024]{1,0:T(8,128)(2,1)}, bf16[2048,1024]{1,0:T(8,128)(2,1)}, bf16[2048,1024]{1,0:T(8,128)(2,1)S(1)}) fusion(f32[2048,1024]{1,0:T(8,128)} %fusion.4, f32[2048,1024]{1,0:T(8,128)} %fusion.10, bf16[2048,2048]{1,0:T(8,128)(2,1)} %constant_dynamic-update-slice_fusion.8, bf16[2048,3072]{1,0:T(8,128)(2,1)} %all-gather.2.cloned.1.call-done), kind=kOutput, calls=%fused_computation.9 | convolution fusion | flops 8621391872 | bytes 41943040 | tf_op jit(solution)/shard_map/dot_general | solution.py:22
  535.5 13.0 %convolution_convert_fusion.2 = bf16[2048,1024]{1,0:T(8,128)(2,1)} fusion(bf16[2048,2048]{1,0:T(8,128)(2,1)} %copy-done.28, bf16[2048,1024]{1,0:T(8,128)(2,1)S(1)} %get-tuple-element.35), kind=kOutput, calls=%fused_computation.19 | convolution fusion | flops 8592031744 | bytes 16777216 | tf_op jit(solution)/shard_map/dot_general | solution.py:26
  548.5 9.4 convolution_convert_fusion.1
  558.5 13.0 %convolution_convert_fusion.4 = bf16[2048,1024]{1,0:T(8,128)(2,1)} fusion(bf16[2048,2048]{1,0:T(8,128)(2,1)} %constant_dynamic-update-slice_fusion.8, bf16[2048,1024]{1,0:T(8,128)(2,1)S(1)} %copy-done.46), kind=kOutput, calls=%fused_computation.21 | convolution fusion | flops 8592031744 | bytes 16777216 | tf_op jit(solution)/shard_map/dot_general | solution.py:26
  571.5 13.1 %convolution_convert_fusion.3 = bf16[2048,1024]{1,0:T(8,128)(2,1)} fusion(bf16[2048,2048]{1,0:T(8,128)(2,1)} %constant_dynamic-update-slice_fusion.8, bf16[2048,1024]{1,0:T(8,128)(2,1)S(1)} %copy-done.49), kind=kOutput, calls=%fused_computation.20 | convolution fusion | flops 8592031744 | bytes 16777216 | tf_op jit(solution)/shard_map/dot_general | solution.py:26
  624.1 9.6 fusion.70
  647.6 13.7 %collective-permute-done.33 = bf16[512,1024]{1,0:T(8,128)(2,1)S(1)} collective-permute-done((bf16[512,1024]{1,0:T(8,128)(2,1)}, bf16[512,1024]{1,0:T(8,128)(2,1)S(1)}, u32[]{:S(2)}, u32[]{:S(2)}) %collective-permute-start.33) | collective-permute-done | bytes 1048608 | tf_op jit(solution)/shard_map/ppermute | solution.py:287
  664.8 18.8 %collective-permute-done.28 = bf16[512,1024]{1,0:T(8,128)(2,1)S(1)} collective-permute-done((bf16[512,1024]{1,0:T(8,128)(2,1)S(1)}, bf16[512,1024]{1,0:T(8,128)(2,1)S(1)}, u32[]{:S(2)}, u32[]{:S(2)}) %collective-permute-start.28) | collective-permute-done | bytes 1048608 | tf_op jit(solution)/shard_map/ppermute | solution.py:287
  695.8 40.5 %collective-permute-done.35 = bf16[512,1024]{1,0:T(8,128)(2,1)S(1)} collective-permute-done((bf16[512,1024]{1,0:T(8,128)(2,1)S(1)}, bf16[512,1024]{1,0:T(8,128)(2,1)S(1)}, u32[]{:S(2)}, u32[]{:S(2)}) %collective-permute-start.35) | collective-permute-done | bytes 1048608 | tf_op jit(solution)/shard_map/ppermute | solution.py:281
  736.5 14.8 %collective-permute-done.34 = bf16[256,1024]{1,0:T(8,128)(2,1)S(1)} collective-permute-done((bf16[256,1024]{1,0:T(8,128)(2,1)S(1)}, bf16[256,1024]{1,0:T(8,128)(2,1)S(1)}, u32[]{:S(2)}, u32[]{:S(2)}) %collective-permute-start.34) | collective-permute-done | bytes 524320 | tf_op jit(solution)/shard_map/ppermute | solution.py:281
  754.5 17.3 %collective-permute-done.29 = bf16[256,1024]{1,0:T(8,128)(2,1)S(1)} collective-permute-done((bf16[256,1024]{1,0:T(8,128)(2,1)S(1)}, bf16[256,1024]{1,0:T(8,128)(2,1)S(1)}, u32[]{:S(2)}, u32[]{:S(2)}) %collective-permute-start.29) | collective-permute-done | bytes 524320 | tf_op jit(solution)/shard_map/ppermute | solution.py:281
  778.5 23.4 %collective-permute-done.38 = bf16[256,2048]{1,0:T(8,128)(2,1)S(1)} collective-permute-done((bf16[256,2048]{1,0:T(8,128)(2,1)S(1)}, bf16[256,2048]{1,0:T(8,128)(2,1)S(1)}, u32[]{:S(2)}, u32[]{:S(2)}) %collective-permute-start.38) | collective-permute-done | bytes 1048608 | tf_op jit(solution)/shard_map/ppermute | solution.py:287
  812.8 27.4 %shard_map.212 = bf16[1024,1536]{1,0:T(8,128)(2,1)} custom-call(s32[1024]{0:T(1024)} %bitcast.77, bf16[1024,1536]{1,0:T(8,128)(2,1)} %get-tuple-element.36.kept_ref, bf16[1024,512]{1,0:T(8,128)(2,1)} %convolution_convert_fusion.8.do_ref, f32[1024,128]{1,0:T(8,128)} %get-tuple-element.83.cos_ref, f32[1024,128]{1,0:T(8,128)} %get-tuple-element.84.sin_ref, ...), custom_call_target="tpu_custom_call" | custom-call | tf_op jit(solution)/shard_map/pallas_call | solution.py:254
  840.2 11.5 %convolution_convert_fusion = bf16[2048,1536]{1,0:T(8,128)(2,1)} fusion(bf16[1024,1536]{1,0:T(8,128)(2,1)} %shard_map.212, f32[2048]{0:T(1024)S(1)} %bitcast.87, f32[1024]{0:T(1024)S(1)} %copy-done.35, bf16[512,2048]{1,0:T(8,128)(2,1)S(1)} %copy-done.3, bf16[512,2048]{1,0:T(8,128)(2,1)} %collective-permute-done, pred[]{:T(512)S(6)} %eq.18), kind=kOutput, calls=%fused_computation.14 | convolution fusion | flops 6472859648 | bytes 13643777 | tf_op jit(solution)/shard_map/dot_general | solution.py:26
  914.1 10.0 collective-permute-start.45
  932.4 40.9 %collective-permute-done.46 = f32[2,256]{1,0:T(2,128)S(1)} collective-permute-done((f32[2,256]{1,0:T(2,128)S(1)}, f32[2,256]{1,0:T(2,128)S(1)}, u32[]{:S(2)}, u32[]{:S(2)}) %collective-permute-start.46) | collective-permute-done | bytes 2080 | tf_op jit(solution)/shard_map/ppermute | solution.py:281
  978.5 35.5 %reduce-scatter.5.cloned.1.call-done = bf16[256,1536]{1,0:T(8,128)(2,1)} async-done(((bf16[2048,1536]{1,0:T(8,128)(2,1)}), bf16[256,1536]{1,0:T(8,128)(2,1)}) %reduce-scatter.5.cloned.1.call-update) | async-done | bytes 786448 | tf_op jit(solution)/shard_map/reduce_scatter | solution.py:499
  1015.2 51.2 %reduce-scatter.7.cloned.1.call-done = bf16[256,512]{1,0:T(8,128)(2,1)} async-done(((bf16[2048,512]{1,0:T(8,128)(2,1)}), bf16[256,512]{1,0:T(8,128)(2,1)}) %reduce-scatter.7.cloned.1.call-update) | async-done | bytes 262160 | tf_op jit(solution)/shard_map/reduce_scatter | solution.py:499
  (340 shorter events, 335.4 us)
Async XLA Ops:
  7.2 475.3 %all-gather.2.cloned.1.call-start = ((), (), s32[]{:S(2)}) async-start(), calls=%async_computation.4 | async-start | bytes 15728640 | tf_op jit(solution)/shard_map/all_gather | solution.py:410
  18.6 132.7 %collective-permute-start = (bf16[512,2048]{1,0:T(8,128)(2,1)}, bf16[512,2048]{1,0:T(8,128)(2,1)}, u32[]{:S(2)}, u32[]{:S(2)}) collective-permute-start(bf16[512,2048]{1,0:T(8,128)(2,1)} %shard_map.203), channel_id=1, source_target_pairs={{0,2},{2,0},{1,3},{3,1},{4,6},{6,4},{5,7},{7,5},{8,10},{10,8},{9,1... | collective-permute-start | bytes 6291464 | tf_op jit(solution)/shard_map/ppermute | solution.py:284
  29.0 98.5 %collective-permute-start.23 = (bf16[256,3072]{1,0:T(8,128)(2,1)}, bf16[256,3072]{1,0:T(8,128)(2,1)S(1)}, u32[]{:S(2)}, u32[]{:S(2)}) collective-permute-start(bf16[256,3072]{1,0:T(8,128)(2,1)} %get-tuple-element.33), channel_id=1, source_target_pairs={{0,8},{4,12},{8,0},{12,4},{16,24},{20,28},{24,16},{28,20},{1,9},{5... | collective-permute-start | bytes 4718600 | tf_op jit(solution)/shard_map/ppermute | solution.py:281
  36.4 66.2 %collective-permute-start.3 = (bf16[272,1536]{1,0:T(8,128)(2,1)}, bf16[272,1536]{1,0:T(8,128)(2,1)S(1)}, u32[]{:S(2)}, u32[]{:S(2)}) collective-permute-start(bf16[272,1536]{1,0:T(8,128)(2,1)} %get-tuple-element.27), channel_id=1, source_target_pairs={{0,8},{4,12},{8,0},{12,4},{16,24},{20,28},{24,16},{28,20},{1,9},{5... | collective-permute-start | bytes 2506760 | tf_op jit(solution)/shard_map/ppermute | solution.py:281
  36.4 67.9 %collective-permute-start.4 = (bf16[272,1536]{1,0:T(8,128)(2,1)}, bf16[272,1536]{1,0:T(8,128)(2,1)S(1)}, u32[]{:S(2)}, u32[]{:S(2)}) collective-permute-start(bf16[272,1536]{1,0:T(8,128)(2,1)} %get-tuple-element.27), channel_id=1, source_target_pairs={{0,16},{4,20},{8,24},{12,28},{16,0},{20,4},{24,8},{28,12},{1,17},{... | collective-permute-start | bytes 2506760 | tf_op jit(solution)/shard_map/ppermute | solution.py:281
  39.5 83.3 %collective-permute-start.5 = (bf16[272,1536]{1,0:T(8,128)(2,1)}, bf16[272,1536]{1,0:T(8,128)(2,1)S(1)}, u32[]{:S(2)}, u32[]{:S(2)}) collective-permute-start(bf16[272,1536]{1,0:T(8,128)(2,1)} %get-tuple-element.27), channel_id=1, source_target_pairs={{0,24},{4,28},{8,16},{12,20},{16,8},{20,12},{24,0},{28,4},{1,25},{... | collective-permute-start | bytes 2506760 | tf_op jit(solution)/shard_map/ppermute | solution.py:281
  132.4 745.8 %reduce-scatter.11.cloned.1.call-start = ((), (), s32[]{:S(2)}) async-start(), calls=%async_computation.8 | async-start | bytes 5242880 | tf_op jit(solution)/shard_map/reduce_scatter | solution.py:499
  135.9 34.3 %collective-permute-start.7 = (bf16[272,1536]{1,0:T(8,128)(2,1)}, bf16[272,1536]{1,0:T(8,128)(2,1)S(1)}, u32[]{:S(2)}, u32[]{:S(2)}) collective-permute-start(bf16[272,1536]{1,0:T(8,128)(2,1)} %copy-done.17), channel_id=1, source_target_pairs={{0,4},{4,0},{8,12},{12,8},{16,20},{20,16},{24,28},{28,24},{1,5},{5... | collective-permute-start | bytes 2506760 | tf_op jit(solution)/shard_map/ppermute | solution.py:281
  141.8 64.2 %collective-permute-start.8 = (bf16[272,1536]{1,0:T(8,128)(2,1)S(1)}, bf16[272,1536]{1,0:T(8,128)(2,1)S(1)}, u32[]{:S(2)}, u32[]{:S(2)}) collective-permute-start(bf16[272,1536]{1,0:T(8,128)(2,1)S(1)} %copy-done.19), channel_id=1, source_target_pairs={{0,4},{4,0},{8,12},{12,8},{16,20},{20,16},{24,28},{28,24},{1,5},{5... | collective-permute-start | bytes 2506760 | tf_op jit(solution)/shard_map/ppermute | solution.py:281
  144.6 85.7 %collective-permute-start.9 = (bf16[272,1536]{1,0:T(8,128)(2,1)S(1)}, bf16[272,1536]{1,0:T(8,128)(2,1)S(1)}, u32[]{:S(2)}, u32[]{:S(2)}) collective-permute-start(bf16[272,1536]{1,0:T(8,128)(2,1)S(1)} %copy-done.22), channel_id=1, source_target_pairs={{0,4},{4,0},{8,12},{12,8},{16,20},{20,16},{24,28},{28,24},{1,5},{5... | collective-permute-start | bytes 2506760 | tf_op jit(solution)/shard_map/ppermute | solution.py:281
  230.2 46.2 %collective-permute-start.13 = (bf16[1024,512]{1,0:T(8,128)(2,1)}, bf16[1024,512]{1,0:T(8,128)(2,1)S(1)}, u32[]{:S(2)}, u32[]{:S(2)}) collective-permute-start(bf16[1024,512]{1,0:T(8,128)(2,1)} %pad_maximum_fusion.4), channel_id=1, source_target_pairs={{0,4},{4,0},{8,12},{12,8},{16,20},{20,16},{24,28},{28,24},{1,5},{5... | collective-permute-start | bytes 3145736 | tf_op jit(solution)/shard_map/ppermute | solution.py:281
  283.7 98.2 %collective-permute-start.14 = (bf16[512,2048]{1,0:T(8,128)(2,1)}, bf16[512,2048]{1,0:T(8,128)(2,1)}, u32[]{:S(2)}, u32[]{:S(2)}) collective-permute-start(bf16[512,2048]{1,0:T(8,128)(2,1)} %convolution_convert_fusion.7), channel_id=1, source_target_pairs={{0,2},{2,0},{1,3},{3,1},{4,6},{6,4},{5,7},{7,5},{8,10},{10,8},{9,1... | collective-permute-start | bytes 6291464 | tf_op jit(solution)/shard_map/ppermute | solution.py:284
  290.7 89.7 %collective-permute-start.24 = (bf16[256,2048]{1,0:T(8,128)(2,1)S(1)}, bf16[256,2048]{1,0:T(8,128)(2,1)}, u32[]{:S(2)}, u32[]{:S(2)}) collective-permute-start(bf16[256,2048]{1,0:T(8,128)(2,1)S(1)} %get-tuple-element.54), channel_id=1, source_target_pairs={{0,8},{4,12},{8,0},{12,4},{16,24},{20,28},{24,16},{28,20},{1,9},{5... | collective-permute-start | bytes 3145736 | tf_op jit(solution)/shard_map/ppermute | solution.py:281
  385.5 42.8 %collective-permute-start.15 = (bf16[256,2048]{1,0:T(8,128)(2,1)}, bf16[256,2048]{1,0:T(8,128)(2,1)}, u32[]{:S(2)}, u32[]{:S(2)}) collective-permute-start(bf16[256,2048]{1,0:T(8,128)(2,1)} %fusion.20), channel_id=1, source_target_pairs={{0,1},{1,0},{2,3},{3,2},{4,5},{5,4},{6,7},{7,6},{8,9},{9,8},{10,11... | collective-permute-start | bytes 3145736 | tf_op jit(solution)/shard_map/ppermute | solution.py:287
  412.4 64.2 %collective-permute-start.26 = (bf16[1024,2048]{1,0:T(8,128)(2,1)S(1)}, bf16[1024,2048]{1,0:T(8,128)(2,1)S(1)}, u32[]{:S(2)}, u32[]{:S(2)}) collective-permute-start(bf16[1024,2048]{1,0:T(8,128)(2,1)S(1)} %pad_maximum_fusion.1), channel_id=1, source_target_pairs={{0,2},{2,0},{1,3},{3,1},{4,6},{6,4},{5,7},{7,5},{8,10},{10,8},{9,1... | collective-permute-start | bytes 12582920 | tf_op jit(solution)/shard_map/ppermute | solution.py:284
  548.5 375.6 %reduce-scatter.9.cloned.1.call-start = ((), (), s32[]{:S(2)}) async-start(), calls=%async_computation.7 | async-start | bytes 10485760 | tf_op jit(solution)/shard_map/reduce_scatter | solution.py:499
  558.0 66.2 %collective-permute-start.32 = (bf16[1024,2048]{1,0:T(8,128)(2,1)}, bf16[1024,2048]{1,0:T(8,128)(2,1)}, u32[]{:S(2)}, u32[]{:S(2)}) collective-permute-start(bf16[1024,2048]{1,0:T(8,128)(2,1)} %convolution_convert_fusion.1), channel_id=1, source_target_pairs={{0,2},{2,0},{1,3},{3,1},{4,6},{6,4},{5,7},{7,5},{8,10},{10,8},{9,1... | collective-permute-start | bytes 12582920 | tf_op jit(solution)/shard_map/ppermute | solution.py:284
  592.8 421.2 %reduce-scatter.5.cloned.1.call-start = ((), (), s32[]{:S(2)}) async-start(), calls=%async_computation.5 | async-start | bytes 7077888 | tf_op jit(solution)/shard_map/reduce_scatter | solution.py:499
  642.9 40.7 %collective-permute-start.28 = (bf16[512,1024]{1,0:T(8,128)(2,1)S(1)}, bf16[512,1024]{1,0:T(8,128)(2,1)S(1)}, u32[]{:S(2)}, u32[]{:S(2)}) collective-permute-start(bf16[512,1024]{1,0:T(8,128)(2,1)S(1)} %pad_maximum_fusion.6), channel_id=1, source_target_pairs={{0,1},{1,0},{2,3},{3,2},{4,5},{5,4},{6,7},{7,6},{8,9},{9,8},{10,11... | collective-permute-start | bytes 3145736 | tf_op jit(solution)/shard_map/ppermute | solution.py:287
  644.1 48.6 %collective-permute-start.30 = (bf16[512,1024]{1,0:T(8,128)(2,1)S(1)}, bf16[512,1024]{1,0:T(8,128)(2,1)S(1)}, u32[]{:S(2)}, u32[]{:S(2)}) collective-permute-start(bf16[512,1024]{1,0:T(8,128)(2,1)S(1)} %concatenate.108), channel_id=1, source_target_pairs={{0,8},{4,12},{8,0},{12,4},{16,24},{20,28},{24,16},{28,20},{1,9},{5... | collective-permute-start | bytes 3145736 | tf_op jit(solution)/shard_map/ppermute | solution.py:281
  646.7 89.6 %collective-permute-start.35 = (bf16[512,1024]{1,0:T(8,128)(2,1)S(1)}, bf16[512,1024]{1,0:T(8,128)(2,1)S(1)}, u32[]{:S(2)}, u32[]{:S(2)}) collective-permute-start(bf16[512,1024]{1,0:T(8,128)(2,1)S(1)} %concatenate.109), channel_id=1, source_target_pairs={{0,8},{4,12},{8,0},{12,4},{16,24},{20,28},{24,16},{28,20},{1,9},{5... | collective-permute-start | bytes 3145736 | tf_op jit(solution)/shard_map/ppermute | solution.py:281
  662.9 88.4 %collective-permute-start.34 = (bf16[256,1024]{1,0:T(8,128)(2,1)S(1)}, bf16[256,1024]{1,0:T(8,128)(2,1)S(1)}, u32[]{:S(2)}, u32[]{:S(2)}) collective-permute-start(bf16[256,1024]{1,0:T(8,128)(2,1)S(1)} %fusion.33), channel_id=1, source_target_pairs={{0,8},{4,12},{8,0},{12,4},{16,24},{20,28},{24,16},{28,20},{1,9},{5... | collective-permute-start | bytes 1572872 | tf_op jit(solution)/shard_map/ppermute | solution.py:281
  693.4 78.4 %collective-permute-start.29 = (bf16[256,1024]{1,0:T(8,128)(2,1)S(1)}, bf16[256,1024]{1,0:T(8,128)(2,1)S(1)}, u32[]{:S(2)}, u32[]{:S(2)}) collective-permute-start(bf16[256,1024]{1,0:T(8,128)(2,1)S(1)} %get-tuple-element.62), channel_id=1, source_target_pairs={{0,8},{4,12},{8,0},{12,4},{16,24},{20,28},{24,16},{28,20},{1,9},{5... | collective-permute-start | bytes 1572872 | tf_op jit(solution)/shard_map/ppermute | solution.py:281
  694.7 77.2 %collective-permute-start.31 = (bf16[256,1024]{1,0:T(8,128)(2,1)S(1)}, bf16[256,1024]{1,0:T(8,128)(2,1)S(1)}, u32[]{:S(2)}, u32[]{:S(2)}) collective-permute-start(bf16[256,1024]{1,0:T(8,128)(2,1)S(1)} %get-tuple-element.63), channel_id=1, source_target_pairs={{0,1},{1,0},{2,3},{3,2},{4,5},{5,4},{6,7},{7,6},{8,9},{9,8},{10,11... | collective-permute-start | bytes 1572872 | tf_op jit(solution)/shard_map/ppermute | solution.py:287
  851.8 214.6 %reduce-scatter.7.cloned.1.call-start = ((), (), s32[]{:S(2)}) async-start(), calls=%async_computation.6 | async-start | bytes 2359296 | tf_op jit(solution)/shard_map/reduce_scatter | solution.py:499
  905.5 164.9 %collective-permute-start.37 = (bf16[256,2048]{1,0:T(8,128)(2,1)}, bf16[256,2048]{1,0:T(8,128)(2,1)}, u32[]{:S(2)}, u32[]{:S(2)}) collective-permute-start(bf16[256,2048]{1,0:T(8,128)(2,1)} %get-tuple-element.70.own_ref), channel_id=1, source_target_pairs={{0,1},{1,0},{2,3},{3,2},{4,5},{5,4},{6,7},{7,6},{8,9},{9,8},{10,11... | collective-permute-start | bytes 3145736 | tf_op jit(solution)/shard_map/ppermute | solution.py:287
  909.4 165.3 %collective-permute-start.52 = (bf16[128,2048]{1,0:T(8,128)(2,1)}, bf16[128,2048]{1,0:T(8,128)(2,1)}, u32[]{:S(2)}, u32[]{:S(2)}) collective-permute-start(bf16[128,2048]{1,0:T(8,128)(2,1)} %shard_map.218), channel_id=1, source_target_pairs={{0,2},{2,0},{1,3},{3,1},{4,6},{6,4},{5,7},{7,5},{8,10},{10,8},{9,1... | collective-permute-start | bytes 1572872 | tf_op jit(solution)/shard_map/ppermute | solution.py:284
  925.4 48.0 %collective-permute-start.49 = (bf16[256,2048]{1,0:T(8,128)(2,1)S(1)}, bf16[256,2048]{1,0:T(8,128)(2,1)S(1)}, u32[]{:S(2)}, u32[]{:S(2)}) collective-permute-start(bf16[256,2048]{1,0:T(8,128)(2,1)S(1)} %constant_dynamic-slice_fusion.1), channel_id=1, source_target_pairs={{0,8},{4,12},{8,0},{12,4},{16,24},{20,28},{24,16},{28,20},{1,9},{5... | collective-permute-start | bytes 3145736 | tf_op jit(solution)/shard_map/ppermute | solution.py:281
  926.1 47.3 %collective-permute-start.46 = (f32[2,256]{1,0:T(2,128)S(1)}, f32[2,256]{1,0:T(2,128)S(1)}, u32[]{:S(2)}, u32[]{:S(2)}) collective-permute-start(f32[2,256]{1,0:T(2,128)S(1)} %broadcast_select_fusion.2), channel_id=1, source_target_pairs={{0,8},{4,12},{8,0},{12,4},{16,24},{20,28},{24,16},{28,20},{1,9},{5... | collective-permute-start | bytes 6152 | tf_op jit(solution)/shard_map/ppermute | solution.py:281
  931.4 147.6 %collective-permute-start.42 = (bf16[256,2048]{1,0:T(8,128)(2,1)}, bf16[256,2048]{1,0:T(8,128)(2,1)S(1)}, u32[]{:S(2)}, u32[]{:S(2)}) collective-permute-start(bf16[256,2048]{1,0:T(8,128)(2,1)} %add_convert_fusion.1.own_ref), channel_id=1, source_target_pairs={{0,1},{1,0},{2,3},{3,2},{4,5},{5,4},{6,7},{7,6},{8,9},{9,8},{10,11... | collective-permute-start | bytes 3145736 | tf_op jit(solution)/shard_map/ppermute | solution.py:287
  977.9 105.7 %collective-permute-start.50 = (bf16[128,4096]{1,0:T(8,128)(2,1)}, bf16[128,4096]{1,0:T(8,128)(2,1)S(1)}, u32[]{:S(2)}, u32[]{:S(2)}) collective-permute-start(bf16[128,4096]{1,0:T(8,128)(2,1)} %shard_map.216), channel_id=1, source_target_pairs={{0,2},{2,0},{1,3},{3,1},{4,6},{6,4},{5,7},{7,5},{8,10},{10,8},{9,1... | collective-permute-start | bytes 3145736 | tf_op jit(solution)/shard_map/ppermute | solution.py:284
  977.9 100.4 %collective-permute-start.47 = (f32[2,128]{1,0:T(2,128)S(1)}, f32[2,128]{1,0:T(2,128)S(1)}, u32[]{:S(2)}, u32[]{:S(2)}) collective-permute-start(f32[2,128]{1,0:T(2,128)S(1)} %broadcast_select_fusion.3), channel_id=1, source_target_pairs={{0,2},{2,0},{1,3},{3,1},{4,6},{6,4},{5,7},{7,5},{8,10},{10,8},{9,1... | collective-permute-start | bytes 3080 | tf_op jit(solution)/shard_map/ppermute | solution.py:284
  (78 other events, 1737.8 us)
Sparse Core Ops, SparseCore 0:
  132.5 225.6 all-gather.1
  548.6 85.6 reduce-scatter.10
  637.4 153.5 reduce-scatter.8
  851.9 162.0 reduce-scatter.4
  1016.7 49.6 reduce-scatter.6

commit v4 on v3

--- a/solution.py
+++ b/solution.py
@@ -444,9 +444,9 @@
         both = cat([across(by_tp[:mid], 2), swap_tp(by_zl[mid:])])
         h_two = cat([near, both, far_near, swap_core(both)])
 
-        dy_rel = permute_cols(after(cotangent, *parts_qkv[half_s:]), rel, block)
+        dy_rel = permute_cols(cotangent, rel, block)
         dy_ff = cat([rows_of(dy_rel, half * part, part), rows_of(dy_rel, (1 - half) * part, part)])
-        dy_zl = across(dy_ff[:part], 2)
+        dy_zl = across(after(dy_ff[:part], weight_f), 2)
         near = cat([dy_ff, dy_zl, swap_tp(dy_zl)])
         grad_out = cat([near, swap_core(near)])
 
@@ -477,6 +477,11 @@
         grad_hidden = matmul(grad_out, weight_d)
         grad_gate = (grad_hidden * up_pre * gate_sig * (1.0 + gate_pre * (1.0 - gate_sig))).astype(bf16)
         grad_up = (grad_hidden * gate_act).astype(bf16)
+        prod_d = contract_rows(grad_out, hidden).astype(bf16)
+        prod_gu = cat(
+            [contract_rows(h_two, grad_gate).astype(bf16), contract_rows(h_two, grad_up).astype(bf16)], 1
+        )
+        grad_gate, grad_up = after((grad_gate, grad_up), prod_d, prod_gu)
         event_h, grad_h_two = from_tokens(
             lambda where: contract_cols(grad_gate[where], weight_g)
             + contract_cols(grad_up[where], weight_u)
@@ -536,13 +541,13 @@
         def send_unit(s_ref, own, out):
             out[...] = own[pl.ds((1 - s_ref[0]) * unit, unit), :].astype(bf16)
 
-        own_d = scatter(contract_rows(grad_out, hidden), groups)
-        own_gu = scatter(
-            cat([contract_rows(h_two, grad_gate).astype(bf16), contract_rows(h_two, grad_up).astype(bf16)], 1), groups
-        )
-        own_o = scatter(contract_rows(grad_attn, mixed), every)
+        own_d = scatter(prod_d, groups)
+        own_gu = scatter(prod_gu, groups)
+        late_o = contract_rows(grad_attn, mixed).astype(bf16)
+        own_o = scatter(after(late_o, own_d, own_gu), every)
+        grad_mixed = after(grad_mixed, late_o)
         grad_qkv = attend_backward(kept, grad_mixed, seg_row, cosine, sine, 0, heads)
-        own_qkv = scatter(contract_rows(h_one, grad_qkv), every)
+        own_qkv = scatter(after(contract_rows(h_one, grad_qkv).astype(bf16), own_o), every)
 
         (grad_w_down,) = rows_pair(own_d, 1)
         grad_w_gate, grad_w_up = rows_pair(own_gu, 2)

time: 1110 us -> 1110 us (level)
  starting transfers between devices: 55.5 us -> 84.2 us
    reduce_scatter x4, waiting for transfers between devices: 86.7 us -> 44.1 us  [scatter(): lax.psum_scatter(values.astype(bf16), 'shard', scatter_dimension=0, tiled...]
    ppermute x24, starting transfers between devices: 37.3 us -> 67.5 us  [across(): return lax.ppermute(values, 'shard', [(i, i ^ mask) for i in range(shards)])]
    ppermute x13, waiting for transfers between devices: 122 us -> 141 us  [swap_tp(): return lax.ppermute(values, 'tp', [(0, 1), (1, 0)])]
    ppermute x24, waiting for transfers between devices: 385 us -> 397 us  [across(): return lax.ppermute(values, 'shard', [(i, i ^ mask) for i in range(shards)])]
    unnamed x121 -> x123, local copies, waits for them, and re-layouts: 28.1 us -> 32 us
where the time goes in v4:
time: 1110 us
  waiting for transfers between devices  598 us (54%)
  matrix products  207 us (19%)
  Pallas kernels  95.1 us (9%)
  starting transfers between devices  84.2 us (8%)
  local copies, waits for them, and re-layouts  58.1 us (5%)
  other arithmetic  49.3 us (4%)
  between operations  15.2 us (1%)
    ppermute x24, waiting for transfers between devices, across(): return lax.ppermute(values, 'shard', [(i, i ^ mask) for i in range(shards)])  397 us
    ppermute x13, waiting for transfers between devices, swap_tp(): return lax.ppermute(values, 'tp', [(0, 1), (1, 0)])  141 us
    dot_general x12, matrix products, contract_cols(): lax.dot_general(left, right, (((1,), (1,)), ((), ())), preferred_element_...  81.1 us
    dot_general x5, matrix products, matmul(): return jnp.dot(left, right, preferred_element_type=jnp.float32)  69.2 us
    ppermute x24, starting transfers between devices, across(): return lax.ppermute(values, 'shard', [(i, i ^ mask) for i in range(shards)])  67.5 us
    dot_general x5, matrix products, contract_rows(): lax.dot_general(left, right, (((0,), (0,)), ((), ())), preferred_element_...  57.2 us
    reduce_scatter x4, waiting for transfers between devices, scatter(): lax.psum_scatter(values.astype(bf16), 'shard', scatter_dimension=0, tiled...  44.1 us
    pallas_call x11, Pallas kernels, small_call(): pl.pallas_call(body, grid_spec=pltpu.PrefetchScalarGridSpec(num_scalar_pr...  36.4 us
  transfers between devices with their start and end apart: 58, of which 28 were waited for; matrix products, arithmetic and copies ran while one was open for 23% of the time, Pallas kernels for 8%

profile of v4, /device:TPU:0, one launch (start us, length us, event | category | flops | bytes accessed | tf_op | source)
XLA Modules:
  0.0 1107.0 jit_solution(5886552441067165449)
XLA Ops:
  31.6 26.4 %collective-permute-done.23.other = bf16[256,3072]{1,0:T(8,128)(2,1)S(1)} collective-permute-done((bf16[256,3072]{1,0:T(8,128)(2,1)}, bf16[256,3072]{1,0:T(8,128)(2,1)S(1)}, u32[]{:S(2)}, u32[]{:S(2)}) %collective-permute-start.23) | collective-permute-done | bytes 1572896 | tf_op jit(solution)/shard_map/ppermute | solution.py:281
  78.5 30.2 %collective-permute-done.3 = bf16[272,1536]{1,0:T(8,128)(2,1)S(1)} collective-permute-done((bf16[272,1536]{1,0:T(8,128)(2,1)}, bf16[272,1536]{1,0:T(8,128)(2,1)S(1)}, u32[]{:S(2)}, u32[]{:S(2)}) %collective-permute-start.3) | collective-permute-done | bytes 835616 | tf_op jit(solution)/shard_map/ppermute | solution.py:281
  108.7 73.0 %collective-permute-done.4 = bf16[272,1536]{1,0:T(8,128)(2,1)S(1)} collective-permute-done((bf16[272,1536]{1,0:T(8,128)(2,1)}, bf16[272,1536]{1,0:T(8,128)(2,1)S(1)}, u32[]{:S(2)}, u32[]{:S(2)}) %collective-permute-start.4) | collective-permute-done | bytes 835616 | tf_op jit(solution)/shard_map/ppermute | solution.py:281
  181.7 34.1 %collective-permute-start.10 = (bf16[256,512]{1,0:T(8,128)(2,1)S(1)}, bf16[256,512]{1,0:T(8,128)(2,1)S(1)}, u32[]{:S(2)}, u32[]{:S(2)}) collective-permute-start(bf16[256,512]{1,0:T(8,128)(2,1)S(1)} %copy-done.23), channel_id=1, source_target_pairs={{0,8},{4,12},{8,0},{12,4},{16,24},{20,28},{24,16},{28,20},{1,9},{5... | collective-permute-start | bytes 786440 | tf_op jit(solution)/shard_map/ppermute | solution.py:281
  227.5 78.9 %collective-permute-done.11 = bf16[256,512]{1,0:T(8,128)(2,1)S(1)} collective-permute-done((bf16[256,512]{1,0:T(8,128)(2,1)S(1)}, bf16[256,512]{1,0:T(8,128)(2,1)S(1)}, u32[]{:S(2)}, u32[]{:S(2)}) %collective-permute-start.11) | collective-permute-done | bytes 262176 | tf_op jit(solution)/shard_map/ppermute | solution.py:281
  313.8 32.0 %collective-permute-done.9 = bf16[272,1536]{1,0:T(8,128)(2,1)S(1)} collective-permute-done((bf16[272,1536]{1,0:T(8,128)(2,1)S(1)}, bf16[272,1536]{1,0:T(8,128)(2,1)S(1)}, u32[]{:S(2)}, u32[]{:S(2)}) %collective-permute-start.9) | collective-permute-done | bytes 835616 | tf_op jit(solution)/shard_map/ppermute | solution.py:281
  354.3 14.4 %fusion.29.qkv_ref = f32[1024,1536]{1,0:T(8,128)} fusion(bf16[2048,1536]{1,0:T(8,128)(2,1)} %slice_dynamic-update-slice_fusion, f32[2048]{0:T(1024)S(1)} %bitcast.84, f32[1024]{0:T(1024)S(1)} %add_rsqrt_fusion, bf16[512,2048]{1,0:T(8,128)(2,1)S(1)} %copy-done.2, bf16[512,2048]{1,0:T(8,128)(2,1)} %collective-permute-done, pred[]{:T(512)S(6)} %eq.18), kind=kOutput, calls=%fused_computation.68 | convolution fusion | flops 6469713920 | bytes 16789504 | tf_op jit(solution)/shard_map/dot_general | solution.py:22
  368.8 14.6 %shard_map.206 = (bf16[1024,512]{1,0:T(8,128)(2,1)}, bf16[1024,1536]{1,0:T(8,128)(2,1)}) custom-call(s32[1024]{0:T(1024)} %bitcast.76, f32[1024,1536]{1,0:T(8,128)} %fusion.29.qkv_ref, f32[1024,128]{1,0:T(8,128)} %get-tuple-element.93.cos_ref, f32[1024,128]{1,0:T(8,128)} %get-tuple-element.94.sin_ref, s32[1024,1]{1,0:T(8,128)} %copy.25.seg_col, ...), custom_call_target="tpu_custom_call" | custom-call | tf_op jit(solution)/shard_map/pallas_call | solution.py:195
  399.4 23.8 %collective-permute-done.15 = bf16[256,2048]{1,0:T(8,128)(2,1)} collective-permute-done((bf16[256,2048]{1,0:T(8,128)(2,1)S(1)}, bf16[256,2048]{1,0:T(8,128)(2,1)}, u32[]{:S(2)}, u32[]{:S(2)}) %collective-permute-start.15) | collective-permute-done | bytes 1048608 | tf_op jit(solution)/shard_map/ppermute | solution.py:287
  429.6 22.8 %collective-permute-done.16 = bf16[256,2048]{1,0:T(8,128)(2,1)S(1)} collective-permute-done((bf16[256,2048]{1,0:T(8,128)(2,1)S(1)}, bf16[256,2048]{1,0:T(8,128)(2,1)S(1)}, u32[]{:S(2)}, u32[]{:S(2)}) %collective-permute-start.16) | collective-permute-done | bytes 1048608 | tf_op jit(solution)/shard_map/ppermute | solution.py:287
  470.2 30.7 %collective-permute-done.18 = bf16[128,2048]{1,0:T(8,128)(2,1)S(1)} collective-permute-done((bf16[128,2048]{1,0:T(8,128)(2,1)S(1)}, bf16[128,2048]{1,0:T(8,128)(2,1)S(1)}, u32[]{:S(2)}, u32[]{:S(2)}) %collective-permute-start.18) | collective-permute-done | bytes 524320 | tf_op jit(solution)/shard_map/ppermute | solution.py:281
  510.6 17.1 %collective-permute-done.25 = bf16[256,2048]{1,0:T(8,128)(2,1)S(1)} collective-permute-done((bf16[256,2048]{1,0:T(8,128)(2,1)S(1)}, bf16[256,2048]{1,0:T(8,128)(2,1)S(1)}, u32[]{:S(2)}, u32[]{:S(2)}) %collective-permute-start.25) | collective-permute-done | bytes 1048608 | tf_op jit(solution)/shard_map/ppermute | solution.py:287
  531.1 12.8 %fusion.15 = f32[2048,1024]{1,0:T(8,128)} fusion(bf16[2048,2048]{1,0:T(8,128)(2,1)S(1)} %copy-done.32, bf16[2048,3072]{1,0:T(8,128)(2,1)} %all-gather.2.cloned.1.call-done), kind=kOutput, calls=%fused_computation.35 | convolution fusion | flops 8589934592 | bytes 20971520 | tf_op jit(solution)/shard_map/dot_general | solution.py:22
  543.9 12.8 %fusion.10 = f32[2048,1024]{1,0:T(8,128)} fusion(bf16[2048,2048]{1,0:T(8,128)(2,1)S(1)} %copy-done.32, bf16[2048,3072]{1,0:T(8,128)(2,1)} %all-gather.2.cloned.1.call-done), kind=kOutput, calls=%fused_computation.30 | convolution fusion | flops 8589934592 | bytes 20971520 | tf_op jit(solution)/shard_map/dot_general | solution.py:22
  561.3 22.9 %multiply_convert_fusion = (bf16[2048,1024]{1,0:T(8,128)(2,1)}, bf16[2048,1024]{1,0:T(8,128)(2,1)}, bf16[2048,1024]{1,0:T(8,128)(2,1)S(1)}) fusion(f32[2048,1024]{1,0:T(8,128)} %fusion.15, f32[2048,1024]{1,0:T(8,128)} %fusion.10, bf16[2048,2048]{1,0:T(8,128)(2,1)} %constant_dynamic-update-slice_fusion.15, bf16[2048,3072]{1,0:T(8,128)(2,1)} %all-gather.2.cloned.1.call-done), kind=kOutput, calls=%fused_computation.8 | convolution fusion | flops 8621391872 | bytes 41943040 | tf_op jit(solution)/shard_map/dot_general | solution.py:22
  586.3 12.8 %convolution_convert_fusion.4 = bf16[2048,1024]{1,0:T(8,128)(2,1)} fusion(bf16[2048,2048]{1,0:T(8,128)(2,1)} %constant_dynamic-update-slice_fusion.15, bf16[2048,1024]{1,0:T(8,128)(2,1)S(1)} %get-tuple-element.42), kind=kOutput, calls=%fused_computation.21 | convolution fusion | flops 8592031744 | bytes 16777216 | tf_op jit(solution)/shard_map/dot_general | solution.py:26
  599.2 14.9 %convolution_convert_fusion.2 = bf16[2048,1024]{1,0:T(8,128)(2,1)} fusion(bf16[2048,2048]{1,0:T(8,128)(2,1)} %constant_dynamic-update-slice_fusion.8, bf16[2048,1024]{1,0:T(8,128)(2,1)} %get-tuple-element.41), kind=kOutput, calls=%fused_computation.19 | convolution fusion | flops 8592031744 | bytes 16777216 | tf_op jit(solution)/shard_map/dot_general | solution.py:26
  614.1 12.8 %convolution_convert_fusion.3 = bf16[2048,1024]{1,0:T(8,128)(2,1)} fusion(bf16[2048,2048]{1,0:T(8,128)(2,1)} %constant_dynamic-update-slice_fusion.8, bf16[2048,1024]{1,0:T(8,128)(2,1)S(1)} %copy-done.52), kind=kOutput, calls=%fused_computation.20 | convolution fusion | flops 8592031744 | bytes 16777216 | tf_op jit(solution)/shard_map/dot_general | solution.py:26
  635.5 9.5 convolution_convert_fusion.1
  676.1 10.7 fusion.70
  700.5 13.8 %collective-permute-done.33 = bf16[512,1024]{1,0:T(8,128)(2,1)S(1)} collective-permute-done((bf16[512,1024]{1,0:T(8,128)(2,1)}, bf16[512,1024]{1,0:T(8,128)(2,1)S(1)}, u32[]{:S(2)}, u32[]{:S(2)}) %collective-permute-start.33) | collective-permute-done | bytes 1048608 | tf_op jit(solution)/shard_map/ppermute | solution.py:287
  716.0 19.8 %collective-permute-done.28 = bf16[512,1024]{1,0:T(8,128)(2,1)S(1)} collective-permute-done((bf16[512,1024]{1,0:T(8,128)(2,1)S(1)}, bf16[512,1024]{1,0:T(8,128)(2,1)S(1)}, u32[]{:S(2)}, u32[]{:S(2)}) %collective-permute-start.28) | collective-permute-done | bytes 1048608 | tf_op jit(solution)/shard_map/ppermute | solution.py:287
  736.0 9.6 collective-permute-done.30
  747.6 39.4 %collective-permute-done.35 = bf16[512,1024]{1,0:T(8,128)(2,1)S(1)} collective-permute-done((bf16[512,1024]{1,0:T(8,128)(2,1)S(1)}, bf16[512,1024]{1,0:T(8,128)(2,1)S(1)}, u32[]{:S(2)}, u32[]{:S(2)}) %collective-permute-start.35) | collective-permute-done | bytes 1048608 | tf_op jit(solution)/shard_map/ppermute | solution.py:281
  787.3 16.8 %collective-permute-done.34 = bf16[256,1024]{1,0:T(8,128)(2,1)S(1)} collective-permute-done((bf16[256,1024]{1,0:T(8,128)(2,1)S(1)}, bf16[256,1024]{1,0:T(8,128)(2,1)S(1)}, u32[]{:S(2)}, u32[]{:S(2)}) %collective-permute-start.34) | collective-permute-done | bytes 524320 | tf_op jit(solution)/shard_map/ppermute | solution.py:281
  807.3 13.0 %collective-permute-done.29 = bf16[256,1024]{1,0:T(8,128)(2,1)S(1)} collective-permute-done((bf16[256,1024]{1,0:T(8,128)(2,1)S(1)}, bf16[256,1024]{1,0:T(8,128)(2,1)S(1)}, u32[]{:S(2)}, u32[]{:S(2)}) %collective-permute-start.29) | collective-permute-done | bytes 524320 | tf_op jit(solution)/shard_map/ppermute | solution.py:281
  826.8 23.4 %collective-permute-done.38 = bf16[256,2048]{1,0:T(8,128)(2,1)} collective-permute-done((bf16[256,2048]{1,0:T(8,128)(2,1)S(1)}, bf16[256,2048]{1,0:T(8,128)(2,1)}, u32[]{:S(2)}, u32[]{:S(2)}) %collective-permute-start.38) | collective-permute-done | bytes 1048608 | tf_op jit(solution)/shard_map/ppermute | solution.py:287
  869.4 27.2 %shard_map.212 = bf16[1024,1536]{1,0:T(8,128)(2,1)} custom-call(s32[1024]{0:T(1024)} %bitcast.77, bf16[1024,1536]{1,0:T(8,128)(2,1)} %get-tuple-element.43.kept_ref, bf16[1024,512]{1,0:T(8,128)(2,1)} %convolution_convert_fusion.8.do_ref, f32[1024,128]{1,0:T(8,128)} %get-tuple-element.93.cos_ref, f32[1024,128]{1,0:T(8,128)} %get-tuple-element.94.sin_ref, ...), custom_call_target="tpu_custom_call" | custom-call | tf_op jit(solution)/shard_map/pallas_call | solution.py:254
  896.6 11.8 %convolution_convert_fusion = bf16[2048,1536]{1,0:T(8,128)(2,1)} fusion(bf16[1024,1536]{1,0:T(8,128)(2,1)} %shard_map.212, f32[2048]{0:T(1024)S(1)} %bitcast.85, f32[1024]{0:T(1024)S(1)} %copy-done.38, bf16[512,2048]{1,0:T(8,128)(2,1)S(1)} %copy-done.3, bf16[512,2048]{1,0:T(8,128)(2,1)} %collective-permute-done, pred[]{:T(512)S(6)} %eq.18), kind=kOutput, calls=%fused_computation.14 | convolution fusion | flops 6472859648 | bytes 13643777 | tf_op jit(solution)/shard_map/dot_general | solution.py:26
  934.1 20.2 %collective-permute-done.41 = bf16[256,2048]{1,0:T(8,128)(2,1)} collective-permute-done((bf16[256,2048]{1,0:T(8,128)(2,1)}, bf16[256,2048]{1,0:T(8,128)(2,1)}, u32[]{:S(2)}, u32[]{:S(2)}) %collective-permute-start.41) | collective-permute-done | bytes 1048608 | tf_op jit(solution)/shard_map/ppermute | solution.py:287
  987.3 40.1 %collective-permute-done.46 = f32[2,256]{1,0:T(2,128)S(1)} collective-permute-done((f32[2,256]{1,0:T(2,128)S(1)}, f32[2,256]{1,0:T(2,128)S(1)}, u32[]{:S(2)}, u32[]{:S(2)}) %collective-permute-start.46) | collective-permute-done | bytes 2080 | tf_op jit(solution)/shard_map/ppermute | solution.py:281
  1032.5 41.4 %reduce-scatter.11.cloned.1.call-done = bf16[256,1536]{1,0:T(8,128)(2,1)} async-done(((bf16[2048,1536]{1,0:T(8,128)(2,1)}), bf16[256,1536]{1,0:T(8,128)(2,1)}) %reduce-scatter.11.cloned.1.call-update) | async-done | bytes 786448 | tf_op jit(solution)/shard_map/reduce_scatter | solution.py:504
  (341 shorter events, 308.1 us)
Async XLA Ops:
  7.2 456.9 %all-gather.2.cloned.1.call-start = ((), (), s32[]{:S(2)}) async-start(), calls=%async_computation.4 | async-start | bytes 15728640 | tf_op jit(solution)/shard_map/all_gather | solution.py:410
  25.1 42.2 %collective-permute-start.1 = (bf16[128,2048]{1,0:T(8,128)(2,1)}, bf16[128,2048]{1,0:T(8,128)(2,1)S(1)}, u32[]{:S(2)}, u32[]{:S(2)}) collective-permute-start(bf16[128,2048]{1,0:T(8,128)(2,1)} %shard_map.204), channel_id=1, source_target_pairs={{0,2},{2,0},{1,3},{3,1},{4,6},{6,4},{5,7},{7,5},{8,10},{10,8},{9,1... | collective-permute-start | bytes 1572872 | tf_op jit(solution)/shard_map/ppermute | solution.py:284
  25.2 42.1 %collective-permute-start.2 = (bf16[2,128]{1,0:T(2,128)(2,1)S(1)}, bf16[2,128]{1,0:T(2,128)(2,1)S(1)}, u32[]{:S(2)}, u32[]{:S(2)}) collective-permute-start(bf16[2,128]{1,0:T(2,128)(2,1)S(1)} %pad_maximum_fusion.11.own_g), channel_id=1, source_target_pairs={{0,2},{2,0},{1,3},{3,1},{4,6},{6,4},{5,7},{7,5},{8,10},{10,8},{9,1... | collective-permute-start | bytes 1544 | tf_op jit(solution)/shard_map/ppermute | solution.py:284
  30.8 279.6 %collective-permute-start = (bf16[512,2048]{1,0:T(8,128)(2,1)}, bf16[512,2048]{1,0:T(8,128)(2,1)}, u32[]{:S(2)}, u32[]{:S(2)}) collective-permute-start(bf16[512,2048]{1,0:T(8,128)(2,1)} %shard_map.203), channel_id=1, source_target_pairs={{0,2},{2,0},{1,3},{3,1},{4,6},{6,4},{5,7},{7,5},{8,10},{10,8},{9,1... | collective-permute-start | bytes 6291464 | tf_op jit(solution)/shard_map/ppermute | solution.py:284
  62.9 800.0 %reduce-scatter.5.cloned.1.call-start = ((), (), s32[]{:S(2)}) async-start(), calls=%async_computation.5 | async-start | bytes 5242880 | tf_op jit(solution)/shard_map/reduce_scatter | solution.py:504
  72.9 108.8 %collective-permute-start.4 = (bf16[272,1536]{1,0:T(8,128)(2,1)}, bf16[272,1536]{1,0:T(8,128)(2,1)S(1)}, u32[]{:S(2)}, u32[]{:S(2)}) collective-permute-start(bf16[272,1536]{1,0:T(8,128)(2,1)} %get-tuple-element.32), channel_id=1, source_target_pairs={{0,16},{4,20},{8,24},{12,28},{16,0},{20,4},{24,8},{28,12},{1,17},{... | collective-permute-start | bytes 2506760 | tf_op jit(solution)/shard_map/ppermute | solution.py:281
  75.5 106.2 %collective-permute-start.5 = (bf16[272,1536]{1,0:T(8,128)(2,1)}, bf16[272,1536]{1,0:T(8,128)(2,1)S(1)}, u32[]{:S(2)}, u32[]{:S(2)}) collective-permute-start(bf16[272,1536]{1,0:T(8,128)(2,1)} %get-tuple-element.32), channel_id=1, source_target_pairs={{0,24},{4,28},{8,16},{12,20},{16,8},{20,12},{24,0},{28,4},{1,25},{... | collective-permute-start | bytes 2506760 | tf_op jit(solution)/shard_map/ppermute | solution.py:281
  75.6 142.8 %collective-permute-start.6 = (bf16[272,1536]{1,0:T(8,128)(2,1)}, bf16[272,1536]{1,0:T(8,128)(2,1)S(1)}, u32[]{:S(2)}, u32[]{:S(2)}) collective-permute-start(bf16[272,1536]{1,0:T(8,128)(2,1)} %get-tuple-element.32), channel_id=1, source_target_pairs={{0,4},{4,0},{8,12},{12,8},{16,20},{20,16},{24,28},{28,24},{1,5},{5... | collective-permute-start | bytes 2506760 | tf_op jit(solution)/shard_map/ppermute | solution.py:281
  181.7 43.8 %collective-permute-start.10 = (bf16[256,512]{1,0:T(8,128)(2,1)S(1)}, bf16[256,512]{1,0:T(8,128)(2,1)S(1)}, u32[]{:S(2)}, u32[]{:S(2)}) collective-permute-start(bf16[256,512]{1,0:T(8,128)(2,1)S(1)} %copy-done.23), channel_id=1, source_target_pairs={{0,8},{4,12},{8,0},{12,4},{16,24},{20,28},{24,16},{28,20},{1,9},{5... | collective-permute-start | bytes 786440 | tf_op jit(solution)/shard_map/ppermute | solution.py:281
  215.8 90.6 %collective-permute-start.11 = (bf16[256,512]{1,0:T(8,128)(2,1)S(1)}, bf16[256,512]{1,0:T(8,128)(2,1)S(1)}, u32[]{:S(2)}, u32[]{:S(2)}) collective-permute-start(bf16[256,512]{1,0:T(8,128)(2,1)S(1)} %copy-done.23), channel_id=1, source_target_pairs={{0,16},{4,20},{8,24},{12,28},{16,0},{20,4},{24,8},{28,12},{1,17},{... | collective-permute-start | bytes 786440 | tf_op jit(solution)/shard_map/ppermute | solution.py:281
  216.3 92.4 %collective-permute-start.12 = (bf16[256,512]{1,0:T(8,128)(2,1)S(1)}, bf16[256,512]{1,0:T(8,128)(2,1)S(1)}, u32[]{:S(2)}, u32[]{:S(2)}) collective-permute-start(bf16[256,512]{1,0:T(8,128)(2,1)S(1)} %copy-done.23), channel_id=1, source_target_pairs={{0,24},{4,28},{8,16},{12,20},{16,8},{20,12},{24,0},{28,4},{1,25},{... | collective-permute-start | bytes 786440 | tf_op jit(solution)/shard_map/ppermute | solution.py:281
  218.4 95.4 %collective-permute-start.7 = (bf16[272,1536]{1,0:T(8,128)(2,1)S(1)}, bf16[272,1536]{1,0:T(8,128)(2,1)S(1)}, u32[]{:S(2)}, u32[]{:S(2)}) collective-permute-start(bf16[272,1536]{1,0:T(8,128)(2,1)S(1)} %collective-permute-done.3), channel_id=1, source_target_pairs={{0,4},{4,0},{8,12},{12,8},{16,20},{20,16},{24,28},{28,24},{1,5},{5... | collective-permute-start | bytes 2506760 | tf_op jit(solution)/shard_map/ppermute | solution.py:281
  225.5 88.3 %collective-permute-start.8 = (bf16[272,1536]{1,0:T(8,128)(2,1)S(1)}, bf16[272,1536]{1,0:T(8,128)(2,1)S(1)}, u32[]{:S(2)}, u32[]{:S(2)}) collective-permute-start(bf16[272,1536]{1,0:T(8,128)(2,1)S(1)} %collective-permute-done.4), channel_id=1, source_target_pairs={{0,4},{4,0},{8,12},{12,8},{16,20},{20,16},{24,28},{28,24},{1,5},{5... | collective-permute-start | bytes 2506760 | tf_op jit(solution)/shard_map/ppermute | solution.py:281
  306.4 39.5 %collective-permute-start.9 = (bf16[272,1536]{1,0:T(8,128)(2,1)S(1)}, bf16[272,1536]{1,0:T(8,128)(2,1)S(1)}, u32[]{:S(2)}, u32[]{:S(2)}) collective-permute-start(bf16[272,1536]{1,0:T(8,128)(2,1)S(1)} %collective-permute-done.5), channel_id=1, source_target_pairs={{0,4},{4,0},{8,12},{12,8},{16,20},{20,16},{24,28},{28,24},{1,5},{5... | collective-permute-start | bytes 2506760 | tf_op jit(solution)/shard_map/ppermute | solution.py:281
  456.5 49.0 %collective-permute-start.20 = (bf16[768,2048]{1,0:T(8,128)(2,1)}, bf16[768,2048]{1,0:T(8,128)(2,1)}, u32[]{:S(2)}, u32[]{:S(2)}) collective-permute-start(bf16[768,2048]{1,0:T(8,128)(2,1)} %pad_maximum_fusion.2), channel_id=1, source_target_pairs={{0,2},{2,0},{1,3},{3,1},{4,6},{6,4},{5,7},{7,5},{8,10},{10,8},{9,1... | collective-permute-start | bytes 9437192 | tf_op jit(solution)/shard_map/ppermute | solution.py:284
  464.1 38.1 %collective-permute-start.24 = (bf16[256,2048]{1,0:T(8,128)(2,1)S(1)}, bf16[256,2048]{1,0:T(8,128)(2,1)S(1)}, u32[]{:S(2)}, u32[]{:S(2)}) collective-permute-start(bf16[256,2048]{1,0:T(8,128)(2,1)S(1)} %get-tuple-element.39), channel_id=1, source_target_pairs={{0,8},{4,12},{8,0},{12,4},{16,24},{20,28},{24,16},{28,20},{1,9},{5... | collective-permute-start | bytes 3145736 | tf_op jit(solution)/shard_map/ppermute | solution.py:281
  599.1 263.8 %reduce-scatter.7.cloned.1.call-start = ((), (), s32[]{:S(2)}) async-start(), calls=%async_computation.6 | async-start | bytes 10485760 | tf_op jit(solution)/shard_map/reduce_scatter | solution.py:504
  635.4 275.8 %reduce-scatter.9.cloned.1.call-start = ((), (), s32[]{:S(2)}) async-start(), calls=%async_computation.7 | async-start | bytes 2359296 | tf_op jit(solution)/shard_map/reduce_scatter | solution.py:504
  695.9 39.8 %collective-permute-start.28 = (bf16[512,1024]{1,0:T(8,128)(2,1)S(1)}, bf16[512,1024]{1,0:T(8,128)(2,1)S(1)}, u32[]{:S(2)}, u32[]{:S(2)}) collective-permute-start(bf16[512,1024]{1,0:T(8,128)(2,1)S(1)} %pad_maximum_fusion.6), channel_id=1, source_target_pairs={{0,1},{1,0},{2,3},{3,2},{4,5},{5,4},{6,7},{7,6},{8,9},{9,8},{10,11... | collective-permute-start | bytes 3145736 | tf_op jit(solution)/shard_map/ppermute | solution.py:287
  697.1 48.6 %collective-permute-start.30 = (bf16[512,1024]{1,0:T(8,128)(2,1)S(1)}, bf16[512,1024]{1,0:T(8,128)(2,1)S(1)}, u32[]{:S(2)}, u32[]{:S(2)}) collective-permute-start(bf16[512,1024]{1,0:T(8,128)(2,1)S(1)} %concatenate.108), channel_id=1, source_target_pairs={{0,8},{4,12},{8,0},{12,4},{16,24},{20,28},{24,16},{28,20},{1,9},{5... | collective-permute-start | bytes 3145736 | tf_op jit(solution)/shard_map/ppermute | solution.py:281
  698.4 88.6 %collective-permute-start.35 = (bf16[512,1024]{1,0:T(8,128)(2,1)S(1)}, bf16[512,1024]{1,0:T(8,128)(2,1)S(1)}, u32[]{:S(2)}, u32[]{:S(2)}) collective-permute-start(bf16[512,1024]{1,0:T(8,128)(2,1)S(1)} %concatenate.109), channel_id=1, source_target_pairs={{0,8},{4,12},{8,0},{12,4},{16,24},{20,28},{24,16},{28,20},{1,9},{5... | collective-permute-start | bytes 3145736 | tf_op jit(solution)/shard_map/ppermute | solution.py:281
  715.9 88.2 %collective-permute-start.34 = (bf16[256,1024]{1,0:T(8,128)(2,1)S(1)}, bf16[256,1024]{1,0:T(8,128)(2,1)S(1)}, u32[]{:S(2)}, u32[]{:S(2)}) collective-permute-start(bf16[256,1024]{1,0:T(8,128)(2,1)S(1)} %fusion.33), channel_id=1, source_target_pairs={{0,8},{4,12},{8,0},{12,4},{16,24},{20,28},{24,16},{28,20},{1,9},{5... | collective-permute-start | bytes 1572872 | tf_op jit(solution)/shard_map/ppermute | solution.py:281
  746.4 73.9 %collective-permute-start.29 = (bf16[256,1024]{1,0:T(8,128)(2,1)S(1)}, bf16[256,1024]{1,0:T(8,128)(2,1)S(1)}, u32[]{:S(2)}, u32[]{:S(2)}) collective-permute-start(bf16[256,1024]{1,0:T(8,128)(2,1)S(1)} %get-tuple-element.72), channel_id=1, source_target_pairs={{0,8},{4,12},{8,0},{12,4},{16,24},{20,28},{24,16},{28,20},{1,9},{5... | collective-permute-start | bytes 1572872 | tf_op jit(solution)/shard_map/ppermute | solution.py:281
  746.4 73.9 %collective-permute-start.31 = (bf16[256,1024]{1,0:T(8,128)(2,1)S(1)}, bf16[256,1024]{1,0:T(8,128)(2,1)S(1)}, u32[]{:S(2)}, u32[]{:S(2)}) collective-permute-start(bf16[256,1024]{1,0:T(8,128)(2,1)S(1)} %get-tuple-element.73), channel_id=1, source_target_pairs={{0,1},{1,0},{2,3},{3,2},{4,5},{5,4},{6,7},{7,6},{8,9},{9,8},{10,11... | collective-permute-start | bytes 1572872 | tf_op jit(solution)/shard_map/ppermute | solution.py:287
  863.0 210.9 %reduce-scatter.11.cloned.1.call-start = ((), (), s32[]{:S(2)}) async-start(), calls=%async_computation.8 | async-start | bytes 7077888 | tf_op jit(solution)/shard_map/reduce_scatter | solution.py:504
  962.7 115.5 %collective-permute-start.37 = (bf16[256,2048]{1,0:T(8,128)(2,1)}, bf16[256,2048]{1,0:T(8,128)(2,1)}, u32[]{:S(2)}, u32[]{:S(2)}) collective-permute-start(bf16[256,2048]{1,0:T(8,128)(2,1)} %get-tuple-element.80.own_ref), channel_id=1, source_target_pairs={{0,1},{1,0},{2,3},{3,2},{4,5},{5,4},{6,7},{7,6},{8,9},{9,8},{10,11... | collective-permute-start | bytes 3145736 | tf_op jit(solution)/shard_map/ppermute | solution.py:287
  966.9 115.6 %collective-permute-start.52 = (bf16[128,2048]{1,0:T(8,128)(2,1)}, bf16[128,2048]{1,0:T(8,128)(2,1)}, u32[]{:S(2)}, u32[]{:S(2)}) collective-permute-start(bf16[128,2048]{1,0:T(8,128)(2,1)} %shard_map.218), channel_id=1, source_target_pairs={{0,2},{2,0},{1,3},{3,1},{4,6},{6,4},{5,7},{7,5},{8,10},{10,8},{9,1... | collective-permute-start | bytes 1572872 | tf_op jit(solution)/shard_map/ppermute | solution.py:284
  979.3 48.1 %collective-permute-start.49 = (bf16[256,2048]{1,0:T(8,128)(2,1)S(1)}, bf16[256,2048]{1,0:T(8,128)(2,1)S(1)}, u32[]{:S(2)}, u32[]{:S(2)}) collective-permute-start(bf16[256,2048]{1,0:T(8,128)(2,1)S(1)} %constant_dynamic-slice_fusion.1), channel_id=1, source_target_pairs={{0,8},{4,12},{8,0},{12,4},{16,24},{20,28},{24,16},{28,20},{1,9},{5... | collective-permute-start | bytes 3145736 | tf_op jit(solution)/shard_map/ppermute | solution.py:281
  981.2 46.2 %collective-permute-start.46 = (f32[2,256]{1,0:T(2,128)S(1)}, f32[2,256]{1,0:T(2,128)S(1)}, u32[]{:S(2)}, u32[]{:S(2)}) collective-permute-start(f32[2,256]{1,0:T(2,128)S(1)} %broadcast_select_fusion.2), channel_id=1, source_target_pairs={{0,8},{4,12},{8,0},{12,4},{16,24},{20,28},{24,16},{28,20},{1,9},{5... | collective-permute-start | bytes 6152 | tf_op jit(solution)/shard_map/ppermute | solution.py:281
  986.0 100.7 %collective-permute-start.42 = (bf16[256,2048]{1,0:T(8,128)(2,1)S(1)}, bf16[256,2048]{1,0:T(8,128)(2,1)}, u32[]{:S(2)}, u32[]{:S(2)}) collective-permute-start(bf16[256,2048]{1,0:T(8,128)(2,1)S(1)} %add_convert_fusion.1.own_ref), channel_id=1, source_target_pairs={{0,1},{1,0},{2,3},{3,2},{4,5},{5,4},{6,7},{7,6},{8,9},{9,8},{10,11... | collective-permute-start | bytes 3145736 | tf_op jit(solution)/shard_map/ppermute | solution.py:287
  1031.9 58.4 %collective-permute-start.50 = (bf16[128,4096]{1,0:T(8,128)(2,1)}, bf16[128,4096]{1,0:T(8,128)(2,1)S(1)}, u32[]{:S(2)}, u32[]{:S(2)}) collective-permute-start(bf16[128,4096]{1,0:T(8,128)(2,1)} %shard_map.216), channel_id=1, source_target_pairs={{0,2},{2,0},{1,3},{3,1},{4,6},{6,4},{5,7},{7,5},{8,10},{10,8},{9,1... | collective-permute-start | bytes 3145736 | tf_op jit(solution)/shard_map/ppermute | solution.py:284
  1031.9 54.2 %collective-permute-start.47 = (f32[2,128]{1,0:T(2,128)S(1)}, f32[2,128]{1,0:T(2,128)S(1)}, u32[]{:S(2)}, u32[]{:S(2)}) collective-permute-start(f32[2,128]{1,0:T(2,128)S(1)} %broadcast_select_fusion.3), channel_id=1, source_target_pairs={{0,2},{2,0},{1,3},{3,1},{4,6},{6,4},{5,7},{7,5},{8,10},{10,8},{9,1... | collective-permute-start | bytes 3080 | tf_op jit(solution)/shard_map/ppermute | solution.py:284
  (79 other events, 1941.3 us)
Sparse Core Ops, SparseCore 0:
  63.0 309.3 all-gather.1
  599.2 83.7 reduce-scatter.4
  686.1 153.7 reduce-scatter.6
  863.1 48.0 reduce-scatter.8
  913.3 160.4 reduce-scatter.10

commit v5 on v4

--- a/solution.py
+++ b/solution.py
@@ -349,36 +349,30 @@
             first, second = own_g[...], other_g[...]
             low = jnp.where(me == 0, first, second)
             high = jnp.where(me == 0, second, first)
-            line_g = cat([low, high, jnp.zeros((2, 3 * n_attn - block), bf16)], 1)
-            out_qkv[block:, :] = cat([line_g, jnp.zeros((pad - 2, 3 * n_attn), bf16)])
+            line_g = cat([low, high, jnp.zeros((2, n_attn - block), bf16)], 1)
+            out_o[block:, :] = cat([line_g, jnp.zeros((pad - 2, n_attn), bf16)])
 
         block_qkv, block_o = small_call(
             keep_attn, [core], attn_w + [other_a, gains, other_gains],
-            [array_of(block + pad, 3 * n_attn), array_of(block, n_attn)],
+            [array_of(block, 3 * n_attn), array_of(block + pad, n_attn)],
         )
 
         def shard_at(i):
             return shard ^ (((i % half_s) << 1) | (i // half_s))
 
-        def place_line(parts, take):
-            full = jnp.zeros((width, parts[0].shape[1]), bf16)
-            for i, v in enumerate(parts):
-                full = lax.dynamic_update_slice_in_dim(full, take(v), place_of(shard_at(i)) * block, 0)
-            return full
-
-        near_qkv = [block_qkv] + [across(block_qkv, mask) for mask in line]
-        parts_qkv = near_qkv + [across(v, 1) for v in near_qkv]
-        weight_qkv = place_line(parts_qkv, lambda v: v[:block])
-        gain_rows = jnp.stack([v[block : block + 2, :block] for v in parts_qkv])
+        weight_qkv = lax.all_gather(block_qkv, "shard", axis=0, tiled=True, axis_index_groups=every)
+        near_o = cat([block_o] + [across(block_o, mask) for mask in line])
+        parts_o = cat([near_o, across(near_o, 1)]).reshape(shards, block + pad, n_attn)
+        weight_o = jnp.zeros((width, n_attn), bf16)
+        for i in range(shards):
+            weight_o = lax.dynamic_update_slice_in_dim(
+                weight_o, parts_o[i, :block], place_of(shard_at(i)) * block, 0
+            )
+        gain_rows = parts_o[:, block : block + 2, :block]
         away_bits = place_of(jnp.arange(shards, dtype=jnp.int32)) ^ shard
         gain_rows = gain_rows[(away_bits >> 1) + half_s * (away_bits & 1)]
         gains_rel = jnp.transpose(gain_rows, (1, 0, 2)).reshape(2, width).astype(f32)
         gain_a, gain_m = gains_rel[0:1], gains_rel[1:2]
-
-        block_o = after(block_o, *near_qkv[1:])
-        near_o = cat([block_o] + [across(block_o, mask) for mask in line])
-        parts_o = cat([near_o, across(after(near_o, *parts_qkv[half_s:]), 1)])
-        weight_o = place_line([parts_o[i * block : (i + 1) * block] for i in range(shards)], lambda v: v)
 
         def send_ff(s_ref, g, u, d, out):
             start = pl.multiple_of((1 - s_ref[0]) * 2 * n_ff, n_ff)
@@ -407,8 +401,6 @@
             out[pl.ds(pl.multiple_of((1 - low) * block, block), block), :] = other[...]
 
         (pair_f,) = small_call(pair_rows, [zl], [keep_f, recv_f], [array_of(2 * block, 3 * n_ff)])
-        weight_f = lax.all_gather(pair_f, "shard", axis=0, tiled=True, axis_index_groups=groups)
-        weight_g, weight_u, weight_d = [weight_f[:, i * n_ff : (i + 1) * n_ff] for i in range(3)]
 
         seg_row = segments[0]
         cosine, sine = rope_tables(doc_positions(seg_row))
@@ -416,6 +408,9 @@
         x_both = ordered(core, x_own, swap_core(x_own))
         normed_all, inverse_all = norm_parts(x_both.astype(f32))
         h_one = (normed_all * gain_a).astype(bf16)
+        pair_f = after(pair_f, weight_qkv, weight_o, h_one, cosine, sine)
+        weight_f = lax.all_gather(pair_f, "shard", axis=0, tiled=True, axis_index_groups=groups)
+        weight_g, weight_u, weight_d = [weight_f[:, i * n_ff : (i + 1) * n_ff] for i in range(3)]
         qkv = matmul(h_one, weight_qkv)
         mixed, kept = attend_forward(qkv, seg_row, cosine, sine)
 
@@ -446,7 +441,7 @@
 
         dy_rel = permute_cols(cotangent, rel, block)
         dy_ff = cat([rows_of(dy_rel, half * part, part), rows_of(dy_rel, (1 - half) * part, part)])
-        dy_zl = across(after(dy_ff[:part], weight_f), 2)
+        dy_zl = across(after(dy_ff[:part], both), 2)
         near = cat([dy_ff, dy_zl, swap_tp(dy_zl)])
         grad_out = cat([near, swap_core(near)])
 

time: 1110 us -> 1020 us (0.919)
  starting transfers between devices: 84.2 us -> 38.7 us
  waiting for transfers between devices: 598 us -> 555 us
    ppermute x24 -> x17, waiting for transfers between devices: 397 us -> 292 us  [across(): return lax.ppermute(values, 'shard', [(i, i ^ mask) for i in range(shards)])]
    ppermute x24 -> x17, starting transfers between devices: 67.5 us -> 18 us  [across(): return lax.ppermute(values, 'shard', [(i, i ^ mask) for i in range(shards)])]
    all_gather x0 -> x1, waiting for transfers between devices: none -> 40.5 us  [per_device(): lax.all_gather(block_qkv, 'shard', axis=0, tiled=True, axis_index_groups=...]
    unnamed x123 -> x95, local copies, waits for them, and re-layouts: 32 us -> 26.9 us
  transfers between devices with their start and end apart: 58 -> 52, of which waited for: 28 -> 32; matrix products, arithmetic and copies ran while one was open for 23% -> 23% of each run, Pallas kernels for 8% -> 9%
where the time goes in v5:
time: 1020 us; the launch traced here: 1010 us
  waiting for transfers between devices  555 us (54%)
  matrix products  215 us (21%)
  Pallas kernels  94.7 us (9%)
  local copies, waits for them, and re-layouts  52.9 us (5%)
  other arithmetic  42.1 us (4%)
  starting transfers between devices  38.7 us (4%)
  between operations  15.2 us (1%)
    ppermute x17, waiting for transfers between devices, across(): return lax.ppermute(values, 'shard', [(i, i ^ mask) for i in range(shards)])  292 us
    ppermute x13, waiting for transfers between devices, swap_tp(): return lax.ppermute(values, 'tp', [(0, 1), (1, 0)])  148 us
    dot_general x12, matrix products, contract_cols(): lax.dot_general(left, right, (((1,), (1,)), ((), ())), preferred_element_...  89.7 us
    dot_general x5, matrix products, matmul(): return jnp.dot(left, right, preferred_element_type=jnp.float32)  68.8 us
    dot_general x5, matrix products, contract_rows(): lax.dot_general(left, right, (((0,), (0,)), ((), ())), preferred_element_...  56.3 us
    reduce_scatter x4, waiting for transfers between devices, scatter(): lax.psum_scatter(values.astype(bf16), 'shard', scatter_dimension=0, tiled...  49.4 us
    all_gather x1, waiting for transfers between devices, per_device(): lax.all_gather(block_qkv, 'shard', axis=0, tiled=True, axis_index_groups=...  40.5 us
    pallas_call x11, Pallas kernels, small_call(): pl.pallas_call(body, grid_spec=pltpu.PrefetchScalarGridSpec(num_scalar_pr...  36.4 us
  transfers between devices with their start and end apart: 52, of which 32 were waited for; matrix products, arithmetic and copies ran while one was open for 23% of the time, Pallas kernels for 9%

profile of v5, /device:TPU:0, one launch (start us, length us, event | category | flops | bytes accessed | tf_op | source)
XLA Modules:
  0.0 1013.1 jit_solution(15597185505681744815)
XLA Ops:
  30.6 12.2 %collective-permute-done.5 = bf16[272,512]{1,0:T(8,128)(2,1)S(1)} collective-permute-done((bf16[272,512]{1,0:T(8,128)(2,1)S(1)}, bf16[272,512]{1,0:T(8,128)(2,1)S(1)}, u32[]{:S(2)}, u32[]{:S(2)}) %collective-permute-start.5) | collective-permute-done | bytes 278560 | tf_op jit(solution)/shard_map/ppermute | solution.py:281
  42.9 23.1 %collective-permute-done.4 = bf16[272,512]{1,0:T(8,128)(2,1)S(1)} collective-permute-done((bf16[272,512]{1,0:T(8,128)(2,1)S(1)}, bf16[272,512]{1,0:T(8,128)(2,1)S(1)}, u32[]{:S(2)}, u32[]{:S(2)}) %collective-permute-start.4) | collective-permute-done | bytes 278560 | tf_op jit(solution)/shard_map/ppermute | solution.py:281
  84.1 22.5 %collective-permute-done.6 = bf16[1088,512]{1,0:T(8,128)(2,1)} collective-permute-done((bf16[1088,512]{1,0:T(8,128)(2,1)}, bf16[1088,512]{1,0:T(8,128)(2,1)}, u32[]{:S(2)}, u32[]{:S(2)}) %collective-permute-start.6) | collective-permute-done | bytes 1114144 | tf_op jit(solution)/shard_map/ppermute | solution.py:281
  135.4 17.6 %collective-permute-done.16.other = bf16[256,3072]{1,0:T(8,128)(2,1)} collective-permute-done((bf16[256,3072]{1,0:T(8,128)(2,1)}, bf16[256,3072]{1,0:T(8,128)(2,1)}, u32[]{:S(2)}, u32[]{:S(2)}) %collective-permute-start.16) | collective-permute-done | bytes 1572896 | tf_op jit(solution)/shard_map/ppermute | solution.py:281
  156.8 40.5 %all-gather.3.cloned.1.call-done = bf16[2048,1536]{1,0:T(8,128)(2,1)} async-done(((bf16[256,1536]{1,0:T(8,128)(2,1)}), bf16[2048,1536]{1,0:T(8,128)(2,1)}) %all-gather.3.cloned.1.call-update) | async-done | bytes 6291472 | tf_op jit(solution)/shard_map/all_gather | solution.py:363
  198.5 11.8 %fusion.81.qkv_ref = f32[1024,1536]{1,0:T(8,128)} fusion(bf16[1024,2048]{1,0:T(8,128)(2,1)} %get-tuple-element.73, bf16[2048,1536]{1,0:T(8,128)(2,1)} %all-gather.3.cloned.1.call-done), kind=kOutput, calls=%fused_computation.198 | convolution fusion | flops 6442450944 | bytes 16777216 | tf_op jit(solution)/shard_map/dot_general | solution.py:22
  210.3 14.7 %shard_map.206 = (bf16[1024,512]{1,0:T(8,128)(2,1)}, bf16[1024,1536]{1,0:T(8,128)(2,1)}) custom-call(s32[1024]{0:T(1024)} %bitcast.83, f32[1024,1536]{1,0:T(8,128)} %fusion.81.qkv_ref, f32[1024,128]{1,0:T(8,128)} %get-tuple-element.95.cos_ref, f32[1024,128]{1,0:T(8,128)} %get-tuple-element.96.sin_ref, s32[1024,1]{1,0:T(8,128)} %copy.25.seg_col, ...), custom_call_target="tpu_custom_call" | custom-call | tf_op jit(solution)/shard_map/pallas_call | solution.py:195
  240.7 21.2 %collective-permute-done.8 = bf16[256,2048]{1,0:T(8,128)(2,1)} collective-permute-done((bf16[256,2048]{1,0:T(8,128)(2,1)S(1)}, bf16[256,2048]{1,0:T(8,128)(2,1)}, u32[]{:S(2)}, u32[]{:S(2)}) %collective-permute-start.8) | collective-permute-done | bytes 1048608 | tf_op jit(solution)/shard_map/ppermute | solution.py:287
  273.8 17.2 %collective-permute-done.9 = bf16[256,2048]{1,0:T(8,128)(2,1)S(1)} collective-permute-done((bf16[256,2048]{1,0:T(8,128)(2,1)S(1)}, bf16[256,2048]{1,0:T(8,128)(2,1)S(1)}, u32[]{:S(2)}, u32[]{:S(2)}) %collective-permute-start.9) | collective-permute-done | bytes 1048608 | tf_op jit(solution)/shard_map/ppermute | solution.py:287
  294.8 22.8 %collective-permute-done.10 = bf16[256,2048]{1,0:T(8,128)(2,1)S(1)} collective-permute-done((bf16[256,2048]{1,0:T(8,128)(2,1)S(1)}, bf16[256,2048]{1,0:T(8,128)(2,1)S(1)}, u32[]{:S(2)}, u32[]{:S(2)}) %collective-permute-start.10) | collective-permute-done | bytes 1048608 | tf_op jit(solution)/shard_map/ppermute | solution.py:281
  332.3 46.0 %collective-permute-done.17 = bf16[256,2048]{1,0:T(8,128)(2,1)S(1)} collective-permute-done((bf16[256,2048]{1,0:T(8,128)(2,1)S(1)}, bf16[256,2048]{1,0:T(8,128)(2,1)S(1)}, u32[]{:S(2)}, u32[]{:S(2)}) %collective-permute-start.17) | collective-permute-done | bytes 1048608 | tf_op jit(solution)/shard_map/ppermute | solution.py:281
  380.3 21.7 %collective-permute-done.18 = bf16[256,2048]{1,0:T(8,128)(2,1)S(1)} collective-permute-done((bf16[256,2048]{1,0:T(8,128)(2,1)S(1)}, bf16[256,2048]{1,0:T(8,128)(2,1)S(1)}, u32[]{:S(2)}, u32[]{:S(2)}) %collective-permute-start.18) | collective-permute-done | bytes 1048608 | tf_op jit(solution)/shard_map/ppermute | solution.py:287
  422.7 14.8 %fusion.11 = f32[2048,1024]{1,0:T(8,128)} fusion(bf16[2048,2048]{1,0:T(8,128)(2,1)} %constant_dynamic-update-slice_fusion.7, bf16[2048,3072]{1,0:T(8,128)(2,1)} %all-gather.5.cloned.1.call-done), kind=kOutput, calls=%fused_computation.29 | convolution fusion | flops 8589934592 | bytes 20971520 | tf_op jit(solution)/shard_map/dot_general | solution.py:22
  437.5 12.8 %fusion.17 = f32[2048,1024]{1,0:T(8,128)} fusion(bf16[2048,2048]{1,0:T(8,128)(2,1)S(1)} %copy-done.20, bf16[2048,3072]{1,0:T(8,128)(2,1)} %all-gather.5.cloned.1.call-done), kind=kOutput, calls=%fused_computation.35 | convolution fusion | flops 8589934592 | bytes 20971520 | tf_op jit(solution)/shard_map/dot_general | solution.py:22
  450.3 23.2 %multiply_convert_fusion = (bf16[2048,1024]{1,0:T(8,128)(2,1)}, bf16[2048,1024]{1,0:T(8,128)(2,1)}, bf16[2048,1024]{1,0:T(8,128)(2,1)S(1)}) fusion(f32[2048,1024]{1,0:T(8,128)} %fusion.17, f32[2048,1024]{1,0:T(8,128)} %fusion.11, bf16[2048,2048]{1,0:T(8,128)(2,1)} %constant_dynamic-update-slice_fusion.14, bf16[2048,3072]{1,0:T(8,128)(2,1)} %all-gather.5.cloned.1.call-done), kind=kOutput, calls=%fused_computation.8 | convolution fusion | flops 8621391872 | bytes 41943040 | tf_op jit(solution)/shard_map/dot_general | solution.py:22
  475.6 12.8 %convolution_convert_fusion.4 = bf16[2048,1024]{1,0:T(8,128)(2,1)} fusion(bf16[2048,2048]{1,0:T(8,128)(2,1)} %constant_dynamic-update-slice_fusion.14, bf16[2048,1024]{1,0:T(8,128)(2,1)S(1)} %get-tuple-element.40), kind=kOutput, calls=%fused_computation.21 | convolution fusion | flops 8592031744 | bytes 16777216 | tf_op jit(solution)/shard_map/dot_general | solution.py:26
  488.5 14.3 %convolution_convert_fusion.2 = bf16[2048,1024]{1,0:T(8,128)(2,1)} fusion(bf16[2048,2048]{1,0:T(8,128)(2,1)} %constant_dynamic-update-slice_fusion.7, bf16[2048,1024]{1,0:T(8,128)(2,1)} %get-tuple-element.39), kind=kOutput, calls=%fused_computation.19 | convolution fusion | flops 8592031744 | bytes 16777216 | tf_op jit(solution)/shard_map/dot_general | solution.py:26
  502.8 12.8 %convolution_convert_fusion.3 = bf16[2048,1024]{1,0:T(8,128)(2,1)} fusion(bf16[2048,2048]{1,0:T(8,128)(2,1)} %constant_dynamic-update-slice_fusion.7, bf16[2048,1024]{1,0:T(8,128)(2,1)S(1)} %copy-done.34), kind=kOutput, calls=%fused_computation.20 | convolution fusion | flops 8592031744 | bytes 16777216 | tf_op jit(solution)/shard_map/dot_general | solution.py:26
  524.2 10.8 %fusion.13 = f32[1024,2048]{1,0:T(8,128)} fusion(bf16[2048,3072]{1,0:T(8,128)(2,1)} %all-gather.5.cloned.1.call-done, bf16[2048,1024]{1,0:T(8,128)(2,1)} %get-tuple-element.38), kind=kOutput, calls=%fused_computation.31 | convolution fusion | flops 4294967296 | bytes 14680064 | tf_op jit(solution)/shard_map/dot_general | solution.py:32
  561.1 11.1 %fusion.79 = (bf16[1024,2048]{1,0:T(8,128)(2,1)S(1)}, f32[1024,2048]{1,0:T(8,128)S(1)}) fusion(bf16[1024,2048]{1,0:T(8,128)(2,1)} %collective-permute-done.20, f32[1024,2048]{1,0:T(8,128)} %fusion.15, bf16[2048,3072]{1,0:T(8,128)(2,1)} %all-gather.5.cloned.1.call-done, bf16[2048,1024]{1,0:T(8,128)(2,1)} %get-tuple-element.39), kind=kOutput, calls=%fused_computation.196 | convolution fusion | flops 4303355904 | bytes 31457280 | tf_op jit(solution)/shard_map/dot_general | solution.py:32
  574.1 12.0 %fusion.80 = (bf16[1024,2048]{1,0:T(8,128)(2,1)S(1)}, f32[1024,2048]{1,0:T(8,128)}) fusion(bf16[1024,2048]{1,0:T(8,128)(2,1)} %collective-permute-done.25, bf16[2048,3072]{1,0:T(8,128)(2,1)} %all-gather.5.cloned.1.call-done, bf16[2048,1024]{1,0:T(8,128)(2,1)} %copy-done.33), kind=kOutput, calls=%fused_computation.197 | convolution fusion | flops 4301258752 | bytes 23068672 | tf_op jit(solution)/shard_map/dot_general | solution.py:32
  599.0 21.0 %collective-permute-done.26 = bf16[512,1024]{1,0:T(8,128)(2,1)S(1)} collective-permute-done((bf16[512,1024]{1,0:T(8,128)(2,1)S(1)}, bf16[512,1024]{1,0:T(8,128)(2,1)S(1)}, u32[]{:S(2)}, u32[]{:S(2)}) %collective-permute-start.26) | collective-permute-done | bytes 1048608 | tf_op jit(solution)/shard_map/ppermute | solution.py:287
  620.5 15.0 %collective-permute-done.23 = bf16[512,1024]{1,0:T(8,128)(2,1)S(1)} collective-permute-done((bf16[512,1024]{1,0:T(8,128)(2,1)S(1)}, bf16[512,1024]{1,0:T(8,128)(2,1)S(1)}, u32[]{:S(2)}, u32[]{:S(2)}) %collective-permute-start.23) | collective-permute-done | bytes 1048608 | tf_op jit(solution)/shard_map/ppermute | solution.py:281
  635.7 61.4 %collective-permute-done.22 = bf16[256,1024]{1,0:T(8,128)(2,1)S(1)} collective-permute-done((bf16[256,1024]{1,0:T(8,128)(2,1)S(1)}, bf16[256,1024]{1,0:T(8,128)(2,1)S(1)}, u32[]{:S(2)}, u32[]{:S(2)}) %collective-permute-start.22) | collective-permute-done | bytes 524320 | tf_op jit(solution)/shard_map/ppermute | solution.py:281
  698.7 16.4 %collective-permute-done.27 = bf16[256,1024]{1,0:T(8,128)(2,1)S(1)} collective-permute-done((bf16[256,1024]{1,0:T(8,128)(2,1)S(1)}, bf16[256,1024]{1,0:T(8,128)(2,1)S(1)}, u32[]{:S(2)}, u32[]{:S(2)}) %collective-permute-start.27) | collective-permute-done | bytes 524320 | tf_op jit(solution)/shard_map/ppermute | solution.py:281
  718.3 10.5 %collective-permute-done.29 = bf16[256,1024]{1,0:T(8,128)(2,1)S(1)} collective-permute-done((bf16[256,1024]{1,0:T(8,128)(2,1)S(1)}, bf16[256,1024]{1,0:T(8,128)(2,1)S(1)}, u32[]{:S(2)}, u32[]{:S(2)}) %collective-permute-start.29) | collective-permute-done | bytes 524320 | tf_op jit(solution)/shard_map/ppermute | solution.py:287
  733.2 22.1 %collective-permute-done.31 = bf16[256,2048]{1,0:T(8,128)(2,1)} collective-permute-done((bf16[256,2048]{1,0:T(8,128)(2,1)S(1)}, bf16[256,2048]{1,0:T(8,128)(2,1)}, u32[]{:S(2)}, u32[]{:S(2)}) %collective-permute-start.31) | collective-permute-done | bytes 1048608 | tf_op jit(solution)/shard_map/ppermute | solution.py:287
  774.3 27.0 %shard_map.212 = bf16[1024,1536]{1,0:T(8,128)(2,1)} custom-call(s32[1024]{0:T(1024)} %bitcast.84, bf16[1024,1536]{1,0:T(8,128)(2,1)} %get-tuple-element.41.kept_ref, bf16[1024,512]{1,0:T(8,128)(2,1)} %convolution_convert_fusion.8.do_ref, f32[1024,128]{1,0:T(8,128)} %get-tuple-element.95.cos_ref, f32[1024,128]{1,0:T(8,128)} %get-tuple-element.96.sin_ref, ...), custom_call_target="tpu_custom_call" | custom-call | tf_op jit(solution)/shard_map/pallas_call | solution.py:254
  801.3 11.5 %convolution_convert_fusion = bf16[2048,1536]{1,0:T(8,128)(2,1)} fusion(bf16[1024,2048]{1,0:T(8,128)(2,1)} %get-tuple-element.73, bf16[1024,1536]{1,0:T(8,128)(2,1)} %shard_map.212), kind=kOutput, calls=%fused_computation.14 | convolution fusion | flops 6445596672 | bytes 13631488 | tf_op jit(solution)/shard_map/dot_general | solution.py:26
  836.3 24.0 %collective-permute-done.34 = bf16[256,2048]{1,0:T(8,128)(2,1)} collective-permute-done((bf16[256,2048]{1,0:T(8,128)(2,1)}, bf16[256,2048]{1,0:T(8,128)(2,1)}, u32[]{:S(2)}, u32[]{:S(2)}) %collective-permute-start.34) | collective-permute-done | bytes 1048608 | tf_op jit(solution)/shard_map/ppermute | solution.py:287
  889.3 40.2 %collective-permute-done.39 = f32[2,256]{1,0:T(2,128)S(1)} collective-permute-done((f32[2,256]{1,0:T(2,128)S(1)}, f32[2,256]{1,0:T(2,128)S(1)}, u32[]{:S(2)}, u32[]{:S(2)}) %collective-permute-start.39) | collective-permute-done | bytes 2080 | tf_op jit(solution)/shard_map/ppermute | solution.py:281
  934.7 45.1 %reduce-scatter.11.cloned.1.call-done = bf16[256,1536]{1,0:T(8,128)(2,1)} async-done(((bf16[2048,1536]{1,0:T(8,128)(2,1)}), bf16[256,1536]{1,0:T(8,128)(2,1)}) %reduce-scatter.11.cloned.1.call-update) | async-done | bytes 786448 | tf_op jit(solution)/shard_map/reduce_scatter | solution.py:499
  (297 shorter events, 307.7 us)
Async XLA Ops:
  7.2 190.1 %all-gather.3.cloned.1.call-start = ((), (), s32[]{:S(2)}) async-start(), calls=%async_computation.4 | async-start | bytes 7077888 | tf_op jit(solution)/shard_map/all_gather | solution.py:363
  15.6 407.1 %all-gather.5.cloned.1.call-start = ((), (), s32[]{:S(2)}) async-start(), calls=%async_computation.5 | async-start | bytes 15728640 | tf_op jit(solution)/shard_map/all_gather | solution.py:412
  18.8 56.8 %collective-permute-start.15 = (bf16[128,6144]{1,0:T(8,128)(2,1)}, bf16[128,6144]{1,0:T(8,128)(2,1)S(1)}, u32[]{:S(2)}, u32[]{:S(2)}) collective-permute-start(bf16[128,6144]{1,0:T(8,128)(2,1)} %shard_map.207), channel_id=1, source_target_pairs={{0,2},{2,0},{1,3},{3,1},{4,6},{6,4},{5,7},{7,5},{8,10},{10,8},{9,1... | collective-permute-start | bytes 4718600 | tf_op jit(solution)/shard_map/ppermute | solution.py:284
  24.0 101.2 %collective-permute-start = (bf16[512,2048]{1,0:T(8,128)(2,1)}, bf16[512,2048]{1,0:T(8,128)(2,1)}, u32[]{:S(2)}, u32[]{:S(2)}) collective-permute-start(bf16[512,2048]{1,0:T(8,128)(2,1)} %shard_map.203), channel_id=1, source_target_pairs={{0,2},{2,0},{1,3},{3,1},{4,6},{6,4},{5,7},{7,5},{8,10},{10,8},{9,1... | collective-permute-start | bytes 6291464 | tf_op jit(solution)/shard_map/ppermute | solution.py:284
  29.4 36.6 %collective-permute-start.4 = (bf16[272,512]{1,0:T(8,128)(2,1)S(1)}, bf16[272,512]{1,0:T(8,128)(2,1)S(1)}, u32[]{:S(2)}, u32[]{:S(2)}) collective-permute-start(bf16[272,512]{1,0:T(8,128)(2,1)S(1)} %copy-done.14), channel_id=1, source_target_pairs={{0,16},{4,20},{8,24},{12,28},{16,0},{20,4},{24,8},{28,12},{1,17},{... | collective-permute-start | bytes 835592 | tf_op jit(solution)/shard_map/ppermute | solution.py:281
  29.4 36.7 %collective-permute-start.3 = (bf16[272,512]{1,0:T(8,128)(2,1)S(1)}, bf16[272,512]{1,0:T(8,128)(2,1)S(1)}, u32[]{:S(2)}, u32[]{:S(2)}) collective-permute-start(bf16[272,512]{1,0:T(8,128)(2,1)S(1)} %copy-done.14), channel_id=1, source_target_pairs={{0,8},{4,12},{8,0},{12,4},{16,24},{20,28},{24,16},{28,20},{1,9},{5... | collective-permute-start | bytes 835592 | tf_op jit(solution)/shard_map/ppermute | solution.py:281
  67.2 39.5 %collective-permute-start.6 = (bf16[1088,512]{1,0:T(8,128)(2,1)}, bf16[1088,512]{1,0:T(8,128)(2,1)}, u32[]{:S(2)}, u32[]{:S(2)}) collective-permute-start(bf16[1088,512]{1,0:T(8,128)(2,1)} %pad_maximum_fusion.4), channel_id=1, source_target_pairs={{0,4},{4,0},{8,12},{12,8},{16,20},{20,16},{24,28},{28,24},{1,5},{5... | collective-permute-start | bytes 3342344 | tf_op jit(solution)/shard_map/ppermute | solution.py:281
  81.6 71.4 %collective-permute-start.16 = (bf16[256,3072]{1,0:T(8,128)(2,1)}, bf16[256,3072]{1,0:T(8,128)(2,1)}, u32[]{:S(2)}, u32[]{:S(2)}) collective-permute-start(bf16[256,3072]{1,0:T(8,128)(2,1)} %get-tuple-element.35), channel_id=1, source_target_pairs={{0,8},{4,12},{8,0},{12,4},{16,24},{20,28},{24,16},{28,20},{1,9},{5... | collective-permute-start | bytes 4718600 | tf_op jit(solution)/shard_map/ppermute | solution.py:281
  197.3 570.8 %reduce-scatter.5.cloned.1.call-start = ((), (), s32[]{:S(2)}) async-start(), calls=%async_computation.6 | async-start | bytes 5242880 | tf_op jit(solution)/shard_map/reduce_scatter | solution.py:499
  236.6 25.4 %collective-permute-start.8 = (bf16[256,2048]{1,0:T(8,128)(2,1)S(1)}, bf16[256,2048]{1,0:T(8,128)(2,1)}, u32[]{:S(2)}, u32[]{:S(2)}) collective-permute-start(bf16[256,2048]{1,0:T(8,128)(2,1)S(1)} %add_convert_fusion.2), channel_id=1, source_target_pairs={{0,1},{1,0},{2,3},{3,2},{4,5},{5,4},{6,7},{7,6},{8,9},{9,8},{10,11... | collective-permute-start | bytes 3145736 | tf_op jit(solution)/shard_map/ppermute | solution.py:287
  266.7 24.3 %collective-permute-start.9 = (bf16[256,2048]{1,0:T(8,128)(2,1)S(1)}, bf16[256,2048]{1,0:T(8,128)(2,1)S(1)}, u32[]{:S(2)}, u32[]{:S(2)}) collective-permute-start(bf16[256,2048]{1,0:T(8,128)(2,1)S(1)} %get-tuple-element.62), channel_id=1, source_target_pairs={{0,1},{1,0},{2,3},{3,2},{4,5},{5,4},{6,7},{7,6},{8,9},{9,8},{10,11... | collective-permute-start | bytes 3145736 | tf_op jit(solution)/shard_map/ppermute | solution.py:287
  268.4 49.2 %collective-permute-start.10 = (bf16[256,2048]{1,0:T(8,128)(2,1)S(1)}, bf16[256,2048]{1,0:T(8,128)(2,1)S(1)}, u32[]{:S(2)}, u32[]{:S(2)}) collective-permute-start(bf16[256,2048]{1,0:T(8,128)(2,1)S(1)} %get-tuple-element.62), channel_id=1, source_target_pairs={{0,8},{4,12},{8,0},{12,4},{16,24},{20,28},{24,16},{28,20},{1,9},{5... | collective-permute-start | bytes 3145736 | tf_op jit(solution)/shard_map/ppermute | solution.py:281
  291.1 38.8 %collective-permute-start.11 = (bf16[128,2048]{1,0:T(8,128)(2,1)S(1)}, bf16[128,2048]{1,0:T(8,128)(2,1)S(1)}, u32[]{:S(2)}, u32[]{:S(2)}) collective-permute-start(bf16[128,2048]{1,0:T(8,128)(2,1)S(1)} %slice.275), channel_id=1, source_target_pairs={{0,8},{4,12},{8,0},{12,4},{16,24},{20,28},{24,16},{28,20},{1,9},{5... | collective-permute-start | bytes 1572872 | tf_op jit(solution)/shard_map/ppermute | solution.py:281
  332.3 46.0 %collective-permute-start.17 = (bf16[256,2048]{1,0:T(8,128)(2,1)S(1)}, bf16[256,2048]{1,0:T(8,128)(2,1)S(1)}, u32[]{:S(2)}, u32[]{:S(2)}) collective-permute-start(bf16[256,2048]{1,0:T(8,128)(2,1)S(1)} %get-tuple-element.37), channel_id=1, source_target_pairs={{0,8},{4,12},{8,0},{12,4},{16,24},{20,28},{24,16},{28,20},{1,9},{5... | collective-permute-start | bytes 3145736 | tf_op jit(solution)/shard_map/ppermute | solution.py:281
  488.5 279.6 %reduce-scatter.7.cloned.1.call-start = ((), (), s32[]{:S(2)}) async-start(), calls=%async_computation.7 | async-start | bytes 10485760 | tf_op jit(solution)/shard_map/reduce_scatter | solution.py:499
  523.9 293.3 %reduce-scatter.9.cloned.1.call-start = ((), (), s32[]{:S(2)}) async-start(), calls=%async_computation.8 | async-start | bytes 2359296 | tf_op jit(solution)/shard_map/reduce_scatter | solution.py:499
  572.4 26.1 %collective-permute-start.21 = (bf16[512,1024]{1,0:T(8,128)(2,1)S(1)}, bf16[512,1024]{1,0:T(8,128)(2,1)S(1)}, u32[]{:S(2)}, u32[]{:S(2)}) collective-permute-start(bf16[512,1024]{1,0:T(8,128)(2,1)S(1)} %pad_maximum_fusion.5), channel_id=1, source_target_pairs={{0,1},{1,0},{2,3},{3,2},{4,5},{5,4},{6,7},{7,6},{8,9},{9,8},{10,11... | collective-permute-start | bytes 3145736 | tf_op jit(solution)/shard_map/ppermute | solution.py:287
  586.3 33.7 %collective-permute-start.26 = (bf16[512,1024]{1,0:T(8,128)(2,1)S(1)}, bf16[512,1024]{1,0:T(8,128)(2,1)S(1)}, u32[]{:S(2)}, u32[]{:S(2)}) collective-permute-start(bf16[512,1024]{1,0:T(8,128)(2,1)S(1)} %pad_maximum_fusion.6), channel_id=1, source_target_pairs={{0,1},{1,0},{2,3},{3,2},{4,5},{5,4},{6,7},{7,6},{8,9},{9,8},{10,11... | collective-permute-start | bytes 3145736 | tf_op jit(solution)/shard_map/ppermute | solution.py:287
  587.0 48.5 %collective-permute-start.23 = (bf16[512,1024]{1,0:T(8,128)(2,1)S(1)}, bf16[512,1024]{1,0:T(8,128)(2,1)S(1)}, u32[]{:S(2)}, u32[]{:S(2)}) collective-permute-start(bf16[512,1024]{1,0:T(8,128)(2,1)S(1)} %concatenate.113), channel_id=1, source_target_pairs={{0,8},{4,12},{8,0},{12,4},{16,24},{20,28},{24,16},{28,20},{1,9},{5... | collective-permute-start | bytes 3145736 | tf_op jit(solution)/shard_map/ppermute | solution.py:281
  587.2 111.3 %collective-permute-start.28 = (bf16[512,1024]{1,0:T(8,128)(2,1)S(1)}, bf16[512,1024]{1,0:T(8,128)(2,1)S(1)}, u32[]{:S(2)}, u32[]{:S(2)}) collective-permute-start(bf16[512,1024]{1,0:T(8,128)(2,1)S(1)} %concatenate.114), channel_id=1, source_target_pairs={{0,8},{4,12},{8,0},{12,4},{16,24},{20,28},{24,16},{28,20},{1,9},{5... | collective-permute-start | bytes 3145736 | tf_op jit(solution)/shard_map/ppermute | solution.py:281
  598.9 98.2 %collective-permute-start.22 = (bf16[256,1024]{1,0:T(8,128)(2,1)S(1)}, bf16[256,1024]{1,0:T(8,128)(2,1)S(1)}, u32[]{:S(2)}, u32[]{:S(2)}) collective-permute-start(bf16[256,1024]{1,0:T(8,128)(2,1)S(1)} %fusion.35), channel_id=1, source_target_pairs={{0,8},{4,12},{8,0},{12,4},{16,24},{20,28},{24,16},{28,20},{1,9},{5... | collective-permute-start | bytes 1572872 | tf_op jit(solution)/shard_map/ppermute | solution.py:281
  620.4 94.7 %collective-permute-start.27 = (bf16[256,1024]{1,0:T(8,128)(2,1)S(1)}, bf16[256,1024]{1,0:T(8,128)(2,1)S(1)}, u32[]{:S(2)}, u32[]{:S(2)}) collective-permute-start(bf16[256,1024]{1,0:T(8,128)(2,1)S(1)} %fusion.31), channel_id=1, source_target_pairs={{0,8},{4,12},{8,0},{12,4},{16,24},{20,28},{24,16},{28,20},{1,9},{5... | collective-permute-start | bytes 1572872 | tf_op jit(solution)/shard_map/ppermute | solution.py:281
  768.0 211.8 %reduce-scatter.11.cloned.1.call-start = ((), (), s32[]{:S(2)}) async-start(), calls=%async_computation.9 | async-start | bytes 7077888 | tf_op jit(solution)/shard_map/reduce_scatter | solution.py:499
  834.8 25.5 %collective-permute-start.34 = (bf16[256,2048]{1,0:T(8,128)(2,1)}, bf16[256,2048]{1,0:T(8,128)(2,1)}, u32[]{:S(2)}, u32[]{:S(2)}) collective-permute-start(bf16[256,2048]{1,0:T(8,128)(2,1)} %fusion.20), channel_id=1, source_target_pairs={{0,1},{1,0},{2,3},{3,2},{4,5},{5,4},{6,7},{7,6},{8,9},{9,8},{10,11... | collective-permute-start | bytes 3145736 | tf_op jit(solution)/shard_map/ppermute | solution.py:287
  836.3 34.6 %collective-permute-start.44 = (bf16[256,1024]{1,0:T(8,128)(2,1)S(1)}, bf16[256,1024]{1,0:T(8,128)(2,1)S(1)}, u32[]{:S(2)}, u32[]{:S(2)}) collective-permute-start(bf16[256,1024]{1,0:T(8,128)(2,1)S(1)} %constant_dynamic-slice_fusion), channel_id=1, source_target_pairs={{0,8},{4,12},{8,0},{12,4},{16,24},{20,28},{24,16},{28,20},{1,9},{5... | collective-permute-start | bytes 1572872 | tf_op jit(solution)/shard_map/ppermute | solution.py:281
  870.3 113.8 %collective-permute-start.30 = (bf16[256,2048]{1,0:T(8,128)(2,1)}, bf16[256,2048]{1,0:T(8,128)(2,1)}, u32[]{:S(2)}, u32[]{:S(2)}) collective-permute-start(bf16[256,2048]{1,0:T(8,128)(2,1)} %get-tuple-element.78.own_ref), channel_id=1, source_target_pairs={{0,1},{1,0},{2,3},{3,2},{4,5},{5,4},{6,7},{7,6},{8,9},{9,8},{10,11... | collective-permute-start | bytes 3145736 | tf_op jit(solution)/shard_map/ppermute | solution.py:287
  874.5 114.0 %collective-permute-start.45 = (bf16[128,2048]{1,0:T(8,128)(2,1)}, bf16[128,2048]{1,0:T(8,128)(2,1)}, u32[]{:S(2)}, u32[]{:S(2)}) collective-permute-start(bf16[128,2048]{1,0:T(8,128)(2,1)} %shard_map.218), channel_id=1, source_target_pairs={{0,2},{2,0},{1,3},{3,1},{4,6},{6,4},{5,7},{7,5},{8,10},{10,8},{9,1... | collective-permute-start | bytes 1572872 | tf_op jit(solution)/shard_map/ppermute | solution.py:284
  881.6 48.0 %collective-permute-start.42 = (bf16[256,2048]{1,0:T(8,128)(2,1)S(1)}, bf16[256,2048]{1,0:T(8,128)(2,1)S(1)}, u32[]{:S(2)}, u32[]{:S(2)}) collective-permute-start(bf16[256,2048]{1,0:T(8,128)(2,1)S(1)} %constant_dynamic-slice_fusion.1), channel_id=1, source_target_pairs={{0,8},{4,12},{8,0},{12,4},{16,24},{20,28},{24,16},{28,20},{1,9},{5... | collective-permute-start | bytes 3145736 | tf_op jit(solution)/shard_map/ppermute | solution.py:281
  883.5 46.1 %collective-permute-start.39 = (f32[2,256]{1,0:T(2,128)S(1)}, f32[2,256]{1,0:T(2,128)S(1)}, u32[]{:S(2)}, u32[]{:S(2)}) collective-permute-start(f32[2,256]{1,0:T(2,128)S(1)} %broadcast_select_fusion.2), channel_id=1, source_target_pairs={{0,8},{4,12},{8,0},{12,4},{16,24},{20,28},{24,16},{28,20},{1,9},{5... | collective-permute-start | bytes 6152 | tf_op jit(solution)/shard_map/ppermute | solution.py:281
  887.6 105.0 %collective-permute-start.35 = (bf16[256,2048]{1,0:T(8,128)(2,1)S(1)}, bf16[256,2048]{1,0:T(8,128)(2,1)}, u32[]{:S(2)}, u32[]{:S(2)}) collective-permute-start(bf16[256,2048]{1,0:T(8,128)(2,1)S(1)} %add_convert_fusion.1.own_ref), channel_id=1, source_target_pairs={{0,1},{1,0},{2,3},{3,2},{4,5},{5,4},{6,7},{7,6},{8,9},{9,8},{10,11... | collective-permute-start | bytes 3145736 | tf_op jit(solution)/shard_map/ppermute | solution.py:287
  934.2 62.1 %collective-permute-start.43 = (bf16[128,4096]{1,0:T(8,128)(2,1)}, bf16[128,4096]{1,0:T(8,128)(2,1)S(1)}, u32[]{:S(2)}, u32[]{:S(2)}) collective-permute-start(bf16[128,4096]{1,0:T(8,128)(2,1)} %shard_map.216), channel_id=1, source_target_pairs={{0,2},{2,0},{1,3},{3,1},{4,6},{6,4},{5,7},{7,5},{8,10},{10,8},{9,1... | collective-permute-start | bytes 3145736 | tf_op jit(solution)/shard_map/ppermute | solution.py:284
  934.2 57.9 %collective-permute-start.40 = (f32[2,128]{1,0:T(2,128)S(1)}, f32[2,128]{1,0:T(2,128)S(1)}, u32[]{:S(2)}, u32[]{:S(2)}) collective-permute-start(f32[2,128]{1,0:T(2,128)S(1)} %broadcast_select_fusion.3), channel_id=1, source_target_pairs={{0,2},{2,0},{1,3},{3,1},{4,6},{6,4},{5,7},{7,5},{8,10},{10,8},{9,1... | collective-permute-start | bytes 3080 | tf_op jit(solution)/shard_map/ppermute | solution.py:284
  (61 other events, 1264.4 us)
Sparse Core Ops, SparseCore 0:
  15.7 181.5 all-gather.2
  199.1 223.5 all-gather.4
  488.6 86.1 reduce-scatter.4
  577.7 153.5 reduce-scatter.6
  768.2 48.9 reduce-scatter.8
  819.4 160.4 reduce-scatter.10

commit v6 on v5

--- a/solution.py
+++ b/solution.py
@@ -312,7 +312,6 @@
         n_ff = w_gate.shape[1] // 4
         heads = n_attn // HD
         half_s = shards // 2
-        pad = 16
 
         def place_of(number):
             return (number & ~3) | ((number & 1) << 1) | ((number >> 1) & 1)
@@ -335,43 +334,28 @@
         gains = jnp.stack([gain_attn, gain_mlp])
         other_gains = swap_core(gains)
 
-        def keep_attn(s_ref, q, k, v, o, other, own_g, other_g, out_qkv, out_o):
+        def keep_attn(s_ref, q, k, v, o, other, out):
             me = s_ref[0]
             start = pl.multiple_of(me * n_attn, n_attn)
-            mine, theirs = pl.ds(me * unit, unit), pl.ds((1 - me) * unit, unit)
+            mine = pl.ds(pl.multiple_of(me * unit, unit), unit)
+            theirs = pl.ds(pl.multiple_of((1 - me) * unit, unit), unit)
             for h in range(heads):
                 for i, ref in enumerate((q, k, v)):
                     where = slice((3 * h + i) * HD, (3 * h + i + 1) * HD)
-                    out_qkv[mine, where] = ref[:, pl.ds(start + h * HD, HD)]
-            out_o[mine, :] = o[:, pl.ds(start, n_attn)]
-            out_qkv[theirs, :] = other[:, : 3 * n_attn]
-            out_o[theirs, :] = other[:, 3 * n_attn :]
-            first, second = own_g[...], other_g[...]
-            low = jnp.where(me == 0, first, second)
-            high = jnp.where(me == 0, second, first)
-            line_g = cat([low, high, jnp.zeros((2, n_attn - block), bf16)], 1)
-            out_o[block:, :] = cat([line_g, jnp.zeros((pad - 2, n_attn), bf16)])
-
-        block_qkv, block_o = small_call(
-            keep_attn, [core], attn_w + [other_a, gains, other_gains],
-            [array_of(block, 3 * n_attn), array_of(block + pad, n_attn)],
-        )
-
-        def shard_at(i):
-            return shard ^ (((i % half_s) << 1) | (i // half_s))
-
-        weight_qkv = lax.all_gather(block_qkv, "shard", axis=0, tiled=True, axis_index_groups=every)
-        near_o = cat([block_o] + [across(block_o, mask) for mask in line])
-        parts_o = cat([near_o, across(near_o, 1)]).reshape(shards, block + pad, n_attn)
-        weight_o = jnp.zeros((width, n_attn), bf16)
-        for i in range(shards):
-            weight_o = lax.dynamic_update_slice_in_dim(
-                weight_o, parts_o[i, :block], place_of(shard_at(i)) * block, 0
-            )
-        gain_rows = parts_o[:, block : block + 2, :block]
+                    out[mine, where] = ref[:, pl.ds(start + h * HD, HD)]
+            out[mine, 3 * n_attn :] = o[:, pl.ds(start, n_attn)]
+            out[theirs, :] = other[...]
+
+        (block_a,) = small_call(keep_attn, [core], attn_w + [other_a], [array_of(block, 4 * n_attn)])
+        weight_a = lax.all_gather(block_a, "shard", axis=0, tiled=True, axis_index_groups=every)
+        weight_qkv, weight_o = weight_a[:, : 3 * n_attn], weight_a[:, 3 * n_attn :]
+
+        own_g = ordered(core, gains, other_gains, 1)
+        near_g = cat([own_g] + [across(own_g, mask) for mask in line])
+        parts_g = cat([near_g, across(near_g, 1)]).reshape(shards, 2, block)
         away_bits = place_of(jnp.arange(shards, dtype=jnp.int32)) ^ shard
-        gain_rows = gain_rows[(away_bits >> 1) + half_s * (away_bits & 1)]
-        gains_rel = jnp.transpose(gain_rows, (1, 0, 2)).reshape(2, width).astype(f32)
+        parts_g = parts_g[(away_bits >> 1) + half_s * (away_bits & 1)]
+        gains_rel = jnp.transpose(parts_g, (1, 0, 2)).reshape(2, width).astype(f32)
         gain_a, gain_m = gains_rel[0:1], gains_rel[1:2]
 
         def send_ff(s_ref, g, u, d, out):
@@ -408,7 +392,7 @@
         x_both = ordered(core, x_own, swap_core(x_own))
         normed_all, inverse_all = norm_parts(x_both.astype(f32))
         h_one = (normed_all * gain_a).astype(bf16)
-        pair_f = after(pair_f, weight_qkv, weight_o, h_one, cosine, sine)
+        pair_f = after(pair_f, weight_a, h_one, cosine, sine)
         weight_f = lax.all_gather(pair_f, "shard", axis=0, tiled=True, axis_index_groups=groups)
         weight_g, weight_u, weight_d = [weight_f[:, i * n_ff : (i + 1) * n_ff] for i in range(3)]
         qkv = matmul(h_one, weight_qkv)
@@ -463,11 +447,13 @@
 
             low_tp = swap_tp(cat([pick(low, 1), pick(low, 3)]).astype(bf16)).astype(f32)
             high_zl = across(cat([pick(high, 2), pick(high, 3)]).astype(bf16), 2).astype(f32)
-            low_zl = across((pick(low, 2) + pick(low_tp, 1)).astype(bf16), 2).astype(f32)
-            high_tp = swap_tp((pick(high, 1) + pick(high_zl, 1)).astype(bf16)).astype(f32)
+            low_sent = (pick(low, 2) + pick(low_tp, 1)).astype(bf16)
+            high_sent = (pick(high, 1) + pick(high_zl, 1)).astype(bf16)
+            low_zl = across(low_sent, 2).astype(f32)
+            high_tp = swap_tp(high_sent).astype(f32)
             low_sum = pick(low, 0) + pick(low_tp, 0) + low_zl
             high_sum = pick(high, 0) + pick(high_zl, 0) + high_tp
-            return away, cat([low_sum, high_sum], 1)
+            return cat([low_sum, high_sum], 1)
 
         grad_hidden = matmul(grad_out, weight_d)
         grad_gate = (grad_hidden * up_pre * gate_sig * (1.0 + gate_pre * (1.0 - gate_sig))).astype(bf16)
@@ -477,15 +463,10 @@
             [contract_rows(h_two, grad_gate).astype(bf16), contract_rows(h_two, grad_up).astype(bf16)], 1
         )
         grad_gate, grad_up = after((grad_gate, grad_up), prod_d, prod_gu)
-        event_h, grad_h_two = from_tokens(
+        grad_h_two = from_tokens(
             lambda where: contract_cols(grad_gate[where], weight_g)
             + contract_cols(grad_up[where], weight_u)
         )
-        late_hidden = after(hidden, grad_h_two)
-        event_m, mlp = from_tokens(lambda where: contract_cols(late_hidden[where], weight_d))
-        out_part = (after_attn + mlp).astype(bf16)
-        output = join_tokens(out_part, swap_tp(out_part), half, nat, block)
-
         grad_gain_m = jnp.sum(grad_h_two * normed_two, axis=0, keepdims=True)
         dy_part = rows_of(dy_rel, half * part, part).astype(f32)
         grad_after = dy_part + norm_back(grad_h_two * gain_m, normed_two, inverse_two)
@@ -542,6 +523,10 @@
         own_o = scatter(after(late_o, own_d, own_gu), every)
         grad_mixed = after(grad_mixed, late_o)
         grad_qkv = attend_backward(kept, grad_mixed, seg_row, cosine, sine, 0, heads)
+        hidden, grad_qkv = lax.optimization_barrier((hidden, grad_qkv))
+        mlp = from_tokens(lambda where: contract_cols(hidden[where], weight_d))
+        out_part = (after_attn + mlp).astype(bf16)
+        output = join_tokens(out_part, swap_tp(out_part), half, nat, block)
         own_qkv = scatter(after(contract_rows(h_one, grad_qkv).astype(bf16), own_o), every)
 
         (grad_w_down,) = rows_pair(own_d, 1)
@@ -549,6 +534,13 @@
 
         grad_h_one = to_slice(grad_qkv, lambda v: contract_cols(v, weight_qkv))
 
+        normed_part = rows_of(normed_all, core * rows + half * part, part)
+        inverse_part = rows_of(inverse_all, core * rows + half * part, part)
+        grad_gain_a = jnp.sum(grad_h_one * normed_part, axis=0, keepdims=True)
+        grad_x = (grad_after + norm_back(grad_h_one * gain_a, normed_part, inverse_part)).astype(bf16)
+        grad_tokens = join_tokens(grad_x, swap_tp(grad_x), half, nat, block)
+
+        own_qkv = after(own_qkv, output, grad_tokens, grad_w_gate, grad_w_up, grad_w_down)
         own_a = cat([own_qkv, own_o], 1)
         (sent_g,) = small_call(send_unit, [core], [own_a], [array_of(unit, 4 * n_attn)])
         other_a = swap_core(sent_g)
@@ -571,12 +563,6 @@
             join_attn, [core], [own_a, other_a], [array_of(unit, 2 * n_attn, f32)] * 4
         )
 
-        normed_part = rows_of(normed_all, core * rows + half * part, part)
-        inverse_part = rows_of(inverse_all, core * rows + half * part, part)
-        grad_gain_a = jnp.sum(grad_h_one * normed_part, axis=0, keepdims=True)
-        grad_x = (grad_after + norm_back(grad_h_one * gain_a, normed_part, inverse_part)).astype(bf16)
-        grad_tokens = join_tokens(grad_x, swap_tp(grad_x), half, nat, block)
-
         grad_gains = cat([grad_gain_a, grad_gain_m])
         grad_gains = grad_gains + swap_tp(grad_gains)
         for mask in [1 << bit for bit in range(shards.bit_length() - 2, 1, -1)] + [1, 2]:

time: 1020 us -> 1050 us (1.029)
  waiting for transfers between devices: 555 us -> 596 us
  starting transfers between devices: 38.7 us -> 66.9 us
  local copies, waits for them, and re-layouts: 52.9 us -> 30.1 us
    all_gather x1, waiting for transfers between devices: 40.5 us -> 96.1 us  [per_device(): lax.all_gather(block_a, 'shard', axis=0, tiled=True, axis_index_groups=ev...]
    ppermute x17, waiting for transfers between devices: 292 us -> 255 us  [across(): return lax.ppermute(values, 'shard', [(i, i ^ mask) for i in range(shards)])]
    ppermute x17, starting transfers between devices: 18 us -> 47.5 us  [across(): return lax.ppermute(values, 'shard', [(i, i ^ mask) for i in range(shards)])]
    reduce_scatter x4, waiting for transfers between devices: 49.4 us -> 69.8 us  [scatter(): lax.psum_scatter(values.astype(bf16), 'shard', scatter_dimension=0, tiled...]
    dynamic_update_slice x8 -> x0, local copies, waits for them, and re-layouts: 13.4 us -> none  [per_device(): lax.dynamic_update_slice_in_dim(weight_o, parts_o[i, :block], place_of(sh...]
    unnamed x95 -> x87, local copies, waits for them, and re-layouts: 26.9 us -> 21.3 us
  transfers between devices with their start and end apart: 52 -> 52, of which waited for: 32 -> 30; matrix products, arithmetic and copies ran while one was open for 23% -> 20% of each run, Pallas kernels for 9% -> 7%
where the time goes in v6:
time: 1050 us
  waiting for transfers between devices  596 us (57%)
  matrix products  211 us (20%)
  Pallas kernels  86.7 us (8%)
  starting transfers between devices  66.9 us (6%)
  other arithmetic  39.9 us (4%)
  local copies, waits for them, and re-layouts  30.1 us (3%)
  between operations  15.1 us (1%)
    ppermute x17, waiting for transfers between devices, across(): return lax.ppermute(values, 'shard', [(i, i ^ mask) for i in range(shards)])  255 us
    ppermute x13, waiting for transfers between devices, swap_tp(): return lax.ppermute(values, 'tp', [(0, 1), (1, 0)])  151 us
    all_gather x1, waiting for transfers between devices, per_device(): lax.all_gather(block_a, 'shard', axis=0, tiled=True, axis_index_groups=ev...  96.1 us
    dot_general x12, matrix products, contract_cols(): lax.dot_general(left, right, (((1,), (1,)), ((), ())), preferred_element_...  85.6 us
    dot_general x5, matrix products, matmul(): return jnp.dot(left, right, preferred_element_type=jnp.float32)  69.9 us
    reduce_scatter x4, waiting for transfers between devices, scatter(): lax.psum_scatter(values.astype(bf16), 'shard', scatter_dimension=0, tiled...  69.8 us
    dot_general x5, matrix products, contract_rows(): lax.dot_general(left, right, (((0,), (0,)), ((), ())), preferred_element_...  55.5 us
    ppermute x17, starting transfers between devices, across(): return lax.ppermute(values, 'shard', [(i, i ^ mask) for i in range(shards)])  47.5 us
  transfers between devices with their start and end apart: 52, of which 30 were waited for; matrix products, arithmetic and copies ran while one was open for 20% of the time, Pallas kernels for 7%

profile of v6, /device:TPU:0, one launch (start us, length us, event | category | flops | bytes accessed | tf_op | source)
XLA Modules:
  0.0 1045.4 jit_solution(17011087579780480844)
XLA Ops:
  57.5 60.2 %collective-permute-done.16.other = bf16[256,3072]{1,0:T(8,128)(2,1)} collective-permute-done((bf16[256,3072]{1,0:T(8,128)(2,1)}, bf16[256,3072]{1,0:T(8,128)(2,1)}, u32[]{:S(2)}, u32[]{:S(2)}) %collective-permute-start.16) | collective-permute-done | bytes 1572896 | tf_op jit(solution)/shard_map/ppermute | solution.py:281
  121.4 96.1 %all-gather.3.cloned.1.call-done = bf16[2048,2048]{1,0:T(8,128)(2,1)} async-done(((bf16[256,2048]{1,0:T(8,128)(2,1)}), bf16[2048,2048]{1,0:T(8,128)(2,1)}) %all-gather.3.cloned.1.call-update) | async-done | bytes 8388624 | tf_op jit(solution)/shard_map/all_gather | solution.py:350
  218.8 11.7 %fusion.8.qkv_ref = f32[1024,1536]{1,0:T(8,128)} fusion(bf16[1024,2048]{1,0:T(8,128)(2,1)} %get-tuple-element.71, bf16[2048,2048]{1,0:T(8,128)(2,1)} %all-gather.3.cloned.1.call-done), kind=kOutput, calls=%fused_computation.24 | convolution fusion | flops 6442450944 | bytes 16777216 | tf_op jit(solution)/shard_map/dot_general | solution.py:22
  230.5 12.5 %shard_map.206 = (bf16[1024,512]{1,0:T(8,128)(2,1)}, bf16[1024,1536]{1,0:T(8,128)(2,1)}) custom-call(s32[1024]{0:T(1024)} %bitcast.42, f32[1024,1536]{1,0:T(8,128)} %fusion.8.qkv_ref, f32[1024,128]{1,0:T(8,128)} %get-tuple-element.94.cos_ref, f32[1024,128]{1,0:T(8,128)} %get-tuple-element.95.sin_ref, s32[1024,1]{1,0:T(8,128)} %copy.25.seg_col, ...), custom_call_target="tpu_custom_call" | custom-call | tf_op jit(solution)/shard_map/pallas_call | solution.py:195
  257.1 23.9 %collective-permute-done.8 = bf16[256,2048]{1,0:T(8,128)(2,1)} collective-permute-done((bf16[256,2048]{1,0:T(8,128)(2,1)}, bf16[256,2048]{1,0:T(8,128)(2,1)}, u32[]{:S(2)}, u32[]{:S(2)}) %collective-permute-start.8) | collective-permute-done | bytes 1048608 | tf_op jit(solution)/shard_map/ppermute | solution.py:287
  295.6 15.6 %collective-permute-done.9 = bf16[256,2048]{1,0:T(8,128)(2,1)S(1)} collective-permute-done((bf16[256,2048]{1,0:T(8,128)(2,1)S(1)}, bf16[256,2048]{1,0:T(8,128)(2,1)S(1)}, u32[]{:S(2)}, u32[]{:S(2)}) %collective-permute-start.9) | collective-permute-done | bytes 1048608 | tf_op jit(solution)/shard_map/ppermute | solution.py:287
  316.5 22.8 %collective-permute-done.10 = bf16[256,2048]{1,0:T(8,128)(2,1)S(1)} collective-permute-done((bf16[256,2048]{1,0:T(8,128)(2,1)S(1)}, bf16[256,2048]{1,0:T(8,128)(2,1)S(1)}, u32[]{:S(2)}, u32[]{:S(2)}) %collective-permute-start.10) | collective-permute-done | bytes 1048608 | tf_op jit(solution)/shard_map/ppermute | solution.py:281
  355.3 47.2 %collective-permute-done.17 = bf16[256,2048]{1,0:T(8,128)(2,1)S(1)} collective-permute-done((bf16[256,2048]{1,0:T(8,128)(2,1)S(1)}, bf16[256,2048]{1,0:T(8,128)(2,1)S(1)}, u32[]{:S(2)}, u32[]{:S(2)}) %collective-permute-start.17) | collective-permute-done | bytes 1048608 | tf_op jit(solution)/shard_map/ppermute | solution.py:281
  404.4 22.9 %collective-permute-done.18 = bf16[256,2048]{1,0:T(8,128)(2,1)S(1)} collective-permute-done((bf16[256,2048]{1,0:T(8,128)(2,1)S(1)}, bf16[256,2048]{1,0:T(8,128)(2,1)S(1)}, u32[]{:S(2)}, u32[]{:S(2)}) %collective-permute-start.18) | collective-permute-done | bytes 1048608 | tf_op jit(solution)/shard_map/ppermute | solution.py:287
  445.0 14.8 %fusion.19 = f32[2048,1024]{1,0:T(8,128)} fusion(bf16[2048,2048]{1,0:T(8,128)(2,1)} %constant_dynamic-update-slice_fusion.2, bf16[2048,3072]{1,0:T(8,128)(2,1)} %all-gather.5.cloned.1.call-done), kind=kOutput, calls=%fused_computation.37 | convolution fusion | flops 8589934592 | bytes 20971520 | tf_op jit(solution)/shard_map/dot_general | solution.py:22
  459.8 12.8 %fusion.25 = f32[2048,1024]{1,0:T(8,128)} fusion(bf16[2048,2048]{1,0:T(8,128)(2,1)S(1)} %copy-done.19, bf16[2048,3072]{1,0:T(8,128)(2,1)} %all-gather.5.cloned.1.call-done), kind=kOutput, calls=%fused_computation.43 | convolution fusion | flops 8589934592 | bytes 20971520 | tf_op jit(solution)/shard_map/dot_general | solution.py:22
  472.6 23.1 %multiply_convert_fusion = (bf16[2048,1024]{1,0:T(8,128)(2,1)}, bf16[2048,1024]{1,0:T(8,128)(2,1)}, bf16[2048,1024]{1,0:T(8,128)(2,1)S(1)}) fusion(f32[2048,1024]{1,0:T(8,128)} %fusion.25, f32[2048,1024]{1,0:T(8,128)} %fusion.19, bf16[2048,2048]{1,0:T(8,128)(2,1)} %constant_dynamic-update-slice_fusion.9, bf16[2048,3072]{1,0:T(8,128)(2,1)} %all-gather.5.cloned.1.call-done), kind=kOutput, calls=%fused_computation.8 | convolution fusion | flops 8621391872 | bytes 41943040 | tf_op jit(solution)/shard_map/dot_general | solution.py:22
  497.7 12.8 %convolution_convert_fusion.4 = bf16[2048,1024]{1,0:T(8,128)(2,1)} fusion(bf16[2048,2048]{1,0:T(8,128)(2,1)} %constant_dynamic-update-slice_fusion.9, bf16[2048,1024]{1,0:T(8,128)(2,1)S(1)} %get-tuple-element.40), kind=kOutput, calls=%fused_computation.29 | convolution fusion | flops 8592031744 | bytes 16777216 | tf_op jit(solution)/shard_map/dot_general | solution.py:26
  510.6 14.3 %convolution_convert_fusion.2 = bf16[2048,1024]{1,0:T(8,128)(2,1)} fusion(bf16[2048,2048]{1,0:T(8,128)(2,1)} %constant_dynamic-update-slice_fusion.2, bf16[2048,1024]{1,0:T(8,128)(2,1)} %get-tuple-element.38), kind=kOutput, calls=%fused_computation.27 | convolution fusion | flops 8592031744 | bytes 16777216 | tf_op jit(solution)/shard_map/dot_general | solution.py:26
  524.9 12.9 %convolution_convert_fusion.3 = bf16[2048,1024]{1,0:T(8,128)(2,1)} fusion(bf16[2048,2048]{1,0:T(8,128)(2,1)} %constant_dynamic-update-slice_fusion.2, bf16[2048,1024]{1,0:T(8,128)(2,1)S(1)} %copy-done.36), kind=kOutput, calls=%fused_computation.28 | convolution fusion | flops 8592031744 | bytes 16777216 | tf_op jit(solution)/shard_map/dot_general | solution.py:26
  571.9 11.0 %fusion.95 = (bf16[1024,2048]{1,0:T(8,128)(2,1)S(1)}, f32[1024,2048]{1,0:T(8,128)S(1)}) fusion(bf16[1024,2048]{1,0:T(8,128)(2,1)} %collective-permute-done.20, f32[1024,2048]{1,0:T(8,128)} %fusion.23, bf16[2048,3072]{1,0:T(8,128)(2,1)} %all-gather.5.cloned.1.call-done, bf16[2048,1024]{1,0:T(8,128)(2,1)} %get-tuple-element.38), kind=kOutput, calls=%fused_computation.189 | convolution fusion | flops 4303355904 | bytes 31457280 | tf_op jit(solution)/shard_map/dot_general | solution.py:32
  585.5 23.2 %collective-permute-done.21 = bf16[512,1024]{1,0:T(8,128)(2,1)S(1)} collective-permute-done((bf16[512,1024]{1,0:T(8,128)(2,1)S(1)}, bf16[512,1024]{1,0:T(8,128)(2,1)S(1)}, u32[]{:S(2)}, u32[]{:S(2)}) %collective-permute-start.21) | collective-permute-done | bytes 1048608 | tf_op jit(solution)/shard_map/ppermute | solution.py:287
  610.7 15.6 %collective-permute-done.23 = bf16[512,1024]{1,0:T(8,128)(2,1)S(1)} collective-permute-done((bf16[512,1024]{1,0:T(8,128)(2,1)S(1)}, bf16[512,1024]{1,0:T(8,128)(2,1)S(1)}, u32[]{:S(2)}, u32[]{:S(2)}) %collective-permute-start.23) | collective-permute-done | bytes 1048608 | tf_op jit(solution)/shard_map/ppermute | solution.py:281
  626.6 14.7 %collective-permute-done.22 = bf16[256,1024]{1,0:T(8,128)(2,1)S(1)} collective-permute-done((bf16[256,1024]{1,0:T(8,128)(2,1)S(1)}, bf16[256,1024]{1,0:T(8,128)(2,1)S(1)}, u32[]{:S(2)}, u32[]{:S(2)}) %collective-permute-start.22) | collective-permute-done | bytes 524320 | tf_op jit(solution)/shard_map/ppermute | solution.py:281
  642.9 12.9 %collective-permute-done.24 = bf16[256,1024]{1,0:T(8,128)(2,1)S(1)} collective-permute-done((bf16[256,1024]{1,0:T(8,128)(2,1)S(1)}, bf16[256,1024]{1,0:T(8,128)(2,1)S(1)}, u32[]{:S(2)}, u32[]{:S(2)}) %collective-permute-start.24) | collective-permute-done | bytes 524320 | tf_op jit(solution)/shard_map/ppermute | solution.py:287
  659.8 23.5 %collective-permute-done.25 = bf16[256,2048]{1,0:T(8,128)(2,1)} collective-permute-done((bf16[256,2048]{1,0:T(8,128)(2,1)S(1)}, bf16[256,2048]{1,0:T(8,128)(2,1)}, u32[]{:S(2)}, u32[]{:S(2)}) %collective-permute-start.25) | collective-permute-done | bytes 1048608 | tf_op jit(solution)/shard_map/ppermute | solution.py:287
  695.0 57.9 %reduce-scatter.7.cloned.1.call-done.mine = bf16[512,2048]{1,0:T(8,128)(2,1)} async-done(((bf16[2048,2048]{1,0:T(8,128)(2,1)}), bf16[512,2048]{1,0:T(8,128)(2,1)}) %reduce-scatter.7.cloned.1.call-update) | async-done | bytes 2097168 | tf_op jit(solution)/shard_map/reduce_scatter | solution.py:480
  760.4 21.2 %shard_map.211 = bf16[1024,1536]{1,0:T(8,128)(2,1)} custom-call(s32[1024]{0:T(1024)} %bitcast.43, bf16[1024,1536]{1,0:T(8,128)(2,1)} %get-tuple-element.35.kept_ref, bf16[1024,512]{1,0:T(8,128)(2,1)} %convolution_convert_fusion.7.do_ref, f32[1024,128]{1,0:T(8,128)} %get-tuple-element.94.cos_ref, f32[1024,128]{1,0:T(8,128)} %get-tuple-element.95.sin_ref, ...), custom_call_target="tpu_custom_call" | custom-call | tf_op jit(solution)/shard_map/pallas_call | solution.py:254
  781.6 11.8 %convolution_convert_fusion = bf16[2048,1536]{1,0:T(8,128)(2,1)} fusion(bf16[1024,2048]{1,0:T(8,128)(2,1)} %get-tuple-element.71, bf16[1024,1536]{1,0:T(8,128)(2,1)} %shard_map.211), kind=kOutput, calls=%fused_computation.14 | convolution fusion | flops 6445596672 | bytes 13631488 | tf_op jit(solution)/shard_map/dot_general | solution.py:26
  793.4 11.9 %reduce-scatter.9.cloned.1.call-done = bf16[256,512]{1,0:T(8,128)(2,1)} async-done(((bf16[2048,512]{1,0:T(8,128)(2,1)}), bf16[256,512]{1,0:T(8,128)(2,1)}) %reduce-scatter.9.cloned.1.call-update) | async-done | bytes 262160 | tf_op jit(solution)/shard_map/reduce_scatter | solution.py:480
  844.6 13.6 %collective-permute-done.34 = bf16[256,2048]{1,0:T(8,128)(2,1)S(1)} collective-permute-done((bf16[256,2048]{1,0:T(8,128)(2,1)S(1)}, bf16[256,2048]{1,0:T(8,128)(2,1)S(1)}, u32[]{:S(2)}, u32[]{:S(2)}) %collective-permute-start.34) | collective-permute-done | bytes 1048608 | tf_op jit(solution)/shard_map/ppermute | solution.py:287
  865.5 14.8 %collective-permute-done.28 = bf16[512,1024]{1,0:T(8,128)(2,1)S(1)} collective-permute-done((bf16[512,1024]{1,0:T(8,128)(2,1)S(1)}, bf16[512,1024]{1,0:T(8,128)(2,1)S(1)}, u32[]{:S(2)}, u32[]{:S(2)}) %collective-permute-start.28) | collective-permute-done | bytes 1048608 | tf_op jit(solution)/shard_map/ppermute | solution.py:287
  884.2 29.8 %collective-permute-done.30 = bf16[512,1024]{1,0:T(8,128)(2,1)S(1)} collective-permute-done((bf16[512,1024]{1,0:T(8,128)(2,1)S(1)}, bf16[512,1024]{1,0:T(8,128)(2,1)S(1)}, u32[]{:S(2)}, u32[]{:S(2)}) %collective-permute-start.30) | collective-permute-done | bytes 1048608 | tf_op jit(solution)/shard_map/ppermute | solution.py:281
  914.2 21.5 %collective-permute-done.29 = bf16[256,1024]{1,0:T(8,128)(2,1)S(1)} collective-permute-done((bf16[256,1024]{1,0:T(8,128)(2,1)S(1)}, bf16[256,1024]{1,0:T(8,128)(2,1)S(1)}, u32[]{:S(2)}, u32[]{:S(2)}) %collective-permute-start.29) | collective-permute-done | bytes 524320 | tf_op jit(solution)/shard_map/ppermute | solution.py:281
  938.8 16.6 %collective-permute-start.37 = (f32[2,1024]{1,0:T(2,128)S(1)}, f32[2,1024]{1,0:T(2,128)S(1)}, u32[]{:S(2)}, u32[]{:S(2)}) collective-permute-start(f32[2,1024]{1,0:T(2,128)S(1)} %broadcast_select_fusion), channel_id=1, source_target_pairs={{0,16},{4,20},{8,24},{12,28},{16,0},{20,4},{24,8},{28,12},{1,17},{... | collective-permute-start | bytes 24584 | tf_op jit(solution)/shard_map/ppermute | solution.py:281
  959.4 27.0 %collective-permute-done.41.theirs = bf16[256,2048]{1,0:T(8,128)(2,1)} collective-permute-done((bf16[256,2048]{1,0:T(8,128)(2,1)S(1)}, bf16[256,2048]{1,0:T(8,128)(2,1)}, u32[]{:S(2)}, u32[]{:S(2)}) %collective-permute-start.41) | collective-permute-done | bytes 1048608 | tf_op jit(solution)/shard_map/ppermute | solution.py:281
  990.0 14.4 %collective-permute-start.38 = (f32[2,512]{1,0:T(2,128)S(1)}, f32[2,512]{1,0:T(2,128)S(1)}, u32[]{:S(2)}, u32[]{:S(2)}) collective-permute-start(f32[2,512]{1,0:T(2,128)S(1)} %broadcast_select_fusion.1), channel_id=1, source_target_pairs={{0,4},{4,0},{8,12},{12,8},{16,20},{20,16},{24,28},{28,24},{1,5},{5... | collective-permute-start | bytes 12296 | tf_op jit(solution)/shard_map/ppermute | solution.py:281
  (280 shorter events, 285.3 us)
Async XLA Ops:
  7.2 210.3 %all-gather.3.cloned.1.call-start = ((), (), s32[]{:S(2)}) async-start(), calls=%async_computation.4 | async-start | bytes 9437184 | tf_op jit(solution)/shard_map/all_gather | solution.py:350
  14.9 430.1 %all-gather.5.cloned.1.call-start = ((), (), s32[]{:S(2)}) async-start(), calls=%async_computation.5 | async-start | bytes 15728640 | tf_op jit(solution)/shard_map/all_gather | solution.py:396
  20.1 27.3 %collective-permute-start = (bf16[512,2048]{1,0:T(8,128)(2,1)}, bf16[512,2048]{1,0:T(8,128)(2,1)}, u32[]{:S(2)}, u32[]{:S(2)}) collective-permute-start(bf16[512,2048]{1,0:T(8,128)(2,1)} %shard_map.203), channel_id=1, source_target_pairs={{0,2},{2,0},{1,3},{3,1},{4,6},{6,4},{5,7},{7,5},{8,10},{10,8},{9,1... | collective-permute-start | bytes 6291464 | tf_op jit(solution)/shard_map/ppermute | solution.py:284
  23.8 18.6 %collective-permute-start.15 = (bf16[128,6144]{1,0:T(8,128)(2,1)}, bf16[128,6144]{1,0:T(8,128)(2,1)}, u32[]{:S(2)}, u32[]{:S(2)}) collective-permute-start(bf16[128,6144]{1,0:T(8,128)(2,1)} %shard_map.207), channel_id=1, source_target_pairs={{0,2},{2,0},{1,3},{3,1},{4,6},{6,4},{5,7},{7,5},{8,10},{10,8},{9,1... | collective-permute-start | bytes 4718600 | tf_op jit(solution)/shard_map/ppermute | solution.py:284
  47.4 70.3 %collective-permute-start.16 = (bf16[256,3072]{1,0:T(8,128)(2,1)}, bf16[256,3072]{1,0:T(8,128)(2,1)}, u32[]{:S(2)}, u32[]{:S(2)}) collective-permute-start(bf16[256,3072]{1,0:T(8,128)(2,1)} %get-tuple-element.33), channel_id=1, source_target_pairs={{0,8},{4,12},{8,0},{12,4},{16,24},{20,28},{24,16},{28,20},{1,9},{5... | collective-permute-start | bytes 4718600 | tf_op jit(solution)/shard_map/ppermute | solution.py:281
  217.5 477.5 %reduce-scatter.5.cloned.1.call-start = ((), (), s32[]{:S(2)}) async-start(), calls=%async_computation.6 | async-start | bytes 5242880 | tf_op jit(solution)/shard_map/reduce_scatter | solution.py:480
  255.5 25.5 %collective-permute-start.8 = (bf16[256,2048]{1,0:T(8,128)(2,1)}, bf16[256,2048]{1,0:T(8,128)(2,1)}, u32[]{:S(2)}, u32[]{:S(2)}) collective-permute-start(bf16[256,2048]{1,0:T(8,128)(2,1)} %fusion.41), channel_id=1, source_target_pairs={{0,1},{1,0},{2,3},{3,2},{4,5},{5,4},{6,7},{7,6},{8,9},{9,8},{10,11... | collective-permute-start | bytes 3145736 | tf_op jit(solution)/shard_map/ppermute | solution.py:287
  286.8 24.3 %collective-permute-start.9 = (bf16[256,2048]{1,0:T(8,128)(2,1)S(1)}, bf16[256,2048]{1,0:T(8,128)(2,1)S(1)}, u32[]{:S(2)}, u32[]{:S(2)}) collective-permute-start(bf16[256,2048]{1,0:T(8,128)(2,1)S(1)} %get-tuple-element.62), channel_id=1, source_target_pairs={{0,1},{1,0},{2,3},{3,2},{4,5},{5,4},{6,7},{7,6},{8,9},{9,8},{10,11... | collective-permute-start | bytes 3145736 | tf_op jit(solution)/shard_map/ppermute | solution.py:287
  288.4 50.9 %collective-permute-start.10 = (bf16[256,2048]{1,0:T(8,128)(2,1)S(1)}, bf16[256,2048]{1,0:T(8,128)(2,1)S(1)}, u32[]{:S(2)}, u32[]{:S(2)}) collective-permute-start(bf16[256,2048]{1,0:T(8,128)(2,1)S(1)} %get-tuple-element.62), channel_id=1, source_target_pairs={{0,8},{4,12},{8,0},{12,4},{16,24},{20,28},{24,16},{28,20},{1,9},{5... | collective-permute-start | bytes 3145736 | tf_op jit(solution)/shard_map/ppermute | solution.py:281
  311.2 42.3 %collective-permute-start.11 = (bf16[128,2048]{1,0:T(8,128)(2,1)S(1)}, bf16[128,2048]{1,0:T(8,128)(2,1)S(1)}, u32[]{:S(2)}, u32[]{:S(2)}) collective-permute-start(bf16[128,2048]{1,0:T(8,128)(2,1)S(1)} %slice.240), channel_id=1, source_target_pairs={{0,8},{4,12},{8,0},{12,4},{16,24},{20,28},{24,16},{28,20},{1,9},{5... | collective-permute-start | bytes 1572872 | tf_op jit(solution)/shard_map/ppermute | solution.py:281
  355.3 47.2 %collective-permute-start.17 = (bf16[256,2048]{1,0:T(8,128)(2,1)S(1)}, bf16[256,2048]{1,0:T(8,128)(2,1)S(1)}, u32[]{:S(2)}, u32[]{:S(2)}) collective-permute-start(bf16[256,2048]{1,0:T(8,128)(2,1)S(1)} %get-tuple-element.36), channel_id=1, source_target_pairs={{0,8},{4,12},{8,0},{12,4},{16,24},{20,28},{24,16},{28,20},{1,9},{5... | collective-permute-start | bytes 3145736 | tf_op jit(solution)/shard_map/ppermute | solution.py:281
  402.5 24.8 %collective-permute-start.18 = (bf16[256,2048]{1,0:T(8,128)(2,1)S(1)}, bf16[256,2048]{1,0:T(8,128)(2,1)S(1)}, u32[]{:S(2)}, u32[]{:S(2)}) collective-permute-start(bf16[256,2048]{1,0:T(8,128)(2,1)S(1)} %collective-permute-done.17), channel_id=1, source_target_pairs={{0,1},{1,0},{2,3},{3,2},{4,5},{5,4},{6,7},{7,6},{8,9},{9,8},{10,11... | collective-permute-start | bytes 3145736 | tf_op jit(solution)/shard_map/ppermute | solution.py:287
  510.5 242.3 %reduce-scatter.7.cloned.1.call-start = ((), (), s32[]{:S(2)}) async-start(), calls=%async_computation.7 | async-start | bytes 10485760 | tf_op jit(solution)/shard_map/reduce_scatter | solution.py:480
  546.1 259.2 %reduce-scatter.9.cloned.1.call-start = ((), (), s32[]{:S(2)}) async-start(), calls=%async_computation.8 | async-start | bytes 2359296 | tf_op jit(solution)/shard_map/reduce_scatter | solution.py:480
  583.1 25.5 %collective-permute-start.21 = (bf16[512,1024]{1,0:T(8,128)(2,1)S(1)}, bf16[512,1024]{1,0:T(8,128)(2,1)S(1)}, u32[]{:S(2)}, u32[]{:S(2)}) collective-permute-start(bf16[512,1024]{1,0:T(8,128)(2,1)S(1)} %pad_maximum_fusion.4), channel_id=1, source_target_pairs={{0,1},{1,0},{2,3},{3,2},{4,5},{5,4},{6,7},{7,6},{8,9},{9,8},{10,11... | collective-permute-start | bytes 3145736 | tf_op jit(solution)/shard_map/ppermute | solution.py:287
  583.9 42.4 %collective-permute-start.23 = (bf16[512,1024]{1,0:T(8,128)(2,1)S(1)}, bf16[512,1024]{1,0:T(8,128)(2,1)S(1)}, u32[]{:S(2)}, u32[]{:S(2)}) collective-permute-start(bf16[512,1024]{1,0:T(8,128)(2,1)S(1)} %concatenate.121), channel_id=1, source_target_pairs={{0,8},{4,12},{8,0},{12,4},{16,24},{20,28},{24,16},{28,20},{1,9},{5... | collective-permute-start | bytes 3145736 | tf_op jit(solution)/shard_map/ppermute | solution.py:281
  609.1 32.1 %collective-permute-start.22 = (bf16[256,1024]{1,0:T(8,128)(2,1)S(1)}, bf16[256,1024]{1,0:T(8,128)(2,1)S(1)}, u32[]{:S(2)}, u32[]{:S(2)}) collective-permute-start(bf16[256,1024]{1,0:T(8,128)(2,1)S(1)} %fusion.63), channel_id=1, source_target_pairs={{0,8},{4,12},{8,0},{12,4},{16,24},{20,28},{24,16},{28,20},{1,9},{5... | collective-permute-start | bytes 1572872 | tf_op jit(solution)/shard_map/ppermute | solution.py:281
  658.8 24.6 %collective-permute-start.25 = (bf16[256,2048]{1,0:T(8,128)(2,1)S(1)}, bf16[256,2048]{1,0:T(8,128)(2,1)}, u32[]{:S(2)}, u32[]{:S(2)}) collective-permute-start(bf16[256,2048]{1,0:T(8,128)(2,1)S(1)} %get-tuple-element.55), channel_id=1, source_target_pairs={{0,1},{1,0},{2,3},{3,2},{4,5},{5,4},{6,7},{7,6},{8,9},{9,8},{10,11... | collective-permute-start | bytes 3145736 | tf_op jit(solution)/shard_map/ppermute | solution.py:287
  752.9 274.8 %reduce-scatter.11.cloned.1.call-start = ((), (), s32[]{:S(2)}) async-start(), calls=%async_computation.9 | async-start | bytes 7077888 | tf_op jit(solution)/shard_map/reduce_scatter | solution.py:480
  814.8 18.9 %collective-permute-start.27 = (bf16[1024,2048]{1,0:T(8,128)(2,1)}, bf16[1024,2048]{1,0:T(8,128)(2,1)}, u32[]{:S(2)}, u32[]{:S(2)}) collective-permute-start(bf16[1024,2048]{1,0:T(8,128)(2,1)} %convolution_convert_fusion.1), channel_id=1, source_target_pairs={{0,2},{2,0},{1,3},{3,1},{4,6},{6,4},{5,7},{7,5},{8,10},{10,8},{9,1... | collective-permute-start | bytes 12582920 | tf_op jit(solution)/shard_map/ppermute | solution.py:284
  824.3 180.2 %collective-permute-start.43 = (bf16[256,1024]{1,0:T(8,128)(2,1)}, bf16[256,1024]{1,0:T(8,128)(2,1)}, u32[]{:S(2)}, u32[]{:S(2)}) collective-permute-start(bf16[256,1024]{1,0:T(8,128)(2,1)} %constant_dynamic-slice_fusion), channel_id=1, source_target_pairs={{0,8},{4,12},{8,0},{12,4},{16,24},{20,28},{24,16},{28,20},{1,9},{5... | collective-permute-start | bytes 1572872 | tf_op jit(solution)/shard_map/ppermute | solution.py:281
  832.1 26.1 %collective-permute-start.34 = (bf16[256,2048]{1,0:T(8,128)(2,1)S(1)}, bf16[256,2048]{1,0:T(8,128)(2,1)S(1)}, u32[]{:S(2)}, u32[]{:S(2)}) collective-permute-start(bf16[256,2048]{1,0:T(8,128)(2,1)S(1)} %fusion.42), channel_id=1, source_target_pairs={{0,1},{1,0},{2,3},{3,2},{4,5},{5,4},{6,7},{7,6},{8,9},{9,8},{10,11... | collective-permute-start | bytes 3145736 | tf_op jit(solution)/shard_map/ppermute | solution.py:287
  843.7 36.5 %collective-permute-start.28 = (bf16[512,1024]{1,0:T(8,128)(2,1)S(1)}, bf16[512,1024]{1,0:T(8,128)(2,1)S(1)}, u32[]{:S(2)}, u32[]{:S(2)}) collective-permute-start(bf16[512,1024]{1,0:T(8,128)(2,1)S(1)} %pad_maximum_fusion.5), channel_id=1, source_target_pairs={{0,1},{1,0},{2,3},{3,2},{4,5},{5,4},{6,7},{7,6},{8,9},{9,8},{10,11... | collective-permute-start | bytes 3145736 | tf_op jit(solution)/shard_map/ppermute | solution.py:287
  863.8 74.6 %collective-permute-start.36 = (f32[2,2048]{1,0:T(2,128)S(1)}, f32[2,2048]{1,0:T(2,128)S(1)}, u32[]{:S(2)}, u32[]{:S(2)}) collective-permute-start(f32[2,2048]{1,0:T(2,128)S(1)} %pad_maximum_fusion.8), channel_id=1, source_target_pairs={{0,1},{1,0},{2,3},{3,2},{4,5},{5,4},{6,7},{7,6},{8,9},{9,8},{10,11... | collective-permute-start | bytes 49160 | tf_op jit(solution)/shard_map/ppermute | solution.py:287
  865.4 48.6 %collective-permute-start.30 = (bf16[512,1024]{1,0:T(8,128)(2,1)S(1)}, bf16[512,1024]{1,0:T(8,128)(2,1)S(1)}, u32[]{:S(2)}, u32[]{:S(2)}) collective-permute-start(bf16[512,1024]{1,0:T(8,128)(2,1)S(1)} %concatenate.122), channel_id=1, source_target_pairs={{0,8},{4,12},{8,0},{12,4},{16,24},{20,28},{24,16},{28,20},{1,9},{5... | collective-permute-start | bytes 3145736 | tf_op jit(solution)/shard_map/ppermute | solution.py:281
  881.9 53.9 %collective-permute-start.29 = (bf16[256,1024]{1,0:T(8,128)(2,1)S(1)}, bf16[256,1024]{1,0:T(8,128)(2,1)S(1)}, u32[]{:S(2)}, u32[]{:S(2)}) collective-permute-start(bf16[256,1024]{1,0:T(8,128)(2,1)S(1)} %fusion.59), channel_id=1, source_target_pairs={{0,8},{4,12},{8,0},{12,4},{16,24},{20,28},{24,16},{28,20},{1,9},{5... | collective-permute-start | bytes 1572872 | tf_op jit(solution)/shard_map/ppermute | solution.py:281
  882.7 130.5 %collective-permute-start.35 = (bf16[256,2048]{1,0:T(8,128)(2,1)S(1)}, bf16[256,2048]{1,0:T(8,128)(2,1)}, u32[]{:S(2)}, u32[]{:S(2)}) collective-permute-start(bf16[256,2048]{1,0:T(8,128)(2,1)S(1)} %add_convert_fusion.1.own_ref), channel_id=1, source_target_pairs={{0,1},{1,0},{2,3},{3,2},{4,5},{5,4},{6,7},{7,6},{8,9},{9,8},{10,11... | collective-permute-start | bytes 3145736 | tf_op jit(solution)/shard_map/ppermute | solution.py:287
  937.8 17.6 %collective-permute-start.31 = (bf16[256,1024]{1,0:T(8,128)(2,1)S(1)}, bf16[256,1024]{1,0:T(8,128)(2,1)S(1)}, u32[]{:S(2)}, u32[]{:S(2)}) collective-permute-start(bf16[256,1024]{1,0:T(8,128)(2,1)S(1)} %get-tuple-element.67), channel_id=1, source_target_pairs={{0,1},{1,0},{2,3},{3,2},{4,5},{5,4},{6,7},{7,6},{8,9},{9,8},{10,11... | collective-permute-start | bytes 1572872 | tf_op jit(solution)/shard_map/ppermute | solution.py:287
  938.6 47.8 %collective-permute-start.41 = (bf16[256,2048]{1,0:T(8,128)(2,1)S(1)}, bf16[256,2048]{1,0:T(8,128)(2,1)}, u32[]{:S(2)}, u32[]{:S(2)}) collective-permute-start(bf16[256,2048]{1,0:T(8,128)(2,1)S(1)} %constant_dynamic-slice_fusion.1), channel_id=1, source_target_pairs={{0,8},{4,12},{8,0},{12,4},{16,24},{20,28},{24,16},{28,20},{1,9},{5... | collective-permute-start | bytes 3145736 | tf_op jit(solution)/shard_map/ppermute | solution.py:281
  938.8 51.2 %collective-permute-start.37 = (f32[2,1024]{1,0:T(2,128)S(1)}, f32[2,1024]{1,0:T(2,128)S(1)}, u32[]{:S(2)}, u32[]{:S(2)}) collective-permute-start(f32[2,1024]{1,0:T(2,128)S(1)} %broadcast_select_fusion), channel_id=1, source_target_pairs={{0,16},{4,20},{8,24},{12,28},{16,0},{20,4},{24,8},{28,12},{1,17},{... | collective-permute-start | bytes 24584 | tf_op jit(solution)/shard_map/ppermute | solution.py:281
  958.1 58.8 %collective-permute-start.32 = (bf16[256,2048]{1,0:T(8,128)(2,1)}, bf16[256,2048]{1,0:T(8,128)(2,1)S(1)}, u32[]{:S(2)}, u32[]{:S(2)}) collective-permute-start(bf16[256,2048]{1,0:T(8,128)(2,1)} %fusion.45.own_ref), channel_id=1, source_target_pairs={{0,1},{1,0},{2,3},{3,2},{4,5},{5,4},{6,7},{7,6},{8,9},{9,8},{10,11... | collective-permute-start | bytes 3145736 | tf_op jit(solution)/shard_map/ppermute | solution.py:287
  990.0 31.7 %collective-permute-start.42 = (bf16[128,4096]{1,0:T(8,128)(2,1)}, bf16[128,4096]{1,0:T(8,128)(2,1)S(1)}, u32[]{:S(2)}, u32[]{:S(2)}) collective-permute-start(bf16[128,4096]{1,0:T(8,128)(2,1)} %shard_map.214), channel_id=1, source_target_pairs={{0,2},{2,0},{1,3},{3,1},{4,6},{6,4},{5,7},{7,5},{8,10},{10,8},{9,1... | collective-permute-start | bytes 3145736 | tf_op jit(solution)/shard_map/ppermute | solution.py:284
  (59 other events, 1143.7 us)
Sparse Core Ops, SparseCore 0:
  15.0 202.4 all-gather.2
  219.3 224.1 all-gather.4
  510.7 85.6 reduce-scatter.4
  599.2 153.5 reduce-scatter.6
  755.6 49.6 reduce-scatter.8
  807.4 194.1 reduce-scatter.10

commit v7 on v5

--- a/solution.py
+++ b/solution.py
@@ -451,7 +451,7 @@
         gate_act = gate_pre * gate_sig
         hidden = (gate_act * up_pre).astype(bf16)
 
-        def from_tokens(project):
+        def from_tokens(project, gate=None):
             count = 4 * part
             away = swap_core(project(slice(count, 2 * count)).astype(bf16))
             total = project(slice(0, count)) + away.astype(f32)
@@ -461,28 +461,36 @@
             def pick(values, i):
                 return values[i * part : (i + 1) * part]
 
-            low_tp = swap_tp(cat([pick(low, 1), pick(low, 3)]).astype(bf16)).astype(f32)
-            high_zl = across(cat([pick(high, 2), pick(high, 3)]).astype(bf16), 2).astype(f32)
-            low_zl = across((pick(low, 2) + pick(low_tp, 1)).astype(bf16), 2).astype(f32)
-            high_tp = swap_tp((pick(high, 1) + pick(high_zl, 1)).astype(bf16)).astype(f32)
-            low_sum = pick(low, 0) + pick(low_tp, 0) + low_zl
-            high_sum = pick(high, 0) + pick(high_zl, 0) + high_tp
-            return away, cat([low_sum, high_sum], 1)
+            low_sent = cat([pick(low, 1), pick(low, 3)]).astype(bf16)
+            high_sent = cat([pick(high, 2), pick(high, 3)]).astype(bf16)
+            if gate is not None:
+                low_sent, high_sent = after((low_sent, high_sent), gate)
+            low_tp, high_zl = swap_tp(low_sent), across(high_sent, 2)
+            first = (low_tp, high_zl)
+            low_tp, high_zl = low_tp.astype(f32), high_zl.astype(f32)
+            low_zl = across((pick(low, 2) + pick(low_tp, 1)).astype(bf16), 2)
+            high_tp = swap_tp((pick(high, 1) + pick(high_zl, 1)).astype(bf16))
+            second = (low_zl, high_tp)
+            low_sum = pick(low, 0) + pick(low_tp, 0) + low_zl.astype(f32)
+            high_sum = pick(high, 0) + pick(high_zl, 0) + high_tp.astype(f32)
+            return (low_sent, first, second), cat([low_sum, high_sum], 1)
 
         grad_hidden = matmul(grad_out, weight_d)
         grad_gate = (grad_hidden * up_pre * gate_sig * (1.0 + gate_pre * (1.0 - gate_sig))).astype(bf16)
         grad_up = (grad_hidden * gate_act).astype(bf16)
         prod_d = contract_rows(grad_out, hidden).astype(bf16)
+        late_hidden = after(hidden, prod_d)
+        (sent_m, first_m, second_m), mlp = from_tokens(lambda where: contract_cols(late_hidden[where], weight_d))
+        grad_gate, grad_up = after((grad_gate, grad_up), sent_m)
         prod_gu = cat(
             [contract_rows(h_two, grad_gate).astype(bf16), contract_rows(h_two, grad_up).astype(bf16)], 1
         )
-        grad_gate, grad_up = after((grad_gate, grad_up), prod_d, prod_gu)
-        event_h, grad_h_two = from_tokens(
-            lambda where: contract_cols(grad_gate[where], weight_g)
-            + contract_cols(grad_up[where], weight_u)
+        late_gate, late_up = after((grad_gate, grad_up), prod_gu, first_m)
+        _, grad_h_two = from_tokens(
+            lambda where: contract_cols(late_gate[where], weight_g)
+            + contract_cols(late_up[where], weight_u),
+            second_m,
         )
-        late_hidden = after(hidden, grad_h_two)
-        event_m, mlp = from_tokens(lambda where: contract_cols(late_hidden[where], weight_d))
         out_part = (after_attn + mlp).astype(bf16)
         output = join_tokens(out_part, swap_tp(out_part), half, nat, block)
 
@@ -538,18 +546,23 @@
 
         own_d = scatter(prod_d, groups)
         own_gu = scatter(prod_gu, groups)
-        late_o = contract_rows(grad_attn, mixed).astype(bf16)
-        own_o = scatter(after(late_o, own_d, own_gu), every)
-        grad_mixed = after(grad_mixed, late_o)
         grad_qkv = attend_backward(kept, grad_mixed, seg_row, cosine, sine, 0, heads)
-        own_qkv = scatter(after(contract_rows(h_one, grad_qkv).astype(bf16), own_o), every)
+        own_a = scatter(
+            cat([contract_rows(h_one, grad_qkv).astype(bf16), contract_rows(grad_attn, mixed).astype(bf16)], 1), every
+        )
 
         (grad_w_down,) = rows_pair(own_d, 1)
         grad_w_gate, grad_w_up = rows_pair(own_gu, 2)
 
         grad_h_one = to_slice(grad_qkv, lambda v: contract_cols(v, weight_qkv))
 
-        own_a = cat([own_qkv, own_o], 1)
+        normed_part = rows_of(normed_all, core * rows + half * part, part)
+        inverse_part = rows_of(inverse_all, core * rows + half * part, part)
+        grad_gain_a = jnp.sum(grad_h_one * normed_part, axis=0, keepdims=True)
+        grad_x = (grad_after + norm_back(grad_h_one * gain_a, normed_part, inverse_part)).astype(bf16)
+        grad_tokens = join_tokens(grad_x, swap_tp(grad_x), half, nat, block)
+
+        own_a = after(own_a, output, grad_tokens, grad_w_gate, grad_w_up, grad_w_down)
         (sent_g,) = small_call(send_unit, [core], [own_a], [array_of(unit, 4 * n_attn)])
         other_a = swap_core(sent_g)
 
@@ -571,12 +584,6 @@
             join_attn, [core], [own_a, other_a], [array_of(unit, 2 * n_attn, f32)] * 4
         )
 
-        normed_part = rows_of(normed_all, core * rows + half * part, part)
-        inverse_part = rows_of(inverse_all, core * rows + half * part, part)
-        grad_gain_a = jnp.sum(grad_h_one * normed_part, axis=0, keepdims=True)
-        grad_x = (grad_after + norm_back(grad_h_one * gain_a, normed_part, inverse_part)).astype(bf16)
-        grad_tokens = join_tokens(grad_x, swap_tp(grad_x), half, nat, block)
-
         grad_gains = cat([grad_gain_a, grad_gain_m])
         grad_gains = grad_gains + swap_tp(grad_gains)
         for mask in [1 << bit for bit in range(shards.bit_length() - 2, 1, -1)] + [1, 2]:

time: 1020 us -> 1010 us (level)
  waiting for transfers between devices: 555 us -> 515 us
  starting transfers between devices: 38.7 us -> 61 us
  other arithmetic: 42.1 us -> 55 us
    ppermute x17, waiting for transfers between devices: 292 us -> 252 us  [across(): return lax.ppermute(values, 'shard', [(i, i ^ mask) for i in range(shards)])]
    ppermute x17, starting transfers between devices: 18 us -> 41.6 us  [across(): return lax.ppermute(values, 'shard', [(i, i ^ mask) for i in range(shards)])]
    reduce_scatter x4 -> x3, waiting for transfers between devices: 49.4 us -> 39.9 us  [scatter(): lax.psum_scatter(values.astype(bf16), 'shard', scatter_dimension=0, tiled...]
    concatenate x9 -> x10, other arithmetic: 12.3 us -> 21.6 us  [cat(): return jnp.concatenate(parts, axis=axis)]
    unnamed x95 -> x92, local copies, waits for them, and re-layouts: 26.9 us -> 24.7 us
  transfers between devices with their start and end apart: 52 -> 51, of which waited for: 32 -> 33; matrix products, arithmetic and copies ran while one was open for 23% -> 24% of each run, Pallas kernels for 9% -> 8%
where the time goes in v7:
time: 1010 us
  waiting for transfers between devices  515 us (51%)
  matrix products  213 us (21%)
  Pallas kernels  95.1 us (9%)
  starting transfers between devices  61 us (6%)
  other arithmetic  55 us (5%)
  local copies, waits for them, and re-layouts  53.7 us (5%)
  between operations  14.7 us (1%)
    ppermute x17, waiting for transfers between devices, across(): return lax.ppermute(values, 'shard', [(i, i ^ mask) for i in range(shards)])  252 us
    ppermute x13, waiting for transfers between devices, swap_tp(): return lax.ppermute(values, 'tp', [(0, 1), (1, 0)])  149 us
    dot_general x12, matrix products, contract_cols(): lax.dot_general(left, right, (((1,), (1,)), ((), ())), preferred_element_...  90.9 us
    dot_general x5, matrix products, matmul(): return jnp.dot(left, right, preferred_element_type=jnp.float32)  68.1 us
    dot_general x5, matrix products, contract_rows(): lax.dot_general(left, right, (((0,), (0,)), ((), ())), preferred_element_...  53.8 us
    ppermute x17, starting transfers between devices, across(): return lax.ppermute(values, 'shard', [(i, i ^ mask) for i in range(shards)])  41.6 us
    all_gather x1, waiting for transfers between devices, per_device(): lax.all_gather(block_qkv, 'shard', axis=0, tiled=True, axis_index_groups=...  40.5 us
    reduce_scatter x3, waiting for transfers between devices, scatter(): lax.psum_scatter(values.astype(bf16), 'shard', scatter_dimension=0, tiled...  39.9 us
  transfers between devices with their start and end apart: 51, of which 33 were waited for; matrix products, arithmetic and copies ran while one was open for 24% of the time, Pallas kernels for 8%

profile of v7, /device:TPU:0, one launch (start us, length us, event | category | flops | bytes accessed | tf_op | source)
XLA Modules:
  0.0 1006.8 jit_solution(7062862805249070049)
XLA Ops:
  30.6 12.2 %collective-permute-done.5 = bf16[272,512]{1,0:T(8,128)(2,1)S(1)} collective-permute-done((bf16[272,512]{1,0:T(8,128)(2,1)S(1)}, bf16[272,512]{1,0:T(8,128)(2,1)S(1)}, u32[]{:S(2)}, u32[]{:S(2)}) %collective-permute-start.5) | collective-permute-done | bytes 278560 | tf_op jit(solution)/shard_map/ppermute | solution.py:281
  42.9 23.1 %collective-permute-done.4 = bf16[272,512]{1,0:T(8,128)(2,1)S(1)} collective-permute-done((bf16[272,512]{1,0:T(8,128)(2,1)S(1)}, bf16[272,512]{1,0:T(8,128)(2,1)S(1)}, u32[]{:S(2)}, u32[]{:S(2)}) %collective-permute-start.4) | collective-permute-done | bytes 278560 | tf_op jit(solution)/shard_map/ppermute | solution.py:281
  84.1 22.6 %collective-permute-done.6 = bf16[1088,512]{1,0:T(8,128)(2,1)} collective-permute-done((bf16[1088,512]{1,0:T(8,128)(2,1)}, bf16[1088,512]{1,0:T(8,128)(2,1)}, u32[]{:S(2)}, u32[]{:S(2)}) %collective-permute-start.6) | collective-permute-done | bytes 1114144 | tf_op jit(solution)/shard_map/ppermute | solution.py:281
  135.4 17.6 %collective-permute-done.16.other = bf16[256,3072]{1,0:T(8,128)(2,1)} collective-permute-done((bf16[256,3072]{1,0:T(8,128)(2,1)}, bf16[256,3072]{1,0:T(8,128)(2,1)}, u32[]{:S(2)}, u32[]{:S(2)}) %collective-permute-start.16) | collective-permute-done | bytes 1572896 | tf_op jit(solution)/shard_map/ppermute | solution.py:281
  156.7 40.5 %all-gather.3.cloned.1.call-done = bf16[2048,1536]{1,0:T(8,128)(2,1)} async-done(((bf16[256,1536]{1,0:T(8,128)(2,1)}), bf16[2048,1536]{1,0:T(8,128)(2,1)}) %all-gather.3.cloned.1.call-update) | async-done | bytes 6291472 | tf_op jit(solution)/shard_map/all_gather | solution.py:363
  198.5 11.8 %fusion.81.qkv_ref = f32[1024,1536]{1,0:T(8,128)} fusion(bf16[1024,2048]{1,0:T(8,128)(2,1)} %get-tuple-element.77, bf16[2048,1536]{1,0:T(8,128)(2,1)} %all-gather.3.cloned.1.call-done), kind=kOutput, calls=%fused_computation.197 | convolution fusion | flops 6442450944 | bytes 16777216 | tf_op jit(solution)/shard_map/dot_general | solution.py:22
  210.3 14.7 %shard_map.206 = (bf16[1024,512]{1,0:T(8,128)(2,1)}, bf16[1024,1536]{1,0:T(8,128)(2,1)}) custom-call(s32[1024]{0:T(1024)} %bitcast.81, f32[1024,1536]{1,0:T(8,128)} %fusion.81.qkv_ref, f32[1024,128]{1,0:T(8,128)} %get-tuple-element.99.cos_ref, f32[1024,128]{1,0:T(8,128)} %get-tuple-element.100.sin_ref, s32[1024,1]{1,0:T(8,128)} %copy.27.seg_col, ...), custom_call_target="tpu_custom_call" | custom-call | tf_op jit(solution)/shard_map/pallas_call | solution.py:195
  240.7 21.2 %collective-permute-done.8 = bf16[256,2048]{1,0:T(8,128)(2,1)} collective-permute-done((bf16[256,2048]{1,0:T(8,128)(2,1)S(1)}, bf16[256,2048]{1,0:T(8,128)(2,1)}, u32[]{:S(2)}, u32[]{:S(2)}) %collective-permute-start.8) | collective-permute-done | bytes 1048608 | tf_op jit(solution)/shard_map/ppermute | solution.py:287
  272.9 18.2 %collective-permute-done.9 = bf16[256,2048]{1,0:T(8,128)(2,1)S(1)} collective-permute-done((bf16[256,2048]{1,0:T(8,128)(2,1)S(1)}, bf16[256,2048]{1,0:T(8,128)(2,1)S(1)}, u32[]{:S(2)}, u32[]{:S(2)}) %collective-permute-start.9) | collective-permute-done | bytes 1048608 | tf_op jit(solution)/shard_map/ppermute | solution.py:287
  293.7 24.4 %collective-permute-done.10 = bf16[256,2048]{1,0:T(8,128)(2,1)S(1)} collective-permute-done((bf16[256,2048]{1,0:T(8,128)(2,1)S(1)}, bf16[256,2048]{1,0:T(8,128)(2,1)S(1)}, u32[]{:S(2)}, u32[]{:S(2)}) %collective-permute-start.10) | collective-permute-done | bytes 1048608 | tf_op jit(solution)/shard_map/ppermute | solution.py:281
  321.4 9.6 collective-permute-done.11
  332.9 47.1 %collective-permute-done.17 = bf16[256,2048]{1,0:T(8,128)(2,1)S(1)} collective-permute-done((bf16[256,2048]{1,0:T(8,128)(2,1)S(1)}, bf16[256,2048]{1,0:T(8,128)(2,1)S(1)}, u32[]{:S(2)}, u32[]{:S(2)}) %collective-permute-start.17) | collective-permute-done | bytes 1048608 | tf_op jit(solution)/shard_map/ppermute | solution.py:281
  381.8 22.9 %collective-permute-done.18 = bf16[256,2048]{1,0:T(8,128)(2,1)S(1)} collective-permute-done((bf16[256,2048]{1,0:T(8,128)(2,1)S(1)}, bf16[256,2048]{1,0:T(8,128)(2,1)S(1)}, u32[]{:S(2)}, u32[]{:S(2)}) %collective-permute-start.18) | collective-permute-done | bytes 1048608 | tf_op jit(solution)/shard_map/ppermute | solution.py:287
  422.7 14.9 %fusion.13 = f32[2048,1024]{1,0:T(8,128)} fusion(bf16[2048,2048]{1,0:T(8,128)(2,1)} %constant_dynamic-update-slice_fusion.7, bf16[2048,3072]{1,0:T(8,128)(2,1)} %all-gather.5.cloned.1.call-done), kind=kOutput, calls=%fused_computation.32 | convolution fusion | flops 8589934592 | bytes 20971520 | tf_op jit(solution)/shard_map/dot_general | solution.py:22
  437.5 12.8 %fusion.17 = f32[2048,1024]{1,0:T(8,128)} fusion(bf16[2048,2048]{1,0:T(8,128)(2,1)S(1)} %copy-done.20, bf16[2048,3072]{1,0:T(8,128)(2,1)} %all-gather.5.cloned.1.call-done), kind=kOutput, calls=%fused_computation.36 | convolution fusion | flops 8589934592 | bytes 20971520 | tf_op jit(solution)/shard_map/dot_general | solution.py:22
  450.3 23.0 %multiply_convert_fusion = (bf16[2048,1024]{1,0:T(8,128)(2,1)}, bf16[2048,1024]{1,0:T(8,128)(2,1)}, bf16[2048,1024]{1,0:T(8,128)(2,1)S(1)}) fusion(f32[2048,1024]{1,0:T(8,128)} %fusion.17, f32[2048,1024]{1,0:T(8,128)} %fusion.13, bf16[2048,2048]{1,0:T(8,128)(2,1)} %constant_dynamic-update-slice_fusion.14, bf16[2048,3072]{1,0:T(8,128)(2,1)} %all-gather.5.cloned.1.call-done), kind=kOutput, calls=%fused_computation.8 | convolution fusion | flops 8621391872 | bytes 41943040 | tf_op jit(solution)/shard_map/dot_general | solution.py:22
  475.3 13.3 %convolution_convert_fusion.4 = bf16[2048,1024]{1,0:T(8,128)(2,1)} fusion(bf16[2048,2048]{1,0:T(8,128)(2,1)} %constant_dynamic-update-slice_fusion.14, bf16[2048,1024]{1,0:T(8,128)(2,1)S(1)} %get-tuple-element.40), kind=kOutput, calls=%fused_computation.22 | convolution fusion | flops 8592031744 | bytes 16777216 | tf_op jit(solution)/shard_map/dot_general | solution.py:26
  505.5 12.1 %fusion.79 = (bf16[1024,2048]{1,0:T(8,128)(2,1)S(1)}, f32[1024,2048]{1,0:T(8,128)}) fusion(bf16[1024,2048]{1,0:T(8,128)(2,1)} %collective-permute-done.20, bf16[2048,3072]{1,0:T(8,128)(2,1)} %all-gather.5.cloned.1.call-done, bf16[2048,1024]{1,0:T(8,128)(2,1)} %copy-done.35), kind=kOutput, calls=%fused_computation.195 | convolution fusion | flops 4301258752 | bytes 23068672 | tf_op jit(solution)/shard_map/dot_general | solution.py:32
  520.3 13.3 %convolution_convert_fusion.3 = bf16[2048,1024]{1,0:T(8,128)(2,1)} fusion(bf16[2048,2048]{1,0:T(8,128)(2,1)} %constant_dynamic-update-slice_fusion.7, bf16[2048,1024]{1,0:T(8,128)(2,1)S(1)} %copy-done.33), kind=kOutput, calls=%fused_computation.21 | convolution fusion | flops 8592031744 | bytes 16777216 | tf_op jit(solution)/shard_map/dot_general | solution.py:26
  533.6 11.0 %convolution_convert_fusion.2 = bf16[2048,1024]{1,0:T(8,128)(2,1)} fusion(bf16[2048,2048]{1,0:T(8,128)(2,1)S(1)} %bitcast.85, bf16[2048,1024]{1,0:T(8,128)(2,1)S(1)} %copy-done.36), kind=kOutput, calls=%fused_computation.20 | convolution fusion | flops 8592031744 | bytes 16777216 | tf_op jit(solution)/shard_map/dot_general | solution.py:26
  552.9 11.1 %collective-permute-done.23 = bf16[512,1024]{1,0:T(8,128)(2,1)S(1)} collective-permute-done((bf16[512,1024]{1,0:T(8,128)(2,1)S(1)}, bf16[512,1024]{1,0:T(8,128)(2,1)S(1)}, u32[]{:S(2)}, u32[]{:S(2)}) %collective-permute-start.23) | collective-permute-done | bytes 1048608 | tf_op jit(solution)/shard_map/ppermute | solution.py:281
  600.7 14.3 %fusion.80 = (bf16[1024,2048]{1,0:T(8,128)(2,1)S(1)}, f32[1024,2048]{1,0:T(8,128)}) fusion(bf16[1024,2048]{1,0:T(8,128)(2,1)} %collective-permute-done.26, f32[1024,2048]{1,0:T(8,128)} %fusion.11, bf16[2048,3072]{1,0:T(8,128)(2,1)} %all-gather.5.cloned.1.call-done, bf16[2048,1024]{1,0:T(8,128)(2,1)} %get-tuple-element.43), kind=kOutput, calls=%fused_computation.196 | convolution fusion | flops 4303355904 | bytes 31457280 | tf_op jit(solution)/shard_map/dot_general | solution.py:32
  617.1 21.7 %collective-permute-done.27 = bf16[512,1024]{1,0:T(8,128)(2,1)S(1)} collective-permute-done((bf16[512,1024]{1,0:T(8,128)(2,1)S(1)}, bf16[512,1024]{1,0:T(8,128)(2,1)S(1)}, u32[]{:S(2)}, u32[]{:S(2)}) %collective-permute-start.27) | collective-permute-done | bytes 1048608 | tf_op jit(solution)/shard_map/ppermute | solution.py:287
  640.9 26.0 %collective-permute-done.29 = bf16[512,1024]{1,0:T(8,128)(2,1)S(1)} collective-permute-done((bf16[512,1024]{1,0:T(8,128)(2,1)S(1)}, bf16[512,1024]{1,0:T(8,128)(2,1)S(1)}, u32[]{:S(2)}, u32[]{:S(2)}) %collective-permute-start.29) | collective-permute-done | bytes 1048608 | tf_op jit(solution)/shard_map/ppermute | solution.py:281
  667.2 22.3 %collective-permute-done.28 = bf16[256,1024]{1,0:T(8,128)(2,1)S(1)} collective-permute-done((bf16[256,1024]{1,0:T(8,128)(2,1)S(1)}, bf16[256,1024]{1,0:T(8,128)(2,1)S(1)}, u32[]{:S(2)}, u32[]{:S(2)}) %collective-permute-start.28) | collective-permute-done | bytes 524320 | tf_op jit(solution)/shard_map/ppermute | solution.py:281
  706.6 21.8 %collective-permute-done.31 = bf16[256,2048]{1,0:T(8,128)(2,1)} collective-permute-done((bf16[256,2048]{1,0:T(8,128)(2,1)S(1)}, bf16[256,2048]{1,0:T(8,128)(2,1)}, u32[]{:S(2)}, u32[]{:S(2)}) %collective-permute-start.31) | collective-permute-done | bytes 1048608 | tf_op jit(solution)/shard_map/ppermute | solution.py:287
  740.7 27.3 %shard_map.212 = bf16[1024,1536]{1,0:T(8,128)(2,1)} custom-call(s32[1024]{0:T(1024)} %bitcast.82, bf16[1024,1536]{1,0:T(8,128)(2,1)} %get-tuple-element.47.kept_ref, bf16[1024,512]{1,0:T(8,128)(2,1)} %convolution_convert_fusion.8.do_ref, f32[1024,128]{1,0:T(8,128)} %get-tuple-element.99.cos_ref, f32[1024,128]{1,0:T(8,128)} %get-tuple-element.100.sin_ref, ...), custom_call_target="tpu_custom_call" | custom-call | tf_op jit(solution)/shard_map/pallas_call | solution.py:254
  815.0 21.6 %collective-permute-done.34 = bf16[256,2048]{1,0:T(8,128)(2,1)S(1)} collective-permute-done((bf16[256,2048]{1,0:T(8,128)(2,1)}, bf16[256,2048]{1,0:T(8,128)(2,1)S(1)}, u32[]{:S(2)}, u32[]{:S(2)}) %collective-permute-start.34) | collective-permute-done | bytes 1048608 | tf_op jit(solution)/shard_map/ppermute | solution.py:287
  846.6 11.9 %collective-permute-done.36 = f32[2,2048]{1,0:T(2,128)S(1)} collective-permute-done((f32[2,2048]{1,0:T(2,128)S(1)}, f32[2,2048]{1,0:T(2,128)S(1)}, u32[]{:S(2)}, u32[]{:S(2)}) %collective-permute-start.36) | collective-permute-done | bytes 16416 | tf_op jit(solution)/shard_map/ppermute | solution.py:287
  863.7 30.7 %collective-permute-done.41.theirs = bf16[256,2048]{1,0:T(8,128)(2,1)S(1)} collective-permute-done((bf16[256,2048]{1,0:T(8,128)(2,1)S(1)}, bf16[256,2048]{1,0:T(8,128)(2,1)S(1)}, u32[]{:S(2)}, u32[]{:S(2)}) %collective-permute-start.41) | collective-permute-done | bytes 1048608 | tf_op jit(solution)/shard_map/ppermute | solution.py:281
  899.0 28.8 %collective-permute-start.38 = (f32[2,512]{1,0:T(2,128)S(1)}, f32[2,512]{1,0:T(2,128)S(1)}, u32[]{:S(2)}, u32[]{:S(2)}) collective-permute-start(f32[2,512]{1,0:T(2,128)S(1)} %broadcast_select_fusion.1), channel_id=1, source_target_pairs={{0,4},{4,0},{8,12},{12,8},{16,20},{20,16},{24,28},{28,24},{1,5},{5... | collective-permute-start | bytes 12296 | tf_op jit(solution)/shard_map/ppermute | solution.py:281
  951.7 39.9 %reduce-scatter.4.cloned.1.call-done.own = bf16[256,2048]{1,0:T(8,128)(2,1)} async-done(((bf16[2048,2048]{1,0:T(8,128)(2,1)}), bf16[256,2048]{1,0:T(8,128)(2,1)}) %reduce-scatter.4.cloned.1.call-update) | async-done | bytes 1048592 | tf_op jit(solution)/shard_map/reduce_scatter | solution.py:507
  (290 shorter events, 328.4 us)
Async XLA Ops:
  7.2 190.1 %all-gather.3.cloned.1.call-start = ((), (), s32[]{:S(2)}) async-start(), calls=%async_computation.3 | async-start | bytes 7077888 | tf_op jit(solution)/shard_map/all_gather | solution.py:363
  15.6 407.1 %all-gather.5.cloned.1.call-start = ((), (), s32[]{:S(2)}) async-start(), calls=%async_computation.4 | async-start | bytes 15728640 | tf_op jit(solution)/shard_map/all_gather | solution.py:412
  18.8 56.7 %collective-permute-start.15 = (bf16[128,6144]{1,0:T(8,128)(2,1)}, bf16[128,6144]{1,0:T(8,128)(2,1)S(1)}, u32[]{:S(2)}, u32[]{:S(2)}) collective-permute-start(bf16[128,6144]{1,0:T(8,128)(2,1)} %shard_map.207), channel_id=1, source_target_pairs={{0,2},{2,0},{1,3},{3,1},{4,6},{6,4},{5,7},{7,5},{8,10},{10,8},{9,1... | collective-permute-start | bytes 4718600 | tf_op jit(solution)/shard_map/ppermute | solution.py:284
  24.0 101.2 %collective-permute-start = (bf16[512,2048]{1,0:T(8,128)(2,1)}, bf16[512,2048]{1,0:T(8,128)(2,1)}, u32[]{:S(2)}, u32[]{:S(2)}) collective-permute-start(bf16[512,2048]{1,0:T(8,128)(2,1)} %shard_map.203), channel_id=1, source_target_pairs={{0,2},{2,0},{1,3},{3,1},{4,6},{6,4},{5,7},{7,5},{8,10},{10,8},{9,1... | collective-permute-start | bytes 6291464 | tf_op jit(solution)/shard_map/ppermute | solution.py:284
  29.4 36.6 %collective-permute-start.4 = (bf16[272,512]{1,0:T(8,128)(2,1)S(1)}, bf16[272,512]{1,0:T(8,128)(2,1)S(1)}, u32[]{:S(2)}, u32[]{:S(2)}) collective-permute-start(bf16[272,512]{1,0:T(8,128)(2,1)S(1)} %copy-done.12), channel_id=1, source_target_pairs={{0,16},{4,20},{8,24},{12,28},{16,0},{20,4},{24,8},{28,12},{1,17},{... | collective-permute-start | bytes 835592 | tf_op jit(solution)/shard_map/ppermute | solution.py:281
  29.4 36.7 %collective-permute-start.3 = (bf16[272,512]{1,0:T(8,128)(2,1)S(1)}, bf16[272,512]{1,0:T(8,128)(2,1)S(1)}, u32[]{:S(2)}, u32[]{:S(2)}) collective-permute-start(bf16[272,512]{1,0:T(8,128)(2,1)S(1)} %copy-done.12), channel_id=1, source_target_pairs={{0,8},{4,12},{8,0},{12,4},{16,24},{20,28},{24,16},{28,20},{1,9},{5... | collective-permute-start | bytes 835592 | tf_op jit(solution)/shard_map/ppermute | solution.py:281
  67.2 39.5 %collective-permute-start.6 = (bf16[1088,512]{1,0:T(8,128)(2,1)}, bf16[1088,512]{1,0:T(8,128)(2,1)}, u32[]{:S(2)}, u32[]{:S(2)}) collective-permute-start(bf16[1088,512]{1,0:T(8,128)(2,1)} %pad_maximum_fusion.5), channel_id=1, source_target_pairs={{0,4},{4,0},{8,12},{12,8},{16,20},{20,16},{24,28},{28,24},{1,5},{5... | collective-permute-start | bytes 3342344 | tf_op jit(solution)/shard_map/ppermute | solution.py:281
  81.5 71.4 %collective-permute-start.16 = (bf16[256,3072]{1,0:T(8,128)(2,1)}, bf16[256,3072]{1,0:T(8,128)(2,1)}, u32[]{:S(2)}, u32[]{:S(2)}) collective-permute-start(bf16[256,3072]{1,0:T(8,128)(2,1)} %get-tuple-element.37), channel_id=1, source_target_pairs={{0,8},{4,12},{8,0},{12,4},{16,24},{20,28},{24,16},{28,20},{1,9},{5... | collective-permute-start | bytes 4718600 | tf_op jit(solution)/shard_map/ppermute | solution.py:281
  197.3 615.1 %reduce-scatter.8.cloned.1.call-start = ((), (), s32[]{:S(2)}) async-start(), calls=%async_computation.7 | async-start | bytes 5242880 | tf_op jit(solution)/shard_map/reduce_scatter | solution.py:507
  236.6 25.4 %collective-permute-start.8 = (bf16[256,2048]{1,0:T(8,128)(2,1)S(1)}, bf16[256,2048]{1,0:T(8,128)(2,1)}, u32[]{:S(2)}, u32[]{:S(2)}) collective-permute-start(bf16[256,2048]{1,0:T(8,128)(2,1)S(1)} %add_convert_fusion.2), channel_id=1, source_target_pairs={{0,1},{1,0},{2,3},{3,2},{4,5},{5,4},{6,7},{7,6},{8,9},{9,8},{10,11... | collective-permute-start | bytes 3145736 | tf_op jit(solution)/shard_map/ppermute | solution.py:287
  266.8 24.3 %collective-permute-start.9 = (bf16[256,2048]{1,0:T(8,128)(2,1)S(1)}, bf16[256,2048]{1,0:T(8,128)(2,1)S(1)}, u32[]{:S(2)}, u32[]{:S(2)}) collective-permute-start(bf16[256,2048]{1,0:T(8,128)(2,1)S(1)} %get-tuple-element.66), channel_id=1, source_target_pairs={{0,1},{1,0},{2,3},{3,2},{4,5},{5,4},{6,7},{7,6},{8,9},{9,8},{10,11... | collective-permute-start | bytes 3145736 | tf_op jit(solution)/shard_map/ppermute | solution.py:287
  268.4 49.8 %collective-permute-start.10 = (bf16[256,2048]{1,0:T(8,128)(2,1)S(1)}, bf16[256,2048]{1,0:T(8,128)(2,1)S(1)}, u32[]{:S(2)}, u32[]{:S(2)}) collective-permute-start(bf16[256,2048]{1,0:T(8,128)(2,1)S(1)} %get-tuple-element.66), channel_id=1, source_target_pairs={{0,8},{4,12},{8,0},{12,4},{16,24},{20,28},{24,16},{28,20},{1,9},{5... | collective-permute-start | bytes 3145736 | tf_op jit(solution)/shard_map/ppermute | solution.py:281
  291.2 39.8 %collective-permute-start.11 = (bf16[128,2048]{1,0:T(8,128)(2,1)S(1)}, bf16[128,2048]{1,0:T(8,128)(2,1)S(1)}, u32[]{:S(2)}, u32[]{:S(2)}) collective-permute-start(bf16[128,2048]{1,0:T(8,128)(2,1)S(1)} %slice.275), channel_id=1, source_target_pairs={{0,8},{4,12},{8,0},{12,4},{16,24},{20,28},{24,16},{28,20},{1,9},{5... | collective-permute-start | bytes 1572872 | tf_op jit(solution)/shard_map/ppermute | solution.py:281
  332.9 47.1 %collective-permute-start.17 = (bf16[256,2048]{1,0:T(8,128)(2,1)S(1)}, bf16[256,2048]{1,0:T(8,128)(2,1)S(1)}, u32[]{:S(2)}, u32[]{:S(2)}) collective-permute-start(bf16[256,2048]{1,0:T(8,128)(2,1)S(1)} %get-tuple-element.39), channel_id=1, source_target_pairs={{0,8},{4,12},{8,0},{12,4},{16,24},{20,28},{24,16},{28,20},{1,9},{5... | collective-permute-start | bytes 3145736 | tf_op jit(solution)/shard_map/ppermute | solution.py:281
  380.0 24.6 %collective-permute-start.18 = (bf16[256,2048]{1,0:T(8,128)(2,1)S(1)}, bf16[256,2048]{1,0:T(8,128)(2,1)S(1)}, u32[]{:S(2)}, u32[]{:S(2)}) collective-permute-start(bf16[256,2048]{1,0:T(8,128)(2,1)S(1)} %collective-permute-done.17), channel_id=1, source_target_pairs={{0,1},{1,0},{2,3},{3,2},{4,5},{5,4},{6,7},{7,6},{8,9},{9,8},{10,11... | collective-permute-start | bytes 3145736 | tf_op jit(solution)/shard_map/ppermute | solution.py:287
  498.0 347.2 %reduce-scatter.6.cloned.1.call-start = ((), (), s32[]{:S(2)}) async-start(), calls=%async_computation.6 | async-start | bytes 10485760 | tf_op jit(solution)/shard_map/reduce_scatter | solution.py:507
  518.8 34.1 %collective-permute-start.21 = (bf16[512,1024]{1,0:T(8,128)(2,1)}, bf16[512,1024]{1,0:T(8,128)(2,1)S(1)}, u32[]{:S(2)}, u32[]{:S(2)}) collective-permute-start(bf16[512,1024]{1,0:T(8,128)(2,1)} %pad_maximum_fusion.6), channel_id=1, source_target_pairs={{0,1},{1,0},{2,3},{3,2},{4,5},{5,4},{6,7},{7,6},{8,9},{9,8},{10,11... | collective-permute-start | bytes 3145736 | tf_op jit(solution)/shard_map/ppermute | solution.py:287
  520.2 43.7 %collective-permute-start.23 = (bf16[512,1024]{1,0:T(8,128)(2,1)S(1)}, bf16[512,1024]{1,0:T(8,128)(2,1)S(1)}, u32[]{:S(2)}, u32[]{:S(2)}) collective-permute-start(bf16[512,1024]{1,0:T(8,128)(2,1)S(1)} %concatenate.113), channel_id=1, source_target_pairs={{0,8},{4,12},{8,0},{12,4},{16,24},{20,28},{24,16},{28,20},{1,9},{5... | collective-permute-start | bytes 3145736 | tf_op jit(solution)/shard_map/ppermute | solution.py:281
  579.8 20.9 %collective-permute-start.26 = (bf16[1024,2048]{1,0:T(8,128)(2,1)}, bf16[1024,2048]{1,0:T(8,128)(2,1)}, u32[]{:S(2)}, u32[]{:S(2)}) collective-permute-start(bf16[1024,2048]{1,0:T(8,128)(2,1)} %add_convert_fusion), channel_id=1, source_target_pairs={{0,2},{2,0},{1,3},{3,1},{4,6},{6,4},{5,7},{7,5},{8,10},{10,8},{9,1... | collective-permute-start | bytes 12582920 | tf_op jit(solution)/shard_map/ppermute | solution.py:284
  579.9 411.7 %reduce-scatter.4.cloned.1.call-start = ((), (), s32[]{:S(2)}) async-start(), calls=%async_computation.5 | async-start | bytes 9437184 | tf_op jit(solution)/shard_map/reduce_scatter | solution.py:507
  615.3 23.5 %collective-permute-start.27 = (bf16[512,1024]{1,0:T(8,128)(2,1)S(1)}, bf16[512,1024]{1,0:T(8,128)(2,1)S(1)}, u32[]{:S(2)}, u32[]{:S(2)}) collective-permute-start(bf16[512,1024]{1,0:T(8,128)(2,1)S(1)} %pad_maximum_fusion.7), channel_id=1, source_target_pairs={{0,1},{1,0},{2,3},{3,2},{4,5},{5,4},{6,7},{7,6},{8,9},{9,8},{10,11... | collective-permute-start | bytes 3145736 | tf_op jit(solution)/shard_map/ppermute | solution.py:287
  615.9 51.0 %collective-permute-start.29 = (bf16[512,1024]{1,0:T(8,128)(2,1)S(1)}, bf16[512,1024]{1,0:T(8,128)(2,1)S(1)}, u32[]{:S(2)}, u32[]{:S(2)}) collective-permute-start(bf16[512,1024]{1,0:T(8,128)(2,1)S(1)} %concatenate.114), channel_id=1, source_target_pairs={{0,8},{4,12},{8,0},{12,4},{16,24},{20,28},{24,16},{28,20},{1,9},{5... | collective-permute-start | bytes 3145736 | tf_op jit(solution)/shard_map/ppermute | solution.py:281
  639.2 50.2 %collective-permute-start.28 = (bf16[256,1024]{1,0:T(8,128)(2,1)S(1)}, bf16[256,1024]{1,0:T(8,128)(2,1)S(1)}, u32[]{:S(2)}, u32[]{:S(2)}) collective-permute-start(bf16[256,1024]{1,0:T(8,128)(2,1)S(1)} %fusion.31), channel_id=1, source_target_pairs={{0,8},{4,12},{8,0},{12,4},{16,24},{20,28},{24,16},{28,20},{1,9},{5... | collective-permute-start | bytes 1572872 | tf_op jit(solution)/shard_map/ppermute | solution.py:281
  705.3 23.1 %collective-permute-start.31 = (bf16[256,2048]{1,0:T(8,128)(2,1)S(1)}, bf16[256,2048]{1,0:T(8,128)(2,1)}, u32[]{:S(2)}, u32[]{:S(2)}) collective-permute-start(bf16[256,2048]{1,0:T(8,128)(2,1)S(1)} %get-tuple-element.59), channel_id=1, source_target_pairs={{0,1},{1,0},{2,3},{3,2},{4,5},{5,4},{6,7},{7,6},{8,9},{9,8},{10,11... | collective-permute-start | bytes 3145736 | tf_op jit(solution)/shard_map/ppermute | solution.py:287
  810.3 26.2 %collective-permute-start.34 = (bf16[256,2048]{1,0:T(8,128)(2,1)}, bf16[256,2048]{1,0:T(8,128)(2,1)S(1)}, u32[]{:S(2)}, u32[]{:S(2)}) collective-permute-start(bf16[256,2048]{1,0:T(8,128)(2,1)} %fusion.20), channel_id=1, source_target_pairs={{0,1},{1,0},{2,3},{3,2},{4,5},{5,4},{6,7},{7,6},{8,9},{9,8},{10,11... | collective-permute-start | bytes 3145736 | tf_op jit(solution)/shard_map/ppermute | solution.py:287
  814.2 113.6 %collective-permute-start.43 = (bf16[256,1024]{1,0:T(8,128)(2,1)}, bf16[256,1024]{1,0:T(8,128)(2,1)}, u32[]{:S(2)}, u32[]{:S(2)}) collective-permute-start(bf16[256,1024]{1,0:T(8,128)(2,1)} %constant_dynamic-slice_fusion), channel_id=1, source_target_pairs={{0,8},{4,12},{8,0},{12,4},{16,24},{20,28},{24,16},{28,20},{1,9},{5... | collective-permute-start | bytes 1572872 | tf_op jit(solution)/shard_map/ppermute | solution.py:281
  814.2 123.0 %collective-permute-start.25 = (bf16[256,2048]{1,0:T(8,128)(2,1)}, bf16[256,2048]{1,0:T(8,128)(2,1)}, u32[]{:S(2)}, u32[]{:S(2)}) collective-permute-start(bf16[256,2048]{1,0:T(8,128)(2,1)} %get-tuple-element.82.own_ref), channel_id=1, source_target_pairs={{0,1},{1,0},{2,3},{3,2},{4,5},{5,4},{6,7},{7,6},{8,9},{9,8},{10,11... | collective-permute-start | bytes 3145736 | tf_op jit(solution)/shard_map/ppermute | solution.py:287
  846.5 47.9 %collective-permute-start.41 = (bf16[256,2048]{1,0:T(8,128)(2,1)S(1)}, bf16[256,2048]{1,0:T(8,128)(2,1)S(1)}, u32[]{:S(2)}, u32[]{:S(2)}) collective-permute-start(bf16[256,2048]{1,0:T(8,128)(2,1)S(1)} %constant_dynamic-slice_fusion.1), channel_id=1, source_target_pairs={{0,8},{4,12},{8,0},{12,4},{16,24},{20,28},{24,16},{28,20},{1,9},{5... | collective-permute-start | bytes 3145736 | tf_op jit(solution)/shard_map/ppermute | solution.py:281
  858.5 40.4 %collective-permute-start.37 = (f32[2,1024]{1,0:T(2,128)S(1)}, f32[2,1024]{1,0:T(2,128)S(1)}, u32[]{:S(2)}, u32[]{:S(2)}) collective-permute-start(f32[2,1024]{1,0:T(2,128)S(1)} %broadcast_select_fusion), channel_id=1, source_target_pairs={{0,16},{4,20},{8,24},{12,28},{16,0},{20,4},{24,8},{28,12},{1,17},{... | collective-permute-start | bytes 24584 | tf_op jit(solution)/shard_map/ppermute | solution.py:281
  862.4 78.6 %collective-permute-start.35 = (bf16[256,2048]{1,0:T(8,128)(2,1)}, bf16[256,2048]{1,0:T(8,128)(2,1)S(1)}, u32[]{:S(2)}, u32[]{:S(2)}) collective-permute-start(bf16[256,2048]{1,0:T(8,128)(2,1)} %add_convert_fusion.1.own_ref), channel_id=1, source_target_pairs={{0,1},{1,0},{2,3},{3,2},{4,5},{5,4},{6,7},{7,6},{8,9},{9,8},{10,11... | collective-permute-start | bytes 3145736 | tf_op jit(solution)/shard_map/ppermute | solution.py:287
  899.0 46.7 %collective-permute-start.42 = (bf16[128,4096]{1,0:T(8,128)(2,1)}, bf16[128,4096]{1,0:T(8,128)(2,1)S(1)}, u32[]{:S(2)}, u32[]{:S(2)}) collective-permute-start(bf16[128,4096]{1,0:T(8,128)(2,1)} %shard_map.214), channel_id=1, source_target_pairs={{0,2},{2,0},{1,3},{3,1},{4,6},{6,4},{5,7},{7,5},{8,10},{10,8},{9,1... | collective-permute-start | bytes 3145736 | tf_op jit(solution)/shard_map/ppermute | solution.py:284
  899.0 31.9 %collective-permute-start.38 = (f32[2,512]{1,0:T(2,128)S(1)}, f32[2,512]{1,0:T(2,128)S(1)}, u32[]{:S(2)}, u32[]{:S(2)}) collective-permute-start(f32[2,512]{1,0:T(2,128)S(1)} %broadcast_select_fusion.1), channel_id=1, source_target_pairs={{0,4},{4,0},{8,12},{12,8},{16,20},{20,16},{24,28},{28,24},{1,5},{5... | collective-permute-start | bytes 12296 | tf_op jit(solution)/shard_map/ppermute | solution.py:281
  (59 other events, 922.2 us)
Sparse Core Ops, SparseCore 0:
  15.7 181.5 all-gather.2
  199.1 223.5 all-gather.4
  498.1 86.3 reduce-scatter.7
  587.4 153.6 reduce-scatter.5
  792.8 198.8 reduce-scatter.3

commit v8 on v7

--- a/solution.py
+++ b/solution.py
@@ -508,9 +508,10 @@
                 values.astype(bf16), "shard", scatter_dimension=0, tiled=True, axis_index_groups=members
             )
 
-        def rows_pair(own, count):
-            other = across(rows_of(own, (1 - zl) * block, block), 2)
-
+        def away_rows(own):
+            return across(rows_of(own, (1 - zl) * block, block), 2)
+
+        def rows_pair(own, other, count):
             def send_rows(s_ref, mine, theirs, out):
                 low, away_rows = s_ref[1], pl.multiple_of((1 - s_ref[0]) * unit, unit)
                 rows_m = pl.ds(pl.multiple_of(low * block, block) + away_rows, unit)
@@ -546,13 +547,16 @@
 
         own_d = scatter(prod_d, groups)
         own_gu = scatter(prod_gu, groups)
+        late_o = contract_rows(grad_attn, mixed).astype(bf16)
+        own_o = scatter(after(late_o, own_d, own_gu), every)
+        grad_mixed = after(grad_mixed, late_o)
         grad_qkv = attend_backward(kept, grad_mixed, seg_row, cosine, sine, 0, heads)
-        own_a = scatter(
-            cat([contract_rows(h_one, grad_qkv).astype(bf16), contract_rows(grad_attn, mixed).astype(bf16)], 1), every
-        )
-
-        (grad_w_down,) = rows_pair(own_d, 1)
-        grad_w_gate, grad_w_up = rows_pair(own_gu, 2)
+        other_d, other_gu = away_rows(own_d), away_rows(own_gu)
+        grad_qkv = after(grad_qkv, other_gu)
+        own_qkv = scatter(after(contract_rows(h_one, grad_qkv).astype(bf16), own_o), every)
+
+        (grad_w_down,) = rows_pair(own_d, other_d, 1)
+        grad_w_gate, grad_w_up = rows_pair(own_gu, other_gu, 2)
 
         grad_h_one = to_slice(grad_qkv, lambda v: contract_cols(v, weight_qkv))
 
@@ -562,7 +566,8 @@
         grad_x = (grad_after + norm_back(grad_h_one * gain_a, normed_part, inverse_part)).astype(bf16)
         grad_tokens = join_tokens(grad_x, swap_tp(grad_x), half, nat, block)
 
-        own_a = after(own_a, output, grad_tokens, grad_w_gate, grad_w_up, grad_w_down)
+        own_qkv = after(own_qkv, output, grad_tokens, grad_w_gate, grad_w_up, grad_w_down)
+        own_a = cat([own_qkv, own_o], 1)
         (sent_g,) = small_call(send_unit, [core], [own_a], [array_of(unit, 4 * n_attn)])
         other_a = swap_core(sent_g)
 

time: 1010 us -> 985 us (0.975)
  waiting for transfers between devices: 515 us -> 501 us
  starting transfers between devices: 61 us -> 49.9 us
    ppermute x17, waiting for transfers between devices: 252 us -> 232 us  [across(): return lax.ppermute(values, 'shard', [(i, i ^ mask) for i in range(shards)])]
    ppermute x17, starting transfers between devices: 41.6 us -> 29.3 us  [across(): return lax.ppermute(values, 'shard', [(i, i ^ mask) for i in range(shards)])]
    concatenate x10 -> x9, other arithmetic: 21.6 us -> 13.3 us  [cat(): return jnp.concatenate(parts, axis=axis)]
    reduce_scatter x3 -> x4, waiting for transfers between devices: 39.9 us -> 47.7 us  [scatter(): lax.psum_scatter(values.astype(bf16), 'shard', scatter_dimension=0, tiled...]
    unnamed x92 -> x95, local copies, waits for them, and re-layouts: 24.7 us -> 26 us
  transfers between devices with their start and end apart: 51 -> 52, of which waited for: 33 -> 35; matrix products, arithmetic and copies ran while one was open for 24% -> 24% of each run, Pallas kernels for 8% -> 9%
where the time goes in v8:
time: 985 us; the launch traced here: 978 us
  waiting for transfers between devices  501 us (51%)
  matrix products  216 us (22%)
  Pallas kernels  95.4 us (10%)
  local copies, waits for them, and re-layouts  55 us (6%)
  starting transfers between devices  49.9 us (5%)
  other arithmetic  45.2 us (5%)
  between operations  15.3 us (2%)
    ppermute x17, waiting for transfers between devices, across(): return lax.ppermute(values, 'shard', [(i, i ^ mask) for i in range(shards)])  232 us
    ppermute x13, waiting for transfers between devices, swap_tp(): return lax.ppermute(values, 'tp', [(0, 1), (1, 0)])  147 us
    dot_general x12, matrix products, contract_cols(): lax.dot_general(left, right, (((1,), (1,)), ((), ())), preferred_element_...  93.2 us
    dot_general x5, matrix products, matmul(): return jnp.dot(left, right, preferred_element_type=jnp.float32)  70.2 us
    dot_general x5, matrix products, contract_rows(): lax.dot_general(left, right, (((0,), (0,)), ((), ())), preferred_element_...  53 us
    reduce_scatter x4, waiting for transfers between devices, scatter(): lax.psum_scatter(values.astype(bf16), 'shard', scatter_dimension=0, tiled...  47.7 us
    all_gather x1, waiting for transfers between devices, per_device(): lax.all_gather(block_qkv, 'shard', axis=0, tiled=True, axis_index_groups=...  40.6 us
    pallas_call x11, Pallas kernels, small_call(): pl.pallas_call(body, grid_spec=pltpu.PrefetchScalarGridSpec(num_scalar_pr...  36.7 us
  transfers between devices with their start and end apart: 52, of which 35 were waited for; matrix products, arithmetic and copies ran while one was open for 24% of the time, Pallas kernels for 9%

profile of v8, /device:TPU:0, one launch (start us, length us, event | category | flops | bytes accessed | tf_op | source)
XLA Modules:
  0.0 978.4 jit_solution(15904078680656509911)
XLA Ops:
  30.6 12.2 %collective-permute-done.5 = bf16[272,512]{1,0:T(8,128)(2,1)S(1)} collective-permute-done((bf16[272,512]{1,0:T(8,128)(2,1)S(1)}, bf16[272,512]{1,0:T(8,128)(2,1)S(1)}, u32[]{:S(2)}, u32[]{:S(2)}) %collective-permute-start.5) | collective-permute-done | bytes 278560 | tf_op jit(solution)/shard_map/ppermute | solution.py:281
  42.9 23.1 %collective-permute-done.4 = bf16[272,512]{1,0:T(8,128)(2,1)S(1)} collective-permute-done((bf16[272,512]{1,0:T(8,128)(2,1)S(1)}, bf16[272,512]{1,0:T(8,128)(2,1)S(1)}, u32[]{:S(2)}, u32[]{:S(2)}) %collective-permute-start.4) | collective-permute-done | bytes 278560 | tf_op jit(solution)/shard_map/ppermute | solution.py:281
  84.0 22.6 %collective-permute-done.6 = bf16[1088,512]{1,0:T(8,128)(2,1)} collective-permute-done((bf16[1088,512]{1,0:T(8,128)(2,1)}, bf16[1088,512]{1,0:T(8,128)(2,1)}, u32[]{:S(2)}, u32[]{:S(2)}) %collective-permute-start.6) | collective-permute-done | bytes 1114144 | tf_op jit(solution)/shard_map/ppermute | solution.py:281
  135.5 17.4 %collective-permute-done.16.other = bf16[256,3072]{1,0:T(8,128)(2,1)} collective-permute-done((bf16[256,3072]{1,0:T(8,128)(2,1)}, bf16[256,3072]{1,0:T(8,128)(2,1)}, u32[]{:S(2)}, u32[]{:S(2)}) %collective-permute-start.16) | collective-permute-done | bytes 1572896 | tf_op jit(solution)/shard_map/ppermute | solution.py:281
  156.7 40.6 %all-gather.3.cloned.1.call-done = bf16[2048,1536]{1,0:T(8,128)(2,1)} async-done(((bf16[256,1536]{1,0:T(8,128)(2,1)}), bf16[2048,1536]{1,0:T(8,128)(2,1)}) %all-gather.3.cloned.1.call-update) | async-done | bytes 6291472 | tf_op jit(solution)/shard_map/all_gather | solution.py:363
  198.6 11.8 %fusion.81.qkv_ref = f32[1024,1536]{1,0:T(8,128)} fusion(bf16[1024,2048]{1,0:T(8,128)(2,1)} %get-tuple-element.85, bf16[2048,1536]{1,0:T(8,128)(2,1)} %all-gather.3.cloned.1.call-done), kind=kOutput, calls=%fused_computation.198 | convolution fusion | flops 6442450944 | bytes 16777216 | tf_op jit(solution)/shard_map/dot_general | solution.py:22
  210.3 14.9 %shard_map.206 = (bf16[1024,512]{1,0:T(8,128)(2,1)}, bf16[1024,1536]{1,0:T(8,128)(2,1)}) custom-call(s32[1024]{0:T(1024)} %bitcast.81, f32[1024,1536]{1,0:T(8,128)} %fusion.81.qkv_ref, f32[1024,128]{1,0:T(8,128)} %get-tuple-element.107.cos_ref, f32[1024,128]{1,0:T(8,128)} %get-tuple-element.108.sin_ref, s32[1024,1]{1,0:T(8,128)} %copy.25.seg_col, ...), custom_call_target="tpu_custom_call" | custom-call | tf_op jit(solution)/shard_map/pallas_call | solution.py:195
  240.9 21.2 %collective-permute-done.8 = bf16[256,2048]{1,0:T(8,128)(2,1)} collective-permute-done((bf16[256,2048]{1,0:T(8,128)(2,1)S(1)}, bf16[256,2048]{1,0:T(8,128)(2,1)}, u32[]{:S(2)}, u32[]{:S(2)}) %collective-permute-start.8) | collective-permute-done | bytes 1048608 | tf_op jit(solution)/shard_map/ppermute | solution.py:287
  273.9 17.3 %collective-permute-done.9 = bf16[256,2048]{1,0:T(8,128)(2,1)S(1)} collective-permute-done((bf16[256,2048]{1,0:T(8,128)(2,1)S(1)}, bf16[256,2048]{1,0:T(8,128)(2,1)S(1)}, u32[]{:S(2)}, u32[]{:S(2)}) %collective-permute-start.9) | collective-permute-done | bytes 1048608 | tf_op jit(solution)/shard_map/ppermute | solution.py:287
  294.8 23.3 %collective-permute-done.10 = bf16[256,2048]{1,0:T(8,128)(2,1)S(1)} collective-permute-done((bf16[256,2048]{1,0:T(8,128)(2,1)S(1)}, bf16[256,2048]{1,0:T(8,128)(2,1)S(1)}, u32[]{:S(2)}, u32[]{:S(2)}) %collective-permute-start.10) | collective-permute-done | bytes 1048608 | tf_op jit(solution)/shard_map/ppermute | solution.py:281
  332.9 47.4 %collective-permute-done.17 = bf16[256,2048]{1,0:T(8,128)(2,1)S(1)} collective-permute-done((bf16[256,2048]{1,0:T(8,128)(2,1)S(1)}, bf16[256,2048]{1,0:T(8,128)(2,1)S(1)}, u32[]{:S(2)}, u32[]{:S(2)}) %collective-permute-start.17) | collective-permute-done | bytes 1048608 | tf_op jit(solution)/shard_map/ppermute | solution.py:281
  382.0 22.5 %collective-permute-done.18 = bf16[256,2048]{1,0:T(8,128)(2,1)S(1)} collective-permute-done((bf16[256,2048]{1,0:T(8,128)(2,1)S(1)}, bf16[256,2048]{1,0:T(8,128)(2,1)S(1)}, u32[]{:S(2)}, u32[]{:S(2)}) %collective-permute-start.18) | collective-permute-done | bytes 1048608 | tf_op jit(solution)/shard_map/ppermute | solution.py:287
  422.7 14.9 %fusion.13 = f32[2048,1024]{1,0:T(8,128)} fusion(bf16[2048,2048]{1,0:T(8,128)(2,1)} %constant_dynamic-update-slice_fusion.7, bf16[2048,3072]{1,0:T(8,128)(2,1)} %all-gather.5.cloned.1.call-done), kind=kOutput, calls=%fused_computation.31 | convolution fusion | flops 8589934592 | bytes 20971520 | tf_op jit(solution)/shard_map/dot_general | solution.py:22
  437.6 12.8 %fusion.17 = f32[2048,1024]{1,0:T(8,128)} fusion(bf16[2048,2048]{1,0:T(8,128)(2,1)S(1)} %copy-done.21, bf16[2048,3072]{1,0:T(8,128)(2,1)} %all-gather.5.cloned.1.call-done), kind=kOutput, calls=%fused_computation.35 | convolution fusion | flops 8589934592 | bytes 20971520 | tf_op jit(solution)/shard_map/dot_general | solution.py:22
  450.4 23.2 %multiply_convert_fusion = (bf16[2048,1024]{1,0:T(8,128)(2,1)}, bf16[2048,1024]{1,0:T(8,128)(2,1)}, bf16[2048,1024]{1,0:T(8,128)(2,1)S(1)}) fusion(f32[2048,1024]{1,0:T(8,128)} %fusion.17, f32[2048,1024]{1,0:T(8,128)} %fusion.13, bf16[2048,2048]{1,0:T(8,128)(2,1)} %constant_dynamic-update-slice_fusion.14, bf16[2048,3072]{1,0:T(8,128)(2,1)} %all-gather.5.cloned.1.call-done), kind=kOutput, calls=%fused_computation.7 | convolution fusion | flops 8621391872 | bytes 41943040 | tf_op jit(solution)/shard_map/dot_general | solution.py:22
  475.5 13.0 %convolution_convert_fusion.4 = bf16[2048,1024]{1,0:T(8,128)(2,1)} fusion(bf16[2048,2048]{1,0:T(8,128)(2,1)} %constant_dynamic-update-slice_fusion.14, bf16[2048,1024]{1,0:T(8,128)(2,1)S(1)} %get-tuple-element.44), kind=kOutput, calls=%fused_computation.21 | convolution fusion | flops 8592031744 | bytes 16777216 | tf_op jit(solution)/shard_map/dot_general | solution.py:26
  505.4 12.0 %fusion.79 = (bf16[1024,2048]{1,0:T(8,128)(2,1)S(1)}, f32[1024,2048]{1,0:T(8,128)}) fusion(bf16[1024,2048]{1,0:T(8,128)(2,1)} %collective-permute-done.20, bf16[2048,3072]{1,0:T(8,128)(2,1)} %all-gather.5.cloned.1.call-done, bf16[2048,1024]{1,0:T(8,128)(2,1)} %copy-done.36), kind=kOutput, calls=%fused_computation.196 | convolution fusion | flops 4301258752 | bytes 23068672 | tf_op jit(solution)/shard_map/dot_general | solution.py:32
  520.3 13.4 %convolution_convert_fusion.3 = bf16[2048,1024]{1,0:T(8,128)(2,1)} fusion(bf16[2048,2048]{1,0:T(8,128)(2,1)} %constant_dynamic-update-slice_fusion.7, bf16[2048,1024]{1,0:T(8,128)(2,1)S(1)} %copy-done.34), kind=kOutput, calls=%fused_computation.20 | convolution fusion | flops 8592031744 | bytes 16777216 | tf_op jit(solution)/shard_map/dot_general | solution.py:26
  533.7 11.0 %convolution_convert_fusion.2 = bf16[2048,1024]{1,0:T(8,128)(2,1)} fusion(bf16[2048,2048]{1,0:T(8,128)(2,1)S(1)} %bitcast.85, bf16[2048,1024]{1,0:T(8,128)(2,1)S(1)} %copy-done.37), kind=kOutput, calls=%fused_computation.19 | convolution fusion | flops 8592031744 | bytes 16777216 | tf_op jit(solution)/shard_map/dot_general | solution.py:26
  563.9 10.7 %fusion.9 = f32[1024,2048]{1,0:T(8,128)} fusion(bf16[2048,3072]{1,0:T(8,128)(2,1)} %all-gather.5.cloned.1.call-done, bf16[2048,1024]{1,0:T(8,128)(2,1)} %get-tuple-element.48), kind=kOutput, calls=%fused_computation.27 | convolution fusion | flops 4294967296 | bytes 14680064 | tf_op jit(solution)/shard_map/dot_general | solution.py:32
  605.3 14.4 %fusion.80 = (bf16[1024,2048]{1,0:T(8,128)(2,1)S(1)}, f32[1024,2048]{1,0:T(8,128)}) fusion(bf16[1024,2048]{1,0:T(8,128)(2,1)} %collective-permute-done.26, f32[1024,2048]{1,0:T(8,128)} %fusion.11, bf16[2048,3072]{1,0:T(8,128)(2,1)} %all-gather.5.cloned.1.call-done, bf16[2048,1024]{1,0:T(8,128)(2,1)} %get-tuple-element.47), kind=kOutput, calls=%fused_computation.197 | convolution fusion | flops 4303355904 | bytes 31457280 | tf_op jit(solution)/shard_map/dot_general | solution.py:32
  623.8 20.8 %collective-permute-done.27 = bf16[512,1024]{1,0:T(8,128)(2,1)S(1)} collective-permute-done((bf16[512,1024]{1,0:T(8,128)(2,1)S(1)}, bf16[512,1024]{1,0:T(8,128)(2,1)S(1)}, u32[]{:S(2)}, u32[]{:S(2)}) %collective-permute-start.27) | collective-permute-done | bytes 1048608 | tf_op jit(solution)/shard_map/ppermute | solution.py:287
  648.2 22.7 %collective-permute-done.29 = bf16[512,1024]{1,0:T(8,128)(2,1)S(1)} collective-permute-done((bf16[512,1024]{1,0:T(8,128)(2,1)S(1)}, bf16[512,1024]{1,0:T(8,128)(2,1)S(1)}, u32[]{:S(2)}, u32[]{:S(2)}) %collective-permute-start.29) | collective-permute-done | bytes 1048608 | tf_op jit(solution)/shard_map/ppermute | solution.py:281
  671.1 23.1 %collective-permute-done.28 = bf16[256,1024]{1,0:T(8,128)(2,1)S(1)} collective-permute-done((bf16[256,1024]{1,0:T(8,128)(2,1)S(1)}, bf16[256,1024]{1,0:T(8,128)(2,1)S(1)}, u32[]{:S(2)}, u32[]{:S(2)}) %collective-permute-start.28) | collective-permute-done | bytes 524320 | tf_op jit(solution)/shard_map/ppermute | solution.py:281
  697.8 10.9 %collective-permute-done.30 = bf16[256,1024]{1,0:T(8,128)(2,1)S(1)} collective-permute-done((bf16[256,1024]{1,0:T(8,128)(2,1)S(1)}, bf16[256,1024]{1,0:T(8,128)(2,1)S(1)}, u32[]{:S(2)}, u32[]{:S(2)}) %collective-permute-start.30) | collective-permute-done | bytes 524320 | tf_op jit(solution)/shard_map/ppermute | solution.py:287
  712.8 23.0 %collective-permute-done.31 = bf16[256,2048]{1,0:T(8,128)(2,1)} collective-permute-done((bf16[256,2048]{1,0:T(8,128)(2,1)S(1)}, bf16[256,2048]{1,0:T(8,128)(2,1)}, u32[]{:S(2)}, u32[]{:S(2)}) %collective-permute-start.31) | collective-permute-done | bytes 1048608 | tf_op jit(solution)/shard_map/ppermute | solution.py:287
  757.3 27.2 %shard_map.212 = bf16[1024,1536]{1,0:T(8,128)(2,1)} custom-call(s32[1024]{0:T(1024)} %bitcast.82, bf16[1024,1536]{1,0:T(8,128)(2,1)} %get-tuple-element.51.kept_ref, bf16[1024,512]{1,0:T(8,128)(2,1)} %convolution_convert_fusion.8.do_ref, f32[1024,128]{1,0:T(8,128)} %get-tuple-element.107.cos_ref, f32[1024,128]{1,0:T(8,128)} %get-tuple-element.108.sin_ref, ...), custom_call_target="tpu_custom_call" | custom-call | tf_op jit(solution)/shard_map/pallas_call | solution.py:254
  784.5 12.7 %collective-permute-done.33.theirs = bf16[256,2048]{1,0:T(8,128)(2,1)S(1)} collective-permute-done((bf16[256,2048]{1,0:T(8,128)(2,1)}, bf16[256,2048]{1,0:T(8,128)(2,1)S(1)}, u32[]{:S(2)}, u32[]{:S(2)}) %collective-permute-start.33) | collective-permute-done | bytes 1048608 | tf_op jit(solution)/shard_map/ppermute | solution.py:281
  797.2 12.1 %convolution_convert_fusion = bf16[2048,1536]{1,0:T(8,128)(2,1)} fusion(bf16[1024,2048]{1,0:T(8,128)(2,1)} %get-tuple-element.85, bf16[1024,1536]{1,0:T(8,128)(2,1)} %shard_map.212), kind=kOutput, calls=%fused_computation.14 | convolution fusion | flops 6445596672 | bytes 13631488 | tf_op jit(solution)/shard_map/dot_general | solution.py:26
  841.9 17.5 %collective-permute-done.35 = bf16[256,2048]{1,0:T(8,128)(2,1)} collective-permute-done((bf16[256,2048]{1,0:T(8,128)(2,1)}, bf16[256,2048]{1,0:T(8,128)(2,1)}, u32[]{:S(2)}, u32[]{:S(2)}) %collective-permute-start.35) | collective-permute-done | bytes 1048608 | tf_op jit(solution)/shard_map/ppermute | solution.py:287
  867.4 14.0 %collective-permute-done.37 = f32[2,2048]{1,0:T(2,128)S(1)} collective-permute-done((f32[2,2048]{1,0:T(2,128)S(1)}, f32[2,2048]{1,0:T(2,128)S(1)}, u32[]{:S(2)}, u32[]{:S(2)}) %collective-permute-start.37) | collective-permute-done | bytes 16416 | tf_op jit(solution)/shard_map/ppermute | solution.py:287
  918.9 41.7 %reduce-scatter.11.cloned.1.call-done = bf16[256,1536]{1,0:T(8,128)(2,1)} async-done(((bf16[2048,1536]{1,0:T(8,128)(2,1)}), bf16[256,1536]{1,0:T(8,128)(2,1)}) %reduce-scatter.11.cloned.1.call-update) | async-done | bytes 786448 | tf_op jit(solution)/shard_map/reduce_scatter | solution.py:507
  (296 shorter events, 337.8 us)
Async XLA Ops:
  7.2 190.1 %all-gather.3.cloned.1.call-start = ((), (), s32[]{:S(2)}) async-start(), calls=%async_computation.4 | async-start | bytes 7077888 | tf_op jit(solution)/shard_map/all_gather | solution.py:363
  15.6 407.1 %all-gather.5.cloned.1.call-start = ((), (), s32[]{:S(2)}) async-start(), calls=%async_computation.5 | async-start | bytes 15728640 | tf_op jit(solution)/shard_map/all_gather | solution.py:412
  18.8 56.7 %collective-permute-start.15 = (bf16[128,6144]{1,0:T(8,128)(2,1)}, bf16[128,6144]{1,0:T(8,128)(2,1)S(1)}, u32[]{:S(2)}, u32[]{:S(2)}) collective-permute-start(bf16[128,6144]{1,0:T(8,128)(2,1)} %shard_map.207), channel_id=1, source_target_pairs={{0,2},{2,0},{1,3},{3,1},{4,6},{6,4},{5,7},{7,5},{8,10},{10,8},{9,1... | collective-permute-start | bytes 4718600 | tf_op jit(solution)/shard_map/ppermute | solution.py:284
  24.0 101.2 %collective-permute-start = (bf16[512,2048]{1,0:T(8,128)(2,1)}, bf16[512,2048]{1,0:T(8,128)(2,1)}, u32[]{:S(2)}, u32[]{:S(2)}) collective-permute-start(bf16[512,2048]{1,0:T(8,128)(2,1)} %shard_map.203), channel_id=1, source_target_pairs={{0,2},{2,0},{1,3},{3,1},{4,6},{6,4},{5,7},{7,5},{8,10},{10,8},{9,1... | collective-permute-start | bytes 6291464 | tf_op jit(solution)/shard_map/ppermute | solution.py:284
  24.5 18.4 %collective-permute-start.5 = (bf16[272,512]{1,0:T(8,128)(2,1)S(1)}, bf16[272,512]{1,0:T(8,128)(2,1)S(1)}, u32[]{:S(2)}, u32[]{:S(2)}) collective-permute-start(bf16[272,512]{1,0:T(8,128)(2,1)S(1)} %copy-done.13), channel_id=1, source_target_pairs={{0,24},{4,28},{8,16},{12,20},{16,8},{20,12},{24,0},{28,4},{1,25},{... | collective-permute-start | bytes 835592 | tf_op jit(solution)/shard_map/ppermute | solution.py:281
  29.4 36.6 %collective-permute-start.4 = (bf16[272,512]{1,0:T(8,128)(2,1)S(1)}, bf16[272,512]{1,0:T(8,128)(2,1)S(1)}, u32[]{:S(2)}, u32[]{:S(2)}) collective-permute-start(bf16[272,512]{1,0:T(8,128)(2,1)S(1)} %copy-done.13), channel_id=1, source_target_pairs={{0,16},{4,20},{8,24},{12,28},{16,0},{20,4},{24,8},{28,12},{1,17},{... | collective-permute-start | bytes 835592 | tf_op jit(solution)/shard_map/ppermute | solution.py:281
  29.4 36.7 %collective-permute-start.3 = (bf16[272,512]{1,0:T(8,128)(2,1)S(1)}, bf16[272,512]{1,0:T(8,128)(2,1)S(1)}, u32[]{:S(2)}, u32[]{:S(2)}) collective-permute-start(bf16[272,512]{1,0:T(8,128)(2,1)S(1)} %copy-done.13), channel_id=1, source_target_pairs={{0,8},{4,12},{8,0},{12,4},{16,24},{20,28},{24,16},{28,20},{1,9},{5... | collective-permute-start | bytes 835592 | tf_op jit(solution)/shard_map/ppermute | solution.py:281
  67.2 39.5 %collective-permute-start.6 = (bf16[1088,512]{1,0:T(8,128)(2,1)}, bf16[1088,512]{1,0:T(8,128)(2,1)}, u32[]{:S(2)}, u32[]{:S(2)}) collective-permute-start(bf16[1088,512]{1,0:T(8,128)(2,1)} %pad_maximum_fusion.4), channel_id=1, source_target_pairs={{0,4},{4,0},{8,12},{12,8},{16,20},{20,16},{24,28},{28,24},{1,5},{5... | collective-permute-start | bytes 3342344 | tf_op jit(solution)/shard_map/ppermute | solution.py:281
  81.5 71.4 %collective-permute-start.16 = (bf16[256,3072]{1,0:T(8,128)(2,1)}, bf16[256,3072]{1,0:T(8,128)(2,1)}, u32[]{:S(2)}, u32[]{:S(2)}) collective-permute-start(bf16[256,3072]{1,0:T(8,128)(2,1)} %get-tuple-element.41), channel_id=1, source_target_pairs={{0,8},{4,12},{8,0},{12,4},{16,24},{20,28},{24,16},{28,20},{1,9},{5... | collective-permute-start | bytes 4718600 | tf_op jit(solution)/shard_map/ppermute | solution.py:281
  197.3 550.0 %reduce-scatter.7.cloned.1.call-start = ((), (), s32[]{:S(2)}) async-start(), calls=%async_computation.7 | async-start | bytes 5242880 | tf_op jit(solution)/shard_map/reduce_scatter | solution.py:507
  236.8 25.4 %collective-permute-start.8 = (bf16[256,2048]{1,0:T(8,128)(2,1)S(1)}, bf16[256,2048]{1,0:T(8,128)(2,1)}, u32[]{:S(2)}, u32[]{:S(2)}) collective-permute-start(bf16[256,2048]{1,0:T(8,128)(2,1)S(1)} %add_convert_fusion.2), channel_id=1, source_target_pairs={{0,1},{1,0},{2,3},{3,2},{4,5},{5,4},{6,7},{7,6},{8,9},{9,8},{10,11... | collective-permute-start | bytes 3145736 | tf_op jit(solution)/shard_map/ppermute | solution.py:287
  266.9 24.3 %collective-permute-start.9 = (bf16[256,2048]{1,0:T(8,128)(2,1)S(1)}, bf16[256,2048]{1,0:T(8,128)(2,1)S(1)}, u32[]{:S(2)}, u32[]{:S(2)}) collective-permute-start(bf16[256,2048]{1,0:T(8,128)(2,1)S(1)} %get-tuple-element.74), channel_id=1, source_target_pairs={{0,1},{1,0},{2,3},{3,2},{4,5},{5,4},{6,7},{7,6},{8,9},{9,8},{10,11... | collective-permute-start | bytes 3145736 | tf_op jit(solution)/shard_map/ppermute | solution.py:287
  268.6 49.6 %collective-permute-start.10 = (bf16[256,2048]{1,0:T(8,128)(2,1)S(1)}, bf16[256,2048]{1,0:T(8,128)(2,1)S(1)}, u32[]{:S(2)}, u32[]{:S(2)}) collective-permute-start(bf16[256,2048]{1,0:T(8,128)(2,1)S(1)} %get-tuple-element.74), channel_id=1, source_target_pairs={{0,8},{4,12},{8,0},{12,4},{16,24},{20,28},{24,16},{28,20},{1,9},{5... | collective-permute-start | bytes 3145736 | tf_op jit(solution)/shard_map/ppermute | solution.py:281
  291.3 39.7 %collective-permute-start.11 = (bf16[128,2048]{1,0:T(8,128)(2,1)S(1)}, bf16[128,2048]{1,0:T(8,128)(2,1)S(1)}, u32[]{:S(2)}, u32[]{:S(2)}) collective-permute-start(bf16[128,2048]{1,0:T(8,128)(2,1)S(1)} %slice.275), channel_id=1, source_target_pairs={{0,8},{4,12},{8,0},{12,4},{16,24},{20,28},{24,16},{28,20},{1,9},{5... | collective-permute-start | bytes 1572872 | tf_op jit(solution)/shard_map/ppermute | solution.py:281
  332.9 47.4 %collective-permute-start.17 = (bf16[256,2048]{1,0:T(8,128)(2,1)S(1)}, bf16[256,2048]{1,0:T(8,128)(2,1)S(1)}, u32[]{:S(2)}, u32[]{:S(2)}) collective-permute-start(bf16[256,2048]{1,0:T(8,128)(2,1)S(1)} %get-tuple-element.43), channel_id=1, source_target_pairs={{0,8},{4,12},{8,0},{12,4},{16,24},{20,28},{24,16},{28,20},{1,9},{5... | collective-permute-start | bytes 3145736 | tf_op jit(solution)/shard_map/ppermute | solution.py:281
  380.3 24.3 %collective-permute-start.18 = (bf16[256,2048]{1,0:T(8,128)(2,1)S(1)}, bf16[256,2048]{1,0:T(8,128)(2,1)S(1)}, u32[]{:S(2)}, u32[]{:S(2)}) collective-permute-start(bf16[256,2048]{1,0:T(8,128)(2,1)S(1)} %collective-permute-done.17), channel_id=1, source_target_pairs={{0,1},{1,0},{2,3},{3,2},{4,5},{5,4},{6,7},{7,6},{8,9},{9,8},{10,11... | collective-permute-start | bytes 3145736 | tf_op jit(solution)/shard_map/ppermute | solution.py:287
  497.9 249.4 %reduce-scatter.5.cloned.1.call-start = ((), (), s32[]{:S(2)}) async-start(), calls=%async_computation.6 | async-start | bytes 10485760 | tf_op jit(solution)/shard_map/reduce_scatter | solution.py:507
  518.7 34.7 %collective-permute-start.21 = (bf16[512,1024]{1,0:T(8,128)(2,1)}, bf16[512,1024]{1,0:T(8,128)(2,1)S(1)}, u32[]{:S(2)}, u32[]{:S(2)}) collective-permute-start(bf16[512,1024]{1,0:T(8,128)(2,1)} %pad_maximum_fusion.5), channel_id=1, source_target_pairs={{0,1},{1,0},{2,3},{3,2},{4,5},{5,4},{6,7},{7,6},{8,9},{9,8},{10,11... | collective-permute-start | bytes 3145736 | tf_op jit(solution)/shard_map/ppermute | solution.py:287
  520.2 43.7 %collective-permute-start.23 = (bf16[512,1024]{1,0:T(8,128)(2,1)S(1)}, bf16[512,1024]{1,0:T(8,128)(2,1)S(1)}, u32[]{:S(2)}, u32[]{:S(2)}) collective-permute-start(bf16[512,1024]{1,0:T(8,128)(2,1)S(1)} %concatenate.113), channel_id=1, source_target_pairs={{0,8},{4,12},{8,0},{12,4},{16,24},{20,28},{24,16},{28,20},{1,9},{5... | collective-permute-start | bytes 3145736 | tf_op jit(solution)/shard_map/ppermute | solution.py:281
  552.9 262.5 %reduce-scatter.9.cloned.1.call-start = ((), (), s32[]{:S(2)}) async-start(), calls=%async_computation.8 | async-start | bytes 2359296 | tf_op jit(solution)/shard_map/reduce_scatter | solution.py:507
  583.0 22.4 %collective-permute-start.26 = (bf16[1024,2048]{1,0:T(8,128)(2,1)S(1)}, bf16[1024,2048]{1,0:T(8,128)(2,1)}, u32[]{:S(2)}, u32[]{:S(2)}) collective-permute-start(bf16[1024,2048]{1,0:T(8,128)(2,1)S(1)} %add_convert_fusion), channel_id=1, source_target_pairs={{0,2},{2,0},{1,3},{3,1},{4,6},{6,4},{5,7},{7,5},{8,10},{10,8},{9,1... | collective-permute-start | bytes 12582920 | tf_op jit(solution)/shard_map/ppermute | solution.py:284
  619.9 24.7 %collective-permute-start.27 = (bf16[512,1024]{1,0:T(8,128)(2,1)S(1)}, bf16[512,1024]{1,0:T(8,128)(2,1)S(1)}, u32[]{:S(2)}, u32[]{:S(2)}) collective-permute-start(bf16[512,1024]{1,0:T(8,128)(2,1)S(1)} %pad_maximum_fusion.6), channel_id=1, source_target_pairs={{0,1},{1,0},{2,3},{3,2},{4,5},{5,4},{6,7},{7,6},{8,9},{9,8},{10,11... | collective-permute-start | bytes 3145736 | tf_op jit(solution)/shard_map/ppermute | solution.py:287
  620.7 50.2 %collective-permute-start.29 = (bf16[512,1024]{1,0:T(8,128)(2,1)S(1)}, bf16[512,1024]{1,0:T(8,128)(2,1)S(1)}, u32[]{:S(2)}, u32[]{:S(2)}) collective-permute-start(bf16[512,1024]{1,0:T(8,128)(2,1)S(1)} %concatenate.114), channel_id=1, source_target_pairs={{0,8},{4,12},{8,0},{12,4},{16,24},{20,28},{24,16},{28,20},{1,9},{5... | collective-permute-start | bytes 3145736 | tf_op jit(solution)/shard_map/ppermute | solution.py:281
  645.1 49.1 %collective-permute-start.28 = (bf16[256,1024]{1,0:T(8,128)(2,1)S(1)}, bf16[256,1024]{1,0:T(8,128)(2,1)S(1)}, u32[]{:S(2)}, u32[]{:S(2)}) collective-permute-start(bf16[256,1024]{1,0:T(8,128)(2,1)S(1)} %fusion.31), channel_id=1, source_target_pairs={{0,8},{4,12},{8,0},{12,4},{16,24},{20,28},{24,16},{28,20},{1,9},{5... | collective-permute-start | bytes 1572872 | tf_op jit(solution)/shard_map/ppermute | solution.py:281
  711.3 24.4 %collective-permute-start.31 = (bf16[256,2048]{1,0:T(8,128)(2,1)S(1)}, bf16[256,2048]{1,0:T(8,128)(2,1)}, u32[]{:S(2)}, u32[]{:S(2)}) collective-permute-start(bf16[256,2048]{1,0:T(8,128)(2,1)S(1)} %get-tuple-element.67), channel_id=1, source_target_pairs={{0,1},{1,0},{2,3},{3,2},{4,5},{5,4},{6,7},{7,6},{8,9},{9,8},{10,11... | collective-permute-start | bytes 3145736 | tf_op jit(solution)/shard_map/ppermute | solution.py:287
  747.3 213.2 %reduce-scatter.11.cloned.1.call-start = ((), (), s32[]{:S(2)}) async-start(), calls=%async_computation.9 | async-start | bytes 7077888 | tf_op jit(solution)/shard_map/reduce_scatter | solution.py:507
  749.7 47.5 %collective-permute-start.33 = (bf16[256,2048]{1,0:T(8,128)(2,1)}, bf16[256,2048]{1,0:T(8,128)(2,1)S(1)}, u32[]{:S(2)}, u32[]{:S(2)}) collective-permute-start(bf16[256,2048]{1,0:T(8,128)(2,1)} %constant_dynamic-slice_fusion.1), channel_id=1, source_target_pairs={{0,8},{4,12},{8,0},{12,4},{16,24},{20,28},{24,16},{28,20},{1,9},{5... | collective-permute-start | bytes 3145736 | tf_op jit(solution)/shard_map/ppermute | solution.py:281
  833.1 26.3 %collective-permute-start.35 = (bf16[256,2048]{1,0:T(8,128)(2,1)}, bf16[256,2048]{1,0:T(8,128)(2,1)}, u32[]{:S(2)}, u32[]{:S(2)}) collective-permute-start(bf16[256,2048]{1,0:T(8,128)(2,1)} %fusion.20), channel_id=1, source_target_pairs={{0,1},{1,0},{2,3},{3,2},{4,5},{5,4},{6,7},{7,6},{8,9},{9,8},{10,11... | collective-permute-start | bytes 3145736 | tf_op jit(solution)/shard_map/ppermute | solution.py:287
  836.2 59.4 %collective-permute-start.43 = (bf16[256,1024]{1,0:T(8,128)(2,1)}, bf16[256,1024]{1,0:T(8,128)(2,1)}, u32[]{:S(2)}, u32[]{:S(2)}) collective-permute-start(bf16[256,1024]{1,0:T(8,128)(2,1)} %constant_dynamic-slice_fusion), channel_id=1, source_target_pairs={{0,8},{4,12},{8,0},{12,4},{16,24},{20,28},{24,16},{28,20},{1,9},{5... | collective-permute-start | bytes 1572872 | tf_op jit(solution)/shard_map/ppermute | solution.py:281
  837.7 67.3 %collective-permute-start.25 = (bf16[256,2048]{1,0:T(8,128)(2,1)}, bf16[256,2048]{1,0:T(8,128)(2,1)}, u32[]{:S(2)}, u32[]{:S(2)}) collective-permute-start(bf16[256,2048]{1,0:T(8,128)(2,1)} %get-tuple-element.90.own_ref), channel_id=1, source_target_pairs={{0,1},{1,0},{2,3},{3,2},{4,5},{5,4},{6,7},{7,6},{8,9},{9,8},{10,11... | collective-permute-start | bytes 3145736 | tf_op jit(solution)/shard_map/ppermute | solution.py:287
  841.9 66.9 %collective-permute-start.42 = (bf16[128,4096]{1,0:T(8,128)(2,1)}, bf16[128,4096]{1,0:T(8,128)(2,1)}, u32[]{:S(2)}, u32[]{:S(2)}) collective-permute-start(bf16[128,4096]{1,0:T(8,128)(2,1)} %shard_map.214), channel_id=1, source_target_pairs={{0,2},{2,0},{1,3},{3,1},{4,6},{6,4},{5,7},{7,5},{8,10},{10,8},{9,1... | collective-permute-start | bytes 3145736 | tf_op jit(solution)/shard_map/ppermute | solution.py:284
  883.9 30.1 %collective-permute-start.36 = (bf16[256,2048]{1,0:T(8,128)(2,1)S(1)}, bf16[256,2048]{1,0:T(8,128)(2,1)S(1)}, u32[]{:S(2)}, u32[]{:S(2)}) collective-permute-start(bf16[256,2048]{1,0:T(8,128)(2,1)S(1)} %add_convert_fusion.1.own_ref), channel_id=1, source_target_pairs={{0,1},{1,0},{2,3},{3,2},{4,5},{5,4},{6,7},{7,6},{8,9},{9,8},{10,11... | collective-permute-start | bytes 3145736 | tf_op jit(solution)/shard_map/ppermute | solution.py:287
  (61 other events, 956.5 us)
Sparse Core Ops, SparseCore 0:
  15.7 181.5 all-gather.2
  199.1 223.5 all-gather.4
  498.0 86.3 reduce-scatter.6
  587.3 153.6 reduce-scatter.4
  747.4 67.9 reduce-scatter.8
  817.6 142.9 reduce-scatter.10

commit v9 on v8

--- a/solution.py
+++ b/solution.py
@@ -482,15 +482,11 @@
         late_hidden = after(hidden, prod_d)
         (sent_m, first_m, second_m), mlp = from_tokens(lambda where: contract_cols(late_hidden[where], weight_d))
         grad_gate, grad_up = after((grad_gate, grad_up), sent_m)
-        prod_gu = cat(
-            [contract_rows(h_two, grad_gate).astype(bf16), contract_rows(h_two, grad_up).astype(bf16)], 1
-        )
-        late_gate, late_up = after((grad_gate, grad_up), prod_gu, first_m)
-        _, grad_h_two = from_tokens(
-            lambda where: contract_cols(late_gate[where], weight_g)
-            + contract_cols(late_up[where], weight_u),
-            second_m,
-        )
+        grad_gu = cat([grad_gate, grad_up], 1)
+        prod_gu = contract_rows(h_two, grad_gu).astype(bf16)
+        late_gu = after(grad_gu, prod_gu, first_m)
+        weight_gu = weight_f[:, : 2 * n_ff]
+        _, grad_h_two = from_tokens(lambda where: contract_cols(late_gu[where], weight_gu), second_m)
         out_part = (after_attn + mlp).astype(bf16)
         output = join_tokens(out_part, swap_tp(out_part), half, nat, block)
 

time: 985 us -> 975 us (0.990)
  waiting for transfers between devices: 501 us -> 526 us
  matrix products: 216 us -> 199 us
  starting transfers between devices: 49.9 us -> 34.2 us
    ppermute x17, starting transfers between devices: 29.3 us -> 14.3 us  [across(): return lax.ppermute(values, 'shard', [(i, i ^ mask) for i in range(shards)])]
    ppermute x17, waiting for transfers between devices: 232 us -> 247 us  [across(): return lax.ppermute(values, 'shard', [(i, i ^ mask) for i in range(shards)])]
    dot_general x12 -> x10, matrix products: 93.2 us -> 78.4 us  [contract_cols(): lax.dot_general(left, right, (((1,), (1,)), ((), ())), preferred_element_...]
    unnamed x95 -> x90, local copies, waits for them, and re-layouts: 26 us -> 31 us
    dot_general x5 -> x4, matrix products: 53 us -> 51 us  [contract_rows(): lax.dot_general(left, right, (((0,), (0,)), ((), ())), preferred_element_...]
  transfers between devices with their start and end apart: 52 -> 52, of which waited for: 35 -> 36; matrix products, arithmetic and copies ran while one was open for 24% -> 21% of each run, Pallas kernels for 9% -> 9%
where the time goes in v9:
time: 975 us; the launch traced here: 968 us
  waiting for transfers between devices  526 us (54%)
  matrix products  199 us (20%)
  Pallas kernels  95.2 us (10%)
  local copies, waits for them, and re-layouts  60.7 us (6%)
  other arithmetic  36.9 us (4%)
  starting transfers between devices  34.2 us (4%)
  between operations  15.1 us (2%)
    ppermute x17, waiting for transfers between devices, across(): return lax.ppermute(values, 'shard', [(i, i ^ mask) for i in range(shards)])  247 us
    ppermute x13, waiting for transfers between devices, swap_tp(): return lax.ppermute(values, 'tp', [(0, 1), (1, 0)])  153 us
    dot_general x10, matrix products, contract_cols(): lax.dot_general(left, right, (((1,), (1,)), ((), ())), preferred_element_...  78.4 us
    dot_general x5, matrix products, matmul(): return jnp.dot(left, right, preferred_element_type=jnp.float32)  70.1 us
    reduce_scatter x4, waiting for transfers between devices, scatter(): lax.psum_scatter(values.astype(bf16), 'shard', scatter_dimension=0, tiled...  53.9 us
    dot_general x4, matrix products, contract_rows(): lax.dot_general(left, right, (((0,), (0,)), ((), ())), preferred_element_...  51 us
    all_gather x1, waiting for transfers between devices, per_device(): lax.all_gather(block_qkv, 'shard', axis=0, tiled=True, axis_index_groups=...  40.6 us
    pallas_call x11, Pallas kernels, small_call(): pl.pallas_call(body, grid_spec=pltpu.PrefetchScalarGridSpec(num_scalar_pr...  36.6 us
  transfers between devices with their start and end apart: 52, of which 36 were waited for; matrix products, arithmetic and copies ran while one was open for 21% of the time, Pallas kernels for 9%

profile of v9, /device:TPU:0, one launch (start us, length us, event | category | flops | bytes accessed | tf_op | source)
XLA Modules:
  0.0 968.1 jit_solution(2751552501380390624)
XLA Ops:
  30.6 12.2 %collective-permute-done.5 = bf16[272,512]{1,0:T(8,128)(2,1)S(1)} collective-permute-done((bf16[272,512]{1,0:T(8,128)(2,1)S(1)}, bf16[272,512]{1,0:T(8,128)(2,1)S(1)}, u32[]{:S(2)}, u32[]{:S(2)}) %collective-permute-start.5) | collective-permute-done | bytes 278560 | tf_op jit(solution)/shard_map/ppermute | solution.py:281
  42.9 23.1 %collective-permute-done.4 = bf16[272,512]{1,0:T(8,128)(2,1)S(1)} collective-permute-done((bf16[272,512]{1,0:T(8,128)(2,1)S(1)}, bf16[272,512]{1,0:T(8,128)(2,1)S(1)}, u32[]{:S(2)}, u32[]{:S(2)}) %collective-permute-start.4) | collective-permute-done | bytes 278560 | tf_op jit(solution)/shard_map/ppermute | solution.py:281
  84.0 22.6 %collective-permute-done.6 = bf16[1088,512]{1,0:T(8,128)(2,1)} collective-permute-done((bf16[1088,512]{1,0:T(8,128)(2,1)}, bf16[1088,512]{1,0:T(8,128)(2,1)}, u32[]{:S(2)}, u32[]{:S(2)}) %collective-permute-start.6) | collective-permute-done | bytes 1114144 | tf_op jit(solution)/shard_map/ppermute | solution.py:281
  135.4 17.5 %collective-permute-done.16.other = bf16[256,3072]{1,0:T(8,128)(2,1)} collective-permute-done((bf16[256,3072]{1,0:T(8,128)(2,1)}, bf16[256,3072]{1,0:T(8,128)(2,1)}, u32[]{:S(2)}, u32[]{:S(2)}) %collective-permute-start.16) | collective-permute-done | bytes 1572896 | tf_op jit(solution)/shard_map/ppermute | solution.py:281
  156.6 40.6 %all-gather.3.cloned.1.call-done = bf16[2048,1536]{1,0:T(8,128)(2,1)} async-done(((bf16[256,1536]{1,0:T(8,128)(2,1)}), bf16[2048,1536]{1,0:T(8,128)(2,1)}) %all-gather.3.cloned.1.call-update) | async-done | bytes 6291472 | tf_op jit(solution)/shard_map/all_gather | solution.py:363
  198.6 11.7 %fusion.86.qkv_ref = f32[1024,1536]{1,0:T(8,128)} fusion(bf16[1024,2048]{1,0:T(8,128)(2,1)} %get-tuple-element.83, bf16[2048,1536]{1,0:T(8,128)(2,1)} %all-gather.3.cloned.1.call-done), kind=kOutput, calls=%fused_computation.194 | convolution fusion | flops 6442450944 | bytes 16777216 | tf_op jit(solution)/shard_map/dot_general | solution.py:22
  210.4 14.9 %shard_map.206 = (bf16[1024,512]{1,0:T(8,128)(2,1)}, bf16[1024,1536]{1,0:T(8,128)(2,1)}) custom-call(s32[1024]{0:T(1024)} %bitcast.79, f32[1024,1536]{1,0:T(8,128)} %fusion.86.qkv_ref, f32[1024,128]{1,0:T(8,128)} %get-tuple-element.105.cos_ref, f32[1024,128]{1,0:T(8,128)} %get-tuple-element.106.sin_ref, s32[1024,1]{1,0:T(8,128)} %copy.23.seg_col, ...), custom_call_target="tpu_custom_call" | custom-call | tf_op jit(solution)/shard_map/pallas_call | solution.py:195
  240.9 21.2 %collective-permute-done.8 = bf16[256,2048]{1,0:T(8,128)(2,1)} collective-permute-done((bf16[256,2048]{1,0:T(8,128)(2,1)S(1)}, bf16[256,2048]{1,0:T(8,128)(2,1)}, u32[]{:S(2)}, u32[]{:S(2)}) %collective-permute-start.8) | collective-permute-done | bytes 1048608 | tf_op jit(solution)/shard_map/ppermute | solution.py:287
  273.1 18.2 %collective-permute-done.9 = bf16[256,2048]{1,0:T(8,128)(2,1)S(1)} collective-permute-done((bf16[256,2048]{1,0:T(8,128)(2,1)S(1)}, bf16[256,2048]{1,0:T(8,128)(2,1)S(1)}, u32[]{:S(2)}, u32[]{:S(2)}) %collective-permute-start.9) | collective-permute-done | bytes 1048608 | tf_op jit(solution)/shard_map/ppermute | solution.py:287
  293.9 24.2 %collective-permute-done.10 = bf16[256,2048]{1,0:T(8,128)(2,1)S(1)} collective-permute-done((bf16[256,2048]{1,0:T(8,128)(2,1)S(1)}, bf16[256,2048]{1,0:T(8,128)(2,1)S(1)}, u32[]{:S(2)}, u32[]{:S(2)}) %collective-permute-start.10) | collective-permute-done | bytes 1048608 | tf_op jit(solution)/shard_map/ppermute | solution.py:281
  333.0 47.3 %collective-permute-done.17 = bf16[256,2048]{1,0:T(8,128)(2,1)S(1)} collective-permute-done((bf16[256,2048]{1,0:T(8,128)(2,1)S(1)}, bf16[256,2048]{1,0:T(8,128)(2,1)S(1)}, u32[]{:S(2)}, u32[]{:S(2)}) %collective-permute-start.17) | collective-permute-done | bytes 1048608 | tf_op jit(solution)/shard_map/ppermute | solution.py:281
  382.0 22.9 %collective-permute-done.18 = bf16[256,2048]{1,0:T(8,128)(2,1)S(1)} collective-permute-done((bf16[256,2048]{1,0:T(8,128)(2,1)S(1)}, bf16[256,2048]{1,0:T(8,128)(2,1)S(1)}, u32[]{:S(2)}, u32[]{:S(2)}) %collective-permute-start.18) | collective-permute-done | bytes 1048608 | tf_op jit(solution)/shard_map/ppermute | solution.py:287
  422.7 15.2 %fusion.6 = f32[2048,1024]{1,0:T(8,128)} fusion(bf16[2048,2048]{1,0:T(8,128)(2,1)} %constant_dynamic-update-slice_fusion.7, bf16[2048,3072]{1,0:T(8,128)(2,1)} %all-gather.5.cloned.1.call-done), kind=kOutput, calls=%fused_computation.18 | convolution fusion | flops 8589934592 | bytes 20971520 | tf_op jit(solution)/shard_map/dot_general | solution.py:22
  437.9 12.8 %fusion.8 = f32[2048,1024]{1,0:T(8,128)} fusion(bf16[2048,2048]{1,0:T(8,128)(2,1)S(1)} %copy-done.24, bf16[2048,3072]{1,0:T(8,128)(2,1)} %all-gather.5.cloned.1.call-done), kind=kOutput, calls=%fused_computation.20 | convolution fusion | flops 8589934592 | bytes 20971520 | tf_op jit(solution)/shard_map/dot_general | solution.py:22
  450.8 22.9 %multiply_convert_fusion = (bf16[2048,1024]{1,0:T(8,128)(2,1)}, bf16[2048,1024]{1,0:T(8,128)(2,1)}, bf16[2048,1024]{1,0:T(8,128)(2,1)S(1)}) fusion(f32[2048,1024]{1,0:T(8,128)} %fusion.8, f32[2048,1024]{1,0:T(8,128)} %fusion.6, bf16[2048,2048]{1,0:T(8,128)(2,1)} %constant_dynamic-update-slice_fusion.14, bf16[2048,3072]{1,0:T(8,128)(2,1)} %all-gather.5.cloned.1.call-done), kind=kOutput, calls=%fused_computation.5 | convolution fusion | flops 8621391872 | bytes 41943040 | tf_op jit(solution)/shard_map/dot_general | solution.py:22
  475.6 13.0 %convolution_convert_fusion.3 = bf16[2048,1024]{1,0:T(8,128)(2,1)} fusion(bf16[2048,2048]{1,0:T(8,128)(2,1)} %constant_dynamic-update-slice_fusion.14, bf16[2048,1024]{1,0:T(8,128)(2,1)S(1)} %get-tuple-element.43), kind=kOutput, calls=%fused_computation.29 | convolution fusion | flops 8592031744 | bytes 16777216 | tf_op jit(solution)/shard_map/dot_general | solution.py:26
  505.5 12.0 %fusion.84 = (bf16[1024,2048]{1,0:T(8,128)(2,1)S(1)}, f32[1024,2048]{1,0:T(8,128)}) fusion(bf16[1024,2048]{1,0:T(8,128)(2,1)} %collective-permute-done.20, bf16[2048,3072]{1,0:T(8,128)(2,1)} %all-gather.5.cloned.1.call-done, bf16[2048,1024]{1,0:T(8,128)(2,1)} %copy-done.37), kind=kOutput, calls=%fused_computation.192 | convolution fusion | flops 4301258752 | bytes 23068672 | tf_op jit(solution)/shard_map/dot_general | solution.py:32
  526.4 22.3 %convolution_convert_fusion.1 = bf16[2048,2048]{1,0:T(8,128)(2,1)} fusion(bf16[2048,2048]{1,0:T(8,128)(2,1)} %constant_dynamic-update-slice_fusion.7, bf16[2048,2048]{1,0:T(8,128)(2,1)S(1)} %constant_dynamic-update-slice_fusion.19), kind=kOutput, calls=%fused_computation.13 | convolution fusion | flops 17184063488 | bytes 25165824 | tf_op jit(solution)/shard_map/dot_general | solution.py:26
  548.8 15.2 %collective-permute-done.23 = bf16[512,1024]{1,0:T(8,128)(2,1)S(1)} collective-permute-done((bf16[512,1024]{1,0:T(8,128)(2,1)S(1)}, bf16[512,1024]{1,0:T(8,128)(2,1)S(1)}, u32[]{:S(2)}, u32[]{:S(2)}) %collective-permute-start.23) | collective-permute-done | bytes 1048608 | tf_op jit(solution)/shard_map/ppermute | solution.py:281
  564.0 12.6 %fusion.16 = bf16[1024,2048]{1,0:T(8,128)(2,1)S(1)} fusion(bf16[2048,3072]{1,0:T(8,128)(2,1)} %all-gather.5.cloned.1.call-done, bf16[2048,2048]{1,0:T(8,128)(2,1)} %copy-done.13), kind=kOutput, calls=%fused_computation.27 | convolution fusion | flops 8592031744 | bytes 16777216 | tf_op jit(solution)/shard_map/dot_general | solution.py:32
  578.7 15.6 %collective-permute-done.22 = bf16[256,1024]{1,0:T(8,128)(2,1)S(1)} collective-permute-done((bf16[256,1024]{1,0:T(8,128)(2,1)S(1)}, bf16[256,1024]{1,0:T(8,128)(2,1)S(1)}, u32[]{:S(2)}, u32[]{:S(2)}) %collective-permute-start.22) | collective-permute-done | bytes 524320 | tf_op jit(solution)/shard_map/ppermute | solution.py:281
  597.8 15.4 %fusion.85 = (bf16[1024,2048]{1,0:T(8,128)(2,1)S(1)}, f32[1024,2048]{1,0:T(8,128)}) fusion(bf16[1024,2048]{1,0:T(8,128)(2,1)} %collective-permute-done.26, bf16[2048,3072]{1,0:T(8,128)(2,1)} %all-gather.5.cloned.1.call-done, bf16[2048,2048]{1,0:T(8,128)(2,1)} %copy-done.13), kind=kOutput, calls=%fused_computation.193 | convolution fusion | flops 8596226048 | bytes 29360128 | tf_op jit(solution)/shard_map/dot_general | solution.py:32
  614.1 24.3 %collective-permute-done.27 = bf16[512,1024]{1,0:T(8,128)(2,1)S(1)} collective-permute-done((bf16[512,1024]{1,0:T(8,128)(2,1)S(1)}, bf16[512,1024]{1,0:T(8,128)(2,1)S(1)}, u32[]{:S(2)}, u32[]{:S(2)}) %collective-permute-start.27) | collective-permute-done | bytes 1048608 | tf_op jit(solution)/shard_map/ppermute | solution.py:287
  638.9 25.1 %collective-permute-done.29 = bf16[512,1024]{1,0:T(8,128)(2,1)S(1)} collective-permute-done((bf16[512,1024]{1,0:T(8,128)(2,1)S(1)}, bf16[512,1024]{1,0:T(8,128)(2,1)S(1)}, u32[]{:S(2)}, u32[]{:S(2)}) %collective-permute-start.29) | collective-permute-done | bytes 1048608 | tf_op jit(solution)/shard_map/ppermute | solution.py:281
  664.3 24.7 %collective-permute-done.28 = bf16[256,1024]{1,0:T(8,128)(2,1)S(1)} collective-permute-done((bf16[256,1024]{1,0:T(8,128)(2,1)S(1)}, bf16[256,1024]{1,0:T(8,128)(2,1)S(1)}, u32[]{:S(2)}, u32[]{:S(2)}) %collective-permute-start.28) | collective-permute-done | bytes 524320 | tf_op jit(solution)/shard_map/ppermute | solution.py:281
  692.7 10.0 %collective-permute-done.30 = bf16[256,1024]{1,0:T(8,128)(2,1)S(1)} collective-permute-done((bf16[256,1024]{1,0:T(8,128)(2,1)S(1)}, bf16[256,1024]{1,0:T(8,128)(2,1)S(1)}, u32[]{:S(2)}, u32[]{:S(2)}) %collective-permute-start.30) | collective-permute-done | bytes 524320 | tf_op jit(solution)/shard_map/ppermute | solution.py:287
  706.6 22.4 %collective-permute-done.31 = bf16[256,2048]{1,0:T(8,128)(2,1)} collective-permute-done((bf16[256,2048]{1,0:T(8,128)(2,1)S(1)}, bf16[256,2048]{1,0:T(8,128)(2,1)}, u32[]{:S(2)}, u32[]{:S(2)}) %collective-permute-start.31) | collective-permute-done | bytes 1048608 | tf_op jit(solution)/shard_map/ppermute | solution.py:287
  751.0 27.2 %shard_map.212 = bf16[1024,1536]{1,0:T(8,128)(2,1)} custom-call(s32[1024]{0:T(1024)} %bitcast.80, bf16[1024,1536]{1,0:T(8,128)(2,1)} %get-tuple-element.49.kept_ref, bf16[1024,512]{1,0:T(8,128)(2,1)} %convolution_convert_fusion.7.do_ref, f32[1024,128]{1,0:T(8,128)} %get-tuple-element.105.cos_ref, f32[1024,128]{1,0:T(8,128)} %get-tuple-element.106.sin_ref, ...), custom_call_target="tpu_custom_call" | custom-call | tf_op jit(solution)/shard_map/pallas_call | solution.py:254
  787.4 12.1 %convolution_convert_fusion = bf16[2048,1536]{1,0:T(8,128)(2,1)} fusion(bf16[1024,2048]{1,0:T(8,128)(2,1)} %get-tuple-element.83, bf16[1024,1536]{1,0:T(8,128)(2,1)} %shard_map.212), kind=kOutput, calls=%fused_computation.12 | convolution fusion | flops 6445596672 | bytes 13631488 | tf_op jit(solution)/shard_map/dot_general | solution.py:26
  834.8 18.3 %collective-permute-done.35 = bf16[256,2048]{1,0:T(8,128)(2,1)} collective-permute-done((bf16[256,2048]{1,0:T(8,128)(2,1)}, bf16[256,2048]{1,0:T(8,128)(2,1)}, u32[]{:S(2)}, u32[]{:S(2)}) %collective-permute-start.35) | collective-permute-done | bytes 1048608 | tf_op jit(solution)/shard_map/ppermute | solution.py:287
  861.0 14.0 %collective-permute-done.37 = f32[2,2048]{1,0:T(2,128)S(1)} collective-permute-done((f32[2,2048]{1,0:T(2,128)S(1)}, f32[2,2048]{1,0:T(2,128)S(1)}, u32[]{:S(2)}, u32[]{:S(2)}) %collective-permute-start.37) | collective-permute-done | bytes 16416 | tf_op jit(solution)/shard_map/ppermute | solution.py:287
  906.7 43.7 %reduce-scatter.11.cloned.1.call-done = bf16[256,1536]{1,0:T(8,128)(2,1)} async-done(((bf16[2048,1536]{1,0:T(8,128)(2,1)}), bf16[256,1536]{1,0:T(8,128)(2,1)}) %reduce-scatter.11.cloned.1.call-update) | async-done | bytes 786448 | tf_op jit(solution)/shard_map/reduce_scatter | solution.py:503
  (287 shorter events, 297.8 us)
Async XLA Ops:
  7.2 190.1 %all-gather.3.cloned.1.call-start = ((), (), s32[]{:S(2)}) async-start(), calls=%async_computation.4 | async-start | bytes 7077888 | tf_op jit(solution)/shard_map/all_gather | solution.py:363
  15.6 407.1 %all-gather.5.cloned.1.call-start = ((), (), s32[]{:S(2)}) async-start(), calls=%async_computation.5 | async-start | bytes 15728640 | tf_op jit(solution)/shard_map/all_gather | solution.py:412
  18.8 56.7 %collective-permute-start.15 = (bf16[128,6144]{1,0:T(8,128)(2,1)}, bf16[128,6144]{1,0:T(8,128)(2,1)S(1)}, u32[]{:S(2)}, u32[]{:S(2)}) collective-permute-start(bf16[128,6144]{1,0:T(8,128)(2,1)} %shard_map.207), channel_id=1, source_target_pairs={{0,2},{2,0},{1,3},{3,1},{4,6},{6,4},{5,7},{7,5},{8,10},{10,8},{9,1... | collective-permute-start | bytes 4718600 | tf_op jit(solution)/shard_map/ppermute | solution.py:284
  24.0 101.2 %collective-permute-start = (bf16[512,2048]{1,0:T(8,128)(2,1)}, bf16[512,2048]{1,0:T(8,128)(2,1)}, u32[]{:S(2)}, u32[]{:S(2)}) collective-permute-start(bf16[512,2048]{1,0:T(8,128)(2,1)} %shard_map.203), channel_id=1, source_target_pairs={{0,2},{2,0},{1,3},{3,1},{4,6},{6,4},{5,7},{7,5},{8,10},{10,8},{9,1... | collective-permute-start | bytes 6291464 | tf_op jit(solution)/shard_map/ppermute | solution.py:284
  24.5 18.4 %collective-permute-start.5 = (bf16[272,512]{1,0:T(8,128)(2,1)S(1)}, bf16[272,512]{1,0:T(8,128)(2,1)S(1)}, u32[]{:S(2)}, u32[]{:S(2)}) collective-permute-start(bf16[272,512]{1,0:T(8,128)(2,1)S(1)} %copy-done.16), channel_id=1, source_target_pairs={{0,24},{4,28},{8,16},{12,20},{16,8},{20,12},{24,0},{28,4},{1,25},{... | collective-permute-start | bytes 835592 | tf_op jit(solution)/shard_map/ppermute | solution.py:281
  29.4 36.6 %collective-permute-start.4 = (bf16[272,512]{1,0:T(8,128)(2,1)S(1)}, bf16[272,512]{1,0:T(8,128)(2,1)S(1)}, u32[]{:S(2)}, u32[]{:S(2)}) collective-permute-start(bf16[272,512]{1,0:T(8,128)(2,1)S(1)} %copy-done.16), channel_id=1, source_target_pairs={{0,16},{4,20},{8,24},{12,28},{16,0},{20,4},{24,8},{28,12},{1,17},{... | collective-permute-start | bytes 835592 | tf_op jit(solution)/shard_map/ppermute | solution.py:281
  29.4 36.7 %collective-permute-start.3 = (bf16[272,512]{1,0:T(8,128)(2,1)S(1)}, bf16[272,512]{1,0:T(8,128)(2,1)S(1)}, u32[]{:S(2)}, u32[]{:S(2)}) collective-permute-start(bf16[272,512]{1,0:T(8,128)(2,1)S(1)} %copy-done.16), channel_id=1, source_target_pairs={{0,8},{4,12},{8,0},{12,4},{16,24},{20,28},{24,16},{28,20},{1,9},{5... | collective-permute-start | bytes 835592 | tf_op jit(solution)/shard_map/ppermute | solution.py:281
  67.2 39.5 %collective-permute-start.6 = (bf16[1088,512]{1,0:T(8,128)(2,1)}, bf16[1088,512]{1,0:T(8,128)(2,1)}, u32[]{:S(2)}, u32[]{:S(2)}) collective-permute-start(bf16[1088,512]{1,0:T(8,128)(2,1)} %pad_maximum_fusion.3), channel_id=1, source_target_pairs={{0,4},{4,0},{8,12},{12,8},{16,20},{20,16},{24,28},{28,24},{1,5},{5... | collective-permute-start | bytes 3342344 | tf_op jit(solution)/shard_map/ppermute | solution.py:281
  81.5 71.4 %collective-permute-start.16 = (bf16[256,3072]{1,0:T(8,128)(2,1)}, bf16[256,3072]{1,0:T(8,128)(2,1)}, u32[]{:S(2)}, u32[]{:S(2)}) collective-permute-start(bf16[256,3072]{1,0:T(8,128)(2,1)} %get-tuple-element.40), channel_id=1, source_target_pairs={{0,8},{4,12},{8,0},{12,4},{16,24},{20,28},{24,16},{28,20},{1,9},{5... | collective-permute-start | bytes 4718600 | tf_op jit(solution)/shard_map/ppermute | solution.py:281
  197.3 543.4 %reduce-scatter.7.cloned.1.call-start = ((), (), s32[]{:S(2)}) async-start(), calls=%async_computation.7 | async-start | bytes 5242880 | tf_op jit(solution)/shard_map/reduce_scatter | solution.py:503
  236.8 25.4 %collective-permute-start.8 = (bf16[256,2048]{1,0:T(8,128)(2,1)S(1)}, bf16[256,2048]{1,0:T(8,128)(2,1)}, u32[]{:S(2)}, u32[]{:S(2)}) collective-permute-start(bf16[256,2048]{1,0:T(8,128)(2,1)S(1)} %add_convert_fusion.1), channel_id=1, source_target_pairs={{0,1},{1,0},{2,3},{3,2},{4,5},{5,4},{6,7},{7,6},{8,9},{9,8},{10,11... | collective-permute-start | bytes 3145736 | tf_op jit(solution)/shard_map/ppermute | solution.py:287
  267.0 24.3 %collective-permute-start.9 = (bf16[256,2048]{1,0:T(8,128)(2,1)S(1)}, bf16[256,2048]{1,0:T(8,128)(2,1)S(1)}, u32[]{:S(2)}, u32[]{:S(2)}) collective-permute-start(bf16[256,2048]{1,0:T(8,128)(2,1)S(1)} %get-tuple-element.72), channel_id=1, source_target_pairs={{0,1},{1,0},{2,3},{3,2},{4,5},{5,4},{6,7},{7,6},{8,9},{9,8},{10,11... | collective-permute-start | bytes 3145736 | tf_op jit(solution)/shard_map/ppermute | solution.py:287
  268.6 49.6 %collective-permute-start.10 = (bf16[256,2048]{1,0:T(8,128)(2,1)S(1)}, bf16[256,2048]{1,0:T(8,128)(2,1)S(1)}, u32[]{:S(2)}, u32[]{:S(2)}) collective-permute-start(bf16[256,2048]{1,0:T(8,128)(2,1)S(1)} %get-tuple-element.72), channel_id=1, source_target_pairs={{0,8},{4,12},{8,0},{12,4},{16,24},{20,28},{24,16},{28,20},{1,9},{5... | collective-permute-start | bytes 3145736 | tf_op jit(solution)/shard_map/ppermute | solution.py:281
  291.4 39.7 %collective-permute-start.11 = (bf16[128,2048]{1,0:T(8,128)(2,1)S(1)}, bf16[128,2048]{1,0:T(8,128)(2,1)S(1)}, u32[]{:S(2)}, u32[]{:S(2)}) collective-permute-start(bf16[128,2048]{1,0:T(8,128)(2,1)S(1)} %slice.271), channel_id=1, source_target_pairs={{0,8},{4,12},{8,0},{12,4},{16,24},{20,28},{24,16},{28,20},{1,9},{5... | collective-permute-start | bytes 1572872 | tf_op jit(solution)/shard_map/ppermute | solution.py:281
  332.9 47.3 %collective-permute-start.17 = (bf16[256,2048]{1,0:T(8,128)(2,1)S(1)}, bf16[256,2048]{1,0:T(8,128)(2,1)S(1)}, u32[]{:S(2)}, u32[]{:S(2)}) collective-permute-start(bf16[256,2048]{1,0:T(8,128)(2,1)S(1)} %get-tuple-element.42), channel_id=1, source_target_pairs={{0,8},{4,12},{8,0},{12,4},{16,24},{20,28},{24,16},{28,20},{1,9},{5... | collective-permute-start | bytes 3145736 | tf_op jit(solution)/shard_map/ppermute | solution.py:281
  380.2 24.6 %collective-permute-start.18 = (bf16[256,2048]{1,0:T(8,128)(2,1)S(1)}, bf16[256,2048]{1,0:T(8,128)(2,1)S(1)}, u32[]{:S(2)}, u32[]{:S(2)}) collective-permute-start(bf16[256,2048]{1,0:T(8,128)(2,1)S(1)} %collective-permute-done.17), channel_id=1, source_target_pairs={{0,1},{1,0},{2,3},{3,2},{4,5},{5,4},{6,7},{7,6},{8,9},{9,8},{10,11... | collective-permute-start | bytes 3145736 | tf_op jit(solution)/shard_map/ppermute | solution.py:287
  498.2 243.0 %reduce-scatter.5.cloned.1.call-start = ((), (), s32[]{:S(2)}) async-start(), calls=%async_computation.6 | async-start | bytes 10485760 | tf_op jit(solution)/shard_map/reduce_scatter | solution.py:503
  518.8 30.0 %collective-permute-start.21 = (bf16[512,1024]{1,0:T(8,128)(2,1)}, bf16[512,1024]{1,0:T(8,128)(2,1)S(1)}, u32[]{:S(2)}, u32[]{:S(2)}) collective-permute-start(bf16[512,1024]{1,0:T(8,128)(2,1)} %pad_maximum_fusion.4), channel_id=1, source_target_pairs={{0,1},{1,0},{2,3},{3,2},{4,5},{5,4},{6,7},{7,6},{8,9},{9,8},{10,11... | collective-permute-start | bytes 3145736 | tf_op jit(solution)/shard_map/ppermute | solution.py:287
  520.2 43.8 %collective-permute-start.23 = (bf16[512,1024]{1,0:T(8,128)(2,1)S(1)}, bf16[512,1024]{1,0:T(8,128)(2,1)S(1)}, u32[]{:S(2)}, u32[]{:S(2)}) collective-permute-start(bf16[512,1024]{1,0:T(8,128)(2,1)S(1)} %concatenate.113), channel_id=1, source_target_pairs={{0,8},{4,12},{8,0},{12,4},{16,24},{20,28},{24,16},{28,20},{1,9},{5... | collective-permute-start | bytes 3145736 | tf_op jit(solution)/shard_map/ppermute | solution.py:281
  548.7 260.5 %reduce-scatter.9.cloned.1.call-start = ((), (), s32[]{:S(2)}) async-start(), calls=%async_computation.8 | async-start | bytes 2359296 | tf_op jit(solution)/shard_map/reduce_scatter | solution.py:503
  576.6 21.2 %collective-permute-start.26 = (bf16[1024,2048]{1,0:T(8,128)(2,1)S(1)}, bf16[1024,2048]{1,0:T(8,128)(2,1)}, u32[]{:S(2)}, u32[]{:S(2)}) collective-permute-start(bf16[1024,2048]{1,0:T(8,128)(2,1)S(1)} %fusion.16), channel_id=1, source_target_pairs={{0,2},{2,0},{1,3},{3,1},{4,6},{6,4},{5,7},{7,5},{8,10},{10,8},{9,1... | collective-permute-start | bytes 12582920 | tf_op jit(solution)/shard_map/ppermute | solution.py:284
  613.5 24.9 %collective-permute-start.27 = (bf16[512,1024]{1,0:T(8,128)(2,1)S(1)}, bf16[512,1024]{1,0:T(8,128)(2,1)S(1)}, u32[]{:S(2)}, u32[]{:S(2)}) collective-permute-start(bf16[512,1024]{1,0:T(8,128)(2,1)S(1)} %pad_maximum_fusion.5), channel_id=1, source_target_pairs={{0,1},{1,0},{2,3},{3,2},{4,5},{5,4},{6,7},{7,6},{8,9},{9,8},{10,11... | collective-permute-start | bytes 3145736 | tf_op jit(solution)/shard_map/ppermute | solution.py:287
  614.1 49.9 %collective-permute-start.29 = (bf16[512,1024]{1,0:T(8,128)(2,1)S(1)}, bf16[512,1024]{1,0:T(8,128)(2,1)S(1)}, u32[]{:S(2)}, u32[]{:S(2)}) collective-permute-start(bf16[512,1024]{1,0:T(8,128)(2,1)S(1)} %concatenate.114), channel_id=1, source_target_pairs={{0,8},{4,12},{8,0},{12,4},{16,24},{20,28},{24,16},{28,20},{1,9},{5... | collective-permute-start | bytes 3145736 | tf_op jit(solution)/shard_map/ppermute | solution.py:281
  638.8 50.1 %collective-permute-start.28 = (bf16[256,1024]{1,0:T(8,128)(2,1)S(1)}, bf16[256,1024]{1,0:T(8,128)(2,1)S(1)}, u32[]{:S(2)}, u32[]{:S(2)}) collective-permute-start(bf16[256,1024]{1,0:T(8,128)(2,1)S(1)} %fusion.36), channel_id=1, source_target_pairs={{0,8},{4,12},{8,0},{12,4},{16,24},{20,28},{24,16},{28,20},{1,9},{5... | collective-permute-start | bytes 1572872 | tf_op jit(solution)/shard_map/ppermute | solution.py:281
  705.3 23.7 %collective-permute-start.31 = (bf16[256,2048]{1,0:T(8,128)(2,1)S(1)}, bf16[256,2048]{1,0:T(8,128)(2,1)}, u32[]{:S(2)}, u32[]{:S(2)}) collective-permute-start(bf16[256,2048]{1,0:T(8,128)(2,1)S(1)} %get-tuple-element.65), channel_id=1, source_target_pairs={{0,1},{1,0},{2,3},{3,2},{4,5},{5,4},{6,7},{7,6},{8,9},{9,8},{10,11... | collective-permute-start | bytes 3145736 | tf_op jit(solution)/shard_map/ppermute | solution.py:287
  741.2 209.2 %reduce-scatter.11.cloned.1.call-start = ((), (), s32[]{:S(2)}) async-start(), calls=%async_computation.9 | async-start | bytes 7077888 | tf_op jit(solution)/shard_map/reduce_scatter | solution.py:503
  743.6 43.9 %collective-permute-start.33 = (bf16[256,2048]{1,0:T(8,128)(2,1)}, bf16[256,2048]{1,0:T(8,128)(2,1)S(1)}, u32[]{:S(2)}, u32[]{:S(2)}) collective-permute-start(bf16[256,2048]{1,0:T(8,128)(2,1)} %constant_dynamic-slice_fusion.1), channel_id=1, source_target_pairs={{0,8},{4,12},{8,0},{12,4},{16,24},{20,28},{24,16},{28,20},{1,9},{5... | collective-permute-start | bytes 3145736 | tf_op jit(solution)/shard_map/ppermute | solution.py:281
  826.8 26.3 %collective-permute-start.35 = (bf16[256,2048]{1,0:T(8,128)(2,1)}, bf16[256,2048]{1,0:T(8,128)(2,1)}, u32[]{:S(2)}, u32[]{:S(2)}) collective-permute-start(bf16[256,2048]{1,0:T(8,128)(2,1)} %fusion.29), channel_id=1, source_target_pairs={{0,1},{1,0},{2,3},{3,2},{4,5},{5,4},{6,7},{7,6},{8,9},{9,8},{10,11... | collective-permute-start | bytes 3145736 | tf_op jit(solution)/shard_map/ppermute | solution.py:287
  829.8 52.1 %collective-permute-start.43 = (bf16[256,1024]{1,0:T(8,128)(2,1)}, bf16[256,1024]{1,0:T(8,128)(2,1)}, u32[]{:S(2)}, u32[]{:S(2)}) collective-permute-start(bf16[256,1024]{1,0:T(8,128)(2,1)} %constant_dynamic-slice_fusion), channel_id=1, source_target_pairs={{0,8},{4,12},{8,0},{12,4},{16,24},{20,28},{24,16},{28,20},{1,9},{5... | collective-permute-start | bytes 1572872 | tf_op jit(solution)/shard_map/ppermute | solution.py:281
  830.7 60.6 %collective-permute-start.25 = (bf16[256,2048]{1,0:T(8,128)(2,1)}, bf16[256,2048]{1,0:T(8,128)(2,1)}, u32[]{:S(2)}, u32[]{:S(2)}) collective-permute-start(bf16[256,2048]{1,0:T(8,128)(2,1)} %get-tuple-element.88.own_ref), channel_id=1, source_target_pairs={{0,1},{1,0},{2,3},{3,2},{4,5},{5,4},{6,7},{7,6},{8,9},{9,8},{10,11... | collective-permute-start | bytes 3145736 | tf_op jit(solution)/shard_map/ppermute | solution.py:287
  834.8 60.2 %collective-permute-start.42 = (bf16[128,4096]{1,0:T(8,128)(2,1)}, bf16[128,4096]{1,0:T(8,128)(2,1)}, u32[]{:S(2)}, u32[]{:S(2)}) collective-permute-start(bf16[128,4096]{1,0:T(8,128)(2,1)} %shard_map.214), channel_id=1, source_target_pairs={{0,2},{2,0},{1,3},{3,1},{4,6},{6,4},{5,7},{7,5},{8,10},{10,8},{9,1... | collective-permute-start | bytes 3145736 | tf_op jit(solution)/shard_map/ppermute | solution.py:284
  877.4 24.5 %collective-permute-start.36 = (bf16[256,2048]{1,0:T(8,128)(2,1)S(1)}, bf16[256,2048]{1,0:T(8,128)(2,1)S(1)}, u32[]{:S(2)}, u32[]{:S(2)}) collective-permute-start(bf16[256,2048]{1,0:T(8,128)(2,1)S(1)} %add_convert_fusion.own_ref), channel_id=1, source_target_pairs={{0,1},{1,0},{2,3},{3,2},{4,5},{5,4},{6,7},{7,6},{8,9},{9,8},{10,11... | collective-permute-start | bytes 3145736 | tf_op jit(solution)/shard_map/ppermute | solution.py:287
  (58 other events, 878.9 us)
Sparse Core Ops, SparseCore 0:
  15.7 181.5 all-gather.2
  199.1 223.5 all-gather.4
  498.3 86.2 reduce-scatter.6
  587.6 153.5 reduce-scatter.4
  743.9 65.2 reduce-scatter.8
  811.4 138.9 reduce-scatter.10

commit v10 on v9

--- a/solution.py
+++ b/solution.py
@@ -475,10 +475,10 @@
             high_sum = pick(high, 0) + pick(high_zl, 0) + high_tp.astype(f32)
             return (low_sent, first, second), cat([low_sum, high_sum], 1)
 
-        grad_hidden = matmul(grad_out, weight_d)
+        prod_d = contract_rows(grad_out, hidden).astype(bf16)
+        grad_hidden = matmul(after(grad_out, prod_d), weight_d)
         grad_gate = (grad_hidden * up_pre * gate_sig * (1.0 + gate_pre * (1.0 - gate_sig))).astype(bf16)
         grad_up = (grad_hidden * gate_act).astype(bf16)
-        prod_d = contract_rows(grad_out, hidden).astype(bf16)
         late_hidden = after(hidden, prod_d)
         (sent_m, first_m, second_m), mlp = from_tokens(lambda where: contract_cols(late_hidden[where], weight_d))
         grad_gate, grad_up = after((grad_gate, grad_up), sent_m)

time: 975 us -> 969 us (level)
  transfers between devices with their start and end apart: 52 -> 52, of which waited for: 36 -> 33; matrix products, arithmetic and copies ran while one was open for 21% -> 24% of each run, Pallas kernels for 9% -> 8%
where the time goes in v10:
time: 969 us; the launch traced here: 962 us
  waiting for transfers between devices  518 us (53%)
  matrix products  198 us (20%)
  Pallas kernels  91 us (9%)
  local copies, waits for them, and re-layouts  62.4 us (6%)
  starting transfers between devices  40.6 us (4%)
  other arithmetic  37.8 us (4%)
  between operations  15.1 us (2%)
    ppermute x17, waiting for transfers between devices, across(): return lax.ppermute(values, 'shard', [(i, i ^ mask) for i in range(shards)])  253 us
    ppermute x13, waiting for transfers between devices, swap_tp(): return lax.ppermute(values, 'tp', [(0, 1), (1, 0)])  151 us
    dot_general x10, matrix products, contract_cols(): lax.dot_general(left, right, (((1,), (1,)), ((), ())), preferred_element_...  78.6 us
    dot_general x5, matrix products, matmul(): return jnp.dot(left, right, preferred_element_type=jnp.float32)  69.7 us
    dot_general x4, matrix products, contract_rows(): lax.dot_general(left, right, (((0,), (0,)), ((), ())), preferred_element_...  49.6 us
    reduce_scatter x4, waiting for transfers between devices, scatter(): lax.psum_scatter(values.astype(bf16), 'shard', scatter_dimension=0, tiled...  49 us
    all_gather x1, waiting for transfers between devices, per_device(): lax.all_gather(block_qkv, 'shard', axis=0, tiled=True, axis_index_groups=...  40.6 us
    pallas_call x11, Pallas kernels, small_call(): pl.pallas_call(body, grid_spec=pltpu.PrefetchScalarGridSpec(num_scalar_pr...  36.6 us
  transfers between devices with their start and end apart: 52, of which 33 were waited for; matrix products, arithmetic and copies ran while one was open for 24% of the time, Pallas kernels for 8%

profile of v10, /device:TPU:0, one launch (start us, length us, event | category | flops | bytes accessed | tf_op | source)
XLA Modules:
  0.0 962.5 jit_solution(18172407956895278772)
XLA Ops:
  30.6 12.2 %collective-permute-done.5 = bf16[272,512]{1,0:T(8,128)(2,1)S(1)} collective-permute-done((bf16[272,512]{1,0:T(8,128)(2,1)S(1)}, bf16[272,512]{1,0:T(8,128)(2,1)S(1)}, u32[]{:S(2)}, u32[]{:S(2)}) %collective-permute-start.5) | collective-permute-done | bytes 278560 | tf_op jit(solution)/shard_map/ppermute | solution.py:281
  42.9 23.1 %collective-permute-done.4 = bf16[272,512]{1,0:T(8,128)(2,1)S(1)} collective-permute-done((bf16[272,512]{1,0:T(8,128)(2,1)S(1)}, bf16[272,512]{1,0:T(8,128)(2,1)S(1)}, u32[]{:S(2)}, u32[]{:S(2)}) %collective-permute-start.4) | collective-permute-done | bytes 278560 | tf_op jit(solution)/shard_map/ppermute | solution.py:281
  84.1 22.6 %collective-permute-done.6 = bf16[1088,512]{1,0:T(8,128)(2,1)} collective-permute-done((bf16[1088,512]{1,0:T(8,128)(2,1)}, bf16[1088,512]{1,0:T(8,128)(2,1)}, u32[]{:S(2)}, u32[]{:S(2)}) %collective-permute-start.6) | collective-permute-done | bytes 1114144 | tf_op jit(solution)/shard_map/ppermute | solution.py:281
  135.4 17.5 %collective-permute-done.16.other = bf16[256,3072]{1,0:T(8,128)(2,1)} collective-permute-done((bf16[256,3072]{1,0:T(8,128)(2,1)}, bf16[256,3072]{1,0:T(8,128)(2,1)}, u32[]{:S(2)}, u32[]{:S(2)}) %collective-permute-start.16) | collective-permute-done | bytes 1572896 | tf_op jit(solution)/shard_map/ppermute | solution.py:281
  156.7 40.6 %all-gather.3.cloned.1.call-done = bf16[2048,1536]{1,0:T(8,128)(2,1)} async-done(((bf16[256,1536]{1,0:T(8,128)(2,1)}), bf16[2048,1536]{1,0:T(8,128)(2,1)}) %all-gather.3.cloned.1.call-update) | async-done | bytes 6291472 | tf_op jit(solution)/shard_map/all_gather | solution.py:363
  198.8 11.7 %fusion.86.qkv_ref = f32[1024,1536]{1,0:T(8,128)} fusion(bf16[1024,2048]{1,0:T(8,128)(2,1)} %get-tuple-element.84, bf16[2048,1536]{1,0:T(8,128)(2,1)} %all-gather.3.cloned.1.call-done), kind=kOutput, calls=%fused_computation.194 | convolution fusion | flops 6442450944 | bytes 16777216 | tf_op jit(solution)/shard_map/dot_general | solution.py:22
  210.5 13.3 %shard_map.206 = (bf16[1024,512]{1,0:T(8,128)(2,1)}, bf16[1024,1536]{1,0:T(8,128)(2,1)}) custom-call(s32[1024]{0:T(1024)} %bitcast.79, f32[1024,1536]{1,0:T(8,128)} %fusion.86.qkv_ref, f32[1024,128]{1,0:T(8,128)} %get-tuple-element.108.cos_ref, f32[1024,128]{1,0:T(8,128)} %get-tuple-element.109.sin_ref, s32[1024,1]{1,0:T(8,128)} %copy.23.seg_col, ...), custom_call_target="tpu_custom_call" | custom-call | tf_op jit(solution)/shard_map/pallas_call | solution.py:195
  239.5 21.2 %collective-permute-done.8 = bf16[256,2048]{1,0:T(8,128)(2,1)} collective-permute-done((bf16[256,2048]{1,0:T(8,128)(2,1)S(1)}, bf16[256,2048]{1,0:T(8,128)(2,1)}, u32[]{:S(2)}, u32[]{:S(2)}) %collective-permute-start.8) | collective-permute-done | bytes 1048608 | tf_op jit(solution)/shard_map/ppermute | solution.py:287
  273.0 16.9 %collective-permute-done.9 = bf16[256,2048]{1,0:T(8,128)(2,1)S(1)} collective-permute-done((bf16[256,2048]{1,0:T(8,128)(2,1)S(1)}, bf16[256,2048]{1,0:T(8,128)(2,1)S(1)}, u32[]{:S(2)}, u32[]{:S(2)}) %collective-permute-start.9) | collective-permute-done | bytes 1048608 | tf_op jit(solution)/shard_map/ppermute | solution.py:287
  293.9 24.4 %collective-permute-done.10 = bf16[256,2048]{1,0:T(8,128)(2,1)S(1)} collective-permute-done((bf16[256,2048]{1,0:T(8,128)(2,1)S(1)}, bf16[256,2048]{1,0:T(8,128)(2,1)S(1)}, u32[]{:S(2)}, u32[]{:S(2)}) %collective-permute-start.10) | collective-permute-done | bytes 1048608 | tf_op jit(solution)/shard_map/ppermute | solution.py:281
  333.0 47.0 %collective-permute-done.17 = bf16[256,2048]{1,0:T(8,128)(2,1)S(1)} collective-permute-done((bf16[256,2048]{1,0:T(8,128)(2,1)S(1)}, bf16[256,2048]{1,0:T(8,128)(2,1)S(1)}, u32[]{:S(2)}, u32[]{:S(2)}) %collective-permute-start.17) | collective-permute-done | bytes 1048608 | tf_op jit(solution)/shard_map/ppermute | solution.py:281
  382.0 22.9 %collective-permute-done.18 = bf16[256,2048]{1,0:T(8,128)(2,1)S(1)} collective-permute-done((bf16[256,2048]{1,0:T(8,128)(2,1)S(1)}, bf16[256,2048]{1,0:T(8,128)(2,1)S(1)}, u32[]{:S(2)}, u32[]{:S(2)}) %collective-permute-start.18) | collective-permute-done | bytes 1048608 | tf_op jit(solution)/shard_map/ppermute | solution.py:287
  422.7 14.8 %fusion.8 = f32[2048,1024]{1,0:T(8,128)} fusion(bf16[2048,2048]{1,0:T(8,128)(2,1)} %constant_dynamic-update-slice_fusion.7, bf16[2048,3072]{1,0:T(8,128)(2,1)} %all-gather.5.cloned.1.call-done), kind=kOutput, calls=%fused_computation.20 | convolution fusion | flops 8589934592 | bytes 20971520 | tf_op jit(solution)/shard_map/dot_general | solution.py:22
  437.5 15.2 %multiply_convert_fusion.2 = (bf16[2048,1024]{1,0:T(8,128)(2,1)S(1)}, f32[2048,1024]{1,0:T(8,128)}) fusion(f32[2048,1024]{1,0:T(8,128)} %fusion.8, bf16[2048,2048]{1,0:T(8,128)(2,1)S(1)} %copy-done.22, bf16[2048,3072]{1,0:T(8,128)(2,1)} %all-gather.5.cloned.1.call-done), kind=kOutput, calls=%fused_computation.8 | convolution fusion | flops 8602517504 | bytes 33554432 | tf_op jit(solution)/shard_map/dot_general | solution.py:22
  454.6 13.2 %convolution_convert_fusion.3 = bf16[2048,1024]{1,0:T(8,128)(2,1)} fusion(bf16[2048,2048]{1,0:T(8,128)(2,1)} %constant_dynamic-update-slice_fusion.14, bf16[2048,1024]{1,0:T(8,128)(2,1)S(1)} %get-tuple-element.44), kind=kOutput, calls=%fused_computation.29 | convolution fusion | flops 8592031744 | bytes 16777216 | tf_op jit(solution)/shard_map/dot_general | solution.py:26
  477.5 20.6 %multiply_convert_fusion = (bf16[2048,1024]{1,0:T(8,128)(2,1)S(1)}, bf16[2048,1024]{1,0:T(8,128)(2,1)S(1)}) fusion(f32[2048,1024]{1,0:T(8,128)} %fusion.8, f32[2048,1024]{1,0:T(8,128)} %get-tuple-element.102, bf16[2048,2048]{1,0:T(8,128)(2,1)} %constant_dynamic-update-slice_fusion.14, bf16[2048,3072]{1,0:T(8,128)(2,1)} %all-gather.5.cloned.1.call-done), kind=kOutput, calls=%fused_computation.5 | convolution fusion | flops 8617197568 | bytes 37748736 | tf_op jit(solution)/shard_map/dot_general | solution.py:22
  498.1 12.1 %fusion.84 = (bf16[1024,2048]{1,0:T(8,128)(2,1)S(1)}, f32[1024,2048]{1,0:T(8,128)}) fusion(bf16[1024,2048]{1,0:T(8,128)(2,1)} %collective-permute-done.20, bf16[2048,3072]{1,0:T(8,128)(2,1)} %all-gather.5.cloned.1.call-done, bf16[2048,1024]{1,0:T(8,128)(2,1)} %copy-done.35), kind=kOutput, calls=%fused_computation.192 | convolution fusion | flops 4301258752 | bytes 23068672 | tf_op jit(solution)/shard_map/dot_general | solution.py:32
  520.6 20.8 %convolution_convert_fusion.1 = bf16[2048,2048]{1,0:T(8,128)(2,1)} fusion(bf16[2048,2048]{1,0:T(8,128)(2,1)S(1)} %bitcast.83, bf16[2048,2048]{1,0:T(8,128)(2,1)S(1)} %constant_dynamic-update-slice_fusion.19), kind=kOutput, calls=%fused_computation.13 | convolution fusion | flops 17184063488 | bytes 25165824 | tf_op jit(solution)/shard_map/dot_general | solution.py:26
  541.5 21.0 %collective-permute-done.23 = bf16[512,1024]{1,0:T(8,128)(2,1)S(1)} collective-permute-done((bf16[512,1024]{1,0:T(8,128)(2,1)}, bf16[512,1024]{1,0:T(8,128)(2,1)S(1)}, u32[]{:S(2)}, u32[]{:S(2)}) %collective-permute-start.23) | collective-permute-done | bytes 1048608 | tf_op jit(solution)/shard_map/ppermute | solution.py:281
  562.5 12.7 %fusion.16 = bf16[1024,2048]{1,0:T(8,128)(2,1)S(1)} fusion(bf16[2048,3072]{1,0:T(8,128)(2,1)} %all-gather.5.cloned.1.call-done, bf16[2048,2048]{1,0:T(8,128)(2,1)} %copy-done.11), kind=kOutput, calls=%fused_computation.27 | convolution fusion | flops 8592031744 | bytes 16777216 | tf_op jit(solution)/shard_map/dot_general | solution.py:32
  578.4 21.9 %collective-permute-done.22 = bf16[256,1024]{1,0:T(8,128)(2,1)S(1)} collective-permute-done((bf16[256,1024]{1,0:T(8,128)(2,1)S(1)}, bf16[256,1024]{1,0:T(8,128)(2,1)S(1)}, u32[]{:S(2)}, u32[]{:S(2)}) %collective-permute-start.22) | collective-permute-done | bytes 524320 | tf_op jit(solution)/shard_map/ppermute | solution.py:281
  602.3 15.4 %fusion.85 = (bf16[1024,2048]{1,0:T(8,128)(2,1)S(1)}, f32[1024,2048]{1,0:T(8,128)}) fusion(bf16[1024,2048]{1,0:T(8,128)(2,1)} %collective-permute-done.26, bf16[2048,3072]{1,0:T(8,128)(2,1)} %all-gather.5.cloned.1.call-done, bf16[2048,2048]{1,0:T(8,128)(2,1)} %copy-done.11), kind=kOutput, calls=%fused_computation.193 | convolution fusion | flops 8596226048 | bytes 29360128 | tf_op jit(solution)/shard_map/dot_general | solution.py:32
  622.8 20.5 %collective-permute-done.27 = bf16[512,1024]{1,0:T(8,128)(2,1)S(1)} collective-permute-done((bf16[512,1024]{1,0:T(8,128)(2,1)S(1)}, bf16[512,1024]{1,0:T(8,128)(2,1)S(1)}, u32[]{:S(2)}, u32[]{:S(2)}) %collective-permute-start.27) | collective-permute-done | bytes 1048608 | tf_op jit(solution)/shard_map/ppermute | solution.py:287
  646.6 24.6 %collective-permute-done.29 = bf16[512,1024]{1,0:T(8,128)(2,1)S(1)} collective-permute-done((bf16[512,1024]{1,0:T(8,128)(2,1)S(1)}, bf16[512,1024]{1,0:T(8,128)(2,1)S(1)}, u32[]{:S(2)}, u32[]{:S(2)}) %collective-permute-start.29) | collective-permute-done | bytes 1048608 | tf_op jit(solution)/shard_map/ppermute | solution.py:281
  671.4 11.6 %collective-permute-done.28 = bf16[256,1024]{1,0:T(8,128)(2,1)S(1)} collective-permute-done((bf16[256,1024]{1,0:T(8,128)(2,1)S(1)}, bf16[256,1024]{1,0:T(8,128)(2,1)S(1)}, u32[]{:S(2)}, u32[]{:S(2)}) %collective-permute-start.28) | collective-permute-done | bytes 524320 | tf_op jit(solution)/shard_map/ppermute | solution.py:281
  700.8 23.2 %collective-permute-done.31 = bf16[256,2048]{1,0:T(8,128)(2,1)} collective-permute-done((bf16[256,2048]{1,0:T(8,128)(2,1)S(1)}, bf16[256,2048]{1,0:T(8,128)(2,1)}, u32[]{:S(2)}, u32[]{:S(2)}) %collective-permute-start.31) | collective-permute-done | bytes 1048608 | tf_op jit(solution)/shard_map/ppermute | solution.py:287
  745.4 24.5 %shard_map.212 = bf16[1024,1536]{1,0:T(8,128)(2,1)} custom-call(s32[1024]{0:T(1024)} %bitcast.80, bf16[1024,1536]{1,0:T(8,128)(2,1)} %get-tuple-element.51.kept_ref, bf16[1024,512]{1,0:T(8,128)(2,1)} %convolution_convert_fusion.7.do_ref, f32[1024,128]{1,0:T(8,128)} %get-tuple-element.108.cos_ref, f32[1024,128]{1,0:T(8,128)} %get-tuple-element.109.sin_ref, ...), custom_call_target="tpu_custom_call" | custom-call | tf_op jit(solution)/shard_map/pallas_call | solution.py:254
  770.0 16.3 %collective-permute-done.33.theirs = bf16[256,2048]{1,0:T(8,128)(2,1)S(1)} collective-permute-done((bf16[256,2048]{1,0:T(8,128)(2,1)}, bf16[256,2048]{1,0:T(8,128)(2,1)S(1)}, u32[]{:S(2)}, u32[]{:S(2)}) %collective-permute-start.33) | collective-permute-done | bytes 1048608 | tf_op jit(solution)/shard_map/ppermute | solution.py:281
  786.3 12.0 %convolution_convert_fusion = bf16[2048,1536]{1,0:T(8,128)(2,1)} fusion(bf16[1024,2048]{1,0:T(8,128)(2,1)} %get-tuple-element.84, bf16[1024,1536]{1,0:T(8,128)(2,1)} %shard_map.212), kind=kOutput, calls=%fused_computation.12 | convolution fusion | flops 6445596672 | bytes 13631488 | tf_op jit(solution)/shard_map/dot_general | solution.py:26
  828.1 19.2 %collective-permute-done.35 = bf16[256,2048]{1,0:T(8,128)(2,1)} collective-permute-done((bf16[256,2048]{1,0:T(8,128)(2,1)}, bf16[256,2048]{1,0:T(8,128)(2,1)}, u32[]{:S(2)}, u32[]{:S(2)}) %collective-permute-start.35) | collective-permute-done | bytes 1048608 | tf_op jit(solution)/shard_map/ppermute | solution.py:287
  855.2 14.0 %collective-permute-done.37 = f32[2,2048]{1,0:T(2,128)S(1)} collective-permute-done((f32[2,2048]{1,0:T(2,128)S(1)}, f32[2,2048]{1,0:T(2,128)S(1)}, u32[]{:S(2)}, u32[]{:S(2)}) %collective-permute-start.37) | collective-permute-done | bytes 16416 | tf_op jit(solution)/shard_map/ppermute | solution.py:287
  900.9 44.0 %reduce-scatter.11.cloned.1.call-done = bf16[256,1536]{1,0:T(8,128)(2,1)} async-done(((bf16[2048,1536]{1,0:T(8,128)(2,1)}), bf16[256,1536]{1,0:T(8,128)(2,1)}) %reduce-scatter.11.cloned.1.call-update) | async-done | bytes 786448 | tf_op jit(solution)/shard_map/reduce_scatter | solution.py:503
  (288 shorter events, 296.6 us)
Async XLA Ops:
  7.2 190.1 %all-gather.3.cloned.1.call-start = ((), (), s32[]{:S(2)}) async-start(), calls=%async_computation.4 | async-start | bytes 7077888 | tf_op jit(solution)/shard_map/all_gather | solution.py:363
  15.6 407.1 %all-gather.5.cloned.1.call-start = ((), (), s32[]{:S(2)}) async-start(), calls=%async_computation.5 | async-start | bytes 15728640 | tf_op jit(solution)/shard_map/all_gather | solution.py:412
  18.8 56.7 %collective-permute-start.15 = (bf16[128,6144]{1,0:T(8,128)(2,1)}, bf16[128,6144]{1,0:T(8,128)(2,1)S(1)}, u32[]{:S(2)}, u32[]{:S(2)}) collective-permute-start(bf16[128,6144]{1,0:T(8,128)(2,1)} %shard_map.207), channel_id=1, source_target_pairs={{0,2},{2,0},{1,3},{3,1},{4,6},{6,4},{5,7},{7,5},{8,10},{10,8},{9,1... | collective-permute-start | bytes 4718600 | tf_op jit(solution)/shard_map/ppermute | solution.py:284
  24.0 101.2 %collective-permute-start = (bf16[512,2048]{1,0:T(8,128)(2,1)}, bf16[512,2048]{1,0:T(8,128)(2,1)}, u32[]{:S(2)}, u32[]{:S(2)}) collective-permute-start(bf16[512,2048]{1,0:T(8,128)(2,1)} %shard_map.203), channel_id=1, source_target_pairs={{0,2},{2,0},{1,3},{3,1},{4,6},{6,4},{5,7},{7,5},{8,10},{10,8},{9,1... | collective-permute-start | bytes 6291464 | tf_op jit(solution)/shard_map/ppermute | solution.py:284
  29.4 36.6 %collective-permute-start.4 = (bf16[272,512]{1,0:T(8,128)(2,1)S(1)}, bf16[272,512]{1,0:T(8,128)(2,1)S(1)}, u32[]{:S(2)}, u32[]{:S(2)}) collective-permute-start(bf16[272,512]{1,0:T(8,128)(2,1)S(1)} %copy-done.14), channel_id=1, source_target_pairs={{0,16},{4,20},{8,24},{12,28},{16,0},{20,4},{24,8},{28,12},{1,17},{... | collective-permute-start | bytes 835592 | tf_op jit(solution)/shard_map/ppermute | solution.py:281
  29.4 36.7 %collective-permute-start.3 = (bf16[272,512]{1,0:T(8,128)(2,1)S(1)}, bf16[272,512]{1,0:T(8,128)(2,1)S(1)}, u32[]{:S(2)}, u32[]{:S(2)}) collective-permute-start(bf16[272,512]{1,0:T(8,128)(2,1)S(1)} %copy-done.14), channel_id=1, source_target_pairs={{0,8},{4,12},{8,0},{12,4},{16,24},{20,28},{24,16},{28,20},{1,9},{5... | collective-permute-start | bytes 835592 | tf_op jit(solution)/shard_map/ppermute | solution.py:281
  67.2 39.5 %collective-permute-start.6 = (bf16[1088,512]{1,0:T(8,128)(2,1)}, bf16[1088,512]{1,0:T(8,128)(2,1)}, u32[]{:S(2)}, u32[]{:S(2)}) collective-permute-start(bf16[1088,512]{1,0:T(8,128)(2,1)} %pad_maximum_fusion.3), channel_id=1, source_target_pairs={{0,4},{4,0},{8,12},{12,8},{16,20},{20,16},{24,28},{28,24},{1,5},{5... | collective-permute-start | bytes 3342344 | tf_op jit(solution)/shard_map/ppermute | solution.py:281
  81.5 71.4 %collective-permute-start.16 = (bf16[256,3072]{1,0:T(8,128)(2,1)}, bf16[256,3072]{1,0:T(8,128)(2,1)}, u32[]{:S(2)}, u32[]{:S(2)}) collective-permute-start(bf16[256,3072]{1,0:T(8,128)(2,1)} %get-tuple-element.41), channel_id=1, source_target_pairs={{0,8},{4,12},{8,0},{12,4},{16,24},{20,28},{24,16},{28,20},{1,9},{5... | collective-permute-start | bytes 4718600 | tf_op jit(solution)/shard_map/ppermute | solution.py:281
  197.3 538.3 %reduce-scatter.7.cloned.1.call-start = ((), (), s32[]{:S(2)}) async-start(), calls=%async_computation.7 | async-start | bytes 5242880 | tf_op jit(solution)/shard_map/reduce_scatter | solution.py:503
  235.4 25.4 %collective-permute-start.8 = (bf16[256,2048]{1,0:T(8,128)(2,1)S(1)}, bf16[256,2048]{1,0:T(8,128)(2,1)}, u32[]{:S(2)}, u32[]{:S(2)}) collective-permute-start(bf16[256,2048]{1,0:T(8,128)(2,1)S(1)} %add_convert_fusion.1), channel_id=1, source_target_pairs={{0,1},{1,0},{2,3},{3,2},{4,5},{5,4},{6,7},{7,6},{8,9},{9,8},{10,11... | collective-permute-start | bytes 3145736 | tf_op jit(solution)/shard_map/ppermute | solution.py:287
  265.6 24.3 %collective-permute-start.9 = (bf16[256,2048]{1,0:T(8,128)(2,1)S(1)}, bf16[256,2048]{1,0:T(8,128)(2,1)S(1)}, u32[]{:S(2)}, u32[]{:S(2)}) collective-permute-start(bf16[256,2048]{1,0:T(8,128)(2,1)S(1)} %get-tuple-element.74), channel_id=1, source_target_pairs={{0,1},{1,0},{2,3},{3,2},{4,5},{5,4},{6,7},{7,6},{8,9},{9,8},{10,11... | collective-permute-start | bytes 3145736 | tf_op jit(solution)/shard_map/ppermute | solution.py:287
  267.2 51.0 %collective-permute-start.10 = (bf16[256,2048]{1,0:T(8,128)(2,1)S(1)}, bf16[256,2048]{1,0:T(8,128)(2,1)S(1)}, u32[]{:S(2)}, u32[]{:S(2)}) collective-permute-start(bf16[256,2048]{1,0:T(8,128)(2,1)S(1)} %get-tuple-element.74), channel_id=1, source_target_pairs={{0,8},{4,12},{8,0},{12,4},{16,24},{20,28},{24,16},{28,20},{1,9},{5... | collective-permute-start | bytes 3145736 | tf_op jit(solution)/shard_map/ppermute | solution.py:281
  290.0 41.3 %collective-permute-start.11 = (bf16[128,2048]{1,0:T(8,128)(2,1)S(1)}, bf16[128,2048]{1,0:T(8,128)(2,1)S(1)}, u32[]{:S(2)}, u32[]{:S(2)}) collective-permute-start(bf16[128,2048]{1,0:T(8,128)(2,1)S(1)} %slice.271), channel_id=1, source_target_pairs={{0,8},{4,12},{8,0},{12,4},{16,24},{20,28},{24,16},{28,20},{1,9},{5... | collective-permute-start | bytes 1572872 | tf_op jit(solution)/shard_map/ppermute | solution.py:281
  333.0 47.0 %collective-permute-start.17 = (bf16[256,2048]{1,0:T(8,128)(2,1)S(1)}, bf16[256,2048]{1,0:T(8,128)(2,1)S(1)}, u32[]{:S(2)}, u32[]{:S(2)}) collective-permute-start(bf16[256,2048]{1,0:T(8,128)(2,1)S(1)} %get-tuple-element.43), channel_id=1, source_target_pairs={{0,8},{4,12},{8,0},{12,4},{16,24},{20,28},{24,16},{28,20},{1,9},{5... | collective-permute-start | bytes 3145736 | tf_op jit(solution)/shard_map/ppermute | solution.py:281
  380.0 24.8 %collective-permute-start.18 = (bf16[256,2048]{1,0:T(8,128)(2,1)S(1)}, bf16[256,2048]{1,0:T(8,128)(2,1)S(1)}, u32[]{:S(2)}, u32[]{:S(2)}) collective-permute-start(bf16[256,2048]{1,0:T(8,128)(2,1)S(1)} %collective-permute-done.17), channel_id=1, source_target_pairs={{0,1},{1,0},{2,3},{3,2},{4,5},{5,4},{6,7},{7,6},{8,9},{9,8},{10,11... | collective-permute-start | bytes 3145736 | tf_op jit(solution)/shard_map/ppermute | solution.py:287
  477.4 258.1 %reduce-scatter.5.cloned.1.call-start = ((), (), s32[]{:S(2)}) async-start(), calls=%async_computation.6 | async-start | bytes 10485760 | tf_op jit(solution)/shard_map/reduce_scatter | solution.py:503
  512.4 29.1 %collective-permute-start.21 = (bf16[512,1024]{1,0:T(8,128)(2,1)}, bf16[512,1024]{1,0:T(8,128)(2,1)}, u32[]{:S(2)}, u32[]{:S(2)}) collective-permute-start(bf16[512,1024]{1,0:T(8,128)(2,1)} %pad_maximum_fusion.4), channel_id=1, source_target_pairs={{0,1},{1,0},{2,3},{3,2},{4,5},{5,4},{6,7},{7,6},{8,9},{9,8},{10,11... | collective-permute-start | bytes 3145736 | tf_op jit(solution)/shard_map/ppermute | solution.py:287
  513.6 48.8 %collective-permute-start.23 = (bf16[512,1024]{1,0:T(8,128)(2,1)}, bf16[512,1024]{1,0:T(8,128)(2,1)S(1)}, u32[]{:S(2)}, u32[]{:S(2)}) collective-permute-start(bf16[512,1024]{1,0:T(8,128)(2,1)} %concatenate.113), channel_id=1, source_target_pairs={{0,8},{4,12},{8,0},{12,4},{16,24},{20,28},{24,16},{28,20},{1,9},{5... | collective-permute-start | bytes 3145736 | tf_op jit(solution)/shard_map/ppermute | solution.py:281
  541.5 261.9 %reduce-scatter.9.cloned.1.call-start = ((), (), s32[]{:S(2)}) async-start(), calls=%async_computation.8 | async-start | bytes 2359296 | tf_op jit(solution)/shard_map/reduce_scatter | solution.py:503
  575.2 27.2 %collective-permute-start.26 = (bf16[1024,2048]{1,0:T(8,128)(2,1)S(1)}, bf16[1024,2048]{1,0:T(8,128)(2,1)}, u32[]{:S(2)}, u32[]{:S(2)}) collective-permute-start(bf16[1024,2048]{1,0:T(8,128)(2,1)S(1)} %fusion.16), channel_id=1, source_target_pairs={{0,2},{2,0},{1,3},{3,1},{4,6},{6,4},{5,7},{7,5},{8,10},{10,8},{9,1... | collective-permute-start | bytes 12582920 | tf_op jit(solution)/shard_map/ppermute | solution.py:284
  578.1 22.2 %collective-permute-start.22 = (bf16[256,1024]{1,0:T(8,128)(2,1)S(1)}, bf16[256,1024]{1,0:T(8,128)(2,1)S(1)}, u32[]{:S(2)}, u32[]{:S(2)}) collective-permute-start(bf16[256,1024]{1,0:T(8,128)(2,1)S(1)} %fusion.40), channel_id=1, source_target_pairs={{0,8},{4,12},{8,0},{12,4},{16,24},{20,28},{24,16},{28,20},{1,9},{5... | collective-permute-start | bytes 1572872 | tf_op jit(solution)/shard_map/ppermute | solution.py:281
  618.0 25.3 %collective-permute-start.27 = (bf16[512,1024]{1,0:T(8,128)(2,1)S(1)}, bf16[512,1024]{1,0:T(8,128)(2,1)S(1)}, u32[]{:S(2)}, u32[]{:S(2)}) collective-permute-start(bf16[512,1024]{1,0:T(8,128)(2,1)S(1)} %pad_maximum_fusion.5), channel_id=1, source_target_pairs={{0,1},{1,0},{2,3},{3,2},{4,5},{5,4},{6,7},{7,6},{8,9},{9,8},{10,11... | collective-permute-start | bytes 3145736 | tf_op jit(solution)/shard_map/ppermute | solution.py:287
  620.1 51.1 %collective-permute-start.29 = (bf16[512,1024]{1,0:T(8,128)(2,1)S(1)}, bf16[512,1024]{1,0:T(8,128)(2,1)S(1)}, u32[]{:S(2)}, u32[]{:S(2)}) collective-permute-start(bf16[512,1024]{1,0:T(8,128)(2,1)S(1)} %concatenate.114), channel_id=1, source_target_pairs={{0,8},{4,12},{8,0},{12,4},{16,24},{20,28},{24,16},{28,20},{1,9},{5... | collective-permute-start | bytes 3145736 | tf_op jit(solution)/shard_map/ppermute | solution.py:281
  643.7 39.3 %collective-permute-start.28 = (bf16[256,1024]{1,0:T(8,128)(2,1)S(1)}, bf16[256,1024]{1,0:T(8,128)(2,1)S(1)}, u32[]{:S(2)}, u32[]{:S(2)}) collective-permute-start(bf16[256,1024]{1,0:T(8,128)(2,1)S(1)} %fusion.36), channel_id=1, source_target_pairs={{0,8},{4,12},{8,0},{12,4},{16,24},{20,28},{24,16},{28,20},{1,9},{5... | collective-permute-start | bytes 1572872 | tf_op jit(solution)/shard_map/ppermute | solution.py:281
  699.8 24.2 %collective-permute-start.31 = (bf16[256,2048]{1,0:T(8,128)(2,1)S(1)}, bf16[256,2048]{1,0:T(8,128)(2,1)}, u32[]{:S(2)}, u32[]{:S(2)}) collective-permute-start(bf16[256,2048]{1,0:T(8,128)(2,1)S(1)} %get-tuple-element.67), channel_id=1, source_target_pairs={{0,1},{1,0},{2,3},{3,2},{4,5},{5,4},{6,7},{7,6},{8,9},{9,8},{10,11... | collective-permute-start | bytes 3145736 | tf_op jit(solution)/shard_map/ppermute | solution.py:287
  735.6 209.3 %reduce-scatter.11.cloned.1.call-start = ((), (), s32[]{:S(2)}) async-start(), calls=%async_computation.9 | async-start | bytes 7077888 | tf_op jit(solution)/shard_map/reduce_scatter | solution.py:503
  738.0 48.3 %collective-permute-start.33 = (bf16[256,2048]{1,0:T(8,128)(2,1)}, bf16[256,2048]{1,0:T(8,128)(2,1)S(1)}, u32[]{:S(2)}, u32[]{:S(2)}) collective-permute-start(bf16[256,2048]{1,0:T(8,128)(2,1)} %constant_dynamic-slice_fusion.1), channel_id=1, source_target_pairs={{0,8},{4,12},{8,0},{12,4},{16,24},{20,28},{24,16},{28,20},{1,9},{5... | collective-permute-start | bytes 3145736 | tf_op jit(solution)/shard_map/ppermute | solution.py:281
  820.9 26.3 %collective-permute-start.35 = (bf16[256,2048]{1,0:T(8,128)(2,1)}, bf16[256,2048]{1,0:T(8,128)(2,1)}, u32[]{:S(2)}, u32[]{:S(2)}) collective-permute-start(bf16[256,2048]{1,0:T(8,128)(2,1)} %fusion.29), channel_id=1, source_target_pairs={{0,1},{1,0},{2,3},{3,2},{4,5},{5,4},{6,7},{7,6},{8,9},{9,8},{10,11... | collective-permute-start | bytes 3145736 | tf_op jit(solution)/shard_map/ppermute | solution.py:287
  824.0 51.8 %collective-permute-start.43 = (bf16[256,1024]{1,0:T(8,128)(2,1)}, bf16[256,1024]{1,0:T(8,128)(2,1)}, u32[]{:S(2)}, u32[]{:S(2)}) collective-permute-start(bf16[256,1024]{1,0:T(8,128)(2,1)} %constant_dynamic-slice_fusion), channel_id=1, source_target_pairs={{0,8},{4,12},{8,0},{12,4},{16,24},{20,28},{24,16},{28,20},{1,9},{5... | collective-permute-start | bytes 1572872 | tf_op jit(solution)/shard_map/ppermute | solution.py:281
  824.0 61.3 %collective-permute-start.25 = (bf16[256,2048]{1,0:T(8,128)(2,1)}, bf16[256,2048]{1,0:T(8,128)(2,1)}, u32[]{:S(2)}, u32[]{:S(2)}) collective-permute-start(bf16[256,2048]{1,0:T(8,128)(2,1)} %get-tuple-element.89.own_ref), channel_id=1, source_target_pairs={{0,1},{1,0},{2,3},{3,2},{4,5},{5,4},{6,7},{7,6},{8,9},{9,8},{10,11... | collective-permute-start | bytes 3145736 | tf_op jit(solution)/shard_map/ppermute | solution.py:287
  828.1 60.9 %collective-permute-start.42 = (bf16[128,4096]{1,0:T(8,128)(2,1)}, bf16[128,4096]{1,0:T(8,128)(2,1)}, u32[]{:S(2)}, u32[]{:S(2)}) collective-permute-start(bf16[128,4096]{1,0:T(8,128)(2,1)} %shard_map.214), channel_id=1, source_target_pairs={{0,2},{2,0},{1,3},{3,1},{4,6},{6,4},{5,7},{7,5},{8,10},{10,8},{9,1... | collective-permute-start | bytes 3145736 | tf_op jit(solution)/shard_map/ppermute | solution.py:284
  871.5 24.5 %collective-permute-start.36 = (bf16[256,2048]{1,0:T(8,128)(2,1)S(1)}, bf16[256,2048]{1,0:T(8,128)(2,1)S(1)}, u32[]{:S(2)}, u32[]{:S(2)}) collective-permute-start(bf16[256,2048]{1,0:T(8,128)(2,1)S(1)} %add_convert_fusion.own_ref), channel_id=1, source_target_pairs={{0,1},{1,0},{2,3},{3,2},{4,5},{5,4},{6,7},{7,6},{8,9},{9,8},{10,11... | collective-permute-start | bytes 3145736 | tf_op jit(solution)/shard_map/ppermute | solution.py:287
  (58 other events, 903.2 us)
Sparse Core Ops, SparseCore 0:
  15.7 181.5 all-gather.2
  199.1 223.5 all-gather.4
  477.6 86.2 reduce-scatter.6
  566.8 153.5 reduce-scatter.4
  735.7 67.5 reduce-scatter.8
  805.5 139.2 reduce-scatter.10
